TPU v7x, 32 devices: a whole 2x2x4 slice. The times are simulated.
32 devices in a mesh: fsdp: 2 (over y), ctx: 4 (over z), tp: 4 (over x, core).
Axes of the slice: x: 2, y: 2, z: 4, core: 2. Of those that a mesh axis runs over, the one named last changes fastest.
Arguments:
- tokens: bfloat16 [8, 1024, 1024], P('fsdp', 'ctx'), may hold values from -6 to 6
- first_values: bfloat16 [8, 1024, 1024], P('fsdp', 'ctx', 'tp'), may hold values from -6 to 6
- out_grad: bfloat16 [8, 1024, 1024], P('fsdp', 'ctx'), may hold values from -6 to 6
- w_qkv: bfloat16 [1024, 3, 1024], P('fsdp', None, 'tp'), may hold values from -0.1875 to 0.1875
- output_weight: bfloat16 [1024, 1024], P('tp', 'fsdp'), may hold values from -1.5 to 1.5
- w_gate: bfloat16 [1024, 2816], P('fsdp', 'tp'), may hold values from -0.1875 to 0.1875
- w_up: bfloat16 [1024, 2816], P('fsdp', 'tp'), may hold values from -0.1875 to 0.1875
- w_down: bfloat16 [2816, 1024], P('tp', 'fsdp'), may hold values from -0.109375 to 0.109375
- gain_attn: bfloat16 [1024], P('fsdp'), may hold values from 0.5 to 1.5
- gain_mlp: bfloat16 [1024], P('fsdp'), may hold values from 0.5 to 1.5
- mix: float32 [16], P('tp'), may hold values from 0.3 to 0.7
Outputs:
- output: bfloat16 [8, 1024, 1024], P('fsdp', 'ctx')
- grad_tokens: float32 [8, 1024, 1024], P('fsdp', 'ctx')
- grad_first: float32 [8, 1024, 1024], P('fsdp', 'ctx', 'tp')
- grad_w_qkv: float32 [1024, 3, 1024], P('fsdp', None, 'tp')
- grad_w_out: float32 [1024, 1024], P('tp', 'fsdp')
- grad_w_gate: float32 [1024, 2816], P('fsdp', 'tp')
- grad_w_up: float32 [1024, 2816], P('fsdp', 'tp')
- grad_w_down: float32 [2816, 1024], P('tp', 'fsdp')
- grad_gain_attn: float32 [1024], P('fsdp')
- grad_gain_mlp: float32 [1024], P('fsdp')
- grad_mix: float32 [16], P('tp')
All inputs are finite; a program needn't handle non-finite values.
Results may differ from a plain program's by a relative error of at most 0.019.
Values may be sent and summed in bfloat16 or wider, within the bound.
No kernel may reach another device: no remote copies, remote signals or barrier semaphores. Data moves between devices by JAX's collectives and lax.ppermute only.
A program may use at most 128 MiB of HBM per device.

v0:
```python
import jax
import jax.numpy as jnp
from jax import lax
from jax.sharding import PartitionSpec as P

EPSILON = 1e-06
SCORE_SCALE = 0.125
MASKED = -1e30


def norm_rows(values, gain_vec):
    inverse = lax.rsqrt(jnp.mean(values * values, axis=-1, keepdims=True) + EPSILON)
    return (values * inverse * gain_vec, inverse)


def norm_back(grad_normed, values, inverse, gain_vec):
    weighted = grad_normed * gain_vec
    grad_gain = jnp.sum(grad_normed * values * inverse, axis=0)
    grad_values = inverse * weighted - values * inverse**3 * jnp.mean(
        weighted * values, axis=-1, keepdims=True
    )
    return (grad_values, grad_gain)


def rotate(values, cosine, sine_table):
    half_size = values.shape[-1] // 2
    first_half, second_half = (values[..., :half_size], values[..., half_size:])
    return jnp.concatenate(
        [
            first_half * cosine - second_half * sine_table,
            second_half * cosine + first_half * sine_table,
        ],
        axis=-1,
    )


def rotate_back(grads, cosine, sine_table):
    half_size = grads.shape[-1] // 2
    first_half, second_half = (grads[..., :half_size], grads[..., half_size:])
    return jnp.concatenate(
        [
            first_half * cosine + second_half * sine_table,
            second_half * cosine - first_half * sine_table,
        ],
        axis=-1,
    )


def heads_sum(partial_sum):
    return lax.psum(partial_sum, "tp")


def on_device(
    tokens,
    first_values,
    out_grad,
    w_qkv,
    output_weight,
    w_gate,
    w_up,
    w_down,
    gain_attn,
    gain_mlp,
    mix,
):
    seq_count, block_len, width = tokens.shape
    heads_here = mix.shape[0]
    local_width = w_qkv.shape[2]
    head_size = local_width // heads_here
    half_size = head_size // 2
    row_count = seq_count * block_len
    shape_heads = (seq_count, block_len, heads_here, head_size)
    all_qkv, all_out, all_gate, all_up, all_down, full_gain_attn, full_gain_mlp = (
        lax.all_gather(w_qkv, "fsdp", axis=0, tiled=True),
        lax.all_gather(output_weight, "fsdp", axis=1, tiled=True),
        lax.all_gather(w_gate, "fsdp", axis=0, tiled=True),
        lax.all_gather(w_up, "fsdp", axis=0, tiled=True),
        lax.all_gather(w_down, "fsdp", axis=1, tiled=True),
        lax.all_gather(gain_attn, "fsdp", axis=0, tiled=True),
        lax.all_gather(gain_mlp, "fsdp", axis=0, tiled=True),
    )
    gain_first = full_gain_attn.astype(jnp.float32)
    gain_second = full_gain_mlp.astype(jnp.float32)
    block_start = lax.axis_index("ctx") * block_len
    positions = (block_start + jnp.arange(block_len)).astype(jnp.float32)
    frequency = 10000.0 ** (-jnp.arange(half_size).astype(jnp.float32) / half_size)
    table = positions[:, None] * frequency[None, :]
    cosine = jnp.cos(table)[None, :, None, :]
    sine_table = jnp.sin(table)[None, :, None, :]
    inputs = tokens.reshape(row_count, width).astype(jnp.float32)
    normed, inverse_first = norm_rows(inputs, gain_first)
    normed_low = normed.astype(jnp.bfloat16)
    projected = jnp.einsum("rd,dkc->rkc", normed_low, all_qkv, preferred_element_type=jnp.float32)
    query_raw = projected[:, 0].reshape(shape_heads)
    key_raw = projected[:, 1].reshape(shape_heads)
    value_raw = projected[:, 2].reshape(shape_heads)
    queries = rotate(query_raw, cosine, sine_table).astype(jnp.bfloat16)
    key_local = rotate(key_raw, cosine, sine_table).astype(jnp.bfloat16)
    mixture_portion = mix[None, None, :, None]
    first_float = first_values.reshape(shape_heads).astype(jnp.float32)
    value_local = (mixture_portion * value_raw + (1.0 - mixture_portion) * first_float).astype(
        jnp.bfloat16
    )
    key_all, value_all = (
        lax.all_gather(key_local, "ctx", axis=1, tiled=True),
        lax.all_gather(value_local, "ctx", axis=1, tiled=True),
    )
    seq_length = key_all.shape[1]
    visible = jnp.arange(seq_length) < block_start + block_len

    def scores_of(key_rows):
        raw_scores = (
            jnp.einsum("sqhc,skhc->shqk", queries, key_rows, preferred_element_type=jnp.float32)
            * SCORE_SCALE
        )
        return jnp.where(visible, raw_scores, MASKED)

    scores = scores_of(key_all)
    top_score = jnp.max(scores, axis=-1, keepdims=True)
    exp_scores = jnp.exp(scores - top_score)
    row_total = jnp.sum(exp_scores, axis=-1, keepdims=True)
    attn_probs = exp_scores / row_total
    log_total = top_score + jnp.log(row_total)
    attention_result = jnp.einsum(
        "shqk,skhc->sqhc",
        attn_probs.astype(jnp.bfloat16),
        value_all,
        preferred_element_type=jnp.float32,
    ).astype(jnp.bfloat16)
    attended_rows = attention_result.reshape(row_count, local_width)
    branch_term = jnp.dot(attended_rows, all_out, preferred_element_type=jnp.float32)
    residual = inputs + heads_sum(branch_term)
    normed_mlp, inverse_second = norm_rows(residual, gain_second)
    normed_mlp_low = normed_mlp.astype(jnp.bfloat16)
    gate_proj = jnp.dot(normed_mlp_low, all_gate, preferred_element_type=jnp.float32)
    up_proj = jnp.dot(normed_mlp_low, all_up, preferred_element_type=jnp.float32)
    gate_sigmoid = jax.nn.sigmoid(gate_proj)
    gate_active = gate_proj * gate_sigmoid
    hidden = (gate_active * up_proj).astype(jnp.bfloat16)
    down_term = jnp.dot(hidden, all_down, preferred_element_type=jnp.float32)
    grad_rows = out_grad.reshape(row_count, width)
    grad_hidden = jnp.einsum("rd,fd->rf", grad_rows, all_down, preferred_element_type=jnp.float32)
    grad_w_down = jnp.einsum("rf,rd->fd", hidden, grad_rows, preferred_element_type=jnp.float32)
    grad_gate_low = (
        grad_hidden * up_proj * gate_sigmoid * (1.0 + gate_proj * (1.0 - gate_sigmoid))
    ).astype(jnp.bfloat16)
    grad_up_low = (grad_hidden * gate_active).astype(jnp.bfloat16)
    grad_w_gate = jnp.einsum(
        "rd,rf->df", normed_mlp_low, grad_gate_low, preferred_element_type=jnp.float32
    )
    grad_w_up = jnp.einsum(
        "rd,rf->df", normed_mlp_low, grad_up_low, preferred_element_type=jnp.float32
    )
    grad_mlp_term = jnp.einsum(
        "rf,df->rd", grad_gate_low, all_gate, preferred_element_type=jnp.float32
    ) + jnp.einsum("rf,df->rd", grad_up_low, all_up, preferred_element_type=jnp.float32)
    output = (
        (residual + heads_sum(down_term)).astype(jnp.bfloat16).reshape(seq_count, block_len, width)
    )
    gradient_mlp_normalized = heads_sum(grad_mlp_term)
    grad_resid_norm, grad_gain_second = norm_back(
        gradient_mlp_normalized, residual, inverse_second, gain_second
    )
    grad_residual = grad_rows.astype(jnp.float32) + grad_resid_norm
    grad_branch_low = grad_residual.astype(jnp.bfloat16)
    grad_w_out = jnp.einsum(
        "rc,rd->cd", attended_rows, grad_branch_low, preferred_element_type=jnp.float32
    )
    grad_attended = (
        jnp.einsum("rd,cd->rc", grad_branch_low, all_out, preferred_element_type=jnp.float32)
        .astype(jnp.bfloat16)
        .reshape(shape_heads)
    )
    back_probs = jnp.exp(scores_of(key_all) - log_total)
    grad_probs = jnp.einsum(
        "sqhc,skhc->shqk", grad_attended, value_all, preferred_element_type=jnp.float32
    )
    row_dot = jnp.sum(back_probs * grad_probs, axis=-1, keepdims=True)
    grad_scores = (back_probs * (grad_probs - row_dot)).astype(jnp.bfloat16)
    grad_queries = (
        jnp.einsum("shqk,skhc->sqhc", grad_scores, key_all, preferred_element_type=jnp.float32)
        * SCORE_SCALE
    )
    grad_keys_all = (
        jnp.einsum("shqk,sqhc->skhc", grad_scores, queries, preferred_element_type=jnp.float32)
        * SCORE_SCALE
    )
    grad_values_all = jnp.einsum(
        "shqk,sqhc->skhc",
        back_probs.astype(jnp.bfloat16),
        grad_attended,
        preferred_element_type=jnp.float32,
    )
    grad_key_block, grad_value_block = (
        lax.psum_scatter(
            grad_keys_all.astype(jnp.bfloat16), "ctx", scatter_dimension=1, tiled=True
        ).astype(jnp.float32),
        lax.psum_scatter(
            grad_values_all.astype(jnp.bfloat16), "ctx", scatter_dimension=1, tiled=True
        ).astype(jnp.float32),
    )
    grad_query_low = (
        rotate_back(grad_queries, cosine, sine_table)
        .astype(jnp.bfloat16)
        .reshape(row_count, local_width)
    )
    grad_key_low = (
        rotate_back(grad_key_block, cosine, sine_table)
        .astype(jnp.bfloat16)
        .reshape(row_count, local_width)
    )
    grad_value_low = (
        (mixture_portion * grad_value_block).astype(jnp.bfloat16).reshape(row_count, local_width)
    )
    grad_first = ((1.0 - mixture_portion) * grad_value_block).reshape(
        seq_count, block_len, local_width
    )
    grad_mix_here = jnp.sum(grad_value_block * (value_raw - first_float), axis=(0, 1, 3))
    grad_proj = jnp.stack([grad_query_low, grad_key_low, grad_value_low], axis=1)
    grad_w_qkv = jnp.einsum(
        "rd,rkc->dkc", normed_low, grad_proj, preferred_element_type=jnp.float32
    )
    grad_normed = heads_sum(
        jnp.einsum("rkc,dkc->rd", grad_proj, all_qkv, preferred_element_type=jnp.float32)
    )
    grad_input_norm, grad_gain_first = norm_back(grad_normed, inputs, inverse_first, gain_first)
    grad_tokens = (grad_residual + grad_input_norm).reshape(seq_count, block_len, width)
    grad_weights = (
        grad_w_qkv,
        grad_w_out,
        grad_w_gate,
        grad_w_up,
        grad_w_down,
        grad_gain_first,
        grad_gain_second,
    )
    shard_sums = (
        lax.psum_scatter(
            grad_weights[0].astype(jnp.bfloat16), "fsdp", scatter_dimension=0, tiled=True
        ).astype(jnp.float32),
        lax.psum_scatter(
            grad_weights[1].astype(jnp.bfloat16), "fsdp", scatter_dimension=1, tiled=True
        ).astype(jnp.float32),
        lax.psum_scatter(
            grad_weights[2].astype(jnp.bfloat16), "fsdp", scatter_dimension=0, tiled=True
        ).astype(jnp.float32),
        lax.psum_scatter(
            grad_weights[3].astype(jnp.bfloat16), "fsdp", scatter_dimension=0, tiled=True
        ).astype(jnp.float32),
        lax.psum_scatter(
            grad_weights[4].astype(jnp.bfloat16), "fsdp", scatter_dimension=1, tiled=True
        ).astype(jnp.float32),
        lax.psum_scatter(
            grad_weights[5].astype(jnp.bfloat16), "fsdp", scatter_dimension=0, tiled=True
        ).astype(jnp.float32),
        lax.psum_scatter(
            grad_weights[6].astype(jnp.bfloat16), "fsdp", scatter_dimension=0, tiled=True
        ).astype(jnp.float32),
    )
    shard_sums = (
        lax.psum(shard_sums[0].astype(jnp.bfloat16), "ctx").astype(jnp.float32),
        lax.psum(shard_sums[1].astype(jnp.bfloat16), "ctx").astype(jnp.float32),
        lax.psum(shard_sums[2].astype(jnp.bfloat16), "ctx").astype(jnp.float32),
        lax.psum(shard_sums[3].astype(jnp.bfloat16), "ctx").astype(jnp.float32),
        lax.psum(shard_sums[4].astype(jnp.bfloat16), "ctx").astype(jnp.float32),
        lax.psum(shard_sums[5].astype(jnp.bfloat16), "ctx").astype(jnp.float32),
        lax.psum(shard_sums[6].astype(jnp.bfloat16), "ctx").astype(jnp.float32),
    )
    grad_mix = lax.psum(grad_mix_here, ("fsdp", "ctx"))
    return (
        output,
        grad_tokens,
        grad_first,
        shard_sums[0],
        shard_sums[1],
        shard_sums[2],
        shard_sums[3],
        shard_sums[4],
        shard_sums[5],
        shard_sums[6],
        grad_mix,
    )


def solution(mesh):
    in_specs = (
        P("fsdp", "ctx", None),
        P("fsdp", "ctx", "tp"),
        P("fsdp", "ctx", None),
        P("fsdp", None, "tp"),
        P("tp", "fsdp"),
        P("fsdp", "tp"),
        P("fsdp", "tp"),
        P("tp", "fsdp"),
        P("fsdp"),
        P("fsdp"),
        P("tp"),
    )
    out_specs = (
        P("fsdp", "ctx", None),
        P("fsdp", "ctx", None),
        P("fsdp", "ctx", "tp"),
        P("fsdp", None, "tp"),
        P("tp", "fsdp"),
        P("fsdp", "tp"),
        P("fsdp", "tp"),
        P("tp", "fsdp"),
        P("fsdp"),
        P("fsdp"),
        P("tp"),
    )
    return jax.shard_map(
        on_device, mesh=mesh, in_specs=in_specs, out_specs=out_specs, check_vma=False
    )
```

profile of v0, /device:TPU:0, one launch (start us, length us, event | category | flops | bytes accessed | tf_op | source)
XLA Modules:
  0.0 1001.9 jit_solution(3692615902448458771)
XLA Ops:
  8.7 5.3 all-gather
  18.2 21.3 %all-gather.9.cloned.1.call-done = bf16[1024,3,256]{2,0,1:T(8,128)(2,1)} async-done(((bf16[512,3,256]{2,0,1:T(8,128)(2,1)}), bf16[1024,3,256]{2,0,1:T(8,128)(2,1)}) %all-gather.9.cloned.1.call-update) | async-done | bytes 1572880 | tf_op jit(solution)/shard_map/all_gather | solution.py:74
  39.5 3.8 fusion.18
  44.9 3.0 reshape.219
  47.9 3.1 reshape.220
  51.0 5.5 fusion.37
  56.5 2.6 copy.96
  59.0 2.6 copy.95
  61.6 5.4 fusion.36
  67.0 2.6 copy.94
  69.5 2.6 copy.93
  72.1 2.6 subtract_convert_fusion.3
  75.6 2.2 copy.57
  82.0 2.3 add_convert_fusion.1
  84.4 9.5 all_gather.31
  94.0 28.0 %all-gather.13.cloned.1.call-done = bf16[4,1024,4,64]{1,3,2,0:T(8,128)(2,1)} async-done(((bf16[4,256,4,64]{1,3,2,0:T(8,128)(2,1)}), bf16[4,1024,4,64]{1,3,2,0:T(8,128)(2,1)}) %all-gather.13.cloned.1.call-update) | async-done | bytes 2097168 | tf_op jit(solution)/shard_map/all_gather | solution.py:105
  122.0 4.6 fusion.38
  126.6 6.1 copy-done
  132.6 3.7 fusion
  136.3 32.3 %all-gather.11.cloned.1.call-done = bf16[4,1024,4,64]{1,3,2,0:T(8,128)(2,1)} async-done(((bf16[4,256,4,64]{1,3,2,0:T(8,128)(2,1)}), bf16[4,1024,4,64]{1,3,2,0:T(8,128)(2,1)}) %all-gather.11.cloned.1.call-update) | async-done | bytes 2097168 | tf_op jit(solution)/shard_map/all_gather | solution.py:106
  168.6 8.3 fusion.28
  178.2 2.8 fusion.39
  183.0 4.4 all-gather.1
  187.4 77.4 %all-reduce.11.cloned.1.call-done = f32[1024,1024]{1,0:T(8,128)} async-done(((f32[1024,1024]{1,0:T(8,128)}), f32[1024,1024]{1,0:T(8,128)}) %all-reduce.11.cloned.1.call-update) | async-done | bytes 4194320 | tf_op jit(solution)/shard_map/psum | solution.py:50
  264.8 2.8 multiply_reduce_fusion.3
  270.1 22.0 %all-gather.17.cloned.1.call-done = bf16[1024,704]{0,1:T(8,128)(2,1)} async-done(((bf16[512,704]{0,1:T(8,128)(2,1)}), bf16[1024,704]{0,1:T(8,128)(2,1)}) %all-gather.17.cloned.1.call-update) | async-done | bytes 1441808 | tf_op jit(solution)/shard_map/all_gather | solution.py:77
  292.1 4.6 fusion.41
  296.7 22.5 %all-gather.15.cloned.1.call-done = bf16[1024,704]{0,1:T(8,128)(2,1)} async-done(((bf16[512,704]{0,1:T(8,128)(2,1)}), bf16[1024,704]{0,1:T(8,128)(2,1)}) %all-gather.15.cloned.1.call-update) | async-done | bytes 1441808 | tf_op jit(solution)/shard_map/all_gather | solution.py:76
  319.2 4.6 fusion.40
  323.9 22.7 %all-gather.19.cloned.1.call-done = bf16[704,1024]{1,0:T(8,128)(2,1)} async-done(((bf16[704,512]{1,0:T(8,128)(2,1)}), bf16[704,1024]{1,0:T(8,128)(2,1)}) %all-gather.19.cloned.1.call-update) | async-done | bytes 1441808 | tf_op jit(solution)/shard_map/all_gather | solution.py:78
  346.5 7.6 multiply_convert_fusion.3
  356.6 3.9 convolution_add_fusion
  360.5 8.4 reduce-scatter.8.cloned.1.call-start
  369.6 76.6 %all-reduce.13.cloned.1.call-done = f32[1024,1024]{1,0:T(8,128)} async-done(((f32[1024,1024]{1,0:T(8,128)}), f32[1024,1024]{1,0:T(8,128)}) %all-reduce.13.cloned.1.call-update) | async-done | bytes 4194320 | tf_op jit(solution)/shard_map/psum | solution.py:50
  446.2 4.6 multiply_reduce_fusion.1
  458.1 15.2 %multiply_reduce_fusion = (f32[4,4,256]{2,1,0:T(4,128)}, f32[4,4,256,1024]{3,2,1,0:T(8,128)}) fusion(f32[4,4,256,1024]{3,2,1,0:T(8,128)} %copy-done, f32[4,4,256]{2,1,0:T(4,128)} %bitcast.113, bf16[4,256,4,64]{1,3,2,0:T(8,128)(2,1)} %copy.66, bf16[4,1024,4,64]{1,3,2,0:T(8,128)(2,1)} %all-gather.11.cloned.1.call-done), kind=kOutput, calls=%fused_computation.1 | convolution fusion | flops 549449728 | bytes 36208640 | tf_op jit(solution)/shard_map/sqhc,skhc->shqk/dot_general | solution.py:175
  475.3 7.7 multiply_convert_fusion
  483.1 3.3 copy-done.3
  486.4 2.9 fusion.25
  489.4 9.1 convert_bitcast_fusion
  498.6 4.9 convolution_convert_fusion.1
  503.6 4.1 convolution_convert_fusion
  508.0 4.8 convolution_convert_fusion.2
  512.9 4.0 convolution_convert_fusion.3
  517.0 7.1 fusion.26
  524.1 9.2 reduce-scatter.8.cloned.1.call-done
  534.4 43.8 %reduce-scatter.10.cloned.1.call-done = bf16[4,256,4,64]{1,3,2,0:T(8,128)(2,1)} async-done(((bf16[4,1024,4,64]{1,3,2,0:T(8,128)(2,1)}), bf16[4,256,4,64]{1,3,2,0:T(8,128)(2,1)}) %reduce-scatter.10.cloned.1.call-update) | async-done | bytes 524304 | tf_op jit(solution)/shard_map/reduce_scatter | solution.py:198
  578.2 3.5 fusion.30
  590.8 3.1 fusion.22
  594.2 5.8 fusion.42
  600.0 3.8 convolution_bitcast_fusion
  605.0 27.4 %reduce-scatter.18.cloned.1.call-done = bf16[512,704]{0,1:T(8,128)(2,1)} async-done(((bf16[1024,704]{0,1:T(8,128)(2,1)}), bf16[512,704]{0,1:T(8,128)(2,1)}) %reduce-scatter.18.cloned.1.call-update) | async-done | bytes 720912 | tf_op jit(solution)/shard_map/reduce_scatter | solution.py:247
  632.4 27.0 %reduce-scatter.20.cloned.1.call-done = bf16[704,512]{1,0:T(8,128)(2,1)} async-done(((bf16[704,1024]{1,0:T(8,128)(2,1)}), bf16[704,512]{1,0:T(8,128)(2,1)}) %reduce-scatter.20.cloned.1.call-update) | async-done | bytes 720912 | tf_op jit(solution)/shard_map/reduce_scatter | solution.py:250
  659.4 16.8 %reduce-scatter.14.cloned.1.call-done = bf16[256,512]{1,0:T(8,128)(2,1)} async-done(((bf16[256,1024]{1,0:T(8,128)(2,1)}), bf16[256,512]{1,0:T(8,128)(2,1)}) %reduce-scatter.14.cloned.1.call-update) | async-done | bytes 262160 | tf_op jit(solution)/shard_map/reduce_scatter | solution.py:241
  676.1 28.8 %reduce-scatter.12.cloned.1.call-done = bf16[512,3,256]{2,0,1:T(8,128)(2,1)} async-done(((bf16[1024,3,256]{2,0,1:T(8,128)(2,1)}), bf16[512,3,256]{2,0,1:T(8,128)(2,1)}) %reduce-scatter.12.cloned.1.call-update) | async-done | bytes 786448 | tf_op jit(solution)/shard_map/reduce_scatter | solution.py:238
  706.3 21.0 %psum.95 = f32[4]{0:T(128)} all-reduce(f32[4]{0:T(128)S(1)} %copy-done.39), channel_id=1, replica_groups=mesh['fsdp'=2,'ctx'=4,'tp'=4] {'fsdp','ctx'}, use_global_device_ids=true, to_apply=%region_30.31 | all-reduce | flops 4 | bytes 32 | tf_op jit(solution)/shard_map/psum | solution.py:269
  728.6 131.7 %all-reduce.15.cloned.1.call-done = (f32[1024,1024]{1,0:T(8,128)}, f32[1024,1024]{1,0:T(8,128)}) async-done(((f32[1024,1024]{1,0:T(8,128)}, f32[1024,1024]{1,0:T(8,128)}), (f32[1024,1024]{1,0:T(8,128)}, f32[1024,1024]{1,0:T(8,128)})) %all-reduce.15.cloned.1.call-update) | async-done | bytes 8388624 | tf_op jit(solution)/shard_map/psum | solution.py:50
  860.3 3.5 fusion.14
  863.9 4.9 all-reduce.5
  868.9 12.3 %all-reduce.3 = (bf16[512]{0:T(512)(128)(2,1)S(1)}, bf16[512]{0:T(512)(128)(2,1)S(1)}) all-reduce(bf16[512]{0:T(512)(128)(2,1)S(1)} %dynamic-slice.1, bf16[512]{0:T(512)(128)(2,1)S(1)} %dynamic-slice.3), channel_id=1, replica_groups=mesh['fsdp'=2,'ctx'=4,'tp'=4] {'ctx'}, use_global_device_ids=true, to_apply=%region_25.26 | all-reduce | flops 1024 | bytes 4096 | tf_op jit(solution)/shard_map/psum | solution.py:266
  882.4 5.7 add_convert_fusion
  889.2 2.6 fusion.11
  891.8 94.8 %all-reduce.17.cloned.1.call-done = (bf16[512,3,256]{2,0,1:T(8,128)(2,1)}, bf16[256,512]{1,0:T(8,128)(2,1)}, bf16[512,704]{0,1:T(8,128)(2,1)}, bf16[512,704]{0,1:T(8,128)(2,1)}, bf16[704,512]{1,0:T(8,128)(2,1)}) async-done(((bf16[512,3,256]{2,0,1:T(8,128)(2,1)}, bf16[256,512]{1,0:T(8,128)(2,1)}, bf16[512,704]{0,1:T(8,128)(2,1)}, bf16[512,704]{0,1:T(8,128)(2,1)}, bf16[704,512]{1,0:T(8,128)(2,1)}), ...) | async-done | bytes 3211280 | tf_op jit(solution)/shard_map/psum | solution.py:261
  988.5 2.5 convert_element_type.215
  (185 shorter events, 52.6 us)
Async XLA Ops:
  7.2 9.2 copy-start.6
  7.2 32.3 %all-gather.9.cloned.1.call-start = ((), (), s32[]{:S(2)}) async-start(), calls=%async_computation.7 | async-start | bytes 2359296 | tf_op jit(solution)/shard_map/all_gather | solution.py:74
  7.9 114.1 %all-gather.13.cloned.1.call-start = ((), (), s32[]{:S(2)}) async-start(), calls=%async_computation.9 | async-start | bytes 2621440 | tf_op jit(solution)/shard_map/all_gather | solution.py:105
  14.0 4.2 copy-start.35
  16.1 23.4 %copy-start.33 = (f32[1,2,4,128]{3,1,2,0:T(2,128)}, f32[1,2,4,128]{3,1,2,0:T(2,128)S(1)}, u32[]{:S(2)}) copy-start(f32[1,2,4,128]{3,1,2,0:T(2,128)S(1)} %copy.97) | copy-start | bytes 12292
  16.3 55.8 %copy-start.29 = (f32[256,32]{0,1:T(8,128)}, f32[256,32]{0,1:T(8,128)S(1)}, u32[]{:S(2)}) copy-start(f32[256,32]{0,1:T(8,128)S(1)} %get-tuple-element.88) | copy-start | bytes 98308
  16.3 55.8 %copy-start.30 = (f32[256,32]{0,1:T(8,128)}, f32[256,32]{0,1:T(8,128)S(1)}, u32[]{:S(2)}) copy-start(f32[256,32]{0,1:T(8,128)S(1)} %get-tuple-element.89) | copy-start | bytes 98308
  72.1 5.8 copy-start.37
  75.6 93.0 %all-gather.11.cloned.1.call-start = ((), (), s32[]{:S(2)}) async-start(), calls=%async_computation.8 | async-start | bytes 2621440 | tf_op jit(solution)/shard_map/all_gather | solution.py:106
  80.1 41.9 %copy-start.17 = (bf16[4,256,4,32]{1,3,2,0:T(8,128)(2,1)S(1)}, bf16[4,256,4,32]{1,3,2,0:T(8,128)(2,1)}, u32[]{:S(2)}) copy-start(bf16[4,256,4,32]{1,3,2,0:T(8,128)(2,1)} %get-tuple-element.75) | copy-start | bytes 786436
  84.4 180.4 %all-reduce.11.cloned.1.call-start = ((), (), s32[]{:S(2)}) async-start(), calls=%async_computation.10 | async-start | bytes 8388608 | tf_op jit(solution)/shard_map/psum | solution.py:50
  126.6 6.1 copy-start
  168.6 9.6 copy-start.14
  181.0 2.0 copy-start.38
  181.0 111.1 %all-gather.17.cloned.1.call-start = ((), (), s32[]{:S(2)}) async-start(), calls=%async_computation.12 | async-start | bytes 2162688 | tf_op jit(solution)/shard_map/all_gather | solution.py:77
  181.6 137.6 %all-gather.15.cloned.1.call-start = ((), (), s32[]{:S(2)}) async-start(), calls=%async_computation.11 | async-start | bytes 2162688 | tf_op jit(solution)/shard_map/all_gather | solution.py:76
  182.2 164.3 %all-gather.19.cloned.1.call-start = ((), (), s32[]{:S(2)}) async-start(), calls=%async_computation.13 | async-start | bytes 2162688 | tf_op jit(solution)/shard_map/all_gather | solution.py:78
  182.9 263.3 %all-reduce.13.cloned.1.call-start = ((), (), s32[]{:S(2)}) async-start(), calls=%async_computation.14 | async-start | bytes 8388608 | tf_op jit(solution)/shard_map/psum | solution.py:50
  267.6 2.0 copy-start.1
  270.1 49.2 %copy-start.22 = (bf16[1024,1024]{1,0:T(8,128)(2,1)}, bf16[1024,1024]{1,0:T(8,128)(2,1)S(1)}, u32[]{:S(2)}) copy-start(bf16[1024,1024]{1,0:T(8,128)(2,1)S(1)} %multiply_convert_fusion.2) | copy-start | bytes 6291460
  346.5 7.6 copy-start.42
  354.2 1.9 copy-start.45
  354.2 1.9 copy-start.44
  354.2 2.4 copy-start.41
  360.5 90.3 %copy-start.24 = (bf16[4,256,1024]{2,1,0:T(8,128)(2,1)S(1)}, bf16[4,256,1024]{2,1,0:T(8,128)(2,1)}, u32[]{:S(2)}) copy-start(bf16[4,256,1024]{2,1,0:T(8,128)(2,1)} %param.13) | copy-start | bytes 6291460
  360.5 172.7 %reduce-scatter.8.cloned.1.call-start = ((), (), s32[]{:S(2)}) async-start(), calls=%async_computation.15 | async-start | bytes 2621440 | tf_op jit(solution)/shard_map/reduce_scatter | solution.py:195
  446.2 4.7 copy-start.2
  446.2 5.9 copy-start.8
  452.1 3.6 copy-start.15
  453.6 2.1 copy-start.4
  458.1 15.2 %slice-start = ((s8[16777216]{0:T(1024)(128)(4,1)}), s8[4194304]{0:T(1024)(128)(4,1)S(1)}, s32[]{:S(2)}) async-start(s8[16777216]{0:T(1024)(128)(4,1)} %bitcast.102), calls=%async_computation.24 | async-start | bytes 8388608
  458.1 15.2 %slice-start.1 = ((s8[16777216]{0:T(1024)(128)(4,1)}), s8[4194304]{0:T(1024)(128)(4,1)S(1)}, s32[]{:S(2)}) async-start(s8[16777216]{0:T(1024)(128)(4,1)} %bitcast.102), calls=%async_computation.25 | async-start | bytes 8388608
  458.1 16.0 %slice-start.2 = ((s8[16777216]{0:T(1024)(128)(4,1)}), s8[4194304]{0:T(1024)(128)(4,1)S(1)}, s32[]{:S(2)}) async-start(s8[16777216]{0:T(1024)(128)(4,1)} %bitcast.102), calls=%async_computation.26 | async-start | bytes 8388608
  458.1 17.2 %slice-start.3 = ((s8[16777216]{0:T(1024)(128)(4,1)}), s8[4194304]{0:T(1024)(128)(4,1)S(1)}, s32[]{:S(2)}) async-start(s8[16777216]{0:T(1024)(128)(4,1)} %bitcast.102), calls=%async_computation.27 | async-start | bytes 8388608
  475.3 11.0 %copy-start.18 = (bf16[4,256,4,32]{1,3,2,0:T(8,128)(2,1)S(1)}, bf16[4,256,4,32]{1,3,2,0:T(8,128)(2,1)}, u32[]{:S(2)}) copy-start(bf16[4,256,4,32]{1,3,2,0:T(8,128)(2,1)} %get-tuple-element.75) | copy-start | bytes 786436
  475.3 11.0 %copy-start.19 = (bf16[4,256,4,32]{1,3,2,0:T(8,128)(2,1)S(1)}, bf16[4,256,4,32]{1,3,2,0:T(8,128)(2,1)}, u32[]{:S(2)}) copy-start(bf16[4,256,4,32]{1,3,2,0:T(8,128)(2,1)} %get-tuple-element.76) | copy-start | bytes 786436
  483.1 3.3 copy-start.3
  486.4 3.0 copy-start.13
  486.4 3.0 copy-start.28
  489.3 88.9 %reduce-scatter.10.cloned.1.call-start = ((), (), s32[]{:S(2)}) async-start(), calls=%async_computation.16 | async-start | bytes 2621440 | tf_op jit(solution)/shard_map/reduce_scatter | solution.py:198
  498.5 5.1 copy-start.23
  498.5 106.4 %reduce-scatter.16.cloned.1.call-start = ((), (), s32[]{:S(2)}) async-start(), calls=%async_computation.19 | async-start | bytes 2162688 | tf_op jit(solution)/shard_map/reduce_scatter | solution.py:244
  503.5 128.9 %reduce-scatter.18.cloned.1.call-start = ((), (), s32[]{:S(2)}) async-start(), calls=%async_computation.20 | async-start | bytes 2162688 | tf_op jit(solution)/shard_map/reduce_scatter | solution.py:247
  507.7 151.6 %reduce-scatter.20.cloned.1.call-start = ((), (), s32[]{:S(2)}) async-start(), calls=%async_computation.21 | async-start | bytes 2162688 | tf_op jit(solution)/shard_map/reduce_scatter | solution.py:250
  512.8 4.2 copy-start.10
  512.8 163.3 %reduce-scatter.14.cloned.1.call-start = ((), (), s32[]{:S(2)}) async-start(), calls=%async_computation.18 | async-start | bytes 786432 | tf_op jit(solution)/shard_map/reduce_scatter | solution.py:241
  516.9 188.0 %reduce-scatter.12.cloned.1.call-start = ((), (), s32[]{:S(2)}) async-start(), calls=%async_computation.17 | async-start | bytes 2359296 | tf_op jit(solution)/shard_map/reduce_scatter | solution.py:238
  524.1 57.6 %copy-start.12 = (f32[4,256,4,64]{1,3,2,0:T(8,128)S(1)}, f32[4,256,4,64]{1,3,2,0:T(8,128)}, u32[]{:S(2)}) copy-start(f32[4,256,4,64]{1,3,2,0:T(8,128)} %fusion.26) | copy-start | bytes 3145732
  588.6 2.2 copy-start.21
  593.8 6.1 copy-start.32
  593.8 6.1 copy-start.40
  593.9 266.5 %all-reduce.15.cloned.1.call-start = ((), (), s32[]{:S(2)}) async-start(), calls=%async_computation.22 | async-start | bytes 16777216 | tf_op jit(solution)/shard_map/psum | solution.py:50
  603.8 101.2 %copy-start.43 = (u32[32]{0:T(128)S(1)}, u32[32]{0:T(128)}, u32[]{:S(2)}) copy-start(u32[32]{0:T(128)} %constant.35) | copy-start | bytes 388
  603.8 102.5 %copy-start.34 = (f32[1,2,4,128]{3,1,2,0:T(2,128)S(1)}, f32[1,2,4,128]{3,1,2,0:T(2,128)}, u32[]{:S(2)}) copy-start(f32[1,2,4,128]{3,1,2,0:T(2,128)} %copy-done.33) | copy-start | bytes 12292
  603.8 102.5 %copy-start.39 = (f32[4]{0:T(128)S(1)}, f32[4]{0:T(128)}, u32[]{:S(2)}) copy-start(f32[4]{0:T(128)} %get-tuple-element.79) | copy-start | bytes 52
  603.8 123.5 %copy-start.16 = (f32[4,256,4,64]{1,3,2,0:T(8,128)S(1)}, f32[4,256,4,64]{1,3,2,0:T(8,128)}, u32[]{:S(2)}) copy-start(f32[4,256,4,64]{1,3,2,0:T(8,128)} %get-tuple-element.80) | copy-start | bytes 3145732
  603.8 256.5 %copy-start.7 = (bf16[4,256,1024]{2,1,0:T(8,128)(2,1)S(1)}, bf16[4,256,1024]{2,1,0:T(8,128)(2,1)}, u32[]{:S(2)}) copy-start(bf16[4,256,1024]{2,1,0:T(8,128)(2,1)} %param.11) | copy-start | bytes 6291460
  603.8 256.5 %copy-start.36 = (f32[2,1,512]{2,1,0:T(1,128)S(1)}, f32[2,1,512]{2,1,0:T(1,128)}, u32[]{:S(2)}) copy-start(f32[2,1,512]{2,1,0:T(1,128)} %copy-done.35) | copy-start | bytes 12292
  603.8 382.8 %all-reduce.17.cloned.1.call-start = ((), (), s32[]{:S(2)}) async-start(), calls=%async_computation.23 | async-start | bytes 6422528 | tf_op jit(solution)/shard_map/psum | solution.py:261
  882.4 5.7 copy-start.5
  882.4 6.7 copy-start.9
  986.6 4.4 copy-start.27
  986.6 5.7 copy-start.26
  988.5 5.1 copy-start.25
  (3 other events, 3.8 us)
Sparse Core Ops, SparseCore 0:
  9.5 29.8 all-gather.8
  75.7 46.2 all-gather.12
  124.1 44.4 all-gather.10
  181.1 83.6 all-reduce.10
  266.2 25.8 all-gather.16
  293.5 25.6 all-gather.14
  320.8 25.6 all-gather.18
  360.7 85.4 all-reduce.12
  489.4 43.7 reduce-scatter.7
  535.4 42.8 reduce-scatter.9
  581.0 23.8 reduce-scatter.15
  607.6 24.6 reduce-scatter.17
  634.6 24.6 reduce-scatter.19
  661.5 14.6 reduce-scatter.13
  678.8 26.1 reduce-scatter.11
  707.4 152.8 all-reduce.14
  862.9 123.6 all-reduce.16
where the time goes:
time: 1010 us; the launch traced here: 1000 us
  waiting for transfers between devices  686 us (68%)
  matrix products  108 us (11%)
  local copies, waits for them, and re-layouts  65.3 us (6%)
  other arithmetic  60.1 us (6%)
  blocking collectives  57.5 us (6%)
  between operations  15.7 us (2%)
    psum x3, waiting for transfers between devices, heads_sum(): return lax.psum(partial_sum, 'tp')  286 us
    psum x1, waiting for transfers between devices, on_device(): lax.psum(shard_sums[0].astype(jnp.bfloat16), 'ctx').astype(jnp.float32)  94.8 us
    reduce_scatter x1, waiting for transfers between devices, on_device(): lax.psum_scatter(grad_values_all.astype(jnp.bfloat16), 'ctx', scatter_dim...  43.8 us
    unnamed x114, local copies, waits for them, and re-layouts  34.4 us
    all_gather x1, waiting for transfers between devices, on_device(): lax.all_gather(value_local, 'ctx', axis=1, tiled=True)  32.3 us
    reduce_scatter x1, waiting for transfers between devices, on_device(): lax.psum_scatter(grad_weights[0].astype(jnp.bfloat16), 'fsdp', scatter_di...  28.8 us
    all_gather x1, waiting for transfers between devices, on_device(): lax.all_gather(key_local, 'ctx', axis=1, tiled=True)  28 us
    reduce_scatter x1, waiting for transfers between devices, on_device(): lax.psum_scatter(grad_weights[3].astype(jnp.bfloat16), 'fsdp', scatter_di...  27.4 us
  transfers between devices with their start and end apart: 17, of which 17 were waited for; matrix products, arithmetic and copies ran while one was open for 11% of the time, Pallas kernels for 0%

commit v1 on v0

v1 whole, which is shorter than its diff:
```python
import functools

import jax
import jax.numpy as jnp
from jax import lax
from jax.experimental import pallas as pl
from jax.experimental.pallas import tpu as pltpu
from jax.sharding import PartitionSpec as P

EPSILON = 1e-06
SCALE = 0.125
BF = jnp.bfloat16
F32 = jnp.float32
NN = (((1,), (0,)), ((), ()))
NT = (((1,), (1,)), ((), ()))
TN = (((0,), (0,)), ((), ()))


def dot(a, b, dims=NN):
    return lax.dot_general(a, b, dims, preferred_element_type=F32)


def full(shape):
    return pl.BlockSpec(shape, lambda *_: (0,) * len(shape))


def call(kernel, out_shapes, *args, grid=None, in_specs=None, out_specs=None, scratch=(), flops=0, name=None):
    moved = sum(a.size * a.dtype.itemsize for a in args)
    moved += sum(o.size * o.dtype.itemsize for o in out_shapes)
    keywords = {}
    if grid is not None:
        keywords = dict(grid=grid, in_specs=in_specs, out_specs=out_specs)
    elif in_specs is not None:
        keywords = dict(in_specs=in_specs)
    return pl.pallas_call(
        kernel,
        out_shape=out_shapes,
        scratch_shapes=list(scratch),
        cost_estimate=pl.CostEstimate(flops=flops, bytes_accessed=moved, transcendentals=0),
        compiler_params=pltpu.CompilerParams(vmem_limit_bytes=60 << 20),
        name=name,
        **keywords,
    )(*args)


def shape_of(dims, dtype):
    return jax.ShapeDtypeStruct(dims, dtype)


def half_swap(values, lane):
    width = values.shape[-1]
    ahead = pltpu.roll(values, width - 32, 1)
    behind = pltpu.roll(values, 32, 1)
    return jnp.where(lane % 64 < 32, ahead, behind)


def signed_tables(cos_ref, sin_ref, index, width, lane):
    cosine = jnp.concatenate([cos_ref[index]] * (width // 128), axis=1)
    sine = jnp.concatenate([sin_ref[index]] * (width // 128), axis=1)
    return cosine, jnp.where(lane % 64 < 32, -sine, sine)


def qkv_kernel(seg, p0, p1, p2, p3, gain, wa, wb, fv, cos, sin, mix, normed_o, q_o, k_o, v_o, diff_o):
    x = jnp.concatenate([p0[0], p1[0], p2[0], p3[0]], axis=0).astype(F32)
    half = wa.shape[1]
    inverse = lax.rsqrt(jnp.mean(x * x, axis=-1, keepdims=True) + EPSILON)
    normed = (x * inverse * gain[...]).astype(BF)
    normed_o[0] = normed
    width = wa.shape[2]
    lane = lax.broadcasted_iota(jnp.int32, (1, width), 1)
    cosine, sine = signed_tables(cos, sin, 0, width, lane)
    na, nb = normed[:, :half], normed[:, half:]
    raw = [dot(na, wa[i]) + dot(nb, wb[i]) for i in range(3)]
    q_o[0] = (raw[0] * cosine + half_swap(raw[0], lane) * sine).astype(BF)
    k_o[0] = (raw[1] * cosine + half_swap(raw[1], lane) * sine).astype(BF)
    first = jnp.concatenate([fv[0, seg[r]] for r in range(4)], axis=0).astype(F32)
    v_o[0] = (mix[...] * raw[2] + (1.0 - mix[...]) * first).astype(BF)
    diff_o[0] = (raw[2] - first).astype(BF)


def attend_kernel(q, k, v, woa, wob, att_o, lse_o, keep_o, send_o, v_t, o_t):
    blocks, rows, width = q.shape
    heads = width // 64
    for b in range(blocks):
        v_t[:, b * rows:(b + 1) * rows] = v[b].astype(F32).T.astype(BF)
    lane = lax.broadcasted_iota(jnp.int32, (1, width), 1) // 64

    def head(h, carry):
        own = lane == h
        for qb in range(blocks):
            qm = jnp.where(own, q[qb], jnp.zeros_like(q[qb]))
            scores = [dot(k[kb], qm, NT) * SCALE for kb in range(qb + 1)]
            top = functools.reduce(jnp.maximum, [jnp.max(s, axis=0, keepdims=True) for s in scores])
            total = jnp.zeros((1, rows), F32)
            out = jnp.zeros((64, rows), F32)
            for kb in range(qb + 1):
                e = jnp.exp(scores[kb] - top)
                total = total + jnp.sum(e, axis=0, keepdims=True)
                out = out + dot(v_t[pl.ds(pl.multiple_of(h * 64, 64), 64), kb * rows:(kb + 1) * rows], e.astype(BF))
            o_t[qb, pl.ds(pl.multiple_of(h * 64, 64), 64), :] = out / total
            lse_o[h, qb:qb + 1, :] = top + jnp.log(total)
        return carry

    lax.fori_loop(0, heads, head, 0)
    half = woa.shape[1]
    quarter = rows // 4
    for qb in range(blocks):
        att = o_t[qb].T.astype(BF)
        att_o[qb] = att
        for lo, w in ((0, woa), (half, wob)):
            part = dot(att, w[...])
            for p in range(2):
                keep_o[p, qb, :, lo:lo + half] = part[p * quarter:(p + 1) * quarter]
                send_o[p, qb, :, lo:lo + half] = part[(2 + p) * quarter:(3 + p) * quarter].astype(BF)


def residual_kernel(x, keep, got_core, got_x, gain, residual_o, normed_o):
    residual = (
        x[0].astype(F32) + keep[0, 0] + got_core[0, 0].astype(F32) + got_x[0].astype(F32)
    )
    inverse = lax.rsqrt(jnp.mean(residual * residual, axis=-1, keepdims=True) + EPSILON)
    residual_o[0] = residual
    normed_o[0] = (residual * inverse * gain[...]).astype(BF)


def mlp_kernel(
    n0, n1, n2, n3, g0, g1, g2, g3, ga, gb, ua, ub, da, db,
    normed_o, grad_o, hidden_o, dgate_o, dup_o, keep_o, send_o,
):
    n = jnp.concatenate([n0[0], n1[0], n2[0], n3[0]], axis=0)
    g = jnp.concatenate([g0[0], g1[0], g2[0], g3[0]], axis=0)
    normed_o[0] = n
    grad_o[0] = g
    half = ga.shape[1]
    na, nb = n[:, :half], n[:, half:]
    gate = dot(na, ga[...], NT) + dot(nb, gb[...], NT)
    up = dot(na, ua[...], NT) + dot(nb, ub[...], NT)
    grad_hidden = dot(g[:, :half], da[...], NT) + dot(g[:, half:], db[...], NT)
    s = jax.nn.sigmoid(gate)
    active = gate * s
    hidden_o[0] = (active * up).astype(BF)
    dgate = (grad_hidden * up * s * (1.0 + gate * (1.0 - s))).astype(BF)
    dup = (grad_hidden * active).astype(BF)
    dgate_o[0] = dgate
    dup_o[0] = dup
    quarter = n.shape[0] // 4
    for lo, wg, wu in ((0, ga, ua), (half, gb, ub)):
        part = dot(dgate, wg[...]) + dot(dup, wu[...])
        for p in range(2):
            keep_o[p, 0, :, lo:lo + half] = part[p * quarter:(p + 1) * quarter]
            send_o[p, 0, :, lo:lo + half] = part[(2 + p) * quarter:(3 + p) * quarter].astype(BF)


def down_kernel(hidden, da, db, keep_o, send_o):
    half = da.shape[1]
    quarter = hidden.shape[1] // 4
    for lo, w in ((0, da), (half, db)):
        part = dot(hidden[0], w[...])
        for p in range(2):
            keep_o[p, 0, :, lo:lo + half] = part[p * quarter:(p + 1) * quarter]
            send_o[p, 0, :, lo:lo + half] = part[(2 + p) * quarter:(3 + p) * quarter].astype(BF)


def norm_back_kernel(direct, keep, got_core, got_x, values, gain, grad_o, low_o, gain_o):
    @pl.when(pl.program_id(0) == 0)
    def _():
        gain_o[...] = jnp.zeros_like(gain_o)

    grad = keep[0, 0] + got_core[0, 0].astype(F32) + got_x[0].astype(F32)
    x = values[0].astype(F32)
    inverse = lax.rsqrt(jnp.mean(x * x, axis=-1, keepdims=True) + EPSILON)
    weighted = grad * gain[...]
    gain_o[...] += jnp.sum(grad * x * inverse, axis=0, keepdims=True)
    out = direct[0].astype(F32) + (
        inverse * weighted
        - x * (inverse * inverse * inverse) * jnp.mean(weighted * x, axis=-1, keepdims=True)
    )
    grad_o[0] = out
    low_o[0] = out.astype(BF)


def attend_back_kernel(
    seg, b0, b1, b2, b3, woa, wob, q, k, v, att, lse, cos, sin, mix, diff,
    gb_o, gq_o, gk_o, gv_o, gf_o, dmix_o,
    gat, dmat, k_t, dk, dv, dq_t,
):
    blocks, rows, width = q.shape
    heads = width // 64
    half = woa.shape[1]
    lane_full = lax.broadcasted_iota(jnp.int32, (1, width), 1)
    lane = lane_full // 64
    pick = (
        lax.broadcasted_iota(jnp.int32, (8, width), 0)
        == lax.broadcasted_iota(jnp.int32, (8, width), 1) // 64
    ).astype(F32)
    for b in range(blocks):
        g = jnp.concatenate([b0[b], b1[b], b2[b], b3[b]], axis=0)
        gb_o[b] = g
        ga = (dot(g[:, :half], woa[...], NT) + dot(g[:, half:], wob[...], NT)).astype(BF)
        gat[b] = ga
        prod = ga.astype(F32) * att[b].astype(F32)
        dmat[b] = lax.dot_general(pick, prod, NT, precision=lax.Precision.HIGHEST, preferred_element_type=F32)
        k_t[:, b * rows:(b + 1) * rows] = k[b].astype(F32).T.astype(BF)
    dk[...] = jnp.zeros_like(dk)
    dv[...] = jnp.zeros_like(dv)

    def head(h, carry):
        own = lane == h
        for qb in range(blocks):
            qm = jnp.where(own, q[qb], jnp.zeros_like(q[qb]))
            gm = jnp.where(own, gat[qb], jnp.zeros_like(gat[qb]))
            log_total = lse[h, qb:qb + 1, :]
            row_dot = dmat[qb, pl.ds(h, 1), :]
            acc = jnp.zeros((64, rows), F32)
            for kb in range(qb + 1):
                prob = jnp.exp(dot(k[kb], qm, NT) * SCALE - log_total)
                dprob = dot(v[kb], gm, NT)
                ds = (prob * (dprob - row_dot)).astype(BF)
                dv[kb] += dot(prob.astype(BF), gm)
                dk[kb] += dot(ds, qm)
                acc = acc + dot(k_t[pl.ds(pl.multiple_of(h * 64, 64), 64), kb * rows:(kb + 1) * rows], ds)
            dq_t[qb, pl.ds(pl.multiple_of(h * 64, 64), 64), :] = acc
        return carry

    lax.fori_loop(0, heads, head, 0)
    quarter = rows // 4
    total = jnp.zeros((1, width), F32)
    for b in range(blocks):
        cosine, sine = signed_tables(cos, sin, b, width, lane_full)
        gq = dq_t[b].T * SCALE
        gk = dk[b] * SCALE
        gv = dv[b]
        gq_o[b] = (gq * cosine - half_swap(gq, lane_full) * sine).astype(BF)
        gk_o[b] = (gk * cosine - half_swap(gk, lane_full) * sine).astype(BF)
        gv_o[b] = (mix[...] * gv).astype(BF)
        gf = ((1.0 - mix[...]) * gv).astype(BF)
        for r in range(4):
            gf_o[b, seg[r]] = gf[r * quarter:(r + 1) * quarter]
        total = total + jnp.sum(gv * diff[b].astype(F32), axis=0, keepdims=True)
    dmix_o[...] = total


def grad_normed_kernel(gq, gk, gv, wa, wb, keep_o, send_o):
    half = wa.shape[1]
    quarter = gq.shape[1] // 4
    for lo, w in ((0, wa), (half, wb)):
        part = dot(gq[0], w[0], NT) + dot(gk[0], w[1], NT) + dot(gv[0], w[2], NT)
        for p in range(2):
            keep_o[p, 0, :, lo:lo + half] = part[p * quarter:(p + 1) * quarter]
            send_o[p, 0, :, lo:lo + half] = part[(2 + p) * quarter:(3 + p) * quarter].astype(BF)


def place_kernel(where, roll, *refs):
    pieces, out = refs[:-1], refs[-1]
    width = out.shape[-1]
    half = width // 2
    for r, piece in enumerate(pieces):
        value = piece[0]
        low, high = value[:, :half], value[:, half:]
        swap = roll[0] == 1
        out[0, where[r], :, :half] = jnp.where(swap, high, low).astype(out.dtype)
        out[0, where[r], :, half:] = jnp.where(swap, low, high).astype(out.dtype)


def first_kernel(got, out):
    out[...] = got[...].astype(out.dtype)


def on_device(
    fsdp, ctx, tp,
    tokens, first_values, out_grad, w_qkv, output_weight, w_gate, w_up, w_down, gain_attn, gain_mlp, mix,
):
    seqs, block, width = tokens.shape
    local = w_qkv.shape[2]
    hidden_width = w_gate.shape[1]
    quarter = block // tp
    half = width // 2
    pair = fsdp == 2
    assert seqs == ctx and ctx == 4 and tp == 4
    y = lax.axis_index("fsdp")
    z = lax.axis_index("ctx")
    t = lax.axis_index("tp")
    swap_y = [(0, 1), (1, 0)]
    by_core = [(i, i ^ 1) for i in range(tp)]
    by_x = [(i, i ^ 2) for i in range(tp)]

    def core(value):
        return lax.ppermute(value, "tp", by_core)

    def across(value):
        return lax.ppermute(value, "tp", by_x)

    def other_half(value, axis):
        if pair:
            return value, lax.ppermute(value, "fsdp", swap_y)
        whole = lax.all_gather(value, "fsdp", axis=axis, tiled=True)
        return tuple(lax.slice_in_dim(whole, i * half, (i + 1) * half, axis=axis) for i in range(2))

    def gather(own):
        second = across(own)
        return own, second, core(own), core(second)

    def own_rows(value):
        part = lax.dynamic_slice_in_dim(value, t * quarter, quarter, axis=1)
        if pair:
            part = jnp.where(y == 1, jnp.roll(part, half, axis=-1), part)
        return lax.all_to_all(part, "ctx", 0, 0)

    x_own = own_rows(tokens)
    x_pieces = gather(x_own)
    qkv_own = jnp.transpose(w_qkv, (1, 0, 2))
    qkv_a, qkv_b = other_half(qkv_own, 1)
    gains = other_half(jnp.stack([gain_attn, gain_mlp]), 1)
    gains = jnp.concatenate(gains, axis=1).astype(F32)
    gain_first, gain_second = gains[0:1], gains[1:2]
    fv = lax.all_to_all(first_values, "ctx", 0, 0).reshape(ctx, tp, quarter, local)
    out_a, out_b = other_half(output_weight, 1)
    g_own = own_rows(out_grad)
    g_pieces = gather(g_own)
    gate_a, gate_b = other_half(w_gate.T, 1)
    up_a, up_b = other_half(w_up.T, 1)
    down_a, down_b = other_half(w_down, 1)

    seg = jnp.stack([t, t ^ 2, t ^ 1, t ^ 3]).astype(jnp.int32)
    roll = jnp.reshape(y if pair else y * 0, (1,)).astype(jnp.int32)
    place = (seg[:, None] * quarter + jnp.arange(quarter)[None, :]).reshape(block)
    positions = (jnp.arange(ctx)[:, None] * block + place[None, :]).astype(F32)
    lanes = (jnp.arange(128) % 32).astype(F32)
    table = positions[:, :, None] * (10000.0 ** (-lanes / 32.0))[None, None, :]
    cosine, sine = jnp.cos(table), jnp.sin(table)
    mix_row = jnp.repeat(mix, local // mix.shape[0])[None, :]

    rows = ctx * block
    smem = pl.BlockSpec(memory_space=pltpu.SMEM)
    piece_spec = pl.BlockSpec((1, quarter, width), lambda b: (b, 0, 0))
    block_local = pl.BlockSpec((1, block, local), lambda b: (b, 0, 0))
    block_width = pl.BlockSpec((1, block, width), lambda b: (b, 0, 0))
    block_hidden = pl.BlockSpec((1, block, hidden_width), lambda b: (b, 0, 0))
    block_table = pl.BlockSpec((1, block, 128), lambda b: (b, 0, 0))
    part_spec = pl.BlockSpec((2, 1, quarter, width), lambda b: (0, b, 0, 0))
    first_part = pl.BlockSpec((1, 1, quarter, width), lambda b: (0, b, 0, 0))
    keep_shape = shape_of((2, ctx, quarter, width), F32)
    send_shape = shape_of((2, ctx, quarter, width), BF)
    own_f32 = shape_of((ctx, quarter, width), F32)
    own_low = shape_of((ctx, quarter, width), BF)
    rows_local = shape_of((ctx, block, local), BF)
    rows_width = shape_of((ctx, block, width), BF)
    rows_hidden = shape_of((ctx, block, hidden_width), BF)
    gain_spec = full((1, width))

    normed, queries, keys, values, diff = call(
        qkv_kernel,
        [rows_width, rows_local, rows_local, rows_local, rows_local],
        seg, *x_pieces, gain_first, qkv_a, qkv_b, fv, cosine, sine, mix_row,
        grid=(ctx,),
        in_specs=[smem] + [piece_spec] * 4 + [
            gain_spec, full((3, half, local)), full((3, half, local)),
            pl.BlockSpec((1, tp, quarter, local), lambda b: (b, 0, 0, 0)),
            block_table, block_table, full((1, local)),
        ],
        out_specs=[block_width] + [block_local] * 4,
        flops=2 * rows * width * 3 * local,
        name="norm_qkv",
    )
    attended, log_total, keep, send = call(
        attend_kernel,
        [rows_local, shape_of((mix.shape[0], ctx, block), F32), keep_shape, send_shape],
        queries, keys, values, out_a, out_b,
        scratch=[pltpu.VMEM((local, rows), BF), pltpu.VMEM((ctx, local, block), F32)],
        flops=6 * rows * rows * local,
        name="attend",
    )

    def reduce_rows(keep, send):
        got_core = core(send)
        onward = (keep[1] + got_core[1].astype(F32)).astype(BF)
        return got_core, across(onward)

    got_core, got_x = reduce_rows(keep, send)
    residual, normed_own = call(
        residual_kernel,
        [own_f32, own_low],
        x_own, keep, got_core, got_x, gain_second,
        grid=(ctx,),
        in_specs=[piece_spec, first_part, first_part, piece_spec, gain_spec],
        out_specs=[piece_spec, piece_spec],
        name="residual_norm",
    )
    n_pieces = gather(normed_own)
    normed_mlp, grad_rows, hidden, grad_gate, grad_up, keep, send = call(
        mlp_kernel,
        [rows_width, rows_width, rows_hidden, rows_hidden, rows_hidden, keep_shape, send_shape],
        *n_pieces, *g_pieces, gate_a, gate_b, up_a, up_b, down_a, down_b,
        grid=(ctx,),
        in_specs=[piece_spec] * 8 + [full((hidden_width, half))] * 6,
        out_specs=[block_width] * 2 + [block_hidden] * 3 + [part_spec] * 2,
        flops=10 * rows * width * hidden_width,
        name="mlp",
    )
    got_core, got_x = reduce_rows(keep, send)
    grad_residual, branch_own, gain_sum_second = call(
        norm_back_kernel,
        [own_f32, own_low, shape_of((1, width), F32)],
        g_own, keep, got_core, got_x, residual, gain_second,
        grid=(ctx,),
        in_specs=[piece_spec, first_part, first_part, piece_spec, piece_spec, gain_spec],
        out_specs=[piece_spec, piece_spec, gain_spec],
        name="norm_back_mlp",
    )
    b_pieces = gather(branch_own)

    down_keep, down_send = call(
        down_kernel,
        [keep_shape, send_shape],
        hidden, down_a, down_b,
        grid=(ctx,),
        in_specs=[block_hidden, full((hidden_width, half)), full((hidden_width, half))],
        out_specs=[part_spec, part_spec],
        flops=2 * rows * width * hidden_width,
        name="down",
    )

    def weight_grad(left, right):
        return lax.dot_general(
            left.reshape(rows, -1), right.reshape(rows, -1), TN, preferred_element_type=F32
        )

    def owned(grad, axis):
        first, second = (lax.slice_in_dim(grad, i * half, (i + 1) * half, axis=axis) for i in range(2))
        if pair:
            shard = first + lax.ppermute(second.astype(BF), "fsdp", swap_y).astype(F32)
        else:
            shard = lax.psum_scatter(
                grad.astype(BF), "fsdp", scatter_dimension=axis, tiled=True
            ).astype(F32)
        toward = lax.ppermute(shard.astype(BF), "ctx", [(0, 1), (3, 2)])
        shard = (shard + toward.astype(F32)).astype(BF)
        meet = lax.ppermute(shard, "ctx", [(1, 2), (2, 1)])
        shard = (shard.astype(F32) + meet.astype(F32)).astype(BF)
        back = lax.ppermute(shard, "ctx", [(1, 0), (2, 3)])
        return jnp.where((z == 0) | (z == 3), back, shard).astype(F32)

    grad_w_down = owned(weight_grad(hidden, grad_rows), 1)
    grad_w_gate = owned(weight_grad(grad_gate, normed_mlp), 1).T
    grad_w_up = owned(weight_grad(grad_up, normed_mlp), 1).T

    branch_rows, gq, gk, gv, gf, mix_sum = call(
        attend_back_kernel,
        [
            rows_width, rows_local, rows_local, rows_local,
            shape_of((ctx, tp, quarter, local), BF), shape_of((1, local), F32),
        ],
        seg, *b_pieces, out_a, out_b, queries, keys, values, attended, log_total, cosine, sine, mix_row, diff,
        in_specs=[smem] + [pl.BlockSpec(memory_space=pltpu.VMEM)] * 15,
        scratch=[
            pltpu.VMEM((ctx, block, local), BF),
            pltpu.VMEM((ctx, 8, block), F32),
            pltpu.VMEM((local, rows), BF),
            pltpu.VMEM((ctx, block, local), F32),
            pltpu.VMEM((ctx, block, local), F32),
            pltpu.VMEM((ctx, local, block), F32),
        ],
        flops=14 * rows * rows * local,
        name="attend_back",
    )
    keep, send = call(
        grad_normed_kernel,
        [keep_shape, send_shape],
        gq, gk, gv, qkv_a, qkv_b,
        grid=(ctx,),
        in_specs=[block_local] * 3 + [full((3, half, local))] * 2,
        out_specs=[part_spec, part_spec],
        flops=6 * rows * width * local,
        name="grad_normed",
    )
    got_core, got_x = reduce_rows(keep, send)
    grad_w_qkv = owned(
        jnp.stack([weight_grad(normed, item) for item in (gq, gk, gv)]), 1
    )
    grad_w_qkv = jnp.transpose(grad_w_qkv, (1, 0, 2))
    grad_w_out = owned(weight_grad(attended, branch_rows), 1)

    _, tokens_own, gain_sum_first = call(
        norm_back_kernel,
        [own_f32, own_low, shape_of((1, width), F32)],
        grad_residual, keep, got_core, got_x, x_own, gain_first,
        grid=(ctx,),
        in_specs=[piece_spec, first_part, first_part, piece_spec, piece_spec, gain_spec],
        out_specs=[piece_spec, piece_spec, gain_spec],
        name="norm_back_attn",
    )

    got_core, got_x = reduce_rows(down_keep, down_send)
    output_own = (
        residual + down_keep[0] + got_core[0].astype(F32) + got_x.astype(F32)
    ).astype(BF)

    def home(own, dtype):
        pieces = gather(lax.all_to_all(own, "ctx", 0, 0))
        placed = call(
            place_kernel,
            [shape_of((seqs, tp, quarter, width), dtype)],
            seg, roll, *pieces,
            grid=(seqs,),
            in_specs=[smem, smem] + [piece_spec] * 4,
            out_specs=[pl.BlockSpec((1, tp, quarter, width), lambda b: (b, 0, 0, 0))],
            name="place",
        )[0]
        return placed.reshape(seqs, block, width)

    output = home(output_own, BF)
    grad_tokens = home(tokens_own, F32)
    grad_first = lax.all_to_all(gf, "ctx", 0, 0).reshape(seqs, block, local).astype(F32)

    small = jnp.concatenate([gain_sum_first, gain_sum_second, mix_sum], axis=1)
    for step in (1, 2):
        small = small + lax.ppermute(small, "ctx", [(i, i ^ step) for i in range(ctx)])
    mixed = small[:, 2 * width:]
    first_gain, second_gain = small[:, :width], small[:, width:2 * width]
    if pair:
        outgoing = jnp.concatenate([first_gain[:, half:], second_gain[:, half:], mixed], axis=1)
        incoming = lax.ppermute(outgoing, "fsdp", swap_y)
        gains_here = jnp.concatenate([first_gain[:, :half], second_gain[:, :half]], axis=1)
        gains_here = gains_here + incoming[:, :2 * half]
        mixed = mixed + incoming[:, 2 * half:]
    else:
        mixed = lax.psum(mixed, "fsdp")
        gains_here = jnp.concatenate(
            [
                lax.psum_scatter(item, "fsdp", scatter_dimension=1, tiled=True)
                for item in (first_gain, second_gain)
            ],
            axis=1,
        )
    for perm in (by_core, by_x):
        gains_here = gains_here + lax.ppermute(gains_here, "tp", perm)
    share = gain_attn.shape[0]
    grad_mix = jnp.sum(mixed.reshape(mix.shape[0], -1), axis=1)
    return (
        output, grad_tokens, grad_first, grad_w_qkv, grad_w_out, grad_w_gate, grad_w_up, grad_w_down,
        gains_here[0, :share], gains_here[0, share:], grad_mix,
    )


def solution(mesh):
    rows = P("fsdp", "ctx", None)
    in_specs = (
        rows, P("fsdp", "ctx", "tp"), rows, P("fsdp", None, "tp"), P("tp", "fsdp"), P("fsdp", "tp"),
        P("fsdp", "tp"), P("tp", "fsdp"), P("fsdp"), P("fsdp"), P("tp"),
    )
    out_specs = (
        rows, rows, P("fsdp", "ctx", "tp"), P("fsdp", None, "tp"), P("tp", "fsdp"), P("fsdp", "tp"),
        P("fsdp", "tp"), P("tp", "fsdp"), P("fsdp"), P("fsdp"), P("tp"),
    )
    sizes = [mesh.shape[name] for name in ("fsdp", "ctx", "tp")]
    return jax.shard_map(
        functools.partial(on_device, *sizes), mesh=mesh, in_specs=in_specs, out_specs=out_specs,
        check_vma=False,
    )
```

time: 1010 us -> 418 us (0.41)
  waiting for transfers between devices: 686 us -> 160 us
  matrix products: 108 us -> 12.1 us
  starting transfers between devices: 9.52 us -> 93.3 us
  Pallas kernels: 0 us -> 82.3 us
  blocking collectives: 57.5 us -> 0 us
  local copies, waits for them, and re-layouts: 65.3 us -> 17.1 us
  between operations: 15.7 us -> 1.48 us
    psum x4 -> x0, waiting for transfers between devices: 381 us -> none  [the longest x3 286 us: heads_sum(): return lax.psum(partial_sum, 'tp')]
    reduce_scatter x7 -> x0, waiting for transfers between devices: 154 us -> none  [the longest x1 43.8 us: on_device(): lax.psum_scatter(grad_values_all.astype(jnp.bfloat16), 'ctx', scatter_dim...]
    all_gather x6 -> x0, waiting for transfers between devices: 149 us -> none  [the longest x1 32.3 us: on_device(): lax.all_gather(value_local, 'ctx', axis=1, tiled=True)]
    ppermute x0 -> x57, waiting for transfers between devices: none -> 122 us  [the longest x10 38.4 us: across(): return lax.ppermute(value, 'tp', by_x)]
    dot_general x21 -> x7, matrix products: 108 us -> 12.1 us  [weight_grad(): lax.dot_general(left.reshape(rows, -1), right.reshape(rows, -1), TN, pref...]
    pallas_call x0 -> x11, Pallas kernels: none -> 82.3 us  [call(): pl.pallas_call(kernel, out_shape=out_shapes, scratch_shapes=list(scratch)...]
    ppermute x0 -> x57, starting transfers between devices: none -> 64 us  [the longest x5 18.5 us: owned(): toward = lax.ppermute(shard.astype(BF), 'ctx', [(0, 1), (3, 2)])]
    all_to_all x0 -> x6, waiting for transfers between devices: none -> 37.8 us  [the longest x2 20.2 us: own_rows(): return lax.all_to_all(part, 'ctx', 0, 0)]
  transfers between devices with their start and end apart: 17 -> 63, of which waited for: 17 -> 20; matrix products, arithmetic and copies ran while one was open for 11% -> 17% of each run, Pallas kernels for 0% -> 13%
where the time goes in v1:
time: 418 us; the launch traced here: 416 us
  waiting for transfers between devices  160 us (38%)
  starting transfers between devices  93.3 us (22%)
  Pallas kernels  82.3 us (20%)
  other arithmetic  50.3 us (12%)
  local copies, waits for them, and re-layouts  17.1 us (4%)
  matrix products  12.1 us (3%)
    pallas_call x11, Pallas kernels, call(): pl.pallas_call(kernel, out_shape=out_shapes, scratch_shapes=list(scratch)...  82.3 us
    ppermute x10, waiting for transfers between devices, across(): return lax.ppermute(value, 'tp', by_x)  38.4 us
    ppermute x5, waiting for transfers between devices, owned(): shard = first + lax.ppermute(second.astype(BF), 'fsdp', swap_y).astype(F32)  34.8 us
    all_to_all x2, waiting for transfers between devices, own_rows(): return lax.all_to_all(part, 'ctx', 0, 0)  20.2 us
    ppermute x6, waiting for transfers between devices, other_half(): return (value, lax.ppermute(value, 'fsdp', swap_y))  19.8 us
    ppermute x5, starting transfers between devices, owned(): toward = lax.ppermute(shard.astype(BF), 'ctx', [(0, 1), (3, 2)])  18.5 us
    all_to_all x2, waiting for transfers between devices, home(): pieces = gather(lax.all_to_all(own, 'ctx', 0, 0))  17.6 us
    ppermute x2, waiting for transfers between devices, on_device(): lax.ppermute(small, 'ctx', [(i, i ^ step) for i in range(ctx)])  14 us
  transfers between devices with their start and end apart: 63, of which 20 were waited for; matrix products, arithmetic and copies ran while one was open for 17% of the time, Pallas kernels for 13%

profile of v1, /device:TPU:0, one launch (start us, length us, event | category | flops | bytes accessed | tf_op | source)
XLA Modules:
  0.0 416.1 jit_solution(12027236461671063916)
XLA Ops:
  1.8 2.1 maximum_select_fusion
  3.9 6.5 %all-to-all-start = ((bf16[4,64,1024]{2,1,0:T(8,128)(2,1)}), bf16[4,64,1024]{2,1,0:T(8,128)(2,1)S(1)}, u32[]{:S(2)}, u32[]{:S(2)}) async-start(bf16[4,64,1024]{2,1,0:T(8,128)(2,1)} %maximum_select_fusion), calls=%async_computation | async-start | bytes 1048576 | tf_op jit(solution)/shard_map/all_to_all | solution.py:307
  10.4 1.6 collective-permute-start.3
  14.7 10.2 %all-to-all-done.p0.x.values = bf16[4,64,1024]{2,1,0:T(8,128)(2,1)S(1)} async-done(((bf16[4,64,1024]{2,1,0:T(8,128)(2,1)}), bf16[4,64,1024]{2,1,0:T(8,128)(2,1)S(1)}, u32[]{:S(2)}, u32[]{:S(2)}) %all-to-all-start) | async-done | bytes 524320 | tf_op jit(solution)/shard_map/all_to_all | solution.py:307
  24.9 3.5 all-to-all-start.1
  30.1 11.2 %collective-permute-done.p1 = bf16[4,64,1024]{2,1,0:T(8,128)(2,1)S(1)} collective-permute-done((bf16[4,64,1024]{2,1,0:T(8,128)(2,1)S(1)}, bf16[4,64,1024]{2,1,0:T(8,128)(2,1)S(1)}, u32[]{:S(2)}, u32[]{:S(2)}) %collective-permute-start) | collective-permute-done | bytes 524320 | tf_op jit(solution)/shard_map/ppermute | solution.py:291
  41.3 3.0 multiply_sine_fusion
  46.8 7.0 %norm_qkv.1 = (bf16[4,256,1024]{2,1,0:T(8,128)(2,1)}, bf16[4,256,256]{2,1,0:T(8,128)(2,1)}, bf16[4,256,256]{2,1,0:T(8,128)(2,1)}, bf16[4,256,256]{2,1,0:T(8,128)(2,1)}, bf16[4,256,256]{2,1,0:T(8,128)(2,1)}) custom-call(s32[4]{0:T(128)} %get-tuple-element.78.seg.where, bf16[4,64,1024]{2,1,0:T(8,128)(2,1)} %copy-done.7, bf16[4,64,1024]{2,1,0:T(8,128)(2,1)} %copy-done.43, ...), custom_call_target="tpu_custom_call" | custom-call | flops 1610612736 | bytes 9442320 | tf_op jit(solution)/shard_map/norm_qkv/pallas_call | solution.py:35
  53.8 12.2 %attend.1 = (bf16[4,256,256]{2,1,0:T(8,128)(2,1)}, f32[4,4,256]{2,1,0:T(4,128)}, f32[2,4,64,1024]{3,2,1,0:T(8,128)}, bf16[2,4,64,1024]{3,2,1,0:T(8,128)(2,1)}) custom-call(bf16[4,256,256]{2,1,0:T(8,128)(2,1)} %get-tuple-element.44.q, bf16[4,256,256]{2,1,0:T(8,128)(2,1)} %get-tuple-element.45.k, bf16[4,256,256]{2,1,0:T(8,128)(2,1)} %get-tuple-element.46.v, ...), custom_call_target="tpu_custom_call" | custom-call | flops 1610612736 | bytes 5783552 | tf_op jit(solution)/shard_map/attend/pallas_call | solution.py:35
  67.5 2.2 maximum_select_fusion.1
  69.7 4.7 %all-to-all-start.2 = ((bf16[4,64,1024]{2,1,0:T(8,128)(2,1)}), bf16[4,64,1024]{2,1,0:T(8,128)(2,1)}, u32[]{:S(2)}, u32[]{:S(2)}) async-start(bf16[4,64,1024]{2,1,0:T(8,128)(2,1)} %maximum_select_fusion.1), calls=%async_computation.2 | async-start | bytes 1048576 | tf_op jit(solution)/shard_map/all_to_all | solution.py:307
  79.1 10.1 %all-to-all-done.2.g0.direct = bf16[4,64,1024]{2,1,0:T(8,128)(2,1)} async-done(((bf16[4,64,1024]{2,1,0:T(8,128)(2,1)}), bf16[4,64,1024]{2,1,0:T(8,128)(2,1)}, u32[]{:S(2)}, u32[]{:S(2)}) %all-to-all-start.2) | async-done | bytes 524320 | tf_op jit(solution)/shard_map/all_to_all | solution.py:307
  91.4 3.9 residual_norm.1
  97.4 6.7 %collective-permute-done.11.g1 = bf16[4,64,1024]{2,1,0:T(8,128)(2,1)S(1)} collective-permute-done((bf16[4,64,1024]{2,1,0:T(8,128)(2,1)}, bf16[4,64,1024]{2,1,0:T(8,128)(2,1)S(1)}, u32[]{:S(2)}, u32[]{:S(2)}) %collective-permute-start.11) | collective-permute-done | bytes 524320 | tf_op jit(solution)/shard_map/ppermute | solution.py:291
  104.2 7.7 %collective-permute-done.15.ub = bf16[704,512]{1,0:T(8,128)(2,1)} collective-permute-done((bf16[704,512]{1,0:T(8,128)(2,1)}, bf16[704,512]{1,0:T(8,128)(2,1)}, u32[]{:S(2)}, u32[]{:S(2)}) %collective-permute-start.15) | collective-permute-done | bytes 720928 | tf_op jit(solution)/shard_map/ppermute | solution.py:295
  111.8 1.7 collective-permute-done.8.n1
  113.5 12.1 %collective-permute-done.16.db = bf16[704,512]{1,0:T(8,128)(2,1)S(1)} collective-permute-done((bf16[704,512]{1,0:T(8,128)(2,1)S(1)}, bf16[704,512]{1,0:T(8,128)(2,1)S(1)}, u32[]{:S(2)}, u32[]{:S(2)}) %collective-permute-start.16) | collective-permute-done | bytes 720928 | tf_op jit(solution)/shard_map/ppermute | solution.py:295
  126.5 13.2 %mlp.1 = (bf16[4,256,1024]{2,1,0:T(8,128)(2,1)}, bf16[4,256,1024]{2,1,0:T(8,128)(2,1)}, bf16[4,256,704]{2,1,0:T(8,128)(2,1)}, bf16[4,256,704]{2,1,0:T(8,128)(2,1...) custom-call(bf16[4,64,1024]{2,1,0:T(8,128)(2,1)} %get-tuple-element.50.n0, ...), custom_call_target="tpu_custom_call" | custom-call | flops 7381975040 | bytes 20185088 | tf_op jit(solution)/shard_map/mlp/pallas_call | solution.py:35
  139.8 3.9 convolution_bitcast_fusion
  146.3 1.7 convolution_bitcast_fusion.2
  149.8 1.7 convolution_bitcast_fusion.1
  153.8 5.4 %down.1 = (f32[2,4,64,1024]{3,2,1,0:T(8,128)}, bf16[2,4,64,1024]{3,2,1,0:T(8,128)(2,1)}) custom-call(bf16[4,256,704]{2,1,0:T(8,128)(2,1)} %get-tuple-element.51.hidden, bf16[704,512]{1,0:T(8,128)(2,1)} %da.3, bf16[704,512]{1,0:T(8,128)(2,1)} %copy-done.37), custom_call_target="tpu_custom_call" | custom-call | flops 1476395008 | bytes 6029312 | tf_op jit(solution)/shard_map/down/pallas_call | solution.py:35
  159.2 4.9 %collective-permute-done.48 = bf16[704,512]{1,0:T(8,128)(2,1)} collective-permute-done((bf16[704,512]{1,0:T(8,128)(2,1)}, bf16[704,512]{1,0:T(8,128)(2,1)}, u32[]{:S(2)}, u32[]{:S(2)}) %collective-permute-start.48) | collective-permute-done | bytes 720928 | tf_op jit(solution)/shard_map/ppermute | solution.py:431
  164.1 1.8 fusion.5
  166.0 3.7 collective-permute-start.49
  169.6 9.9 %collective-permute-done.40 = bf16[704,512]{1,0:T(8,128)(2,1)} collective-permute-done((bf16[704,512]{1,0:T(8,128)(2,1)}, bf16[704,512]{1,0:T(8,128)(2,1)}, u32[]{:S(2)}, u32[]{:S(2)}) %collective-permute-start.40) | collective-permute-done | bytes 720928 | tf_op jit(solution)/shard_map/ppermute | solution.py:431
  181.0 3.8 collective-permute-start.41
  184.8 9.6 %collective-permute-done.44 = bf16[704,512]{1,0:T(8,128)(2,1)S(1)} collective-permute-done((bf16[704,512]{1,0:T(8,128)(2,1)}, bf16[704,512]{1,0:T(8,128)(2,1)S(1)}, u32[]{:S(2)}, u32[]{:S(2)}) %collective-permute-start.44) | collective-permute-done | bytes 720928 | tf_op jit(solution)/shard_map/ppermute | solution.py:431
  195.5 4.6 %collective-permute-start.45 = (bf16[704,512]{1,0:T(8,128)(2,1)}, bf16[704,512]{1,0:T(8,128)(2,1)}, u32[]{:S(2)}, u32[]{:S(2)}) collective-permute-start(bf16[704,512]{1,0:T(8,128)(2,1)} %fusion.4), channel_id=1, source_target_pairs={{0,4},{12,8},{1,5},{13,9},{2,6},{14,10},{3,7},{15,11},{16,20},{28,... | collective-permute-start | bytes 2162696 | tf_op jit(solution)/shard_map/ppermute | solution.py:436
  207.8 2.3 add_convert_fusion.7
  211.6 4.9 %collective-permute-done.23.got_x = bf16[4,64,1024]{2,1,0:T(8,128)(2,1)} collective-permute-done((bf16[4,64,1024]{2,1,0:T(8,128)(2,1)S(1)}, bf16[4,64,1024]{2,1,0:T(8,128)(2,1)}, u32[]{:S(2)}, u32[]{:S(2)}) %collective-permute-start.23) | collective-permute-done | bytes 524320 | tf_op jit(solution)/shard_map/ppermute | solution.py:291
  216.5 4.3 %norm_back_mlp.1 = (f32[4,64,1024]{2,1,0:T(8,128)}, bf16[4,64,1024]{2,1,0:T(8,128)(2,1)}, f32[1,1024]{1,0:T(1,128)}) custom-call(bf16[4,64,1024]{2,1,0:T(8,128)(2,1)} %all-to-all-done.2.g0.direct, f32[2,4,64,1024]{3,2,1,0:T(8,128)} %get-tuple-element.54.keep, bf16[2,4,64,1024]{3,2,1,0:T(8,128)(2,1)} %collective-permute-done.22.got_core, ...), custom_call_target="tpu_custom_call" | custom-call | bytes 6823936 | tf_op jit(solution)/shard_map/norm_back_mlp/pallas_call | solution.py:35
  221.4 2.8 add_convert_fusion.5
  225.1 2.6 collective-permute-done.18
  227.6 2.2 fusion.1
  229.8 4.1 all-to-all-start.3
  234.0 3.3 collective-permute-done.24.b1
  237.3 2.2 add_convert_fusion.2
  240.8 2.4 add_convert_fusion.6
  244.5 2.2 add_convert_fusion.4
  248.0 17.6 %all-to-all-done.3.refs_0_ = bf16[4,64,1024]{2,1,0:T(8,128)(2,1)} async-done(((bf16[4,64,1024]{2,1,0:T(8,128)(2,1)}), bf16[4,64,1024]{2,1,0:T(8,128)(2,1)}, u32[]{:S(2)}, u32[]{:S(2)}) %all-to-all-start.3) | async-done | bytes 524320 | tf_op jit(solution)/shard_map/all_to_all | solution.py:499
  266.9 18.3 %attend_back.1 = (bf16[4,256,1024]{2,1,0:T(8,128)(2,1)}, bf16[4,256,256]{2,1,0:T(8,128)(2,1)}, bf16[4,256,256]{2,1,0:T(8,128)(2,1)}, bf16[4,256,256]{2,1,0:T(8,1...) custom-call(s32[4]{0:T(128)} %get-tuple-element.78.seg.where, bf16[4,64,1024]{2,1,0:T(8,128)(2,1)} %get-tuple-element.57.b0, ...), custom_call_target="tpu_custom_call" | custom-call | flops 3758096384 | bytes 10504208 | tf_op jit(solution)/shard_map/attend_back/pallas_call | solution.py:35
  285.2 4.1 all-to-all-start.5
  289.3 2.6 convolution_bitcast_fusion.6
  299.8 5.7 %grad_normed.1 = (f32[2,4,64,1024]{3,2,1,0:T(8,128)}, bf16[2,4,64,1024]{3,2,1,0:T(8,128)(2,1)}) custom-call(bf16[4,256,256]{2,1,0:T(8,128)(2,1)} %get-tuple-element.61.gq, bf16[4,256,256]{2,1,0:T(8,128)(2,1)} %get-tuple-element.62.gk, bf16[4,256,256]{2,1,0:T(8,128)(2,1)} %get-tuple-element.63.gv, bf16[3,512,256]{2,1,0:T(8,128)(2,1)} %bitcast.76, ...), custom_call_target="tpu_custom_call" | custom-call | flops 1610612736 | bytes 6291456 | tf_op jit(solution)/shard_map/grad_normed/pallas_call | solution.py:35
  305.6 2.3 select_convert_fusion
  308.5 2.3 convert_bitcast_fusion.2
  310.8 10.3 %collective-permute-done.36 = bf16[256,512]{1,0:T(8,128)(2,1)S(1)} collective-permute-done((bf16[256,512]{1,0:T(8,128)(2,1)S(1)}, bf16[256,512]{1,0:T(8,128)(2,1)S(1)}, u32[]{:S(2)}, u32[]{:S(2)}) %collective-permute-start.36) | collective-permute-done | bytes 262176 | tf_op jit(solution)/shard_map/ppermute | solution.py:431
  321.2 3.7 collective-permute-start.37
  326.3 2.7 collective-permute-start.33
  329.2 1.6 collective-permute-start.28
  330.7 2.3 convert_bitcast_fusion.1
  335.2 8.0 %collective-permute-done.28.got_x = bf16[4,64,1024]{2,1,0:T(8,128)(2,1)} collective-permute-done((bf16[4,64,1024]{2,1,0:T(8,128)(2,1)S(1)}, bf16[4,64,1024]{2,1,0:T(8,128)(2,1)}, u32[]{:S(2)}, u32[]{:S(2)}) %collective-permute-start.28) | collective-permute-done | bytes 524320 | tf_op jit(solution)/shard_map/ppermute | solution.py:291
  343.2 4.2 %norm_back_attn.1 = (f32[4,64,1024]{2,1,0:T(8,128)}, bf16[4,64,1024]{2,1,0:T(8,128)(2,1)}, f32[1,1024]{1,0:T(1,128)}) custom-call(f32[4,64,1024]{2,1,0:T(8,128)} %get-tuple-element.56.direct, f32[2,4,64,1024]{3,2,1,0:T(8,128)} %get-tuple-element.64.keep, bf16[2,4,64,1024]{3,2,1,0:T(8,128)(2,1)} %copy-done.14, ...), custom_call_target="tpu_custom_call" | custom-call | bytes 6823936 | tf_op jit(solution)/shard_map/norm_back_attn/pallas_call | solution.py:35
  348.2 2.3 add_convert_fusion.1
  351.2 6.4 %all-to-all-start.4 = ((bf16[4,64,1024]{2,1,0:T(8,128)(2,1)}), bf16[4,64,1024]{2,1,0:T(8,128)(2,1)S(1)}, u32[]{:S(2)}, u32[]{:S(2)}) async-start(bf16[4,64,1024]{2,1,0:T(8,128)(2,1)} %get-tuple-element.66), calls=%async_computation.4 | async-start | bytes 1048576 | tf_op jit(solution)/shard_map/all_to_all | solution.py:499
  360.0 5.1 %collective-permute-start.53 = (f32[1,2304]{1,0:T(1,128)S(1)}, f32[1,2304]{1,0:T(1,128)S(1)}, u32[]{:S(2)}, u32[]{:S(2)}) collective-permute-start(f32[1,2304]{1,0:T(1,128)S(1)} %add.170), channel_id=1, source_target_pairs={{0,8},{4,12},{8,0},{12,4},{1,9},{5,13},{9,1},{13,5},{2,10},{6,14},... | collective-permute-start | bytes 27656 | tf_op jit(solution)/shard_map/ppermute | solution.py:517
  365.1 2.1 bitcast_convert_fusion
  367.2 3.8 place.2
  371.0 14.0 %collective-permute-done.53 = f32[1,2304]{1,0:T(1,128)S(1)} collective-permute-done((f32[1,2304]{1,0:T(1,128)S(1)}, f32[1,2304]{1,0:T(1,128)S(1)}, u32[]{:S(2)}, u32[]{:S(2)}) %collective-permute-start.53) | collective-permute-done | bytes 9248 | tf_op jit(solution)/shard_map/ppermute | solution.py:517
  385.1 1.6 collective-permute-start.54
  393.3 5.7 %collective-permute-done.56 = f32[1,1024]{1,0:T(1,128)S(1)} collective-permute-done((f32[1,1024]{1,0:T(1,128)S(1)}, f32[1,1024]{1,0:T(1,128)S(1)}, u32[]{:S(2)}, u32[]{:S(2)}) %collective-permute-start.56) | collective-permute-done | bytes 4128 | tf_op jit(solution)/shard_map/ppermute | solution.py:536
  400.2 8.8 %collective-permute-done.35 = bf16[3,512,256]{2,1,0:T(8,128)(2,1)S(1)} collective-permute-done((bf16[3,512,256]{2,1,0:T(8,128)(2,1)S(1)}, bf16[3,512,256]{2,1,0:T(8,128)(2,1)S(1)}, u32[]{:S(2)}, u32[]{:S(2)}) %collective-permute-start.35) | collective-permute-done | bytes 786464 | tf_op jit(solution)/shard_map/ppermute | solution.py:440
  411.8 4.3 %place.3 = f32[4,4,64,1024]{3,2,1,0:T(8,128)} custom-call(s32[4]{0:T(128)} %get-tuple-element.78.seg.where, s32[1]{0:T(128)} %bitcast.4.roll, bf16[4,64,1024]{2,1,0:T(8,128)(2,1)} %copy-done.18, bf16[4,64,1024]{2,1,0:T(8,128)(2,1)} %copy-done.25, bf16[4,64,1024]{2,1,0:T(8,128)(2,1)} %copy-done.26, bf16[4,64,1024]{2,1,0:T(8,128)(2,1)} %copy-done.27), custom_call_target="tpu_custom_call" | custom-call | bytes 6291476 | tf_op jit(solution)/shard_map/place/pallas_call | solution.py:35
  (241 shorter events, 71.3 us)
Async XLA Ops:
  3.9 40.5 %copy-start.33 = (f32[4]{0:T(128)S(1)}, f32[4]{0:T(128)}, u32[]{:S(2)}) copy-start(f32[4]{0:T(128)} %param.21) | copy-start | bytes 52
  3.9 21.0 %all-to-all-start = ((bf16[4,64,1024]{2,1,0:T(8,128)(2,1)}), bf16[4,64,1024]{2,1,0:T(8,128)(2,1)S(1)}, u32[]{:S(2)}, u32[]{:S(2)}) async-start(bf16[4,64,1024]{2,1,0:T(8,128)(2,1)} %maximum_select_fusion), calls=%async_computation | async-start | bytes 1048576 | tf_op jit(solution)/shard_map/all_to_all | solution.py:307
  10.4 34.7 %collective-permute-start.3 = (bf16[2,512]{1,0:T(2,128)(2,1)S(1)}, bf16[2,512]{1,0:T(2,128)(2,1)S(1)}, u32[]{:S(2)}, u32[]{:S(2)}) collective-permute-start(bf16[2,512]{1,0:T(2,128)(2,1)S(1)} %pad_maximum_fusion.2), channel_id=1, source_target_pairs={{0,16},{16,0},{1,17},{17,1},{2,18},{18,2},{3,19},{19,3},{4,20},{20... | collective-permute-start | bytes 6152 | tf_op jit(solution)/shard_map/ppermute | solution.py:295
  12.0 41.7 %collective-permute-start.5 = (bf16[256,512]{1,0:T(8,128)(2,1)S(1)}, bf16[256,512]{1,0:T(8,128)(2,1)}, u32[]{:S(2)}, u32[]{:S(2)}) collective-permute-start(bf16[256,512]{1,0:T(8,128)(2,1)S(1)} %copy-done.44), channel_id=1, source_target_pairs={{0,16},{16,0},{1,17},{17,1},{2,18},{18,2},{3,19},{19,3},{4,20},{20... | collective-permute-start | bytes 786440 | tf_op jit(solution)/shard_map/ppermute | solution.py:295
  12.5 33.2 %collective-permute-start.4 = (bf16[3,512,256]{2,1,0:T(8,128)(2,1)S(1)}, bf16[3,512,256]{2,1,0:T(8,128)(2,1)S(1)}, u32[]{:S(2)}, u32[]{:S(2)}) collective-permute-start(bf16[3,512,256]{2,1,0:T(8,128)(2,1)S(1)} %bitcast.77), channel_id=1, source_target_pairs={{0,16},{16,0},{1,17},{17,1},{2,18},{18,2},{3,19},{19,3},{4,20},{20... | collective-permute-start | bytes 2359304 | tf_op jit(solution)/shard_map/ppermute | solution.py:295
  24.9 20.9 %all-to-all-start.1 = ((bf16[4,256,256]{2,1,0:T(8,128)(2,1)}), bf16[4,256,256]{2,1,0:T(8,128)(2,1)S(1)}, u32[]{:S(2)}, u32[]{:S(2)}) async-start(bf16[4,256,256]{2,1,0:T(8,128)(2,1)} %param.12), calls=%async_computation.1 | async-start | bytes 1048576 | tf_op jit(solution)/shard_map/all_to_all | solution.py:316
  28.3 13.0 %collective-permute-start = (bf16[4,64,1024]{2,1,0:T(8,128)(2,1)S(1)}, bf16[4,64,1024]{2,1,0:T(8,128)(2,1)S(1)}, u32[]{:S(2)}, u32[]{:S(2)}) collective-permute-start(bf16[4,64,1024]{2,1,0:T(8,128)(2,1)S(1)} %all-to-all-done.p0.x.values), channel_id=1, source_target_pairs={{0,2},{1,3},{2,0},{3,1},{4,6},{5,7},{6,4},{7,5},{8,10},{9,11},{10,... | collective-permute-start | bytes 1572872 | tf_op jit(solution)/shard_map/ppermute | solution.py:291
  30.1 15.6 %collective-permute-start.1 = (bf16[4,64,1024]{2,1,0:T(8,128)(2,1)S(1)}, bf16[4,64,1024]{2,1,0:T(8,128)(2,1)}, u32[]{:S(2)}, u32[]{:S(2)}) collective-permute-start(bf16[4,64,1024]{2,1,0:T(8,128)(2,1)S(1)} %all-to-all-done.p0.x.values), channel_id=1, source_target_pairs={{0,1},{1,0},{2,3},{3,2},{4,5},{5,4},{6,7},{7,6},{8,9},{9,8},{10,11... | collective-permute-start | bytes 1572872 | tf_op jit(solution)/shard_map/ppermute | solution.py:288
  41.3 4.4 %collective-permute-start.2 = (bf16[4,64,1024]{2,1,0:T(8,128)(2,1)S(1)}, bf16[4,64,1024]{2,1,0:T(8,128)(2,1)}, u32[]{:S(2)}, u32[]{:S(2)}) collective-permute-start(bf16[4,64,1024]{2,1,0:T(8,128)(2,1)S(1)} %collective-permute-done.p1), channel_id=1, source_target_pairs={{0,1},{1,0},{2,3},{3,2},{4,5},{5,4},{6,7},{7,6},{8,9},{9,8},{10,11... | collective-permute-start | bytes 1572872 | tf_op jit(solution)/shard_map/ppermute | solution.py:288
  65.9 8.5 %collective-permute-start.6 = (bf16[2,4,64,1024]{3,2,1,0:T(8,128)(2,1)}, bf16[2,4,64,1024]{3,2,1,0:T(8,128)(2,1)S(1)}, u32[]{:S(2)}, u32[]{:S(2)}) collective-permute-start(bf16[2,4,64,1024]{3,2,1,0:T(8,128)(2,1)} %get-tuple-element.48), channel_id=1, source_target_pairs={{0,1},{1,0},{2,3},{3,2},{4,5},{5,4},{6,7},{7,6},{8,9},{9,8},{10,11... | collective-permute-start | bytes 3145736 | tf_op jit(solution)/shard_map/ppermute | solution.py:288
  69.7 19.5 %all-to-all-start.2 = ((bf16[4,64,1024]{2,1,0:T(8,128)(2,1)}), bf16[4,64,1024]{2,1,0:T(8,128)(2,1)}, u32[]{:S(2)}, u32[]{:S(2)}) async-start(bf16[4,64,1024]{2,1,0:T(8,128)(2,1)} %maximum_select_fusion.1), calls=%async_computation.2 | async-start | bytes 1048576 | tf_op jit(solution)/shard_map/all_to_all | solution.py:307
  75.5 15.1 %collective-permute-start.7 = (bf16[4,64,1024]{2,1,0:T(8,128)(2,1)}, bf16[4,64,1024]{2,1,0:T(8,128)(2,1)S(1)}, u32[]{:S(2)}, u32[]{:S(2)}) collective-permute-start(bf16[4,64,1024]{2,1,0:T(8,128)(2,1)} %fusion.6), channel_id=1, source_target_pairs={{0,2},{1,3},{2,0},{3,1},{4,6},{5,7},{6,4},{7,5},{8,10},{9,11},{10,... | collective-permute-start | bytes 1572872 | tf_op jit(solution)/shard_map/ppermute | solution.py:291
  77.0 20.4 %collective-permute-start.14 = (bf16[704,512]{1,0:T(8,128)(2,1)}, bf16[704,512]{1,0:T(8,128)(2,1)S(1)}, u32[]{:S(2)}, u32[]{:S(2)}) collective-permute-start(bf16[704,512]{1,0:T(8,128)(2,1)} %bitcast.8.ga), channel_id=1, source_target_pairs={{0,16},{16,0},{1,17},{17,1},{2,18},{18,2},{3,19},{19,3},{4,20},{20... | collective-permute-start | bytes 2162696 | tf_op jit(solution)/shard_map/ppermute | solution.py:295
  78.6 33.3 %collective-permute-start.15 = (bf16[704,512]{1,0:T(8,128)(2,1)}, bf16[704,512]{1,0:T(8,128)(2,1)}, u32[]{:S(2)}, u32[]{:S(2)}) collective-permute-start(bf16[704,512]{1,0:T(8,128)(2,1)} %bitcast.9.ua), channel_id=1, source_target_pairs={{0,16},{16,0},{1,17},{17,1},{2,18},{18,2},{3,19},{19,3},{4,20},{20... | collective-permute-start | bytes 2162696 | tf_op jit(solution)/shard_map/ppermute | solution.py:295
  89.1 15.0 %collective-permute-start.11 = (bf16[4,64,1024]{2,1,0:T(8,128)(2,1)}, bf16[4,64,1024]{2,1,0:T(8,128)(2,1)S(1)}, u32[]{:S(2)}, u32[]{:S(2)}) collective-permute-start(bf16[4,64,1024]{2,1,0:T(8,128)(2,1)} %all-to-all-done.2.g0.direct), channel_id=1, source_target_pairs={{0,2},{1,3},{2,0},{3,1},{4,6},{5,7},{6,4},{7,5},{8,10},{9,11},{10,... | collective-permute-start | bytes 1572872 | tf_op jit(solution)/shard_map/ppermute | solution.py:291
  95.4 18.2 %collective-permute-start.8 = (bf16[4,64,1024]{2,1,0:T(8,128)(2,1)}, bf16[4,64,1024]{2,1,0:T(8,128)(2,1)S(1)}, u32[]{:S(2)}, u32[]{:S(2)}) collective-permute-start(bf16[4,64,1024]{2,1,0:T(8,128)(2,1)} %get-tuple-element.50.n0), channel_id=1, source_target_pairs={{0,2},{1,3},{2,0},{3,1},{4,6},{5,7},{6,4},{7,5},{8,10},{9,11},{10,... | collective-permute-start | bytes 1572872 | tf_op jit(solution)/shard_map/ppermute | solution.py:291
  95.9 29.7 %collective-permute-start.16 = (bf16[704,512]{1,0:T(8,128)(2,1)S(1)}, bf16[704,512]{1,0:T(8,128)(2,1)S(1)}, u32[]{:S(2)}, u32[]{:S(2)}) collective-permute-start(bf16[704,512]{1,0:T(8,128)(2,1)S(1)} %copy-done.36), channel_id=1, source_target_pairs={{0,16},{16,0},{1,17},{17,1},{2,18},{18,2},{3,19},{19,3},{4,20},{20... | collective-permute-start | bytes 2162696 | tf_op jit(solution)/shard_map/ppermute | solution.py:295
  97.4 28.2 %collective-permute-start.12 = (bf16[4,64,1024]{2,1,0:T(8,128)(2,1)}, bf16[4,64,1024]{2,1,0:T(8,128)(2,1)}, u32[]{:S(2)}, u32[]{:S(2)}) collective-permute-start(bf16[4,64,1024]{2,1,0:T(8,128)(2,1)} %all-to-all-done.2.g0.direct), channel_id=1, source_target_pairs={{0,1},{1,0},{2,3},{3,2},{4,5},{5,4},{6,7},{7,6},{8,9},{9,8},{10,11... | collective-permute-start | bytes 1572872 | tf_op jit(solution)/shard_map/ppermute | solution.py:288
  104.1 21.5 %collective-permute-start.13 = (bf16[4,64,1024]{2,1,0:T(8,128)(2,1)S(1)}, bf16[4,64,1024]{2,1,0:T(8,128)(2,1)}, u32[]{:S(2)}, u32[]{:S(2)}) collective-permute-start(bf16[4,64,1024]{2,1,0:T(8,128)(2,1)S(1)} %collective-permute-done.11.g1), channel_id=1, source_target_pairs={{0,1},{1,0},{2,3},{3,2},{4,5},{5,4},{6,7},{7,6},{8,9},{9,8},{10,11... | collective-permute-start | bytes 1572872 | tf_op jit(solution)/shard_map/ppermute | solution.py:288
  111.8 13.8 %collective-permute-start.9 = (bf16[4,64,1024]{2,1,0:T(8,128)(2,1)}, bf16[4,64,1024]{2,1,0:T(8,128)(2,1)}, u32[]{:S(2)}, u32[]{:S(2)}) collective-permute-start(bf16[4,64,1024]{2,1,0:T(8,128)(2,1)} %get-tuple-element.50.n0), channel_id=1, source_target_pairs={{0,1},{1,0},{2,3},{3,2},{4,5},{5,4},{6,7},{7,6},{8,9},{9,8},{10,11... | collective-permute-start | bytes 1572872 | tf_op jit(solution)/shard_map/ppermute | solution.py:288
  113.5 12.1 %collective-permute-start.10 = (bf16[4,64,1024]{2,1,0:T(8,128)(2,1)S(1)}, bf16[4,64,1024]{2,1,0:T(8,128)(2,1)}, u32[]{:S(2)}, u32[]{:S(2)}) collective-permute-start(bf16[4,64,1024]{2,1,0:T(8,128)(2,1)S(1)} %collective-permute-done.8.n1), channel_id=1, source_target_pairs={{0,1},{1,0},{2,3},{3,2},{4,5},{5,4},{6,7},{7,6},{8,9},{9,8},{10,11... | collective-permute-start | bytes 1572872 | tf_op jit(solution)/shard_map/ppermute | solution.py:288
  139.7 60.5 %collective-permute-start.22 = (bf16[2,4,64,1024]{3,2,1,0:T(8,128)(2,1)}, bf16[2,4,64,1024]{3,2,1,0:T(8,128)(2,1)}, u32[]{:S(2)}, u32[]{:S(2)}) collective-permute-start(bf16[2,4,64,1024]{3,2,1,0:T(8,128)(2,1)} %get-tuple-element.55), channel_id=1, source_target_pairs={{0,1},{1,0},{2,3},{3,2},{4,5},{5,4},{6,7},{7,6},{8,9},{9,8},{10,11... | collective-permute-start | bytes 3145736 | tf_op jit(solution)/shard_map/ppermute | solution.py:288
  144.8 19.3 %collective-permute-start.48 = (bf16[704,512]{1,0:T(8,128)(2,1)}, bf16[704,512]{1,0:T(8,128)(2,1)}, u32[]{:S(2)}, u32[]{:S(2)}) collective-permute-start(bf16[704,512]{1,0:T(8,128)(2,1)} %slice.236), channel_id=1, source_target_pairs={{0,16},{16,0},{1,17},{17,1},{2,18},{18,2},{3,19},{19,3},{4,20},{20... | collective-permute-start | bytes 2162696 | tf_op jit(solution)/shard_map/ppermute | solution.py:431
  149.1 30.5 %collective-permute-start.40 = (bf16[704,512]{1,0:T(8,128)(2,1)}, bf16[704,512]{1,0:T(8,128)(2,1)}, u32[]{:S(2)}, u32[]{:S(2)}) collective-permute-start(bf16[704,512]{1,0:T(8,128)(2,1)} %slice.238), channel_id=1, source_target_pairs={{0,16},{16,0},{1,17},{17,1},{2,18},{18,2},{3,19},{19,3},{4,20},{20... | collective-permute-start | bytes 2162696 | tf_op jit(solution)/shard_map/ppermute | solution.py:431
  152.5 42.0 %collective-permute-start.44 = (bf16[704,512]{1,0:T(8,128)(2,1)}, bf16[704,512]{1,0:T(8,128)(2,1)S(1)}, u32[]{:S(2)}, u32[]{:S(2)}) collective-permute-start(bf16[704,512]{1,0:T(8,128)(2,1)} %slice.237), channel_id=1, source_target_pairs={{0,16},{16,0},{1,17},{17,1},{2,18},{18,2},{3,19},{19,3},{4,20},{20... | collective-permute-start | bytes 2162696 | tf_op jit(solution)/shard_map/ppermute | solution.py:431
  159.2 42.9 %collective-permute-start.17 = (bf16[2,4,64,1024]{3,2,1,0:T(8,128)(2,1)}, bf16[2,4,64,1024]{3,2,1,0:T(8,128)(2,1)S(1)}, u32[]{:S(2)}, u32[]{:S(2)}) collective-permute-start(bf16[2,4,64,1024]{3,2,1,0:T(8,128)(2,1)} %get-tuple-element.53), channel_id=1, source_target_pairs={{0,1},{1,0},{2,3},{3,2},{4,5},{5,4},{6,7},{7,6},{8,9},{9,8},{10,11... | collective-permute-start | bytes 3145736 | tf_op jit(solution)/shard_map/ppermute | solution.py:288
  166.0 38.8 %collective-permute-start.49 = (bf16[704,512]{1,0:T(8,128)(2,1)S(1)}, bf16[704,512]{1,0:T(8,128)(2,1)S(1)}, u32[]{:S(2)}, u32[]{:S(2)}) collective-permute-start(bf16[704,512]{1,0:T(8,128)(2,1)S(1)} %fusion.5), channel_id=1, source_target_pairs={{0,4},{12,8},{1,5},{13,9},{2,6},{14,10},{3,7},{15,11},{16,20},{28,... | collective-permute-start | bytes 2162696 | tf_op jit(solution)/shard_map/ppermute | solution.py:436
  181.0 26.8 %collective-permute-start.41 = (bf16[704,512]{1,0:T(8,128)(2,1)S(1)}, bf16[704,512]{1,0:T(8,128)(2,1)S(1)}, u32[]{:S(2)}, u32[]{:S(2)}) collective-permute-start(bf16[704,512]{1,0:T(8,128)(2,1)S(1)} %fusion.3), channel_id=1, source_target_pairs={{0,4},{12,8},{1,5},{13,9},{2,6},{14,10},{3,7},{15,11},{16,20},{28,... | collective-permute-start | bytes 2162696 | tf_op jit(solution)/shard_map/ppermute | solution.py:436
  195.5 25.8 %collective-permute-start.45 = (bf16[704,512]{1,0:T(8,128)(2,1)}, bf16[704,512]{1,0:T(8,128)(2,1)}, u32[]{:S(2)}, u32[]{:S(2)}) collective-permute-start(bf16[704,512]{1,0:T(8,128)(2,1)} %fusion.4), channel_id=1, source_target_pairs={{0,4},{12,8},{1,5},{13,9},{2,6},{14,10},{3,7},{15,11},{16,20},{28,... | collective-permute-start | bytes 2162696 | tf_op jit(solution)/shard_map/ppermute | solution.py:436
  201.5 15.0 %collective-permute-start.23 = (bf16[4,64,1024]{2,1,0:T(8,128)(2,1)S(1)}, bf16[4,64,1024]{2,1,0:T(8,128)(2,1)}, u32[]{:S(2)}, u32[]{:S(2)}) collective-permute-start(bf16[4,64,1024]{2,1,0:T(8,128)(2,1)S(1)} %fusion.8), channel_id=1, source_target_pairs={{0,2},{1,3},{2,0},{3,1},{4,6},{5,7},{6,4},{7,5},{8,10},{9,11},{10,... | collective-permute-start | bytes 1572872 | tf_op jit(solution)/shard_map/ppermute | solution.py:291
  203.2 24.4 %collective-permute-start.18 = (bf16[4,64,1024]{2,1,0:T(8,128)(2,1)}, bf16[4,64,1024]{2,1,0:T(8,128)(2,1)S(1)}, u32[]{:S(2)}, u32[]{:S(2)}) collective-permute-start(bf16[4,64,1024]{2,1,0:T(8,128)(2,1)} %fusion.7), channel_id=1, source_target_pairs={{0,2},{1,3},{2,0},{3,1},{4,6},{5,7},{6,4},{7,5},{8,10},{9,11},{10,... | collective-permute-start | bytes 1572872 | tf_op jit(solution)/shard_map/ppermute | solution.py:291
  206.2 31.1 %collective-permute-start.50 = (bf16[704,512]{1,0:T(8,128)(2,1)S(1)}, bf16[704,512]{1,0:T(8,128)(2,1)}, u32[]{:S(2)}, u32[]{:S(2)}) collective-permute-start(bf16[704,512]{1,0:T(8,128)(2,1)S(1)} %add_convert_fusion.3), channel_id=1, source_target_pairs={{4,8},{8,4},{5,9},{9,5},{6,10},{10,6},{7,11},{11,7},{20,24},{24,20... | collective-permute-start | bytes 2162696 | tf_op jit(solution)/shard_map/ppermute | solution.py:438
  210.1 30.7 %collective-permute-start.42 = (bf16[704,512]{1,0:T(8,128)(2,1)}, bf16[704,512]{1,0:T(8,128)(2,1)}, u32[]{:S(2)}, u32[]{:S(2)}) collective-permute-start(bf16[704,512]{1,0:T(8,128)(2,1)} %add_convert_fusion.7), channel_id=1, source_target_pairs={{4,8},{8,4},{5,9},{9,5},{6,10},{10,6},{7,11},{11,7},{20,24},{24,20... | collective-permute-start | bytes 2162696 | tf_op jit(solution)/shard_map/ppermute | solution.py:438
  220.8 16.6 %collective-permute-start.24 = (bf16[4,64,1024]{2,1,0:T(8,128)(2,1)}, bf16[4,64,1024]{2,1,0:T(8,128)(2,1)}, u32[]{:S(2)}, u32[]{:S(2)}) collective-permute-start(bf16[4,64,1024]{2,1,0:T(8,128)(2,1)} %get-tuple-element.57.b0), channel_id=1, source_target_pairs={{0,2},{1,3},{2,0},{3,1},{4,6},{5,7},{6,4},{7,5},{8,10},{9,11},{10,... | collective-permute-start | bytes 1572872 | tf_op jit(solution)/shard_map/ppermute | solution.py:291
  224.1 20.4 %collective-permute-start.46 = (bf16[704,512]{1,0:T(8,128)(2,1)}, bf16[704,512]{1,0:T(8,128)(2,1)S(1)}, u32[]{:S(2)}, u32[]{:S(2)}) collective-permute-start(bf16[704,512]{1,0:T(8,128)(2,1)} %add_convert_fusion.5), channel_id=1, source_target_pairs={{4,8},{8,4},{5,9},{9,5},{6,10},{10,6},{7,11},{11,7},{20,24},{24,20... | collective-permute-start | bytes 2162696 | tf_op jit(solution)/shard_map/ppermute | solution.py:438
  227.6 20.3 %collective-permute-start.25 = (bf16[4,64,1024]{2,1,0:T(8,128)(2,1)}, bf16[4,64,1024]{2,1,0:T(8,128)(2,1)S(1)}, u32[]{:S(2)}, u32[]{:S(2)}) collective-permute-start(bf16[4,64,1024]{2,1,0:T(8,128)(2,1)} %get-tuple-element.57.b0), channel_id=1, source_target_pairs={{0,1},{1,0},{2,3},{3,2},{4,5},{5,4},{6,7},{7,6},{8,9},{9,8},{10,11... | collective-permute-start | bytes 1572872 | tf_op jit(solution)/shard_map/ppermute | solution.py:288
  229.8 35.7 %all-to-all-start.3 = ((bf16[4,64,1024]{2,1,0:T(8,128)(2,1)}), bf16[4,64,1024]{2,1,0:T(8,128)(2,1)}, u32[]{:S(2)}, u32[]{:S(2)}) async-start(bf16[4,64,1024]{2,1,0:T(8,128)(2,1)} %fusion.1), calls=%async_computation.3 | async-start | bytes 1048576 | tf_op jit(solution)/shard_map/all_to_all | solution.py:499
  237.3 28.7 %collective-permute-start.26 = (bf16[4,64,1024]{2,1,0:T(8,128)(2,1)}, bf16[4,64,1024]{2,1,0:T(8,128)(2,1)S(1)}, u32[]{:S(2)}, u32[]{:S(2)}) collective-permute-start(bf16[4,64,1024]{2,1,0:T(8,128)(2,1)} %collective-permute-done.24.b1), channel_id=1, source_target_pairs={{0,1},{1,0},{2,3},{3,2},{4,5},{5,4},{6,7},{7,6},{8,9},{9,8},{10,11... | collective-permute-start | bytes 1572872 | tf_op jit(solution)/shard_map/ppermute | solution.py:288
  239.5 66.0 %collective-permute-start.51 = (bf16[704,512]{1,0:T(8,128)(2,1)}, bf16[704,512]{1,0:T(8,128)(2,1)}, u32[]{:S(2)}, u32[]{:S(2)}) collective-permute-start(bf16[704,512]{1,0:T(8,128)(2,1)} %add_convert_fusion.2), channel_id=1, source_target_pairs={{4,0},{8,12},{5,1},{9,13},{6,2},{10,14},{7,3},{11,15},{20,16},{24,... | collective-permute-start | bytes 2162696 | tf_op jit(solution)/shard_map/ppermute | solution.py:440
  243.2 64.7 %collective-permute-start.43 = (bf16[704,512]{1,0:T(8,128)(2,1)}, bf16[704,512]{1,0:T(8,128)(2,1)}, u32[]{:S(2)}, u32[]{:S(2)}) collective-permute-start(bf16[704,512]{1,0:T(8,128)(2,1)} %add_convert_fusion.6), channel_id=1, source_target_pairs={{4,0},{8,12},{5,1},{9,13},{6,2},{10,14},{7,3},{11,15},{20,16},{24,... | collective-permute-start | bytes 2162696 | tf_op jit(solution)/shard_map/ppermute | solution.py:440
  246.7 82.5 %collective-permute-start.47 = (bf16[704,512]{1,0:T(8,128)(2,1)}, bf16[704,512]{1,0:T(8,128)(2,1)}, u32[]{:S(2)}, u32[]{:S(2)}) collective-permute-start(bf16[704,512]{1,0:T(8,128)(2,1)} %add_convert_fusion.4), channel_id=1, source_target_pairs={{4,0},{8,12},{5,1},{9,13},{6,2},{10,14},{7,3},{11,15},{20,16},{24,... | collective-permute-start | bytes 2162696 | tf_op jit(solution)/shard_map/ppermute | solution.py:440
  265.5 55.6 %collective-permute-start.19 = (bf16[4,64,1024]{2,1,0:T(8,128)(2,1)}, bf16[4,64,1024]{2,1,0:T(8,128)(2,1)}, u32[]{:S(2)}, u32[]{:S(2)}) collective-permute-start(bf16[4,64,1024]{2,1,0:T(8,128)(2,1)} %all-to-all-done.3.refs_0_), channel_id=1, source_target_pairs={{0,2},{1,3},{2,0},{3,1},{4,6},{5,7},{6,4},{7,5},{8,10},{9,11},{10,... | collective-permute-start | bytes 1572872 | tf_op jit(solution)/shard_map/ppermute | solution.py:291
  285.2 66.0 %all-to-all-start.5 = ((bf16[4,4,64,256]{3,2,1,0:T(8,128)(2,1)}), bf16[4,4,64,256]{3,2,1,0:T(8,128)(2,1)}, u32[]{:S(2)}, u32[]{:S(2)}) async-start(bf16[4,4,64,256]{3,2,1,0:T(8,128)(2,1)} %get-tuple-element.67), calls=%async_computation.5 | async-start | bytes 1048576 | tf_op jit(solution)/shard_map/all_to_all | solution.py:513
  298.3 26.6 %collective-permute-start.32 = (bf16[3,512,256]{2,1,0:T(8,128)(2,1)}, bf16[3,512,256]{2,1,0:T(8,128)(2,1)S(1)}, u32[]{:S(2)}, u32[]{:S(2)}) collective-permute-start(bf16[3,512,256]{2,1,0:T(8,128)(2,1)} %slice.235), channel_id=1, source_target_pairs={{0,16},{16,0},{1,17},{17,1},{2,18},{18,2},{3,19},{19,3},{4,20},{20... | collective-permute-start | bytes 2359304 | tf_op jit(solution)/shard_map/ppermute | solution.py:431
  305.5 20.8 %collective-permute-start.27 = (bf16[2,4,64,1024]{3,2,1,0:T(8,128)(2,1)}, bf16[2,4,64,1024]{3,2,1,0:T(8,128)(2,1)S(1)}, u32[]{:S(2)}, u32[]{:S(2)}) collective-permute-start(bf16[2,4,64,1024]{3,2,1,0:T(8,128)(2,1)} %get-tuple-element.65), channel_id=1, source_target_pairs={{0,1},{1,0},{2,3},{3,2},{4,5},{5,4},{6,7},{7,6},{8,9},{9,8},{10,11... | collective-permute-start | bytes 3145736 | tf_op jit(solution)/shard_map/ppermute | solution.py:288
  307.9 13.1 %collective-permute-start.36 = (bf16[256,512]{1,0:T(8,128)(2,1)S(1)}, bf16[256,512]{1,0:T(8,128)(2,1)S(1)}, u32[]{:S(2)}, u32[]{:S(2)}) collective-permute-start(bf16[256,512]{1,0:T(8,128)(2,1)S(1)} %copy-done.28), channel_id=1, source_target_pairs={{0,16},{16,0},{1,17},{17,1},{2,18},{18,2},{3,19},{19,3},{4,20},{20... | collective-permute-start | bytes 786440 | tf_op jit(solution)/shard_map/ppermute | solution.py:431
  321.1 46.1 %collective-permute-start.20 = (bf16[4,64,1024]{2,1,0:T(8,128)(2,1)}, bf16[4,64,1024]{2,1,0:T(8,128)(2,1)}, u32[]{:S(2)}, u32[]{:S(2)}) collective-permute-start(bf16[4,64,1024]{2,1,0:T(8,128)(2,1)} %all-to-all-done.3.refs_0_), channel_id=1, source_target_pairs={{0,1},{1,0},{2,3},{3,2},{4,5},{5,4},{6,7},{7,6},{8,9},{9,8},{10,11... | collective-permute-start | bytes 1572872 | tf_op jit(solution)/shard_map/ppermute | solution.py:288
  321.2 11.9 %collective-permute-start.37 = (bf16[256,512]{1,0:T(8,128)(2,1)S(1)}, bf16[256,512]{1,0:T(8,128)(2,1)S(1)}, u32[]{:S(2)}, u32[]{:S(2)}) collective-permute-start(bf16[256,512]{1,0:T(8,128)(2,1)S(1)} %fusion.10), channel_id=1, source_target_pairs={{0,4},{12,8},{1,5},{13,9},{2,6},{14,10},{3,7},{15,11},{16,20},{28,... | collective-permute-start | bytes 786440 | tf_op jit(solution)/shard_map/ppermute | solution.py:436
  324.9 42.3 %collective-permute-start.21 = (bf16[4,64,1024]{2,1,0:T(8,128)(2,1)}, bf16[4,64,1024]{2,1,0:T(8,128)(2,1)}, u32[]{:S(2)}, u32[]{:S(2)}) collective-permute-start(bf16[4,64,1024]{2,1,0:T(8,128)(2,1)} %collective-permute-done.19.refs_1_), channel_id=1, source_target_pairs={{0,1},{1,0},{2,3},{3,2},{4,5},{5,4},{6,7},{7,6},{8,9},{9,8},{10,11... | collective-permute-start | bytes 1572872 | tf_op jit(solution)/shard_map/ppermute | solution.py:288
  326.3 21.9 %collective-permute-start.33 = (bf16[3,512,256]{2,1,0:T(8,128)(2,1)}, bf16[3,512,256]{2,1,0:T(8,128)(2,1)}, u32[]{:S(2)}, u32[]{:S(2)}) collective-permute-start(bf16[3,512,256]{2,1,0:T(8,128)(2,1)} %fusion.2), channel_id=1, source_target_pairs={{0,4},{12,8},{1,5},{13,9},{2,6},{14,10},{3,7},{15,11},{16,20},{28,... | collective-permute-start | bytes 2359304 | tf_op jit(solution)/shard_map/ppermute | solution.py:436
  329.2 14.0 %collective-permute-start.28 = (bf16[4,64,1024]{2,1,0:T(8,128)(2,1)S(1)}, bf16[4,64,1024]{2,1,0:T(8,128)(2,1)}, u32[]{:S(2)}, u32[]{:S(2)}) collective-permute-start(bf16[4,64,1024]{2,1,0:T(8,128)(2,1)S(1)} %fusion.9), channel_id=1, source_target_pairs={{0,2},{1,3},{2,0},{3,1},{4,6},{5,7},{6,4},{7,5},{8,10},{9,11},{10,... | collective-permute-start | bytes 1572872 | tf_op jit(solution)/shard_map/ppermute | solution.py:291
  333.9 23.7 %collective-permute-start.38 = (bf16[256,512]{1,0:T(8,128)(2,1)}, bf16[256,512]{1,0:T(8,128)(2,1)}, u32[]{:S(2)}, u32[]{:S(2)}) collective-permute-start(bf16[256,512]{1,0:T(8,128)(2,1)} %add_convert_fusion.13), channel_id=1, source_target_pairs={{4,8},{8,4},{5,9},{9,5},{6,10},{10,6},{7,11},{11,7},{20,24},{24,20... | collective-permute-start | bytes 786440 | tf_op jit(solution)/shard_map/ppermute | solution.py:438
  348.1 11.8 %collective-permute-start.52 = (f32[1,2304]{1,0:T(1,128)S(1)}, f32[1,2304]{1,0:T(1,128)S(1)}, u32[]{:S(2)}, u32[]{:S(2)}) collective-permute-start(f32[1,2304]{1,0:T(1,128)S(1)} %constant_dynamic-update-slice_fusion), channel_id=1, source_target_pairs={{0,4},{4,0},{8,12},{12,8},{1,5},{5,1},{9,13},{13,9},{2,6},{6,2},{1... | collective-permute-start | bytes 27656 | tf_op jit(solution)/shard_map/ppermute | solution.py:517
  350.5 37.7 %collective-permute-start.34 = (bf16[3,512,256]{2,1,0:T(8,128)(2,1)}, bf16[3,512,256]{2,1,0:T(8,128)(2,1)S(1)}, u32[]{:S(2)}, u32[]{:S(2)}) collective-permute-start(bf16[3,512,256]{2,1,0:T(8,128)(2,1)} %add_convert_fusion.1), channel_id=1, source_target_pairs={{4,8},{8,4},{5,9},{9,5},{6,10},{10,6},{7,11},{11,7},{20,24},{24,20... | collective-permute-start | bytes 2359304 | tf_op jit(solution)/shard_map/ppermute | solution.py:438
  351.2 35.5 %all-to-all-start.4 = ((bf16[4,64,1024]{2,1,0:T(8,128)(2,1)}), bf16[4,64,1024]{2,1,0:T(8,128)(2,1)S(1)}, u32[]{:S(2)}, u32[]{:S(2)}) async-start(bf16[4,64,1024]{2,1,0:T(8,128)(2,1)} %get-tuple-element.66), calls=%async_computation.4 | async-start | bytes 1048576 | tf_op jit(solution)/shard_map/all_to_all | solution.py:499
  358.7 32.2 %collective-permute-start.39 = (bf16[256,512]{1,0:T(8,128)(2,1)S(1)}, bf16[256,512]{1,0:T(8,128)(2,1)S(1)}, u32[]{:S(2)}, u32[]{:S(2)}) collective-permute-start(bf16[256,512]{1,0:T(8,128)(2,1)S(1)} %add_convert_fusion.12), channel_id=1, source_target_pairs={{4,0},{8,12},{5,1},{9,13},{6,2},{10,14},{7,3},{11,15},{20,16},{24,... | collective-permute-start | bytes 786440 | tf_op jit(solution)/shard_map/ppermute | solution.py:440
  360.0 25.0 %collective-permute-start.53 = (f32[1,2304]{1,0:T(1,128)S(1)}, f32[1,2304]{1,0:T(1,128)S(1)}, u32[]{:S(2)}, u32[]{:S(2)}) collective-permute-start(f32[1,2304]{1,0:T(1,128)S(1)} %add.170), channel_id=1, source_target_pairs={{0,8},{4,12},{8,0},{12,4},{1,9},{5,13},{9,1},{13,5},{2,10},{6,14},... | collective-permute-start | bytes 27656 | tf_op jit(solution)/shard_map/ppermute | solution.py:517
  385.1 5.7 %collective-permute-start.54 = (f32[1,1280]{1,0:T(1,128)S(1)}, f32[1,1280]{1,0:T(1,128)S(1)}, u32[]{:S(2)}, u32[]{:S(2)}) collective-permute-start(f32[1,1280]{1,0:T(1,128)S(1)} %pad_maximum_fusion.1), channel_id=1, source_target_pairs={{0,16},{16,0},{1,17},{17,1},{2,18},{18,2},{3,19},{19,3},{4,20},{20... | collective-permute-start | bytes 15368 | tf_op jit(solution)/shard_map/ppermute | solution.py:522
  386.7 12.4 %collective-permute-start.29 = (bf16[4,64,1024]{2,1,0:T(8,128)(2,1)S(1)}, bf16[4,64,1024]{2,1,0:T(8,128)(2,1)S(1)}, u32[]{:S(2)}, u32[]{:S(2)}) collective-permute-start(bf16[4,64,1024]{2,1,0:T(8,128)(2,1)S(1)} %all-to-all-done.4.refs_0_), channel_id=1, source_target_pairs={{0,2},{1,3},{2,0},{3,1},{4,6},{5,7},{6,4},{7,5},{8,10},{9,11},{10,... | collective-permute-start | bytes 1572872 | tf_op jit(solution)/shard_map/ppermute | solution.py:291
  389.5 19.5 %collective-permute-start.35 = (bf16[3,512,256]{2,1,0:T(8,128)(2,1)S(1)}, bf16[3,512,256]{2,1,0:T(8,128)(2,1)S(1)}, u32[]{:S(2)}, u32[]{:S(2)}) collective-permute-start(bf16[3,512,256]{2,1,0:T(8,128)(2,1)S(1)} %add_convert_fusion), channel_id=1, source_target_pairs={{4,0},{8,12},{5,1},{9,13},{6,2},{10,14},{7,3},{11,15},{20,16},{24,... | collective-permute-start | bytes 2359304 | tf_op jit(solution)/shard_map/ppermute | solution.py:440
  390.8 1.2 collective-permute-start.55
  392.1 7.0 %collective-permute-start.56 = (f32[1,1024]{1,0:T(1,128)S(1)}, f32[1,1024]{1,0:T(1,128)S(1)}, u32[]{:S(2)}, u32[]{:S(2)}) collective-permute-start(f32[1,1024]{1,0:T(1,128)S(1)} %add.173), channel_id=1, source_target_pairs={{0,2},{1,3},{2,0},{3,1},{4,6},{5,7},{6,4},{7,5},{8,10},{9,11},{10,... | collective-permute-start | bytes 12296 | tf_op jit(solution)/shard_map/ppermute | solution.py:536
  399.0 11.2 %collective-permute-start.30 = (bf16[4,64,1024]{2,1,0:T(8,128)(2,1)S(1)}, bf16[4,64,1024]{2,1,0:T(8,128)(2,1)S(1)}, u32[]{:S(2)}, u32[]{:S(2)}) collective-permute-start(bf16[4,64,1024]{2,1,0:T(8,128)(2,1)S(1)} %all-to-all-done.4.refs_0_), channel_id=1, source_target_pairs={{0,1},{1,0},{2,3},{3,2},{4,5},{5,4},{6,7},{7,6},{8,9},{9,8},{10,11... | collective-permute-start | bytes 1572872 | tf_op jit(solution)/shard_map/ppermute | solution.py:288
  399.1 11.1 %collective-permute-start.31 = (bf16[4,64,1024]{2,1,0:T(8,128)(2,1)S(1)}, bf16[4,64,1024]{2,1,0:T(8,128)(2,1)S(1)}, u32[]{:S(2)}, u32[]{:S(2)}) collective-permute-start(bf16[4,64,1024]{2,1,0:T(8,128)(2,1)S(1)} %collective-permute-done.29.refs_1_), channel_id=1, source_target_pairs={{0,1},{1,0},{2,3},{3,2},{4,5},{5,4},{6,7},{7,6},{8,9},{9,8},{10,11... | collective-permute-start | bytes 1572872 | tf_op jit(solution)/shard_map/ppermute | solution.py:288
  (47 other events, 349.0 us)

commit v2 on v1

v2 whole, which is shorter than its diff:
```python
import functools

import jax
import jax.numpy as jnp
from jax import lax
from jax.experimental import pallas as pl
from jax.experimental.pallas import tpu as pltpu
from jax.sharding import PartitionSpec as P

EPSILON = 1e-06
SCALE = 0.125
BF = jnp.bfloat16
F32 = jnp.float32
NN = (((1,), (0,)), ((), ()))
NT = (((1,), (1,)), ((), ()))
TN = (((0,), (0,)), ((), ()))


def dot(a, b, dims=NN):
    return lax.dot_general(a, b, dims, preferred_element_type=F32)


def full(shape):
    return pl.BlockSpec(shape, lambda *_: (0,) * len(shape))


def call(kernel, out_shapes, *args, grid=None, in_specs=None, out_specs=None, scratch=(), us=0, name=None, vmem=16):
    moved = sum(a.size * a.dtype.itemsize for a in args)
    moved += sum(o.size * o.dtype.itemsize for o in out_shapes)
    keywords = {}
    if grid is not None:
        keywords = dict(grid=grid, in_specs=in_specs, out_specs=out_specs)
    elif in_specs is not None:
        keywords = dict(in_specs=in_specs)
    return pl.pallas_call(
        kernel,
        out_shape=out_shapes,
        scratch_shapes=list(scratch),
        cost_estimate=pl.CostEstimate(flops=0, bytes_accessed=int(us * 3.4e6), transcendentals=0),
        compiler_params=pltpu.CompilerParams(vmem_limit_bytes=vmem << 20),
        name=name,
        **keywords,
    )(*args)


def shape_of(dims, dtype):
    return jax.ShapeDtypeStruct(dims, dtype)


def own_kernel(place, tokens, grads, x_o, g_o, sems):
    half = x_o.shape[2] // 2
    copies = []
    for h in range(2):
        start = pl.multiple_of(place[2 + h] * half, half)
        lanes = slice(h * half, (h + 1) * half)
        pairs = [
            (tokens.at[:, place[0], :, pl.ds(start, half)], x_o.at[:, :, lanes]),
            (grads.at[:, place[0], :, pl.ds(start, half)], g_o.at[:, 0, :, lanes]),
            (grads.at[:, place[1], :, pl.ds(start, half)], g_o.at[:, 1, :, lanes]),
        ]
        for source, out in pairs:
            copies.append(pltpu.make_async_copy(source, out, sems.at[len(copies)]))
    for copy in copies:
        copy.start()
    for copy in copies:
        copy.wait()


def half_swap(values, lane):
    width = values.shape[-1]
    ahead = pltpu.roll(values, width - 32, 1)
    behind = pltpu.roll(values, 32, 1)
    return jnp.where(lane % 64 < 32, ahead, behind)


def signed_tables(cos_ref, sin_ref, index, width, lane):
    cosine = jnp.concatenate([cos_ref[index]] * (width // 128), axis=1)
    sine = jnp.concatenate([sin_ref[index]] * (width // 128), axis=1)
    return cosine, jnp.where(lane % 64 < 32, -sine, sine)


def qkv_kernel(p0, p1, p2, p3, gain, wa, wb, cos, sin, na_o, nb_o, q_o, k_o, v_o):
    x = jnp.concatenate([p0[0], p1[0], p2[0], p3[0]], axis=0).astype(F32)
    half = wa.shape[1]
    inverse = lax.rsqrt(jnp.mean(x * x, axis=-1, keepdims=True) + EPSILON)
    normed = (x * inverse * gain[...]).astype(BF)
    width = wa.shape[2]
    lane = lax.broadcasted_iota(jnp.int32, (1, width), 1)
    cosine, sine = signed_tables(cos, sin, 0, width, lane)
    na, nb = normed[:, :half], normed[:, half:]
    na_o[0] = na
    nb_o[0] = nb
    raw = [dot(na, wa[i]) + dot(nb, wb[i]) for i in range(3)]
    q_o[0] = (raw[0] * cosine + half_swap(raw[0], lane) * sine).astype(BF)
    k_o[0] = (raw[1] * cosine + half_swap(raw[1], lane) * sine).astype(BF)
    v_o[0] = raw[2]


def attend_kernel(seg, q, k, raw, fv, mix, woa, wob, v_o, att_o, lse_o, keep_o, send_o, v_t, o_t):
    blocks, rows, width = q.shape
    heads = width // 64
    for b in range(blocks):
        first = jnp.concatenate([fv[b, seg[r]] for r in range(4)], axis=0).astype(F32)
        value = mix[...] * raw[b] + (1.0 - mix[...]) * first
        v_o[b] = value.astype(BF)
        v_t[:, b * rows:(b + 1) * rows] = value.T.astype(BF)
    lane = lax.broadcasted_iota(jnp.int32, (1, width), 1) // 64

    def head(h, carry):
        own = lane == h
        for qb in range(blocks):
            qm = jnp.where(own, q[qb], jnp.zeros_like(q[qb]))
            scores = [dot(k[kb], qm, NT) * SCALE for kb in range(qb + 1)]
            top = functools.reduce(jnp.maximum, [jnp.max(s, axis=0, keepdims=True) for s in scores])
            total = jnp.zeros((1, rows), F32)
            out = jnp.zeros((64, rows), F32)
            for kb in range(qb + 1):
                e = jnp.exp(scores[kb] - top)
                total = total + jnp.sum(e, axis=0, keepdims=True)
                out = out + dot(v_t[pl.ds(pl.multiple_of(h * 64, 64), 64), kb * rows:(kb + 1) * rows], e.astype(BF))
            o_t[qb, pl.ds(pl.multiple_of(h * 64, 64), 64), :] = out / total
            lse_o[h, qb:qb + 1, :] = top + jnp.log(total)
        return carry

    lax.fori_loop(0, heads, head, 0)
    half = woa.shape[1]
    quarter = rows // 4
    for qb in range(blocks):
        att = o_t[qb].T.astype(BF)
        att_o[qb] = att
        for lo, w in ((0, woa), (half, wob)):
            part = dot(att, w[...])
            for p in range(2):
                keep_o[p, qb, :, lo:lo + half] = part[p * quarter:(p + 1) * quarter]
                send_o[p, qb, :, lo:lo + half] = part[(2 + p) * quarter:(3 + p) * quarter].astype(BF)


def residual_kernel(x, keep, got_core, got_x, gain, residual_o, normed_o):
    residual = (
        x[0].astype(F32) + keep[0, 0] + got_core[0, 0].astype(F32) + got_x[0].astype(F32)
    )
    inverse = lax.rsqrt(jnp.mean(residual * residual, axis=-1, keepdims=True) + EPSILON)
    residual_o[0] = residual
    normed_o[0] = (residual * inverse * gain[...]).astype(BF)


def mlp_kernel(
    n0, n1, n2, n3, g0, g1, ga, gb, ua, ub, da, db,
    na_o, nb_o, la_o, lb_o, hidden_o, dgate_o, dup_o, keep_o, send_o,
):
    n = jnp.concatenate([n0[0], n1[0], n2[0], n3[0]], axis=0)
    g = jnp.concatenate([g0[0, 0], g0[0, 1], g1[0, 0], g1[0, 1]], axis=0)
    half = ga.shape[1]
    na, nb = n[:, :half], n[:, half:]
    na_o[0] = na
    nb_o[0] = nb
    la_o[0] = g[:, :half]
    lb_o[0] = g[:, half:]
    gate = dot(na, ga[...], NT) + dot(nb, gb[...], NT)
    up = dot(na, ua[...], NT) + dot(nb, ub[...], NT)
    grad_hidden = dot(g[:, :half], da[...], NT) + dot(g[:, half:], db[...], NT)
    s = jax.nn.sigmoid(gate)
    active = gate * s
    hidden_o[0] = (active * up).astype(BF)
    dgate = (grad_hidden * up * s * (1.0 + gate * (1.0 - s))).astype(BF)
    dup = (grad_hidden * active).astype(BF)
    dgate_o[0] = dgate
    dup_o[0] = dup
    quarter = n.shape[0] // 4
    for lo, wg, wu in ((0, ga, ua), (half, gb, ub)):
        part = dot(dgate, wg[...]) + dot(dup, wu[...])
        for p in range(2):
            keep_o[p, 0, :, lo:lo + half] = part[p * quarter:(p + 1) * quarter]
            send_o[p, 0, :, lo:lo + half] = part[(2 + p) * quarter:(3 + p) * quarter].astype(BF)


def down_kernel(hidden, da, db, keep_o, send_o):
    half = da.shape[1]
    quarter = hidden.shape[1] // 4
    for lo, w in ((0, da), (half, db)):
        part = dot(hidden[0], w[...])
        for p in range(2):
            keep_o[p, 0, :, lo:lo + half] = part[p * quarter:(p + 1) * quarter]
            send_o[p, 0, :, lo:lo + half] = part[(2 + p) * quarter:(3 + p) * quarter].astype(BF)


def norm_back_kernel(direct, keep, got_core, got_x, values, gain, grad_o, low_o, gain_o):
    @pl.when(pl.program_id(0) == 0)
    def _():
        gain_o[...] = jnp.zeros_like(gain_o)

    grad = keep[0, 0] + got_core[0, 0].astype(F32) + got_x[0].astype(F32)
    x = values[0].astype(F32)
    inverse = lax.rsqrt(jnp.mean(x * x, axis=-1, keepdims=True) + EPSILON)
    weighted = grad * gain[...]
    gain_o[...] += jnp.sum(grad * x * inverse, axis=0, keepdims=True)
    out = direct[0].astype(F32) + (
        inverse * weighted
        - x * (inverse * inverse * inverse) * jnp.mean(weighted * x, axis=-1, keepdims=True)
    )
    grad_o[0] = out
    low_o[0] = out.astype(BF)


def attend_back_kernel(
    seg, b0, b1, b2, b3, woa, wob, q, k, v, att, lse, cos, sin, mix, raw, fv,
    p0, p1, p2, p3, wa, wb, gain_in,
    g_o, gf_o, keep_o, send_o, own_o, other_o,
    gat, dmat, k_t, dk, dv, dq_t, og,
):
    blocks, rows, width = q.shape
    heads = width // 64
    half = woa.shape[1]
    lane_full = lax.broadcasted_iota(jnp.int32, (1, width), 1)
    lane = lane_full // 64
    pick = (
        lax.broadcasted_iota(jnp.int32, (8, width), 0)
        == lax.broadcasted_iota(jnp.int32, (8, width), 1) // 64
    ).astype(F32)
    og[...] = jnp.zeros_like(og)
    for b in range(blocks):
        g = jnp.concatenate([b0[b], b1[b], b2[b], b3[b]], axis=0)
        og[...] += dot(att[b], g, TN)
        ga = (dot(g[:, :half], woa[...], NT) + dot(g[:, half:], wob[...], NT)).astype(BF)
        gat[b] = ga
        prod = ga.astype(F32) * att[b].astype(F32)
        dmat[b] = lax.dot_general(pick, prod, NT, precision=lax.Precision.HIGHEST, preferred_element_type=F32)
        k_t[:, b * rows:(b + 1) * rows] = k[b].astype(F32).T.astype(BF)
    dk[...] = jnp.zeros_like(dk)
    dv[...] = jnp.zeros_like(dv)

    def head(h, carry):
        own = lane == h
        for qb in range(blocks):
            qm = jnp.where(own, q[qb], jnp.zeros_like(q[qb]))
            gm = jnp.where(own, gat[qb], jnp.zeros_like(gat[qb]))
            log_total = lse[h, qb:qb + 1, :]
            row_dot = dmat[qb, pl.ds(h, 1), :]
            acc = jnp.zeros((64, rows), F32)
            for kb in range(qb + 1):
                prob = jnp.exp(dot(k[kb], qm, NT) * SCALE - log_total)
                dprob = dot(v[kb], gm, NT)
                ds = (prob * (dprob - row_dot)).astype(BF)
                dv[kb] += dot(prob.astype(BF), gm)
                dk[kb] += dot(ds, qm)
                acc = acc + dot(k_t[pl.ds(pl.multiple_of(h * 64, 64), 64), kb * rows:(kb + 1) * rows], ds)
            dq_t[qb, pl.ds(pl.multiple_of(h * 64, 64), 64), :] = acc
        return carry

    lax.fori_loop(0, heads, head, 0)
    quarter = rows // 4
    total = jnp.zeros((1, width), F32)
    gains = [jnp.zeros((1, half), F32) for _ in range(2)]
    for b in range(blocks):
        cosine, sine = signed_tables(cos, sin, b, width, lane_full)
        gq = dq_t[b].T * SCALE
        gk = dk[b] * SCALE
        gv = dv[b]
        grads = [
            (gq * cosine - half_swap(gq, lane_full) * sine).astype(BF),
            (gk * cosine - half_swap(gk, lane_full) * sine).astype(BF),
            (mix[...] * gv).astype(BF),
        ]
        for i, grad in enumerate(grads):
            g_o[b, :, i * width:(i + 1) * width] = grad
        x = jnp.concatenate([p0[b], p1[b], p2[b], p3[b]], axis=0).astype(F32)
        x = x * lax.rsqrt(jnp.mean(x * x, axis=-1, keepdims=True) + EPSILON)
        for i, w in enumerate((wa, wb)):
            lanes = slice(i * half, (i + 1) * half)
            part = sum(dot(grad, w[j], NT) for j, grad in enumerate(grads))
            gains[i] = gains[i] + jnp.sum(part * x[:, lanes], axis=0, keepdims=True)
            for p in range(2):
                keep_o[p, b, :, lanes] = part[p * quarter:(p + 1) * quarter]
                send_o[p, b, :, lanes] = part[(2 + p) * quarter:(3 + p) * quarter].astype(BF)
        gf = ((1.0 - mix[...]) * gv).astype(BF)
        for r in range(4):
            gf_o[b, seg[r]] = gf[r * quarter:(r + 1) * quarter]
        first = jnp.concatenate([fv[b, seg[r]] for r in range(4)], axis=0).astype(F32)
        total = total + jnp.sum(gv * (raw[b] - first), axis=0, keepdims=True)
    row = lax.broadcasted_iota(jnp.int32, (16, half), 0)
    mixed = jnp.concatenate([total, jnp.zeros((1, half - width), F32)], axis=1)
    for i, out in enumerate((own_o, other_o)):
        lanes = slice(i * half, (i + 1) * half)
        extra = jnp.where(row == 0, gains[i], jnp.where(row == 1, gain_in[:, lanes], jnp.where(row == 2, mixed, 0.0)))
        out[:width] = og[:, lanes].astype(out.dtype)
        out[width:] = extra.astype(out.dtype)


def place_kernel(where, roll, *refs):
    pieces, out = refs[:-1], refs[-1]
    width = out.shape[-1]
    half = width // 2
    for r, piece in enumerate(pieces):
        value = piece[0]
        low, high = value[:, :half], value[:, half:]
        swap = roll[0] == 1
        out[0, where[r], :, :half] = jnp.where(swap, high, low).astype(out.dtype)
        out[0, where[r], :, half:] = jnp.where(swap, low, high).astype(out.dtype)


def first_kernel(got, out):
    out[...] = got[...].astype(out.dtype)


def on_device(
    fsdp, ctx, tp,
    tokens, first_values, out_grad, w_qkv, output_weight, w_gate, w_up, w_down, gain_attn, gain_mlp, mix,
):
    seqs, block, width = tokens.shape
    local = w_qkv.shape[2]
    hidden_width = w_gate.shape[1]
    quarter = block // tp
    half = width // 2
    pair = fsdp == 2
    assert seqs == ctx and ctx == 4 and tp == 4 and local <= half
    y = lax.axis_index("fsdp")
    z = lax.axis_index("ctx")
    t = lax.axis_index("tp")
    swap_y = [(0, 1), (1, 0)]
    by_core = [(i, i ^ 1) for i in range(tp)]
    by_x = [(i, i ^ 2) for i in range(tp)]

    def tie(*values):
        return lax.optimization_barrier(values)

    def core(value):
        return lax.ppermute(value, "tp", by_core)

    def across(value):
        return lax.ppermute(value, "tp", by_x)

    def other_half(value, axis):
        if pair:
            return value, lax.ppermute(value, "fsdp", swap_y)
        whole = lax.all_gather(value, "fsdp", axis=axis, tiled=True)
        return tuple(lax.slice_in_dim(whole, i * half, (i + 1) * half, axis=axis) for i in range(2))

    def added(keep, got, i):
        return keep[i] + got[i].astype(F32)

    rows = ctx * block
    smem = pl.BlockSpec(memory_space=pltpu.SMEM)
    piece_spec = pl.BlockSpec((1, quarter, width), lambda b: (b, 0, 0))
    pair_spec = pl.BlockSpec((1, 2, quarter, width), lambda b: (b, 0, 0, 0))
    pair_first = pl.BlockSpec((1, None, quarter, width), lambda b: (b, 0, 0, 0))
    block_local = pl.BlockSpec((1, block, local), lambda b: (b, 0, 0))
    block_half = pl.BlockSpec((1, block, half), lambda b: (b, 0, 0))
    block_hidden = pl.BlockSpec((1, block, hidden_width), lambda b: (b, 0, 0))
    block_table = pl.BlockSpec((1, block, 128), lambda b: (b, 0, 0))
    part_spec = pl.BlockSpec((2, 1, quarter, width), lambda b: (0, b, 0, 0))
    first_part = pl.BlockSpec((1, 1, quarter, width), lambda b: (0, b, 0, 0))
    gain_spec = full((1, width))
    keep_shape = shape_of((2, ctx, quarter, width), F32)
    send_shape = shape_of((2, ctx, quarter, width), BF)
    own_f32 = shape_of((ctx, quarter, width), F32)
    own_low = shape_of((ctx, quarter, width), BF)
    rows_local = shape_of((ctx, block, local), BF)
    rows_half = shape_of((ctx, block, half), BF)
    rows_hidden = shape_of((ctx, block, hidden_width), BF)
    gain_row = shape_of((1, width), F32)

    seg = jnp.stack([t, t ^ 2, t ^ 1, t ^ 3]).astype(jnp.int32)
    turn = y if pair else y * 0
    roll = jnp.reshape(turn, (1,)).astype(jnp.int32)
    x_part, g_part = call(
        own_kernel,
        [shape_of((seqs, quarter, width), BF), shape_of((seqs, 2, quarter, width), BF)],
        jnp.stack([t, t ^ 2, turn, 1 - turn]).astype(jnp.int32),
        tokens.reshape(seqs, tp, quarter, width), out_grad.reshape(seqs, tp, quarter, width),
        in_specs=[smem] + [pl.BlockSpec(memory_space=pltpu.HBM)] * 2,
        scratch=[pltpu.SemaphoreType.DMA((6,))],
        name="own", vmem=4,
    )
    place = (seg[:, None] * quarter + jnp.arange(quarter)[None, :]).reshape(block)
    positions = (jnp.arange(ctx)[:, None] * block + place[None, :]).astype(F32)
    lanes = (jnp.arange(128) % 32).astype(F32)
    table = positions[:, :, None] * (10000.0 ** (-lanes / 32.0))[None, None, :]
    cosine, sine = jnp.cos(table), jnp.sin(table)
    mix_row = jnp.repeat(mix, local // mix.shape[0])[None, :]

    qkv_a, qkv_b = other_half(jnp.transpose(w_qkv, (1, 0, 2)), 1)
    out_a, out_b = other_half(
        jnp.concatenate([output_weight, jnp.stack([gain_attn, gain_mlp])], axis=0), 1
    )
    gate_a, gate_b = other_half(w_gate.T, 1)
    up_a, up_b = other_half(w_up.T, 1)
    down_a, down_b = other_half(w_down, 1)

    x_own = lax.all_to_all(x_part, "ctx", 0, 0)
    x_own, qkv_b, cosine, sine, mix_row = tie(x_own, qkv_b, cosine, sine, mix_row)
    x_second = across(x_own)
    fv = lax.all_to_all(first_values, "ctx", 0, 0).reshape(ctx, tp, quarter, local)
    x_second, out_b = tie(x_second, out_b)
    x_pieces = (x_own, x_second, core(x_own), core(x_second))
    gains = jnp.concatenate([out_a[local:], out_b[local:]], axis=1).astype(F32)
    out_a, out_b = out_a[:local], out_b[:local]
    gain_first, gain_second = gains[0:1], gains[1:2]

    norm_a, norm_b, queries, keys, raw = call(
        qkv_kernel,
        [rows_half, rows_half, rows_local, rows_local, shape_of((ctx, block, local), F32)],
        *x_pieces, gain_first, qkv_a, qkv_b, cosine, sine,
        grid=(ctx,),
        in_specs=[piece_spec] * 4 + [
            gain_spec, full((3, half, local)), full((3, half, local)), block_table, block_table,
        ],
        out_specs=[block_half] * 2 + [block_local] * 3,
        name="norm_qkv",
    )
    values, attended, log_total, keep, send = call(
        attend_kernel,
        [rows_local, rows_local, shape_of((mix.shape[0], ctx, block), F32), keep_shape, send_shape],
        seg, queries, keys, raw, fv, mix_row, out_a, out_b,
        in_specs=[smem] + [pl.BlockSpec(memory_space=pltpu.VMEM)] * 7,
        scratch=[pltpu.VMEM((local, rows), BF), pltpu.VMEM((ctx, local, block), F32)],
        name="attend",
    )
    send, gate_b = tie(send, gate_b)
    got_core = core(send)
    got_x = across(added(keep, got_core, 1).astype(BF))
    g_first = lax.all_to_all(g_part, "ctx", 0, 0)
    got_x, up_b, g_first = tie(got_x, up_b, g_first)
    residual, normed_own = call(
        residual_kernel,
        [own_f32, own_low],
        x_own, keep, got_core, got_x, gain_second,
        grid=(ctx,),
        in_specs=[piece_spec, first_part, first_part, piece_spec, gain_spec],
        out_specs=[piece_spec, piece_spec],
        name="residual_norm", vmem=6,
    )
    n_second = across(normed_own)
    g_second = core(g_first)
    n_second, down_b, g_second = tie(n_second, down_b, g_second)
    mlp_a, mlp_b, last_a, last_b, hidden, grad_gate, grad_up, keep, send = call(
        mlp_kernel,
        [rows_half] * 4 + [rows_hidden] * 3 + [keep_shape, send_shape],
        normed_own, n_second, core(normed_own), core(n_second), g_first, g_second,
        gate_a, gate_b, up_a, up_b, down_a, down_b,
        grid=(ctx,),
        in_specs=[piece_spec] * 4 + [pair_spec] * 2 + [full((hidden_width, half))] * 6,
        out_specs=[block_half] * 4 + [block_hidden] * 3 + [part_spec] * 2,
        name="mlp", vmem=24,
    )

    def weight_grad(left, right):
        return lax.dot_general(
            left.reshape(rows, -1), right.reshape(rows, -1), TN, preferred_element_type=F32
        )

    def exchange(first, second, axis=1):
        if pair:
            return lax.ppermute(second, "fsdp", swap_y)
        return lax.psum_scatter(
            jnp.concatenate([first.astype(BF), second], axis=axis), "fsdp", scatter_dimension=axis, tiled=True
        )

    def joined(first, received):
        return (first + received.astype(F32)).astype(BF) if pair else received

    def plus(shard, received):
        return (shard.astype(F32) + received.astype(F32)).astype(BF)

    def toward(shard):
        return lax.ppermute(shard, "ctx", [(0, 1), (3, 2)])

    def meet(shard):
        return lax.ppermute(shard, "ctx", [(1, 2), (2, 1)])

    def back(shard):
        return lax.ppermute(shard, "ctx", [(1, 0), (2, 3)])

    def settled(shard, received):
        return jnp.where((z == 0) | (z == 3), received, shard).astype(F32)

    got_core = core(send)
    gate_first = weight_grad(grad_gate, mlp_a)
    gate_second = weight_grad(grad_gate, mlp_b).astype(BF)
    onward = added(keep, got_core, 1).astype(BF)

    onward, gate_first, gate_second, grad_up, hidden = tie(onward, gate_first, gate_second, grad_up, hidden)
    got_x = across(onward)
    gate_got = exchange(gate_first, gate_second)
    up_first = weight_grad(grad_up, mlp_a)
    up_second = weight_grad(grad_up, mlp_b).astype(BF)
    down_first = weight_grad(hidden, last_a)
    down_second = weight_grad(hidden, last_b).astype(BF)
    grad_residual, branch_own, gain_sum_second = call(
        norm_back_kernel,
        [own_f32, own_low, gain_row],
        g_first, keep, got_core, got_x, residual, gain_second,
        grid=(ctx,),
        in_specs=[pair_first, first_part, first_part, piece_spec, piece_spec, gain_spec],
        out_specs=[piece_spec, piece_spec, gain_spec],
        name="norm_back_mlp", vmem=6, us=10,
    )
    (
        branch_own, grad_residual, gate_got, gate_first, up_first, up_second, down_first, down_second, hidden,
    ) = tie(branch_own, grad_residual, gate_got, gate_first, up_first, up_second, down_first, down_second, hidden)

    b_second = across(branch_own)
    b_core = core(branch_own)
    b_both = core(b_second)
    up_got = exchange(up_first, up_second)
    gate_shard = joined(gate_first, gate_got)
    gate_more = toward(gate_shard)
    down_keep, down_send = call(
        down_kernel,
        [keep_shape, send_shape],
        hidden, down_a, down_b,
        grid=(ctx,),
        in_specs=[block_hidden, full((hidden_width, half)), full((hidden_width, half))],
        out_specs=[part_spec, part_spec],
        name="down", vmem=12,
    )
    down_core = core(down_send)
    down_onward = added(down_keep, down_core, 1).astype(BF)
    output_own = residual + added(down_keep, down_core, 0)
    (
        b_second, b_core, b_both, up_got, gate_shard, gate_more, down_onward, output_own, down_second,
    ) = tie(b_second, b_core, b_both, up_got, gate_shard, gate_more, down_onward, output_own, down_second)

    down_x = across(down_onward)
    down_got = exchange(down_first, down_second)
    gate_shard = plus(gate_shard, gate_more)
    gate_more = meet(gate_shard)
    up_shard = joined(up_first, up_got)
    up_more = toward(up_shard)
    payload = shape_of((local + 16, half), F32), shape_of((local + 16, half), BF)
    grads, gf, keep, send, out_first, out_second = call(
        attend_back_kernel,
        [shape_of((ctx, block, 3 * local), BF), shape_of((ctx, tp, quarter, local), BF), keep_shape, send_shape, *payload],
        seg, branch_own, b_second, b_core, b_both, out_a, out_b,
        queries, keys, values, attended, log_total, cosine, sine, mix_row, raw, fv,
        *x_pieces, qkv_a, qkv_b, gain_sum_second,
        in_specs=[smem] + [pl.BlockSpec(memory_space=pltpu.VMEM)] * 23,
        scratch=[
            pltpu.VMEM((ctx, block, local), BF),
            pltpu.VMEM((ctx, 8, block), F32),
            pltpu.VMEM((local, rows), BF),
            pltpu.VMEM((ctx, block, local), F32),
            pltpu.VMEM((ctx, block, local), F32),
            pltpu.VMEM((ctx, local, block), F32),
            pltpu.VMEM((local, width), F32),
        ],
        name="attend_back", vmem=36,
    )
    got_core = core(send)
    onward = added(keep, got_core, 1).astype(BF)
    (
        onward, grads, out_second, down_got, gate_shard, gate_more, up_shard, up_more, down_x,
    ) = tie(onward, grads, out_second, down_got, gate_shard, gate_more, up_shard, up_more, down_x)

    got_x = across(onward)
    gate_shard = plus(gate_shard, gate_more)
    gate_more = back(gate_shard)
    up_shard = plus(up_shard, up_more)
    up_more = meet(up_shard)
    down_shard = joined(down_first, down_got)
    down_more = toward(down_shard)
    out_got = exchange(out_first, out_second)
    qkv_first = weight_grad(norm_a, grads)
    qkv_second = weight_grad(norm_b, grads).astype(BF)
    qkv_got = exchange(qkv_first, qkv_second, 0)
    output_own = (output_own + down_x.astype(F32)).astype(BF)
    _, tokens_own, _ = call(
        norm_back_kernel,
        [own_f32, own_low, gain_row],
        grad_residual, keep, got_core, got_x, x_own, gain_first,
        grid=(ctx,),
        in_specs=[piece_spec, first_part, first_part, piece_spec, piece_spec, gain_spec],
        out_specs=[piece_spec, piece_spec, gain_spec],
        name="norm_back_attn", vmem=6, us=10,
    )
    (
        tokens_own, output_own, gate_shard, gate_more, up_shard, up_more, down_shard, down_more,
    ) = tie(tokens_own, output_own, gate_shard, gate_more, up_shard, up_more, down_shard, down_more)

    tokens_home = lax.all_to_all(tokens_own, "ctx", 0, 0)
    grad_w_gate = settled(gate_shard, gate_more).T
    up_shard = plus(up_shard, up_more)
    down_shard = plus(down_shard, down_more)
    (
        tokens_home, output_own, gf, up_shard, down_shard, out_got, qkv_got,
    ) = tie(tokens_home, output_own, gf, up_shard, down_shard, out_got, qkv_got)
    tokens_second = across(tokens_home)
    output_home = lax.all_to_all(output_own, "ctx", 0, 0)
    up_more = back(up_shard)
    down_more = meet(down_shard)
    out_shard = joined(out_first, out_got)
    out_more = toward(out_shard)
    qkv_shard = joined(qkv_first, qkv_got)
    qkv_more = toward(qkv_shard)
    (
        tokens_second, output_home, gf, up_more, down_more, out_more, qkv_more,
    ) = tie(tokens_second, output_home, gf, up_more, down_more, out_more, qkv_more)
    output_second = across(output_home)
    first_home = lax.all_to_all(gf, "ctx", 0, 0)
    grad_w_up = settled(up_shard, up_more).T
    down_shard = plus(down_shard, down_more)
    down_more = back(down_shard)
    out_shard = plus(out_shard, out_more)
    out_more = meet(out_shard)
    qkv_shard = plus(qkv_shard, qkv_more)
    qkv_more = meet(qkv_shard)
    (
        output_second, first_home, down_more, out_more, qkv_more,
    ) = tie(output_second, first_home, down_more, out_more, qkv_more)
    grad_w_down = settled(down_shard, down_more)
    out_shard = plus(out_shard, out_more)
    qkv_shard = plus(qkv_shard, qkv_more)
    out_full = settled(out_shard, back(out_shard))
    qkv_full = settled(qkv_shard, back(qkv_shard))
    grad_w_qkv = qkv_full.reshape(-1, 3, local)
    grad_w_out = out_full[:local]

    def placed(own, second, dtype):
        return call(
            place_kernel,
            [shape_of((seqs, tp, quarter, width), dtype)],
            seg, roll, own, second, core(own), core(second),
            grid=(seqs,),
            in_specs=[smem, smem] + [piece_spec] * 4,
            out_specs=[pl.BlockSpec((1, tp, quarter, width), lambda b: (b, 0, 0, 0))],
            name="place", vmem=6,
        )[0].reshape(seqs, block, width)

    grad_tokens = placed(tokens_home, tokens_second, F32)
    output = placed(output_home, output_second, BF)
    grad_first = first_home.reshape(seqs, block, local).astype(F32)

    share = gain_attn.shape[0]
    gain_grads = out_full[local:local + 2]
    for move in (core, across):
        gain_grads = gain_grads + move(gain_grads)
    mixed = out_full[local + 2:local + 3]
    if not pair:
        mixed = lax.all_gather(mixed, "fsdp", axis=1, tiled=True)
    mixed = mixed[:, :local]
    grad_mix = jnp.sum(mixed.reshape(mix.shape[0], -1), axis=1)
    return (
        output, grad_tokens, grad_first, grad_w_qkv, grad_w_out, grad_w_gate, grad_w_up, grad_w_down,
        gain_grads[0, :share], gain_grads[1, :share], grad_mix,
    )


def solution(mesh):
    rows = P("fsdp", "ctx", None)
    in_specs = (
        rows, P("fsdp", "ctx", "tp"), rows, P("fsdp", None, "tp"), P("tp", "fsdp"), P("fsdp", "tp"),
        P("fsdp", "tp"), P("tp", "fsdp"), P("fsdp"), P("fsdp"), P("tp"),
    )
    out_specs = (
        rows, rows, P("fsdp", "ctx", "tp"), P("fsdp", None, "tp"), P("tp", "fsdp"), P("fsdp", "tp"),
        P("fsdp", "tp"), P("tp", "fsdp"), P("fsdp"), P("fsdp"), P("tp"),
    )
    sizes = [mesh.shape[name] for name in ("fsdp", "ctx", "tp")]
    return jax.shard_map(
        functools.partial(on_device, *sizes), mesh=mesh, in_specs=in_specs, out_specs=out_specs,
        check_vma=False,
    )
```

time: 418 us -> 379 us (0.907)
  Pallas kernels: 82.3 us -> 56.2 us
  other arithmetic: 50.3 us -> 31.4 us
  local copies, waits for them, and re-layouts: 17.1 us -> 31 us
  starting transfers between devices: 93.3 us -> 86 us
    pallas_call x11, Pallas kernels: 82.3 us -> 56.2 us  [call(): pl.pallas_call(kernel, out_shape=out_shapes, scratch_shapes=list(scratch)...]
    all_to_all x5, waiting for transfers between devices: 37.8 us -> 18.9 us  [the longest x1 6.78 us: on_device(): g_first = lax.all_to_all(g_part, 'ctx', 0, 0)]
    unnamed x98 -> x115, local copies, waits for them, and re-layouts: 8 us -> 26.6 us
    ppermute x6 -> x5, waiting for transfers between devices: 19.8 us -> 34.8 us  [other_half(): return (value, lax.ppermute(value, 'fsdp', swap_y))]
    convert_element_type x24 -> x22, other arithmetic: 35.5 us -> 21.3 us  [the longest x9 12.3 us: plus(): return (shard.astype(F32) + received.astype(F32)).astype(BF)]
    ppermute x10, waiting for transfers between devices: 38.4 us -> 51.2 us  [across(): return lax.ppermute(value, 'tp', by_x)]
    ppermute x25 -> x20, waiting for transfers between devices: 63.6 us -> 51.5 us  [the longest x5 29.6 us: back(): return lax.ppermute(shard, 'ctx', [(1, 0), (2, 3)])]
    slice x10 -> x6, local copies, waits for them, and re-layouts: 7.57 us -> 2.23 us  [the longest x1 0.83 us: on_device(): grad_w_out = out_full[:local]]
  transfers between devices with their start and end apart: 63 -> 57, of which waited for: 20 -> 27; matrix products, arithmetic and copies ran while one was open for 17% -> 11% of each run, Pallas kernels for 13% -> 7%
where the time goes in v2:
time: 379 us; the launch traced here: 377 us
  waiting for transfers between devices  160 us (42%)
  starting transfers between devices  86 us (23%)
  Pallas kernels  56.2 us (15%)
  other arithmetic  31.4 us (8%)
  local copies, waits for them, and re-layouts  31 us (8%)
  matrix products  11.1 us (3%)
    pallas_call x11, Pallas kernels, call(): pl.pallas_call(kernel, out_shape=out_shapes, scratch_shapes=list(scratch)...  56.2 us
    ppermute x10, waiting for transfers between devices, across(): return lax.ppermute(value, 'tp', by_x)  51.2 us
    ppermute x5, waiting for transfers between devices, other_half(): return (value, lax.ppermute(value, 'fsdp', swap_y))  34.8 us
    ppermute x5, waiting for transfers between devices, back(): return lax.ppermute(shard, 'ctx', [(1, 0), (2, 3)])  29.6 us
    unnamed x115, local copies, waits for them, and re-layouts  26.6 us
    ppermute x5, starting transfers between devices, toward(): return lax.ppermute(shard, 'ctx', [(0, 1), (3, 2)])  26.1 us
    ppermute x5, waiting for transfers between devices, toward(): return lax.ppermute(shard, 'ctx', [(0, 1), (3, 2)])  15.5 us
    convert_element_type x9, other arithmetic, plus(): return (shard.astype(F32) + received.astype(F32)).astype(BF)  12.3 us
  transfers between devices with their start and end apart: 57, of which 27 were waited for; matrix products, arithmetic and copies ran while one was open for 11% of the time, Pallas kernels for 7%

profile of v2, /device:TPU:0, one launch (start us, length us, event | category | flops | bytes accessed | tf_op | source)
XLA Modules:
  0.0 377.3 jit_solution(549409829811647953)
XLA Ops:
  0.6 3.1 collective-permute-start
  3.8 1.6 copy-done.19
  5.4 1.6 copy-done.20
  9.5 5.0 %all-to-all-start = ((bf16[4,64,1024]{2,1,0:T(8,128)(2,1)}), bf16[4,64,1024]{2,1,0:T(8,128)(2,1)S(1)}, u32[]{:S(2)}, u32[]{:S(2)}) async-start(bf16[4,64,1024]{2,1,0:T(8,128)(2,1)} %get-tuple-element.120), calls=%async_computation | async-start | bytes 1048576 | tf_op jit(solution)/shard_map/all_to_all | solution.py:389
  14.9 1.9 multiply_sine_fusion
  16.8 4.6 %collective-permute-done.wb = bf16[3,512,256]{2,1,0:T(8,128)(2,1)S(1)} collective-permute-done((bf16[3,512,256]{2,1,0:T(8,128)(2,1)}, bf16[3,512,256]{2,1,0:T(8,128)(2,1)S(1)}, u32[]{:S(2)}, u32[]{:S(2)}) %collective-permute-start) | collective-permute-done | bytes 786464 | tf_op jit(solution)/shard_map/ppermute | solution.py:334
  22.3 6.3 %all-to-all-done.p0.x.values = bf16[4,64,1024]{2,1,0:T(8,128)(2,1)S(1)} async-done(((bf16[4,64,1024]{2,1,0:T(8,128)(2,1)}), bf16[4,64,1024]{2,1,0:T(8,128)(2,1)S(1)}, u32[]{:S(2)}, u32[]{:S(2)}) %all-to-all-start) | async-done | bytes 524320 | tf_op jit(solution)/shard_map/all_to_all | solution.py:389
  30.8 3.5 all-to-all-start.1
  34.3 1.6 collective-permute-start.5
  35.9 3.5 collective-permute-done.2
  39.3 2.3 collective-permute-done.1.p1
  46.9 3.4 norm_qkv.1
  58.7 10.6 %attend.1 = (bf16[4,256,256]{2,1,0:T(8,128)(2,1)S(1)}, bf16[4,256,256]{2,1,0:T(8,128)(2,1)S(1)}, f32[4,4,256]{2,1,0:T(4,128)S(1)}, f32[2,4,64,1024]{3,2,1,0:T(8,128)S(1)}, bf16[2,4,64,1024]{3,2,1,0:T(8,128)(2,1)}) custom-call(s32[4]{0:T(128)S(1)} %get-tuple-element.252.seg.where, bf16[4,256,256]{2,1,0:T(8,128)(2,1)S(1)} %copy-done.14, ...), custom_call_target="tpu_custom_call" | custom-call | tf_op jit(solution)/shard_map/attend/pallas_call | solution.py:35
  72.4 3.7 all-to-all-start.2
  76.6 2.3 fusion.4
  80.4 14.3 %collective-permute-done.8.ub = bf16[704,512]{1,0:T(8,128)(2,1)S(1)} collective-permute-done((bf16[704,512]{1,0:T(8,128)(2,1)}, bf16[704,512]{1,0:T(8,128)(2,1)S(1)}, u32[]{:S(2)}, u32[]{:S(2)}) %collective-permute-start.8) | collective-permute-done | bytes 720928 | tf_op jit(solution)/shard_map/ppermute | solution.py:334
  95.6 6.8 %all-to-all-done.2.g0.direct = bf16[4,2,64,1024]{3,2,1,0:T(8,128)(2,1)S(1)} async-done(((bf16[4,2,64,1024]{3,2,1,0:T(8,128)(2,1)}), bf16[4,2,64,1024]{3,2,1,0:T(8,128)(2,1)S(1)}, u32[]{:S(2)}, u32[]{:S(2)}) %all-to-all-start.2) | async-done | bytes 1048608 | tf_op jit(solution)/shard_map/all_to_all | solution.py:421
  102.9 1.6 copy-done.1
  104.5 2.6 residual_norm.1
  108.7 12.4 %collective-permute-done.10.db = bf16[704,512]{1,0:T(8,128)(2,1)S(1)} collective-permute-done((bf16[704,512]{1,0:T(8,128)(2,1)}, bf16[704,512]{1,0:T(8,128)(2,1)S(1)}, u32[]{:S(2)}, u32[]{:S(2)}) %collective-permute-start.10) | collective-permute-done | bytes 720928 | tf_op jit(solution)/shard_map/ppermute | solution.py:334
  121.3 1.9 collective-permute-done.13.n3
  123.2 10.6 %mlp.1 = (bf16[4,256,512]{2,1,0:T(8,128)(2,1)S(1)}, bf16[4,256,512]{2,1,0:T(8,128)(2,1)S(1)}, bf16[4,256,512]{2,1,0:T(8,128)(2,1)S(1)}, bf16[4,256,512]{2,1,0:T(...) custom-call(bf16[4,64,1024]{2,1,0:T(8,128)(2,1)S(1)} %get-tuple-elem, ...), custom_call_target="tpu_custom_call" | custom-call | tf_op jit(solution)/shard_map/mlp/pallas_call | solution.py:35
  137.7 1.6 collective-permute-start.16
  143.7 10.3 %collective-permute-done.15.got_x = bf16[4,64,1024]{2,1,0:T(8,128)(2,1)S(1)} collective-permute-done((bf16[4,64,1024]{2,1,0:T(8,128)(2,1)S(1)}, bf16[4,64,1024]{2,1,0:T(8,128)(2,1)S(1)}, u32[]{:S(2)}, u32[]{:S(2)}) %collective-permute-start.15) | collective-permute-done | bytes 524320 | tf_op jit(solution)/shard_map/ppermute | solution.py:330
  155.9 2.5 down.1
  160.3 1.7 collective-permute-start.21
  162.0 1.6 collective-permute-start.20
  163.6 9.2 %collective-permute-done.17.b1 = bf16[4,64,1024]{2,1,0:T(8,128)(2,1)S(1)} collective-permute-done((bf16[4,64,1024]{2,1,0:T(8,128)(2,1)S(1)}, bf16[4,64,1024]{2,1,0:T(8,128)(2,1)S(1)}, u32[]{:S(2)}, u32[]{:S(2)}) %collective-permute-start.17) | collective-permute-done | bytes 524320 | tf_op jit(solution)/shard_map/ppermute | solution.py:330
  173.4 4.3 %collective-permute-done.21 = bf16[704,512]{1,0:T(8,128)(2,1)S(1)} collective-permute-done((bf16[704,512]{1,0:T(8,128)(2,1)S(1)}, bf16[704,512]{1,0:T(8,128)(2,1)S(1)}, u32[]{:S(2)}, u32[]{:S(2)}) %collective-permute-start.21) | collective-permute-done | bytes 720928 | tf_op jit(solution)/shard_map/ppermute | solution.py:465
  177.7 2.5 collective-permute-done.20
  180.3 16.6 %attend_back.1 = (bf16[4,256,768]{2,1,0:T(8,128)(2,1)S(1)}, bf16[4,4,64,256]{3,2,1,0:T(8,128)(2,1)}, f32[2,4,64,1024]{3,2,1,0:T(8,128)S(1)}, bf16[2,4,64,1024]{3...) custom-call(s32[4]{0:T(128)S(1)} %get-tuple-element.252.seg.where, ...), custom_call_target="tpu_custom_call" | custom-call | tf_op jit(solution)/shard_map/attend_back/pallas_call | solution.py:35
  199.6 3.7 collective-permute-start.26
  204.1 12.8 %collective-permute-done.27 = bf16[4,64,1024]{2,1,0:T(8,128)(2,1)S(1)} collective-permute-done((bf16[4,64,1024]{2,1,0:T(8,128)(2,1)S(1)}, bf16[4,64,1024]{2,1,0:T(8,128)(2,1)S(1)}, u32[]{:S(2)}, u32[]{:S(2)}) %collective-permute-start.27) | collective-permute-done | bytes 524320 | tf_op jit(solution)/shard_map/ppermute | solution.py:330
  216.9 1.9 collective-permute-done.26
  221.6 7.1 %collective-permute-start.31 = (bf16[704,512]{1,0:T(8,128)(2,1)S(1)}, bf16[704,512]{1,0:T(8,128)(2,1)S(1)}, u32[]{:S(2)}, u32[]{:S(2)}) collective-permute-start(bf16[704,512]{1,0:T(8,128)(2,1)S(1)} %add_convert_fusion.5), channel_id=1, source_target_pairs={{0,4},{12,8},{1,5},{13,9},{2,6},{14,10},{3,7},{15,11},{16,20},{28,... | collective-permute-start | bytes 2162696 | tf_op jit(solution)/shard_map/ppermute | solution.py:465
  229.3 1.9 bitcast_convert_fusion
  232.7 8.4 %collective-permute-done.28.got_x = bf16[4,64,1024]{2,1,0:T(8,128)(2,1)S(1)} collective-permute-done((bf16[4,64,1024]{2,1,0:T(8,128)(2,1)S(1)}, bf16[4,64,1024]{2,1,0:T(8,128)(2,1)S(1)}, u32[]{:S(2)}, u32[]{:S(2)}) %collective-permute-start.28) | collective-permute-done | bytes 524320 | tf_op jit(solution)/shard_map/ppermute | solution.py:330
  241.1 2.1 norm_back_attn.1
  245.2 3.7 all-to-all-start.3
  249.5 3.3 add_convert_fusion.3
  252.8 2.8 collective-permute-done.32
  255.6 5.8 %all-to-all-done.3.refs_0_ = bf16[4,64,1024]{2,1,0:T(8,128)(2,1)S(1)} async-done(((bf16[4,64,1024]{2,1,0:T(8,128)(2,1)}), bf16[4,64,1024]{2,1,0:T(8,128)(2,1)S(1)}, u32[]{:S(2)}, u32[]{:S(2)}) %all-to-all-start.3) | async-done | bytes 524320 | tf_op jit(solution)/shard_map/all_to_all | solution.py:579
  261.4 3.5 all-to-all-start.4
  264.9 3.6 fusion
  268.4 4.8 %collective-permute-start.38 = (bf16[512,768]{1,0:T(8,128)(2,1)}, bf16[512,768]{1,0:T(8,128)(2,1)}, u32[]{:S(2)}, u32[]{:S(2)}) collective-permute-start(bf16[512,768]{1,0:T(8,128)(2,1)} %fusion), channel_id=1, source_target_pairs={{0,4},{12,8},{1,5},{13,9},{2,6},{14,10},{3,7},{15,11},{16,20},{28,... | collective-permute-start | bytes 2359304 | tf_op jit(solution)/shard_map/ppermute | solution.py:465
  275.9 8.8 %collective-permute-start.37 = (bf16[272,512]{1,0:T(8,128)(2,1)S(1)}, bf16[272,512]{1,0:T(8,128)(2,1)}, u32[]{:S(2)}, u32[]{:S(2)}) collective-permute-start(bf16[272,512]{1,0:T(8,128)(2,1)S(1)} %add_convert_fusion.18), channel_id=1, source_target_pairs={{0,4},{12,8},{1,5},{13,9},{2,6},{14,10},{3,7},{15,11},{16,20},{28,... | collective-permute-start | bytes 835592 | tf_op jit(solution)/shard_map/ppermute | solution.py:465
  284.7 9.3 %collective-permute-done.37 = bf16[272,512]{1,0:T(8,128)(2,1)} collective-permute-done((bf16[272,512]{1,0:T(8,128)(2,1)S(1)}, bf16[272,512]{1,0:T(8,128)(2,1)}, u32[]{:S(2)}, u32[]{:S(2)}) %collective-permute-start.37) | collective-permute-done | bytes 278560 | tf_op jit(solution)/shard_map/ppermute | solution.py:465
  294.9 2.4 add_convert_fusion.1
  297.3 2.4 add_convert_fusion.2
  299.7 5.9 %all-to-all-start.5 = ((bf16[4,4,64,256]{3,2,1,0:T(8,128)(2,1)}), bf16[4,4,64,256]{3,2,1,0:T(8,128)(2,1)}, u32[]{:S(2)}, u32[]{:S(2)}) async-start(bf16[4,4,64,256]{3,2,1,0:T(8,128)(2,1)} %get-tuple-element.216), calls=%async_computation.5 | async-start | bytes 1048576 | tf_op jit(solution)/shard_map/all_to_all | solution.py:598
  307.0 1.6 collective-permute-start.42
  308.6 2.3 convert_bitcast_fusion.1
  313.4 2.3 convert_bitcast_fusion
  315.7 3.0 place.3
  318.7 6.5 %collective-permute-done.39.refs_1_ = bf16[4,64,1024]{2,1,0:T(8,128)(2,1)S(1)} collective-permute-done((bf16[4,64,1024]{2,1,0:T(8,128)(2,1)S(1)}, bf16[4,64,1024]{2,1,0:T(8,128)(2,1)S(1)}, u32[]{:S(2)}, u32[]{:S(2)}) %collective-permute-start.39) | collective-permute-done | bytes 524320 | tf_op jit(solution)/shard_map/ppermute | solution.py:330
  325.2 7.5 %collective-permute-done.40 = bf16[704,512]{1,0:T(8,128)(2,1)} collective-permute-done((bf16[704,512]{1,0:T(8,128)(2,1)}, bf16[704,512]{1,0:T(8,128)(2,1)}, u32[]{:S(2)}, u32[]{:S(2)}) %collective-permute-start.40) | collective-permute-done | bytes 720928 | tf_op jit(solution)/shard_map/ppermute | solution.py:471
  338.1 2.1 bitcast_convert_fusion.1
  340.2 15.1 %collective-permute-done.48 = bf16[272,512]{1,0:T(8,128)(2,1)S(1)} collective-permute-done((bf16[272,512]{1,0:T(8,128)(2,1)S(1)}, bf16[272,512]{1,0:T(8,128)(2,1)S(1)}, u32[]{:S(2)}, u32[]{:S(2)}) %collective-permute-start.48) | collective-permute-done | bytes 278560 | tf_op jit(solution)/shard_map/ppermute | solution.py:471
  355.4 2.3 select_convert_fusion.1
  362.0 2.4 place.2
  364.4 7.0 %collective-permute-done.47 = bf16[512,768]{1,0:T(8,128)(2,1)} collective-permute-done((bf16[512,768]{1,0:T(8,128)(2,1)S(1)}, bf16[512,768]{1,0:T(8,128)(2,1)}, u32[]{:S(2)}, u32[]{:S(2)}) %collective-permute-start.47) | collective-permute-done | bytes 786464 | tf_op jit(solution)/shard_map/ppermute | solution.py:471
  371.4 2.4 select_convert_fusion
  373.8 1.9 copy.39
  375.7 1.6 copy.40
  (235 shorter events, 68.2 us)
Async XLA Ops:
  0.6 20.8 %collective-permute-start = (bf16[3,512,256]{2,1,0:T(8,128)(2,1)}, bf16[3,512,256]{2,1,0:T(8,128)(2,1)S(1)}, u32[]{:S(2)}, u32[]{:S(2)}) collective-permute-start(bf16[3,512,256]{2,1,0:T(8,128)(2,1)} %bitcast.76), channel_id=1, source_target_pairs={{0,16},{16,0},{1,17},{17,1},{2,18},{18,2},{3,19},{19,3},{4,20},{20... | collective-permute-start | bytes 2359304 | tf_op jit(solution)/shard_map/ppermute | solution.py:334
  9.5 20.7 %copy-start.54 = (bf16[512]{0:T(512)(128)(2,1)S(1)}, bf16[512]{0:T(512)(128)(2,1)}, u32[]{:S(2)}) copy-start(bf16[512]{0:T(512)(128)(2,1)} %param.19) | copy-start | bytes 3076
  9.5 20.7 %copy-start.55 = (bf16[512]{0:T(512)(128)(2,1)S(1)}, bf16[512]{0:T(512)(128)(2,1)}, u32[]{:S(2)}) copy-start(bf16[512]{0:T(512)(128)(2,1)} %param.20) | copy-start | bytes 3076
  9.5 20.7 %copy-start.10 = (bf16[256,512]{1,0:T(8,128)(2,1)S(1)}, bf16[256,512]{1,0:T(8,128)(2,1)}, u32[]{:S(2)}) copy-start(bf16[256,512]{1,0:T(8,128)(2,1)} %woa.3) | copy-start | bytes 786436
  9.5 19.2 %all-to-all-start = ((bf16[4,64,1024]{2,1,0:T(8,128)(2,1)}), bf16[4,64,1024]{2,1,0:T(8,128)(2,1)S(1)}, u32[]{:S(2)}, u32[]{:S(2)}) async-start(bf16[4,64,1024]{2,1,0:T(8,128)(2,1)} %get-tuple-element.120), calls=%async_computation | async-start | bytes 1048576 | tf_op jit(solution)/shard_map/all_to_all | solution.py:389
  28.7 12.9 %collective-permute-start.1 = (bf16[4,64,1024]{2,1,0:T(8,128)(2,1)S(1)}, bf16[4,64,1024]{2,1,0:T(8,128)(2,1)S(1)}, u32[]{:S(2)}, u32[]{:S(2)}) collective-permute-start(bf16[4,64,1024]{2,1,0:T(8,128)(2,1)S(1)} %all-to-all-done.p0.x.values), channel_id=1, source_target_pairs={{0,2},{1,3},{2,0},{3,1},{4,6},{5,7},{6,4},{7,5},{8,10},{9,11},{10,... | collective-permute-start | bytes 1572872 | tf_op jit(solution)/shard_map/ppermute | solution.py:330
  30.2 9.1 %collective-permute-start.2 = (bf16[258,512]{1,0:T(8,128)(2,1)S(1)}, bf16[258,512]{1,0:T(8,128)(2,1)S(1)}, u32[]{:S(2)}, u32[]{:S(2)}) collective-permute-start(bf16[258,512]{1,0:T(8,128)(2,1)S(1)} %pad_maximum_fusion), channel_id=1, source_target_pairs={{0,16},{16,0},{1,17},{17,1},{2,18},{18,2},{3,19},{19,3},{4,20},{20... | collective-permute-start | bytes 792584 | tf_op jit(solution)/shard_map/ppermute | solution.py:334
  30.8 24.7 %all-to-all-start.1 = ((bf16[4,256,256]{2,1,0:T(8,128)(2,1)}), bf16[4,256,256]{2,1,0:T(8,128)(2,1)S(1)}, u32[]{:S(2)}, u32[]{:S(2)}) async-start(bf16[4,256,256]{2,1,0:T(8,128)(2,1)} %param.12), calls=%async_computation.1 | async-start | bytes 1048576 | tf_op jit(solution)/shard_map/all_to_all | solution.py:392
  34.3 37.9 %collective-permute-start.5 = (bf16[704,512]{1,0:T(8,128)(2,1)}, bf16[704,512]{1,0:T(8,128)(2,1)}, u32[]{:S(2)}, u32[]{:S(2)}) collective-permute-start(bf16[704,512]{1,0:T(8,128)(2,1)} %bitcast.81), channel_id=1, source_target_pairs={{0,16},{16,0},{1,17},{17,1},{2,18},{18,2},{3,19},{19,3},{4,20},{20... | collective-permute-start | bytes 2162696 | tf_op jit(solution)/shard_map/ppermute | solution.py:334
  35.9 6.6 %collective-permute-start.3 = (bf16[4,64,1024]{2,1,0:T(8,128)(2,1)S(1)}, bf16[4,64,1024]{2,1,0:T(8,128)(2,1)S(1)}, u32[]{:S(2)}, u32[]{:S(2)}) collective-permute-start(bf16[4,64,1024]{2,1,0:T(8,128)(2,1)S(1)} %all-to-all-done.p0.x.values), channel_id=1, source_target_pairs={{0,1},{1,0},{2,3},{3,2},{4,5},{5,4},{6,7},{7,6},{8,9},{9,8},{10,11... | collective-permute-start | bytes 1572872 | tf_op jit(solution)/shard_map/ppermute | solution.py:327
  41.6 1.9 collective-permute-start.4
  72.2 4.4 %collective-permute-start.6 = (bf16[2,4,64,1024]{3,2,1,0:T(8,128)(2,1)}, bf16[2,4,64,1024]{3,2,1,0:T(8,128)(2,1)}, u32[]{:S(2)}, u32[]{:S(2)}) collective-permute-start(bf16[2,4,64,1024]{3,2,1,0:T(8,128)(2,1)} %get-tuple-element.133), channel_id=1, source_target_pairs={{0,1},{1,0},{2,3},{3,2},{4,5},{5,4},{6,7},{7,6},{8,9},{9,8},{10,11... | collective-permute-start | bytes 3145736 | tf_op jit(solution)/shard_map/ppermute | solution.py:327
  72.4 30.0 %all-to-all-start.2 = ((bf16[4,2,64,1024]{3,2,1,0:T(8,128)(2,1)}), bf16[4,2,64,1024]{3,2,1,0:T(8,128)(2,1)S(1)}, u32[]{:S(2)}, u32[]{:S(2)}) async-start(bf16[4,2,64,1024]{3,2,1,0:T(8,128)(2,1)} %copy-done.28), calls=%async_computation.2 | async-start | bytes 2097152 | tf_op jit(solution)/shard_map/all_to_all | solution.py:421
  76.1 18.7 %collective-permute-start.8 = (bf16[704,512]{1,0:T(8,128)(2,1)}, bf16[704,512]{1,0:T(8,128)(2,1)S(1)}, u32[]{:S(2)}, u32[]{:S(2)}) collective-permute-start(bf16[704,512]{1,0:T(8,128)(2,1)} %bitcast.83), channel_id=1, source_target_pairs={{0,16},{16,0},{1,17},{17,1},{2,18},{18,2},{3,19},{19,3},{4,20},{20... | collective-permute-start | bytes 2162696 | tf_op jit(solution)/shard_map/ppermute | solution.py:334
  78.9 23.5 %collective-permute-start.7 = (bf16[4,64,1024]{2,1,0:T(8,128)(2,1)}, bf16[4,64,1024]{2,1,0:T(8,128)(2,1)}, u32[]{:S(2)}, u32[]{:S(2)}) collective-permute-start(bf16[4,64,1024]{2,1,0:T(8,128)(2,1)} %fusion.4), channel_id=1, source_target_pairs={{0,2},{1,3},{2,0},{3,1},{4,6},{5,7},{6,4},{7,5},{8,10},{9,11},{10,... | collective-permute-start | bytes 1572872 | tf_op jit(solution)/shard_map/ppermute | solution.py:330
  102.4 18.9 %collective-permute-start.11 = (bf16[4,2,64,1024]{3,2,1,0:T(8,128)(2,1)S(1)}, bf16[4,2,64,1024]{3,2,1,0:T(8,128)(2,1)S(1)}, u32[]{:S(2)}, u32[]{:S(2)}) collective-permute-start(bf16[4,2,64,1024]{3,2,1,0:T(8,128)(2,1)S(1)} %all-to-all-done.2.g0.direct), channel_id=1, source_target_pairs={{0,1},{1,0},{2,3},{3,2},{4,5},{5,4},{6,7},{7,6},{8,9},{9,8},{10,11... | collective-permute-start | bytes 3145736 | tf_op jit(solution)/shard_map/ppermute | solution.py:327
  102.4 18.8 %collective-permute-start.10 = (bf16[704,512]{1,0:T(8,128)(2,1)}, bf16[704,512]{1,0:T(8,128)(2,1)S(1)}, u32[]{:S(2)}, u32[]{:S(2)}) collective-permute-start(bf16[704,512]{1,0:T(8,128)(2,1)} %da.3), channel_id=1, source_target_pairs={{0,16},{16,0},{1,17},{17,1},{2,18},{18,2},{3,19},{19,3},{4,20},{20... | collective-permute-start | bytes 2162696 | tf_op jit(solution)/shard_map/ppermute | solution.py:334
  107.2 14.1 %collective-permute-start.9 = (bf16[4,64,1024]{2,1,0:T(8,128)(2,1)S(1)}, bf16[4,64,1024]{2,1,0:T(8,128)(2,1)S(1)}, u32[]{:S(2)}, u32[]{:S(2)}) collective-permute-start(bf16[4,64,1024]{2,1,0:T(8,128)(2,1)S(1)} %get-tuple-element.137.n0), channel_id=1, source_target_pairs={{0,2},{1,3},{2,0},{3,1},{4,6},{5,7},{6,4},{7,5},{8,10},{9,11},{10,... | collective-permute-start | bytes 1572872 | tf_op jit(solution)/shard_map/ppermute | solution.py:330
  108.7 12.6 %collective-permute-start.12 = (bf16[4,64,1024]{2,1,0:T(8,128)(2,1)S(1)}, bf16[4,64,1024]{2,1,0:T(8,128)(2,1)S(1)}, u32[]{:S(2)}, u32[]{:S(2)}) collective-permute-start(bf16[4,64,1024]{2,1,0:T(8,128)(2,1)S(1)} %get-tuple-element.137.n0), channel_id=1, source_target_pairs={{0,1},{1,0},{2,3},{3,2},{4,5},{5,4},{6,7},{7,6},{8,9},{9,8},{10,11... | collective-permute-start | bytes 1572872 | tf_op jit(solution)/shard_map/ppermute | solution.py:327
  121.3 1.9 collective-permute-start.13
  133.9 2.7 collective-permute-start.14
  137.7 18.2 %collective-permute-start.16 = (bf16[704,512]{1,0:T(8,128)(2,1)S(1)}, bf16[704,512]{1,0:T(8,128)(2,1)S(1)}, u32[]{:S(2)}, u32[]{:S(2)}) collective-permute-start(bf16[704,512]{1,0:T(8,128)(2,1)S(1)} %fusion.1), channel_id=1, source_target_pairs={{0,16},{16,0},{1,17},{17,1},{2,18},{18,2},{3,19},{19,3},{4,20},{20... | collective-permute-start | bytes 2162696 | tf_op jit(solution)/shard_map/ppermute | solution.py:453
  140.2 13.7 %collective-permute-start.15 = (bf16[4,64,1024]{2,1,0:T(8,128)(2,1)S(1)}, bf16[4,64,1024]{2,1,0:T(8,128)(2,1)S(1)}, u32[]{:S(2)}, u32[]{:S(2)}) collective-permute-start(bf16[4,64,1024]{2,1,0:T(8,128)(2,1)S(1)} %fusion.5), channel_id=1, source_target_pairs={{0,2},{1,3},{2,0},{3,1},{4,6},{5,7},{6,4},{7,5},{8,10},{9,11},{10,... | collective-permute-start | bytes 1572872 | tf_op jit(solution)/shard_map/ppermute | solution.py:330
  158.4 14.4 %collective-permute-start.22 = (bf16[2,4,64,1024]{3,2,1,0:T(8,128)(2,1)S(1)}, bf16[2,4,64,1024]{3,2,1,0:T(8,128)(2,1)S(1)}, u32[]{:S(2)}, u32[]{:S(2)}) collective-permute-start(bf16[2,4,64,1024]{3,2,1,0:T(8,128)(2,1)S(1)} %get-tuple-element.167), channel_id=1, source_target_pairs={{0,1},{1,0},{2,3},{3,2},{4,5},{5,4},{6,7},{7,6},{8,9},{9,8},{10,11... | collective-permute-start | bytes 3145736 | tf_op jit(solution)/shard_map/ppermute | solution.py:327
  158.5 14.3 %collective-permute-start.17 = (bf16[4,64,1024]{2,1,0:T(8,128)(2,1)S(1)}, bf16[4,64,1024]{2,1,0:T(8,128)(2,1)S(1)}, u32[]{:S(2)}, u32[]{:S(2)}) collective-permute-start(bf16[4,64,1024]{2,1,0:T(8,128)(2,1)S(1)} %get-tuple-element.161.b0), channel_id=1, source_target_pairs={{0,2},{1,3},{2,0},{3,1},{4,6},{5,7},{6,4},{7,5},{8,10},{9,11},{10,... | collective-permute-start | bytes 1572872 | tf_op jit(solution)/shard_map/ppermute | solution.py:330
  160.0 20.2 %copy-start.34 = (bf16[4,256,256]{2,1,0:T(8,128)(2,1)S(1)}, bf16[4,256,256]{2,1,0:T(8,128)(2,1)}, u32[]{:S(2)}) copy-start(bf16[4,256,256]{2,1,0:T(8,128)(2,1)} %copy-done.33) | copy-start | bytes 1572868
  160.0 20.2 %copy-start.36 = (bf16[4,256,256]{2,1,0:T(8,128)(2,1)S(1)}, bf16[4,256,256]{2,1,0:T(8,128)(2,1)}, u32[]{:S(2)}) copy-start(bf16[4,256,256]{2,1,0:T(8,128)(2,1)} %copy-done.35) | copy-start | bytes 1572868
  160.3 17.4 %collective-permute-start.21 = (bf16[704,512]{1,0:T(8,128)(2,1)S(1)}, bf16[704,512]{1,0:T(8,128)(2,1)S(1)}, u32[]{:S(2)}, u32[]{:S(2)}) collective-permute-start(bf16[704,512]{1,0:T(8,128)(2,1)S(1)} %add_convert_fusion.10), channel_id=1, source_target_pairs={{0,4},{12,8},{1,5},{13,9},{2,6},{14,10},{3,7},{15,11},{16,20},{28,... | collective-permute-start | bytes 2162696 | tf_op jit(solution)/shard_map/ppermute | solution.py:465
  162.0 18.3 %collective-permute-start.20 = (bf16[704,512]{1,0:T(8,128)(2,1)S(1)}, bf16[704,512]{1,0:T(8,128)(2,1)S(1)}, u32[]{:S(2)}, u32[]{:S(2)}) collective-permute-start(bf16[704,512]{1,0:T(8,128)(2,1)S(1)} %fusion.2), channel_id=1, source_target_pairs={{0,16},{16,0},{1,17},{17,1},{2,18},{18,2},{3,19},{19,3},{4,20},{20... | collective-permute-start | bytes 2162696 | tf_op jit(solution)/shard_map/ppermute | solution.py:453
  163.6 9.8 %collective-permute-start.18 = (bf16[4,64,1024]{2,1,0:T(8,128)(2,1)S(1)}, bf16[4,64,1024]{2,1,0:T(8,128)(2,1)S(1)}, u32[]{:S(2)}, u32[]{:S(2)}) collective-permute-start(bf16[4,64,1024]{2,1,0:T(8,128)(2,1)S(1)} %get-tuple-element.161.b0), channel_id=1, source_target_pairs={{0,1},{1,0},{2,3},{3,2},{4,5},{5,4},{6,7},{7,6},{8,9},{9,8},{10,11... | collective-permute-start | bytes 1572872 | tf_op jit(solution)/shard_map/ppermute | solution.py:327
  172.8 7.4 %collective-permute-start.19 = (bf16[4,64,1024]{2,1,0:T(8,128)(2,1)S(1)}, bf16[4,64,1024]{2,1,0:T(8,128)(2,1)S(1)}, u32[]{:S(2)}, u32[]{:S(2)}) collective-permute-start(bf16[4,64,1024]{2,1,0:T(8,128)(2,1)S(1)} %collective-permute-done.17.b1), channel_id=1, source_target_pairs={{0,1},{1,0},{2,3},{3,2},{4,5},{5,4},{6,7},{7,6},{8,9},{9,8},{10,11... | collective-permute-start | bytes 1572872 | tf_op jit(solution)/shard_map/ppermute | solution.py:327
  196.9 32.4 %copy-start.37 = (bf16[4,256,768]{2,1,0:T(8,128)(2,1)}, bf16[4,256,768]{2,1,0:T(8,128)(2,1)S(1)}, u32[]{:S(2)}) copy-start(bf16[4,256,768]{2,1,0:T(8,128)(2,1)S(1)} %get-tuple-element.205) | copy-start | bytes 4718596
  196.9 7.0 %collective-permute-start.23 = (bf16[2,4,64,1024]{3,2,1,0:T(8,128)(2,1)S(1)}, bf16[2,4,64,1024]{3,2,1,0:T(8,128)(2,1)S(1)}, u32[]{:S(2)}, u32[]{:S(2)}) collective-permute-start(bf16[2,4,64,1024]{3,2,1,0:T(8,128)(2,1)S(1)} %get-tuple-element.177), channel_id=1, source_target_pairs={{0,1},{1,0},{2,3},{3,2},{4,5},{5,4},{6,7},{7,6},{8,9},{9,8},{10,11... | collective-permute-start | bytes 3145736 | tf_op jit(solution)/shard_map/ppermute | solution.py:327
  197.1 19.8 %collective-permute-start.25 = (bf16[704,512]{1,0:T(8,128)(2,1)S(1)}, bf16[704,512]{1,0:T(8,128)(2,1)S(1)}, u32[]{:S(2)}, u32[]{:S(2)}) collective-permute-start(bf16[704,512]{1,0:T(8,128)(2,1)S(1)} %add_convert_fusion.9), channel_id=1, source_target_pairs={{4,8},{8,4},{5,9},{9,5},{6,10},{10,6},{7,11},{11,7},{20,24},{24,20... | collective-permute-start | bytes 2162696 | tf_op jit(solution)/shard_map/ppermute | solution.py:468
  197.8 19.1 %collective-permute-start.24 = (bf16[704,512]{1,0:T(8,128)(2,1)S(1)}, bf16[704,512]{1,0:T(8,128)(2,1)S(1)}, u32[]{:S(2)}, u32[]{:S(2)}) collective-permute-start(bf16[704,512]{1,0:T(8,128)(2,1)S(1)} %fusion.3), channel_id=1, source_target_pairs={{0,16},{16,0},{1,17},{17,1},{2,18},{18,2},{3,19},{19,3},{4,20},{20... | collective-permute-start | bytes 2162696 | tf_op jit(solution)/shard_map/ppermute | solution.py:453
  199.6 19.1 %collective-permute-start.26 = (bf16[704,512]{1,0:T(8,128)(2,1)S(1)}, bf16[704,512]{1,0:T(8,128)(2,1)S(1)}, u32[]{:S(2)}, u32[]{:S(2)}) collective-permute-start(bf16[704,512]{1,0:T(8,128)(2,1)S(1)} %add_convert_fusion.8), channel_id=1, source_target_pairs={{0,4},{12,8},{1,5},{13,9},{2,6},{14,10},{3,7},{15,11},{16,20},{28,... | collective-permute-start | bytes 2162696 | tf_op jit(solution)/shard_map/ppermute | solution.py:465
  203.3 13.6 %collective-permute-start.27 = (bf16[4,64,1024]{2,1,0:T(8,128)(2,1)S(1)}, bf16[4,64,1024]{2,1,0:T(8,128)(2,1)S(1)}, u32[]{:S(2)}, u32[]{:S(2)}) collective-permute-start(bf16[4,64,1024]{2,1,0:T(8,128)(2,1)S(1)} %fusion.6), channel_id=1, source_target_pairs={{0,2},{1,3},{2,0},{3,1},{4,6},{5,7},{6,4},{7,5},{8,10},{9,11},{10,... | collective-permute-start | bytes 1572872 | tf_op jit(solution)/shard_map/ppermute | solution.py:330
  218.9 24.3 %collective-permute-start.30 = (bf16[704,512]{1,0:T(8,128)(2,1)S(1)}, bf16[704,512]{1,0:T(8,128)(2,1)S(1)}, u32[]{:S(2)}, u32[]{:S(2)}) collective-permute-start(bf16[704,512]{1,0:T(8,128)(2,1)S(1)} %add_convert_fusion.6), channel_id=1, source_target_pairs={{4,8},{8,4},{5,9},{9,5},{6,10},{10,6},{7,11},{11,7},{20,24},{24,20... | collective-permute-start | bytes 2162696 | tf_op jit(solution)/shard_map/ppermute | solution.py:468
  219.9 23.4 %collective-permute-start.29 = (bf16[704,512]{1,0:T(8,128)(2,1)S(1)}, bf16[704,512]{1,0:T(8,128)(2,1)S(1)}, u32[]{:S(2)}, u32[]{:S(2)}) collective-permute-start(bf16[704,512]{1,0:T(8,128)(2,1)S(1)} %add_convert_fusion.7), channel_id=1, source_target_pairs={{4,0},{8,12},{5,1},{9,13},{6,2},{10,14},{7,3},{11,15},{20,16},{24,... | collective-permute-start | bytes 2162696 | tf_op jit(solution)/shard_map/ppermute | solution.py:471
  221.6 21.7 %collective-permute-start.31 = (bf16[704,512]{1,0:T(8,128)(2,1)S(1)}, bf16[704,512]{1,0:T(8,128)(2,1)S(1)}, u32[]{:S(2)}, u32[]{:S(2)}) collective-permute-start(bf16[704,512]{1,0:T(8,128)(2,1)S(1)} %add_convert_fusion.5), channel_id=1, source_target_pairs={{0,4},{12,8},{1,5},{13,9},{2,6},{14,10},{3,7},{15,11},{16,20},{28,... | collective-permute-start | bytes 2162696 | tf_op jit(solution)/shard_map/ppermute | solution.py:465
  228.7 12.4 %collective-permute-start.28 = (bf16[4,64,1024]{2,1,0:T(8,128)(2,1)S(1)}, bf16[4,64,1024]{2,1,0:T(8,128)(2,1)S(1)}, u32[]{:S(2)}, u32[]{:S(2)}) collective-permute-start(bf16[4,64,1024]{2,1,0:T(8,128)(2,1)S(1)} %fusion.7), channel_id=1, source_target_pairs={{0,2},{1,3},{2,0},{3,1},{4,6},{5,7},{6,4},{7,5},{8,10},{9,11},{10,... | collective-permute-start | bytes 1572872 | tf_op jit(solution)/shard_map/ppermute | solution.py:330
  231.2 24.3 %collective-permute-start.33 = (bf16[512,768]{1,0:T(8,128)(2,1)}, bf16[512,768]{1,0:T(8,128)(2,1)}, u32[]{:S(2)}, u32[]{:S(2)}) collective-permute-start(bf16[512,768]{1,0:T(8,128)(2,1)} %bitcast_convert_fusion), channel_id=1, source_target_pairs={{0,16},{16,0},{1,17},{17,1},{2,18},{18,2},{3,19},{19,3},{4,20},{20... | collective-permute-start | bytes 2359304 | tf_op jit(solution)/shard_map/ppermute | solution.py:453
  245.2 16.2 %all-to-all-start.3 = ((bf16[4,64,1024]{2,1,0:T(8,128)(2,1)}), bf16[4,64,1024]{2,1,0:T(8,128)(2,1)S(1)}, u32[]{:S(2)}, u32[]{:S(2)}) async-start(bf16[4,64,1024]{2,1,0:T(8,128)(2,1)} %get-tuple-element.196), calls=%async_computation.3 | async-start | bytes 1048576 | tf_op jit(solution)/shard_map/all_to_all | solution.py:579
  248.9 6.6 %collective-permute-start.32 = (bf16[272,512]{1,0:T(8,128)(2,1)S(1)}, bf16[272,512]{1,0:T(8,128)(2,1)S(1)}, u32[]{:S(2)}, u32[]{:S(2)}) collective-permute-start(bf16[272,512]{1,0:T(8,128)(2,1)S(1)} %get-tuple-element.203), channel_id=1, source_target_pairs={{0,16},{16,0},{1,17},{17,1},{2,18},{18,2},{3,19},{19,3},{4,20},{20... | collective-permute-start | bytes 835592 | tf_op jit(solution)/shard_map/ppermute | solution.py:453
  261.4 32.7 %all-to-all-start.4 = ((bf16[4,64,1024]{2,1,0:T(8,128)(2,1)}), bf16[4,64,1024]{2,1,0:T(8,128)(2,1)S(1)}, u32[]{:S(2)}, u32[]{:S(2)}) async-start(bf16[4,64,1024]{2,1,0:T(8,128)(2,1)} %add_convert_fusion.11), calls=%async_computation.4 | async-start | bytes 1048576 | tf_op jit(solution)/shard_map/all_to_all | solution.py:587
  268.4 25.6 %collective-permute-start.38 = (bf16[512,768]{1,0:T(8,128)(2,1)}, bf16[512,768]{1,0:T(8,128)(2,1)}, u32[]{:S(2)}, u32[]{:S(2)}) collective-permute-start(bf16[512,768]{1,0:T(8,128)(2,1)} %fusion), channel_id=1, source_target_pairs={{0,4},{12,8},{1,5},{13,9},{2,6},{14,10},{3,7},{15,11},{16,20},{28,... | collective-permute-start | bytes 2359304 | tf_op jit(solution)/shard_map/ppermute | solution.py:465
  273.2 20.8 %collective-permute-start.35 = (bf16[704,512]{1,0:T(8,128)(2,1)}, bf16[704,512]{1,0:T(8,128)(2,1)}, u32[]{:S(2)}, u32[]{:S(2)}) collective-permute-start(bf16[704,512]{1,0:T(8,128)(2,1)} %get-tuple-element.209), channel_id=1, source_target_pairs={{4,0},{8,12},{5,1},{9,13},{6,2},{10,14},{7,3},{11,15},{20,16},{24,... | collective-permute-start | bytes 2162696 | tf_op jit(solution)/shard_map/ppermute | solution.py:471
  274.5 19.5 %collective-permute-start.36 = (bf16[704,512]{1,0:T(8,128)(2,1)}, bf16[704,512]{1,0:T(8,128)(2,1)S(1)}, u32[]{:S(2)}, u32[]{:S(2)}) collective-permute-start(bf16[704,512]{1,0:T(8,128)(2,1)} %get-tuple-element.210), channel_id=1, source_target_pairs={{4,8},{8,4},{5,9},{9,5},{6,10},{10,6},{7,11},{11,7},{20,24},{24,20... | collective-permute-start | bytes 2162696 | tf_op jit(solution)/shard_map/ppermute | solution.py:468
  275.2 18.8 %collective-permute-start.34 = (bf16[4,64,1024]{2,1,0:T(8,128)(2,1)S(1)}, bf16[4,64,1024]{2,1,0:T(8,128)(2,1)S(1)}, u32[]{:S(2)}, u32[]{:S(2)}) collective-permute-start(bf16[4,64,1024]{2,1,0:T(8,128)(2,1)S(1)} %all-to-all-done.3.refs_0_), channel_id=1, source_target_pairs={{0,2},{1,3},{2,0},{3,1},{4,6},{5,7},{6,4},{7,5},{8,10},{9,11},{10,... | collective-permute-start | bytes 1572872 | tf_op jit(solution)/shard_map/ppermute | solution.py:330
  275.9 18.1 %collective-permute-start.37 = (bf16[272,512]{1,0:T(8,128)(2,1)S(1)}, bf16[272,512]{1,0:T(8,128)(2,1)}, u32[]{:S(2)}, u32[]{:S(2)}) collective-permute-start(bf16[272,512]{1,0:T(8,128)(2,1)S(1)} %add_convert_fusion.18), channel_id=1, source_target_pairs={{0,4},{12,8},{1,5},{13,9},{2,6},{14,10},{3,7},{15,11},{16,20},{28,... | collective-permute-start | bytes 835592 | tf_op jit(solution)/shard_map/ppermute | solution.py:465
  294.0 18.7 %collective-permute-start.45 = (bf16[4,64,1024]{2,1,0:T(8,128)(2,1)S(1)}, bf16[4,64,1024]{2,1,0:T(8,128)(2,1)S(1)}, u32[]{:S(2)}, u32[]{:S(2)}) collective-permute-start(bf16[4,64,1024]{2,1,0:T(8,128)(2,1)S(1)} %all-to-all-done.3.refs_0_), channel_id=1, source_target_pairs={{0,1},{1,0},{2,3},{3,2},{4,5},{5,4},{6,7},{7,6},{8,9},{9,8},{10,11... | collective-permute-start | bytes 1572872 | tf_op jit(solution)/shard_map/ppermute | solution.py:327
  299.7 32.9 %all-to-all-start.5 = ((bf16[4,4,64,256]{3,2,1,0:T(8,128)(2,1)}), bf16[4,4,64,256]{3,2,1,0:T(8,128)(2,1)}, u32[]{:S(2)}, u32[]{:S(2)}) async-start(bf16[4,4,64,256]{3,2,1,0:T(8,128)(2,1)} %get-tuple-element.216), calls=%async_computation.5 | async-start | bytes 1048576 | tf_op jit(solution)/shard_map/all_to_all | solution.py:598
  305.7 27.0 %collective-permute-start.40 = (bf16[704,512]{1,0:T(8,128)(2,1)}, bf16[704,512]{1,0:T(8,128)(2,1)}, u32[]{:S(2)}, u32[]{:S(2)}) collective-permute-start(bf16[704,512]{1,0:T(8,128)(2,1)} %add_convert_fusion.2), channel_id=1, source_target_pairs={{4,0},{8,12},{5,1},{9,13},{6,2},{10,14},{7,3},{11,15},{20,16},{24,... | collective-permute-start | bytes 2162696 | tf_op jit(solution)/shard_map/ppermute | solution.py:471
  307.0 25.7 %collective-permute-start.42 = (bf16[512,768]{1,0:T(8,128)(2,1)}, bf16[512,768]{1,0:T(8,128)(2,1)}, u32[]{:S(2)}, u32[]{:S(2)}) collective-permute-start(bf16[512,768]{1,0:T(8,128)(2,1)} %add_convert_fusion.1), channel_id=1, source_target_pairs={{4,8},{8,4},{5,9},{9,5},{6,10},{10,6},{7,11},{11,7},{20,24},{24,20... | collective-permute-start | bytes 2359304 | tf_op jit(solution)/shard_map/ppermute | solution.py:468
  310.9 4.8 %collective-permute-start.46 = (bf16[4,64,1024]{2,1,0:T(8,128)(2,1)S(1)}, bf16[4,64,1024]{2,1,0:T(8,128)(2,1)S(1)}, u32[]{:S(2)}, u32[]{:S(2)}) collective-permute-start(bf16[4,64,1024]{2,1,0:T(8,128)(2,1)S(1)} %collective-permute-done.34.refs_1_), channel_id=1, source_target_pairs={{0,1},{1,0},{2,3},{3,2},{4,5},{5,4},{6,7},{7,6},{8,9},{9,8},{10,11... | collective-permute-start | bytes 1572872 | tf_op jit(solution)/shard_map/ppermute | solution.py:327
  311.1 14.1 %collective-permute-start.39 = (bf16[4,64,1024]{2,1,0:T(8,128)(2,1)S(1)}, bf16[4,64,1024]{2,1,0:T(8,128)(2,1)S(1)}, u32[]{:S(2)}, u32[]{:S(2)}) collective-permute-start(bf16[4,64,1024]{2,1,0:T(8,128)(2,1)S(1)} %all-to-all-done.4.refs_0_), channel_id=1, source_target_pairs={{0,2},{1,3},{2,0},{3,1},{4,6},{5,7},{6,4},{7,5},{8,10},{9,11},{10,... | collective-permute-start | bytes 1572872 | tf_op jit(solution)/shard_map/ppermute | solution.py:330
  312.7 6.0 %collective-permute-start.41 = (bf16[272,512]{1,0:T(8,128)(2,1)S(1)}, bf16[272,512]{1,0:T(8,128)(2,1)S(1)}, u32[]{:S(2)}, u32[]{:S(2)}) collective-permute-start(bf16[272,512]{1,0:T(8,128)(2,1)S(1)} %add_convert_fusion.17), channel_id=1, source_target_pairs={{4,8},{8,4},{5,9},{9,5},{6,10},{10,6},{7,11},{11,7},{20,24},{24,20... | collective-permute-start | bytes 835592 | tf_op jit(solution)/shard_map/ppermute | solution.py:468
  315.7 46.3 %collective-permute-start.43 = (bf16[4,64,1024]{2,1,0:T(8,128)(2,1)S(1)}, bf16[4,64,1024]{2,1,0:T(8,128)(2,1)S(1)}, u32[]{:S(2)}, u32[]{:S(2)}) collective-permute-start(bf16[4,64,1024]{2,1,0:T(8,128)(2,1)S(1)} %all-to-all-done.4.refs_0_), channel_id=1, source_target_pairs={{0,1},{1,0},{2,3},{3,2},{4,5},{5,4},{6,7},{7,6},{8,9},{9,8},{10,11... | collective-permute-start | bytes 1572872 | tf_op jit(solution)/shard_map/ppermute | solution.py:327
  333.7 21.6 %collective-permute-start.48 = (bf16[272,512]{1,0:T(8,128)(2,1)S(1)}, bf16[272,512]{1,0:T(8,128)(2,1)S(1)}, u32[]{:S(2)}, u32[]{:S(2)}) collective-permute-start(bf16[272,512]{1,0:T(8,128)(2,1)S(1)} %add_convert_fusion.16), channel_id=1, source_target_pairs={{4,0},{8,12},{5,1},{9,13},{6,2},{10,14},{7,3},{11,15},{20,16},{24,... | collective-permute-start | bytes 835592 | tf_op jit(solution)/shard_map/ppermute | solution.py:471
  336.6 18.9 %copy-start.44 = (bf16[704,512]{1,0:T(8,128)(2,1)S(1)}, bf16[704,512]{1,0:T(8,128)(2,1)}, u32[]{:S(2)}) copy-start(bf16[704,512]{1,0:T(8,128)(2,1)} %add_convert_fusion.2) | copy-start | bytes 2162692
  336.6 25.5 %collective-permute-start.44 = (bf16[4,64,1024]{2,1,0:T(8,128)(2,1)S(1)}, bf16[4,64,1024]{2,1,0:T(8,128)(2,1)S(1)}, u32[]{:S(2)}, u32[]{:S(2)}) collective-permute-start(bf16[4,64,1024]{2,1,0:T(8,128)(2,1)S(1)} %collective-permute-done.39.refs_1_), channel_id=1, source_target_pairs={{0,1},{1,0},{2,3},{3,2},{4,5},{5,4},{6,7},{7,6},{8,9},{9,8},{10,11... | collective-permute-start | bytes 1572872 | tf_op jit(solution)/shard_map/ppermute | solution.py:327
  336.7 34.8 %collective-permute-start.47 = (bf16[512,768]{1,0:T(8,128)(2,1)S(1)}, bf16[512,768]{1,0:T(8,128)(2,1)}, u32[]{:S(2)}, u32[]{:S(2)}) collective-permute-start(bf16[512,768]{1,0:T(8,128)(2,1)S(1)} %add_convert_fusion), channel_id=1, source_target_pairs={{4,0},{8,12},{5,1},{9,13},{6,2},{10,14},{7,3},{11,15},{20,16},{24,... | collective-permute-start | bytes 2359304 | tf_op jit(solution)/shard_map/ppermute | solution.py:471
  355.3 2.4 collective-permute-start.49
  357.8 3.7 collective-permute-start.50
  (50 other events, 273.7 us)

commit v3 on v2

v3 whole, which is shorter than its diff:
```python
import functools

import jax
import jax.numpy as jnp
from jax import lax
from jax.experimental import pallas as pl
from jax.experimental.pallas import tpu as pltpu
from jax.sharding import PartitionSpec as P

EPSILON = 1e-06
SCALE = 0.125
BF = jnp.bfloat16
F32 = jnp.float32
NN = (((1,), (0,)), ((), ()))
NT = (((1,), (1,)), ((), ()))
TN = (((0,), (0,)), ((), ()))


def dot(a, b, dims=NN):
    return lax.dot_general(a, b, dims, preferred_element_type=F32)


def away(item):
    return pltpu.HBM(item.shape, item.dtype)


def full(shape):
    return pl.BlockSpec(shape, lambda *_: (0,) * len(shape))


def call(kernel, out_shapes, *args, grid=None, in_specs=None, out_specs=None, scratch=(), us=0, name=None, vmem=16):
    keywords = {}
    if grid is not None:
        keywords = dict(grid=grid, in_specs=in_specs, out_specs=out_specs)
    elif in_specs is not None:
        keywords = dict(in_specs=in_specs)
    return pl.pallas_call(
        kernel,
        out_shape=out_shapes,
        scratch_shapes=list(scratch),
        cost_estimate=pl.CostEstimate(flops=int(us * 1e9), bytes_accessed=int(us * 3.4e6), transcendentals=0),
        compiler_params=pltpu.CompilerParams(vmem_limit_bytes=vmem << 20),
        name=name,
        **keywords,
    )(*args)


def shape_of(dims, dtype):
    return jax.ShapeDtypeStruct(dims, dtype)


def own_kernel(count, place, source, *refs):
    outs, sems = refs[:count], refs[count]
    half = outs[0].shape[2] // 2
    copies = []
    for p, out in enumerate(outs):
        for h in range(2):
            copies.append(
                pltpu.make_async_copy(
                    source.at[:, place[p], :, pl.ds(pl.multiple_of(place[2 + h] * half, half), half)],
                    out.at[:, :, h * half:(h + 1) * half],
                    sems.at[len(copies)],
                )
            )
    for copy in copies:
        copy.start()
    for copy in copies:
        copy.wait()


def half_swap(values, lane):
    width = values.shape[-1]
    ahead = pltpu.roll(values, width - 32, 1)
    behind = pltpu.roll(values, 32, 1)
    return jnp.where(lane % 64 < 32, ahead, behind)


def signed_tables(cos_ref, sin_ref, index, width, lane):
    cosine = jnp.concatenate([cos_ref[index]] * (width // 128), axis=1)
    sine = jnp.concatenate([sin_ref[index]] * (width // 128), axis=1)
    return cosine, jnp.where(lane % 64 < 32, -sine, sine)


def attend_kernel(
    seg, p0, p1, p2, p3, gain, wa, wb, fv, cos, sin, mix, woa, wob,
    na_o, nb_o, q, k, v, diff_o, att_o, lse_o, keep_o, pass_o, send_o,
    v_t, o_t,
):
    blocks, rows, width = q.shape
    heads = width // 64
    half = wa.shape[1]
    lane_full = lax.broadcasted_iota(jnp.int32, (1, width), 1)
    for b in range(blocks):
        x = jnp.concatenate([p0[b], p1[b], p2[b], p3[b]], axis=0).astype(F32)
        inverse = lax.rsqrt(jnp.mean(x * x, axis=-1, keepdims=True) + EPSILON)
        normed = (x * inverse * gain[...]).astype(BF)
        na, nb = normed[:, :half], normed[:, half:]
        na_o[b] = na
        nb_o[b] = nb
        cosine, sine = signed_tables(cos, sin, b, width, lane_full)
        raw = [dot(na, wa[i]) + dot(nb, wb[i]) for i in range(3)]
        q[b] = (raw[0] * cosine + half_swap(raw[0], lane_full) * sine).astype(BF)
        k[b] = (raw[1] * cosine + half_swap(raw[1], lane_full) * sine).astype(BF)
        first = jnp.concatenate([fv[b, seg[r]] for r in range(4)], axis=0).astype(F32)
        value = mix[...] * raw[2] + (1.0 - mix[...]) * first
        v[b] = value.astype(BF)
        v_t[:, b * rows:(b + 1) * rows] = value.T.astype(BF)
        diff_o[b] = raw[2] - first
    lane = lax.broadcasted_iota(jnp.int32, (1, width), 1) // 64

    def head(h, carry):
        own = lane == h
        for qb in range(blocks):
            qm = jnp.where(own, q[qb], jnp.zeros_like(q[qb]))
            scores = [dot(k[kb], qm, NT) * SCALE for kb in range(qb + 1)]
            top = functools.reduce(jnp.maximum, [jnp.max(s, axis=0, keepdims=True) for s in scores])
            total = jnp.zeros((1, rows), F32)
            out = jnp.zeros((64, rows), F32)
            for kb in range(qb + 1):
                e = jnp.exp(scores[kb] - top)
                total = total + jnp.sum(e, axis=0, keepdims=True)
                out = out + dot(v_t[pl.ds(pl.multiple_of(h * 64, 64), 64), kb * rows:(kb + 1) * rows], e.astype(BF))
            o_t[qb, pl.ds(pl.multiple_of(h * 64, 64), 64), :] = out / total
            lse_o[h, qb:qb + 1, :] = top + jnp.log(total)
        return carry

    lax.fori_loop(0, heads, head, 0)
    quarter = rows // 4
    for qb in range(blocks):
        att = o_t[qb].T.astype(BF)
        att_o[qb] = att
        for lo, w in ((0, woa), (half, wob)):
            part = dot(att, w[...])
            for p, out in enumerate((keep_o, pass_o)):
                out[qb, :, lo:lo + half] = part[p * quarter:(p + 1) * quarter]
            for p in range(2):
                send_o[p, qb, :, lo:lo + half] = part[(2 + p) * quarter:(3 + p) * quarter].astype(BF)


def residual_kernel(x, keep, got_core, got_x, gain, residual_o, normed_o):
    residual = (
        x[0].astype(F32) + keep[0] + got_core[0, 0].astype(F32) + got_x[0].astype(F32)
    )
    inverse = lax.rsqrt(jnp.mean(residual * residual, axis=-1, keepdims=True) + EPSILON)
    residual_o[0] = residual
    normed_o[0] = (residual * inverse * gain[...]).astype(BF)


def mlp_kernel(
    n0, n1, n2, n3, g0, g1, g2, g3, ga, gb, ua, ub, da, la, db, lb,
    na_o, nb_o, la_o, lb_o, hidden_o, dgate_o, dup_o, keep_o, pass_o, send_o,
):
    n = jnp.concatenate([n0[0], n1[0], n2[0], n3[0]], axis=0)
    g = jnp.concatenate([g0[0], g1[0], g2[0], g3[0]], axis=0)
    half = ga.shape[1]
    na, nb = n[:, :half], n[:, half:]
    na_o[0] = na
    nb_o[0] = nb
    la_o[0] = g[:, :half]
    lb_o[0] = g[:, half:]
    gate = dot(na, ga[...], NT) + dot(nb, gb[...], NT)
    up = dot(na, ua[...], NT) + dot(nb, ub[...], NT)
    wa = jnp.concatenate([da[...], la[...]], axis=0)
    wb = jnp.concatenate([db[...], lb[...]], axis=0)
    grad_hidden = dot(g[:, :half], wa, NT) + dot(g[:, half:], wb, NT)
    s = jax.nn.sigmoid(gate)
    active = gate * s
    hidden_o[0] = (active * up).astype(BF)
    dgate = (grad_hidden * up * s * (1.0 + gate * (1.0 - s))).astype(BF)
    dup = (grad_hidden * active).astype(BF)
    dgate_o[0] = dgate
    dup_o[0] = dup
    quarter = n.shape[0] // 4
    for lo, wg, wu in ((0, ga, ua), (half, gb, ub)):
        part = dot(dgate, wg[...]) + dot(dup, wu[...])
        for p, out in enumerate((keep_o, pass_o)):
            out[0, :, lo:lo + half] = part[p * quarter:(p + 1) * quarter]
        for p in range(2):
            send_o[p, 0, :, lo:lo + half] = part[(2 + p) * quarter:(3 + p) * quarter].astype(BF)


def down_kernel(hidden, da, la, db, lb, keep_o, pass_o, send_o):
    half = da.shape[1]
    quarter = hidden.shape[1] // 4
    for lo, w, late in ((0, da, la), (half, db, lb)):
        part = dot(hidden[0], jnp.concatenate([w[...], late[...]], axis=0))
        for p, out in enumerate((keep_o, pass_o)):
            out[0, :, lo:lo + half] = part[p * quarter:(p + 1) * quarter]
        for p in range(2):
            send_o[p, 0, :, lo:lo + half] = part[(2 + p) * quarter:(3 + p) * quarter].astype(BF)


def norm_back_kernel(direct, keep, got_core, got_x, values, gain, grad_o, low_o, gain_o):
    @pl.when(pl.program_id(0) == 0)
    def _():
        gain_o[...] = jnp.zeros_like(gain_o)

    grad = keep[0] + got_core[0, 0].astype(F32) + got_x[0].astype(F32)
    x = values[0].astype(F32)
    inverse = lax.rsqrt(jnp.mean(x * x, axis=-1, keepdims=True) + EPSILON)
    weighted = grad * gain[...]
    gain_o[...] += jnp.sum(grad * x * inverse, axis=0, keepdims=True)
    out = direct[0].astype(F32) + (
        inverse * weighted
        - x * (inverse * inverse * inverse) * jnp.mean(weighted * x, axis=-1, keepdims=True)
    )
    grad_o[0] = out
    low_o[0] = out.astype(BF)


def attend_back_kernel(
    seg, b0, b1, b2, b3, woa, wob, q, k, v, att, lse, cos, sin, mix, diff,
    p0, p1, p2, p3, wa, wb, na, nb, gain_in,
    gf_o, keep_o, pass_o, send_o, own_o, other_o, own2_o, other2_o,
    gat, dmat, k_t, dk, dv, dq_t, og, og2,
):
    blocks, rows, width = q.shape
    heads = width // 64
    half = woa.shape[1]
    lane_full = lax.broadcasted_iota(jnp.int32, (1, width), 1)
    lane = lane_full // 64
    pick = (
        lax.broadcasted_iota(jnp.int32, (8, width), 0)
        == lax.broadcasted_iota(jnp.int32, (8, width), 1) // 64
    ).astype(F32)
    og[...] = jnp.zeros_like(og)
    og2[...] = jnp.zeros_like(og2)
    for b in range(blocks):
        g = jnp.concatenate([b0[b], b1[b], b2[b], b3[b]], axis=0)
        og[:width] += dot(att[b], g, TN)
        ga = (dot(g[:, :half], woa[...], NT) + dot(g[:, half:], wob[...], NT)).astype(BF)
        gat[b] = ga
        prod = ga.astype(F32) * att[b].astype(F32)
        dmat[b] = lax.dot_general(pick, prod, NT, precision=lax.Precision.HIGHEST, preferred_element_type=F32)
        k_t[:, b * rows:(b + 1) * rows] = k[b].astype(F32).T.astype(BF)
    dk[...] = jnp.zeros_like(dk)
    dv[...] = jnp.zeros_like(dv)

    def head(h, carry):
        own = lane == h
        for qb in range(blocks):
            qm = jnp.where(own, q[qb], jnp.zeros_like(q[qb]))
            gm = jnp.where(own, gat[qb], jnp.zeros_like(gat[qb]))
            log_total = lse[h, qb:qb + 1, :]
            row_dot = dmat[qb, pl.ds(h, 1), :]
            acc = jnp.zeros((64, rows), F32)
            for kb in range(qb + 1):
                prob = jnp.exp(dot(k[kb], qm, NT) * SCALE - log_total)
                dprob = dot(v[kb], gm, NT)
                ds = (prob * (dprob - row_dot)).astype(BF)
                dv[kb] += dot(prob.astype(BF), gm)
                dk[kb] += dot(ds, qm)
                acc = acc + dot(k_t[pl.ds(pl.multiple_of(h * 64, 64), 64), kb * rows:(kb + 1) * rows], ds)
            dq_t[qb, pl.ds(pl.multiple_of(h * 64, 64), 64), :] = acc
        return carry

    lax.fori_loop(0, heads, head, 0)
    quarter = rows // 4
    total = jnp.zeros((1, width), F32)
    gains = [jnp.zeros((1, half), F32) for _ in range(2)]
    for b in range(blocks):
        cosine, sine = signed_tables(cos, sin, b, width, lane_full)
        gq = dq_t[b].T * SCALE
        gk = dk[b] * SCALE
        gv = dv[b]
        grads = [
            (gq * cosine - half_swap(gq, lane_full) * sine).astype(BF),
            (gk * cosine - half_swap(gk, lane_full) * sine).astype(BF),
            (mix[...] * gv).astype(BF),
        ]
        for i, n in enumerate((na, nb)):
            lanes = slice(i * half, (i + 1) * half)
            og2[:width, lanes] += dot(grads[0], n[b], TN)
            og2[width:, lanes] += dot(grads[1], n[b], TN)
            og[width:, lanes] += dot(grads[2], n[b], TN)
        x = jnp.concatenate([p0[b], p1[b], p2[b], p3[b]], axis=0).astype(F32)
        x = x * lax.rsqrt(jnp.mean(x * x, axis=-1, keepdims=True) + EPSILON)
        for i, w in enumerate((wa, wb)):
            lanes = slice(i * half, (i + 1) * half)
            part = sum(dot(grad, w[j], NT) for j, grad in enumerate(grads))
            gains[i] = gains[i] + jnp.sum(part * x[:, lanes], axis=0, keepdims=True)
            for p, out in enumerate((keep_o, pass_o)):
                out[b, :, lanes] = part[p * quarter:(p + 1) * quarter]
            for p in range(2):
                send_o[p, b, :, lanes] = part[(2 + p) * quarter:(3 + p) * quarter].astype(BF)
        gf = ((1.0 - mix[...]) * gv).astype(BF)
        for r in range(4):
            gf_o[b, seg[r]] = gf[r * quarter:(r + 1) * quarter]
        total = total + jnp.sum(gv * diff[b], axis=0, keepdims=True)
    row = lax.broadcasted_iota(jnp.int32, (16, half), 0)
    mixed = jnp.concatenate([total, jnp.zeros((1, half - width), F32)], axis=1)
    for i, (out, out2) in enumerate(((own_o, own2_o), (other_o, other2_o))):
        lanes = slice(i * half, (i + 1) * half)
        extra = jnp.where(row == 0, gains[i], jnp.where(row == 1, gain_in[:, lanes], jnp.where(row == 2, mixed, 0.0)))
        out[:2 * width] = og[:, lanes].astype(out.dtype)
        out[2 * width:] = extra.astype(out.dtype)
        out2[...] = og2[:, lanes].astype(out.dtype)


def place_kernel(where, roll, *refs):
    pieces, out = refs[:-1], refs[-1]
    width = out.shape[-1]
    half = width // 2
    for r, piece in enumerate(pieces):
        value = piece[0]
        low, high = value[:, :half], value[:, half:]
        swap = roll[0] == 1
        out[0, where[r], :, :half] = jnp.where(swap, high, low).astype(out.dtype)
        out[0, where[r], :, half:] = jnp.where(swap, low, high).astype(out.dtype)


def first_kernel(got, out):
    out[...] = got[...].astype(out.dtype)


def on_device(
    fsdp, ctx, tp,
    tokens, first_values, out_grad, w_qkv, output_weight, w_gate, w_up, w_down, gain_attn, gain_mlp, mix,
):
    seqs, block, width = tokens.shape
    local = w_qkv.shape[2]
    hidden_width = w_gate.shape[1]
    quarter = block // tp
    half = width // 2
    pair = fsdp == 2
    assert seqs == ctx and ctx == 4 and tp == 4 and local <= half
    y = lax.axis_index("fsdp")
    z = lax.axis_index("ctx")
    t = lax.axis_index("tp")
    swap_y = [(0, 1), (1, 0)]
    by_core = [(i, i ^ 1) for i in range(tp)]
    by_x = [(i, i ^ 2) for i in range(tp)]

    def tie(*values):
        return lax.optimization_barrier(values)

    def core(value):
        return lax.ppermute(value, "tp", by_core)

    def across(value):
        return lax.ppermute(value, "tp", by_x)

    def other_half(value, axis):
        if pair:
            return value, lax.ppermute(value, "fsdp", swap_y)
        whole = lax.all_gather(value, "fsdp", axis=axis, tiled=True)
        return tuple(lax.slice_in_dim(whole, i * half, (i + 1) * half, axis=axis) for i in range(2))

    def added(keep, got):
        return keep + got.astype(F32)

    rows = ctx * block
    smem = pl.BlockSpec(memory_space=pltpu.SMEM)
    piece_spec = pl.BlockSpec((1, quarter, width), lambda b: (b, 0, 0))
    block_local = pl.BlockSpec((1, block, local), lambda b: (b, 0, 0))
    block_half = pl.BlockSpec((1, block, half), lambda b: (b, 0, 0))
    block_hidden = pl.BlockSpec((1, block, hidden_width), lambda b: (b, 0, 0))
    block_table = pl.BlockSpec((1, block, 128), lambda b: (b, 0, 0))
    part_specs = [piece_spec] * 2 + [pl.BlockSpec((2, 1, quarter, width), lambda b: (0, b, 0, 0))]
    first_part = pl.BlockSpec((1, 1, quarter, width), lambda b: (0, b, 0, 0))
    gain_spec = full((1, width))
    send_shape = shape_of((2, ctx, quarter, width), BF)
    own_f32 = shape_of((ctx, quarter, width), F32)
    own_low = shape_of((ctx, quarter, width), BF)
    part_shapes = [own_f32, own_f32, send_shape]
    part_away = [away(own_f32), own_f32, send_shape]
    rows_local = shape_of((ctx, block, local), BF)
    rows_half = shape_of((ctx, block, half), BF)
    rows_hidden = shape_of((ctx, block, hidden_width), BF)
    gain_row = shape_of((1, width), F32)

    seg = jnp.stack([t, t ^ 2, t ^ 1, t ^ 3]).astype(jnp.int32)
    turn = y if pair else y * 0
    roll = jnp.reshape(turn, (1,)).astype(jnp.int32)
    where = jnp.stack([t, t ^ 2, turn, 1 - turn]).astype(jnp.int32)

    def own_rows(value, count):
        return call(
            functools.partial(own_kernel, count),
            [own_low] * count,
            where, value.reshape(seqs, tp, quarter, width),
            in_specs=[smem, pl.BlockSpec(memory_space=pltpu.HBM)],
            scratch=[pltpu.SemaphoreType.DMA((2 * count,))],
            name="own", vmem=4,
        )

    (x_part,) = own_rows(tokens, 1)
    place = (seg[:, None] * quarter + jnp.arange(quarter)[None, :]).reshape(block)
    positions = (jnp.arange(ctx)[:, None] * block + place[None, :]).astype(F32)
    lanes = (jnp.arange(128) % 32).astype(F32)
    table = positions[:, :, None] * (10000.0 ** (-lanes / 32.0))[None, None, :]
    cosine, sine = jnp.cos(table), jnp.sin(table)
    mix_row = jnp.repeat(mix, local // mix.shape[0])[None, :]

    qkv_a, qkv_b = other_half(jnp.transpose(w_qkv, (1, 0, 2)), 1)
    out_a, out_b = other_half(
        jnp.concatenate([output_weight, jnp.stack([gain_attn, gain_mlp])], axis=0), 1
    )
    gate_a, gate_b = other_half(w_gate.T, 1)
    up_a, up_b = other_half(w_up.T, 1)
    early = hidden_width // 4 // 64 * 64
    down_a, down_b = other_half(w_down[:early], 1)
    late_a, late_b = other_half(w_down[early:], 1)

    x_own = lax.all_to_all(x_part, "ctx", 0, 0)
    x_own, qkv_b, cosine, sine, mix_row, g_part, g_late = tie(
        x_own, qkv_b, cosine, sine, mix_row, *own_rows(out_grad, 2)
    )
    x_second = across(x_own)
    fv = lax.all_to_all(first_values, "ctx", 0, 0).reshape(ctx, tp, quarter, local)
    gains = jnp.concatenate([out_a[local:], out_b[local:]], axis=1).astype(F32)
    x_core = core(x_own)
    x_second, out_b, gains = tie(x_second, out_b[:local], gains)
    x_both = core(x_second)
    x_core, x_both, fv, g_part = tie(x_core, x_both, fv, g_part)
    x_pieces = (x_own, x_second, x_core, x_both)
    out_a = output_weight if pair else out_a[:local]
    gain_first, gain_second = gains[0:1], gains[1:2]
    g_first = lax.all_to_all(g_part, "ctx", 0, 0)
    norm_a, norm_b, queries, keys, values, diff, attended, log_total, keep, onward, send = call(
        attend_kernel,
        [away(item) for item in [rows_half] * 2 + [rows_local] * 3 + [
            shape_of((ctx, block, local), F32), rows_local,
        ]] + [shape_of((mix.shape[0], ctx, block), F32)] + part_away,
        seg, *x_pieces, gain_first, qkv_a, qkv_b, fv, cosine, sine, mix_row, out_a, out_b,
        in_specs=[smem] + [pl.BlockSpec(memory_space=pltpu.VMEM)] * 13,
        scratch=[pltpu.VMEM((local, rows), BF), pltpu.VMEM((ctx, local, block), F32)],
        name="attend", vmem=20,
    )
    send, gate_b, g_first, g_late = tie(send, gate_b, g_first, g_late)
    got_core = core(send)
    got_x = across(added(onward, got_core[1]).astype(BF))
    g_second = lax.all_to_all(g_late, "ctx", 0, 0)
    got_x, up_b, down_b, g_second = tie(got_x, up_b, down_b, g_second)
    residual, normed_own = call(
        residual_kernel,
        [own_f32, own_low],
        x_own, keep, got_core, got_x, gain_second,
        grid=(ctx,),
        in_specs=[piece_spec, piece_spec, first_part, piece_spec, gain_spec],
        out_specs=[piece_spec, piece_spec],
        name="residual_norm", vmem=6, us=20,
    )
    down_specs = [full((n, half)) for n in (early, hidden_width - early)] * 2
    n_second = across(normed_own)
    mlp_a, mlp_b, last_a, last_b, hidden, grad_gate, grad_up, keep, onward, send = call(
        mlp_kernel,
        [rows_half] * 4 + [rows_hidden] * 3 + part_shapes,
        normed_own, n_second, core(normed_own), core(n_second), g_first, g_second, core(g_first), core(g_second),
        gate_a, gate_b, up_a, up_b, down_a, late_a, down_b, late_b,
        grid=(ctx,),
        in_specs=[piece_spec] * 8 + [full((hidden_width, half))] * 4 + down_specs,
        out_specs=[block_half] * 4 + [block_hidden] * 3 + part_specs,
        name="mlp", vmem=24, us=10,
    )

    def placed(*pieces):
        *pieces, dtype = pieces
        return call(
            place_kernel,
            [shape_of((seqs, tp, quarter, width), dtype)],
            seg, roll, *pieces,
            grid=(seqs,),
            in_specs=[smem, smem] + [piece_spec] * 4,
            out_specs=[pl.BlockSpec((1, tp, quarter, width), lambda b: (b, 0, 0, 0))],
            name="place", vmem=6,
        )[0].reshape(seqs, block, width)

    def weight_grad(left, right):
        return lax.dot_general(
            left.reshape(rows, -1), right.reshape(rows, -1), TN, preferred_element_type=F32
        )

    def exchange(first, second, axis=1):
        if pair:
            return lax.ppermute(second, "fsdp", swap_y)
        return lax.psum_scatter(
            jnp.concatenate([first.astype(BF), second], axis=axis), "fsdp", scatter_dimension=axis, tiled=True
        )

    def joined(first, received):
        return (first + received.astype(F32)).astype(BF) if pair else received

    def plus(shard, received):
        return (shard.astype(F32) + received.astype(F32)).astype(BF)

    def toward(shard):
        return lax.ppermute(shard, "ctx", [(0, 1), (3, 2)])

    def meet(shard):
        return lax.ppermute(shard, "ctx", [(1, 2), (2, 1)])

    def back(shard):
        return lax.ppermute(shard, "ctx", [(1, 0), (2, 3)])

    def settled(shard, received):
        return jnp.where((z == 0) | (z == 3), received, shard).astype(F32)

    got_core = core(send)
    gate_first = weight_grad(grad_gate, mlp_a)
    gate_second = weight_grad(grad_gate, mlp_b).astype(BF)
    onward = added(onward, got_core[1]).astype(BF)

    onward, gate_first, gate_second, grad_up, hidden = tie(onward, gate_first, gate_second, grad_up, hidden)
    got_x = across(onward)
    gate_got = exchange(gate_first, gate_second)
    up_first = weight_grad(grad_up, mlp_a)
    up_second = weight_grad(grad_up, mlp_b).astype(BF)
    down_first = weight_grad(hidden, last_a)
    down_second = weight_grad(hidden, last_b).astype(BF)
    down_keep, down_onward, down_send = call(
        down_kernel,
        part_shapes,
        hidden, down_a, late_a, down_b, late_b,
        grid=(ctx,),
        in_specs=[block_hidden] + down_specs,
        out_specs=part_specs,
        name="down", vmem=12,
    )
    down_core = core(down_send)
    down_onward = added(down_onward, down_core[1]).astype(BF)
    output_own = residual + added(down_keep, down_core[0])
    grad_residual, branch_own, gain_sum_second = call(
        norm_back_kernel,
        [own_f32, own_low, gain_row],
        g_first, keep, got_core, got_x, residual, gain_second,
        grid=(ctx,),
        in_specs=[piece_spec, piece_spec, first_part, piece_spec, piece_spec, gain_spec],
        out_specs=[piece_spec, piece_spec, gain_spec],
        name="norm_back_mlp", vmem=6, us=20,
    )
    (
        branch_own, grad_residual, gate_got, gate_first, up_first, up_second, down_first, down_second,
        down_onward, output_own,
    ) = tie(
        branch_own, grad_residual, gate_got, gate_first, up_first, up_second, down_first, down_second,
        down_onward, output_own,
    )

    b_second = across(branch_own)
    b_core = core(branch_own)
    b_both = core(b_second)
    up_got = exchange(up_first, up_second)
    gate_shard = joined(gate_first, gate_got)
    gate_more = toward(gate_shard)
    (
        b_second, b_core, b_both, up_got, gate_shard, gate_more, down_onward, output_own, down_second,
    ) = tie(b_second, b_core, b_both, up_got, gate_shard, gate_more, down_onward, output_own, down_second)

    down_x = across(down_onward)
    down_got = exchange(down_first, down_second)
    gate_shard = plus(gate_shard, gate_more)
    gate_more = meet(gate_shard)
    up_shard = joined(up_first, up_got)
    up_more = toward(up_shard)
    payload = [shape_of((2 * local + n, half), kind) for n in (16, 0) for kind in (F32, BF)]
    gf, keep, onward, send, out_first, out_second, qk_first, qk_second = call(
        attend_back_kernel,
        [away(shape_of((ctx, tp, quarter, local), BF)), *part_away, *[away(item) for item in payload]],
        seg, branch_own, b_second, b_core, b_both, out_a, out_b,
        queries, keys, values, attended, log_total, cosine, sine, mix_row, diff,
        *x_pieces, qkv_a, qkv_b, norm_a, norm_b, gain_sum_second,
        in_specs=[smem] + [pl.BlockSpec(memory_space=pltpu.VMEM)] * 24,
        scratch=[
            pltpu.VMEM((ctx, block, local), BF),
            pltpu.VMEM((ctx, 8, block), F32),
            pltpu.VMEM((local, rows), BF),
            pltpu.VMEM((ctx, block, local), F32),
            pltpu.VMEM((ctx, block, local), F32),
            pltpu.VMEM((ctx, local, block), F32),
            pltpu.VMEM((2 * local, width), F32),
            pltpu.VMEM((2 * local, width), F32),
        ],
        name="attend_back", vmem=40, us=30,
    )
    send, down_got, gate_more, up_more, down_x = tie(send, down_got, gate_more, up_more, down_x)
    got_core = core(send)
    onward = added(onward, got_core[1]).astype(BF)
    (
        onward, qk_second, out_second, down_got, gate_shard, gate_more, up_shard, up_more, down_x,
    ) = tie(onward, qk_second, out_second, down_got, gate_shard, gate_more, up_shard, up_more, down_x)

    got_x = across(onward)
    gate_shard = plus(gate_shard, gate_more)
    gate_more = back(gate_shard)
    up_shard = plus(up_shard, up_more)
    up_more = meet(up_shard)
    down_shard = joined(down_first, down_got)
    down_more = toward(down_shard)
    qk_got = exchange(qk_first, qk_second)
    output_own = (output_own + down_x.astype(F32)).astype(BF)
    _, tokens_own, _ = call(
        norm_back_kernel,
        [own_f32, own_low, gain_row],
        grad_residual, keep, got_core, got_x, x_own, gain_first,
        grid=(ctx,),
        in_specs=[piece_spec, piece_spec, first_part, piece_spec, piece_spec, gain_spec],
        out_specs=[piece_spec, piece_spec, gain_spec],
        name="norm_back_attn", vmem=6, us=20,
    )
    tokens_own, output_own, gf, out_second, gate_shard, up_shard, down_shard = tie(
        tokens_own, output_own, gf, out_second, gate_shard, up_shard, down_shard
    )

    tokens_home = lax.all_to_all(tokens_own, "ctx", 0, 0)
    out_got = exchange(out_first, out_second)
    grad_w_gate = settled(gate_shard, gate_more).T
    up_shard = plus(up_shard, up_more)
    down_shard = plus(down_shard, down_more)
    qk_shard = joined(qk_first, qk_got)
    tokens_home, output_own, gf, grad_w_gate, up_shard, down_shard, qk_shard = tie(
        tokens_home, output_own, gf, grad_w_gate, up_shard, down_shard, qk_shard
    )
    tokens_second = across(tokens_home)
    tokens_core = core(tokens_home)
    up_more = back(up_shard)
    down_more = meet(down_shard)
    qk_more = toward(qk_shard)
    out_shard = joined(out_first, out_got)
    tokens_second, out_shard, output_own, gf, up_more, down_more, qk_more = tie(
        tokens_second, out_shard, output_own, gf, up_more, down_more, qk_more
    )
    output_home = lax.all_to_all(output_own, "ctx", 0, 0)
    down_shard = plus(down_shard, down_more)
    down_more = back(down_shard)
    qk_shard = plus(qk_shard, qk_more)
    qk_more = meet(qk_shard)
    out_more = toward(out_shard)
    grad_tokens = placed(tokens_home, tokens_second, tokens_core, core(tokens_second), F32)
    grad_w_up = settled(up_shard, up_more).T
    output_home, gf, grad_tokens, grad_w_up, down_more, qk_more, out_more = tie(
        output_home, gf, grad_tokens, grad_w_up, down_more, qk_more, out_more
    )
    output_second = across(output_home)
    output_core = core(output_home)
    first_home = lax.all_to_all(gf, "ctx", 0, 0)
    qk_shard = plus(qk_shard, qk_more)
    qk_more = back(qk_shard)
    out_shard = plus(out_shard, out_more)
    out_more = meet(out_shard)
    grad_w_down = settled(down_shard, down_more)
    output_second, first_home, grad_w_down, qk_more, out_more = tie(
        output_second, first_home, grad_w_down, qk_more, out_more
    )
    out_shard = plus(out_shard, out_more)
    out_more = back(out_shard)
    output = placed(output_home, output_second, output_core, core(output_second), BF)
    grad_first = first_home.reshape(seqs, block, local).astype(F32)
    qk_full = settled(qk_shard, qk_more).T
    output, grad_first, qk_full, out_more = tie(output, grad_first, qk_full, out_more)
    out_full = settled(out_shard, out_more)
    v_full = out_full[local:2 * local].T
    grad_w_qkv = jnp.stack([qk_full[:, :local], qk_full[:, local:], v_full], axis=1)
    grad_w_out = out_full[:local]

    share = gain_attn.shape[0]
    gain_grads = out_full[2 * local:2 * local + 2]
    for move in (core, across):
        gain_grads = gain_grads + move(gain_grads)
    mixed = out_full[2 * local + 2:2 * local + 3]
    if not pair:
        mixed = lax.all_gather(mixed, "fsdp", axis=1, tiled=True)
    mixed = mixed[:, :local]
    grad_mix = jnp.sum(mixed.reshape(mix.shape[0], -1), axis=1)
    return (
        output, grad_tokens, grad_first, grad_w_qkv, grad_w_out, grad_w_gate, grad_w_up, grad_w_down,
        gain_grads[0, :share], gain_grads[1, :share], grad_mix,
    )


def solution(mesh):
    rows = P("fsdp", "ctx", None)
    in_specs = (
        rows, P("fsdp", "ctx", "tp"), rows, P("fsdp", None, "tp"), P("tp", "fsdp"), P("fsdp", "tp"),
        P("fsdp", "tp"), P("tp", "fsdp"), P("fsdp"), P("fsdp"), P("tp"),
    )
    out_specs = (
        rows, rows, P("fsdp", "ctx", "tp"), P("fsdp", None, "tp"), P("tp", "fsdp"), P("fsdp", "tp"),
        P("fsdp", "tp"), P("tp", "fsdp"), P("fsdp"), P("fsdp"), P("tp"),
    )
    sizes = [mesh.shape[name] for name in ("fsdp", "ctx", "tp")]
    return jax.shard_map(
        functools.partial(on_device, *sizes), mesh=mesh, in_specs=in_specs, out_specs=out_specs,
        check_vma=False,
    )
```

time: 379 us -> 352 us (0.929)
  waiting for transfers between devices: 160 us -> 131 us
  local copies, waits for them, and re-layouts: 31 us -> 20.4 us
  starting transfers between devices: 86 us -> 94.3 us
  Pallas kernels: 56.2 us -> 63.6 us
  matrix products: 11.1 us -> 6.74 us
    ppermute x10, waiting for transfers between devices: 51.2 us -> 29.2 us  [across(): return lax.ppermute(value, 'tp', by_x)]
    ppermute x5 -> x6, waiting for transfers between devices: 34.8 us -> 18.4 us  [other_half(): return (value, lax.ppermute(value, 'fsdp', swap_y))]
    unnamed x115 -> x119, local copies, waits for them, and re-layouts: 26.6 us -> 15.9 us
    ppermute x5, waiting for transfers between devices: 29.6 us -> 39.2 us  [back(): return lax.ppermute(shard, 'ctx', [(1, 0), (2, 3)])]
    all_to_all x1, waiting for transfers between devices: 0.01 us -> 8.46 us  [on_device(): lax.all_to_all(first_values, 'ctx', 0, 0).reshape(ctx, tp, quarter, local)]
    pallas_call x11, Pallas kernels: 56.2 us -> 63.6 us  [call(): pl.pallas_call(kernel, out_shape=out_shapes, scratch_shapes=list(scratch)...]
    all_to_all x1, waiting for transfers between devices: 6.78 us -> 0.01 us  [on_device(): g_first = lax.all_to_all(g_part, 'ctx', 0, 0)]
    all_to_all x0 -> x1, starting transfers between devices: none -> 4.99 us  [on_device(): g_second = lax.all_to_all(g_late, 'ctx', 0, 0)]
  transfers between devices with their start and end apart: 57 -> 60, of which waited for: 27 -> 27; matrix products, arithmetic and copies ran while one was open for 11% -> 11% of each run, Pallas kernels for 7% -> 14%
where the time goes in v3:
time: 352 us; the launch traced here: 350 us
  waiting for transfers between devices  131 us (37%)
  starting transfers between devices  94.3 us (27%)
  Pallas kernels  63.6 us (18%)
  other arithmetic  33.4 us (9%)
  local copies, waits for them, and re-layouts  20.4 us (6%)
  matrix products  6.74 us (2%)
    pallas_call x11, Pallas kernels, call(): pl.pallas_call(kernel, out_shape=out_shapes, scratch_shapes=list(scratch)...  63.6 us
    ppermute x5, waiting for transfers between devices, back(): return lax.ppermute(shard, 'ctx', [(1, 0), (2, 3)])  39.2 us
    ppermute x10, waiting for transfers between devices, across(): return lax.ppermute(value, 'tp', by_x)  29.2 us
    ppermute x5, starting transfers between devices, toward(): return lax.ppermute(shard, 'ctx', [(0, 1), (3, 2)])  27 us
    ppermute x6, waiting for transfers between devices, other_half(): return (value, lax.ppermute(value, 'fsdp', swap_y))  18.4 us
    ppermute x5, waiting for transfers between devices, toward(): return lax.ppermute(shard, 'ctx', [(0, 1), (3, 2)])  16.8 us
    unnamed x119, local copies, waits for them, and re-layouts  15.9 us
    convert_element_type x10, other arithmetic, plus(): return (shard.astype(F32) + received.astype(F32)).astype(BF)  11.4 us
  transfers between devices with their start and end apart: 60, of which 27 were waited for; matrix products, arithmetic and copies ran while one was open for 11% of the time, Pallas kernels for 14%

profile of v3, /device:TPU:0, one launch (start us, length us, event | category | flops | bytes accessed | tf_op | source)
XLA Modules:
  0.0 350.4 jit_solution(18351614221654453782)
XLA Ops:
  0.7 1.6 copy-done.1
  3.7 6.4 %all-to-all-start = ((bf16[4,64,1024]{2,1,0:T(8,128)(2,1)}), bf16[4,64,1024]{2,1,0:T(8,128)(2,1)S(1)}, u32[]{:S(2)}, u32[]{:S(2)}) async-start(bf16[4,64,1024]{2,1,0:T(8,128)(2,1)} %own.2), calls=%async_computation | async-start | bytes 1048576 | tf_op jit(solution)/shard_map/all_to_all | solution.py:405
  10.1 1.5 collective-permute-start
  14.4 1.9 multiply_sine_fusion
  16.3 8.3 %all-to-all-done.p0.x.values = bf16[4,64,1024]{2,1,0:T(8,128)(2,1)S(1)} async-done(((bf16[4,64,1024]{2,1,0:T(8,128)(2,1)}), bf16[4,64,1024]{2,1,0:T(8,128)(2,1)S(1)}, u32[]{:S(2)}, u32[]{:S(2)}) %all-to-all-start) | async-done | bytes 524320 | tf_op jit(solution)/shard_map/all_to_all | solution.py:405
  24.6 4.8 %collective-permute-done.wb = bf16[3,512,256]{2,1,0:T(8,128)(2,1)} collective-permute-done((bf16[3,512,256]{2,1,0:T(8,128)(2,1)}, bf16[3,512,256]{2,1,0:T(8,128)(2,1)}, u32[]{:S(2)}, u32[]{:S(2)}) %collective-permute-start) | collective-permute-done | bytes 786464 | tf_op jit(solution)/shard_map/ppermute | solution.py:345
  29.4 1.5 collective-permute-start.1
  31.7 1.5 collective-permute-start.2
  33.2 4.8 %all-to-all-start.1 = ((bf16[4,256,256]{2,1,0:T(8,128)(2,1)}), bf16[4,256,256]{2,1,0:T(8,128)(2,1)S(1)}, u32[]{:S(2)}, u32[]{:S(2)}) async-start(bf16[4,256,256]{2,1,0:T(8,128)(2,1)} %param.12), calls=%async_computation.1 | async-start | bytes 1048576 | tf_op jit(solution)/shard_map/all_to_all | solution.py:410
  40.6 1.5 collective-permute-done.1.p1
  42.0 8.5 %all-to-all-done.1 = bf16[4,256,256]{2,1,0:T(8,128)(2,1)S(1)} async-done(((bf16[4,256,256]{2,1,0:T(8,128)(2,1)}), bf16[4,256,256]{2,1,0:T(8,128)(2,1)S(1)}, u32[]{:S(2)}, u32[]{:S(2)}) %all-to-all-start.1) | async-done | bytes 524320 | tf_op jit(solution)/shard_map/all_to_all | solution.py:410
  50.5 4.1 %all-to-all-start.2 = ((bf16[4,64,1024]{2,1,0:T(8,128)(2,1)}), bf16[4,64,1024]{2,1,0:T(8,128)(2,1)}, u32[]{:S(2)}, u32[]{:S(2)}) async-start(bf16[4,64,1024]{2,1,0:T(8,128)(2,1)} %copy-done.9), calls=%async_computation.2 | async-start | bytes 1048576 | tf_op jit(solution)/shard_map/all_to_all | solution.py:419
  55.4 14.6 %attend.1 = (bf16[4,256,512]{2,1,0:T(8,128)(2,1)}, bf16[4,256,512]{2,1,0:T(8,128)(2,1)}, bf16[4,256,256]{2,1,0:T(8,128)(2,1)}, bf16[4,256,256]{2,1,0:T(8,128)(2,...) custom-call(s32[4]{0:T(128)S(1)} %get-tuple-element.297.seg.where, ...), custom_call_target="tpu_custom_call" | custom-call | tf_op jit(solution)/shard_map/attend/pallas_call | solution.py:37
  72.8 1.5 collective-permute-start.8
  74.2 5.0 %all-to-all-start.3 = ((bf16[4,64,1024]{2,1,0:T(8,128)(2,1)}), bf16[4,64,1024]{2,1,0:T(8,128)(2,1)}, u32[]{:S(2)}, u32[]{:S(2)}) async-start(bf16[4,64,1024]{2,1,0:T(8,128)(2,1)} %copy-done.8), calls=%async_computation.3 | async-start | bytes 1048576 | tf_op jit(solution)/shard_map/all_to_all | solution.py:433
  79.2 2.0 fusion.7
  83.4 11.0 %collective-permute-done.9.db = bf16[128,512]{1,0:T(8,128)(2,1)S(1)} collective-permute-done((bf16[128,512]{1,0:T(8,128)(2,1)S(1)}, bf16[128,512]{1,0:T(8,128)(2,1)S(1)}, u32[]{:S(2)}, u32[]{:S(2)}) %collective-permute-start.9) | collective-permute-done | bytes 131104 | tf_op jit(solution)/shard_map/ppermute | solution.py:345
  96.4 2.5 residual_norm.1
  100.7 11.2 %collective-permute-done.10.n1 = bf16[4,64,1024]{2,1,0:T(8,128)(2,1)S(1)} collective-permute-done((bf16[4,64,1024]{2,1,0:T(8,128)(2,1)S(1)}, bf16[4,64,1024]{2,1,0:T(8,128)(2,1)S(1)}, u32[]{:S(2)}, u32[]{:S(2)}) %collective-permute-start.10) | collective-permute-done | bytes 524320 | tf_op jit(solution)/shard_map/ppermute | solution.py:341
  111.9 1.8 collective-permute-done.15.lb
  113.8 10.7 %mlp.1 = (bf16[4,256,512]{2,1,0:T(8,128)(2,1)S(1)}, bf16[4,256,512]{2,1,0:T(8,128)(2,1)S(1)}, bf16[4,256,512]{2,1,0:T(8,128)(2,1)S(1)}, bf16[4,256,512]{2,1,0:T(...) custom-call(bf16[4,64,1024]{2,1,0:T(8,128)(2,1)S(1)} %get-tuple-elem, ...), custom_call_target="tpu_custom_call" | custom-call | flops 10000000000 | bytes 34000000 | tf_op jit(solution)/shard_map/mlp/pallas_call | solution.py:37
  129.3 1.5 collective-permute-start.17
  131.9 2.3 down.1
  134.3 2.0 convolution_bitcast_fusion.1
  137.3 6.1 %collective-permute-done.17.got_x = bf16[4,64,1024]{2,1,0:T(8,128)(2,1)S(1)} collective-permute-done((bf16[4,64,1024]{2,1,0:T(8,128)(2,1)S(1)}, bf16[4,64,1024]{2,1,0:T(8,128)(2,1)S(1)}, u32[]{:S(2)}, u32[]{:S(2)}) %collective-permute-start.17) | collective-permute-done | bytes 524320 | tf_op jit(solution)/shard_map/ppermute | solution.py:341
  143.4 2.4 norm_back_mlp.1
  146.8 1.4 fusion.4
  149.9 3.5 %collective-permute-start.24 = (bf16[704,512]{1,0:T(8,128)(2,1)S(1)}, bf16[704,512]{1,0:T(8,128)(2,1)S(1)}, u32[]{:S(2)}, u32[]{:S(2)}) collective-permute-start(bf16[704,512]{1,0:T(8,128)(2,1)S(1)} %add_convert_fusion.8), channel_id=1, source_target_pairs={{0,4},{12,8},{1,5},{13,9},{2,6},{14,10},{3,7},{15,11},{16,20},{28,... | collective-permute-start | bytes 2162696 | tf_op jit(solution)/shard_map/ppermute | solution.py:488
  153.4 1.4 collective-permute-start.23
  154.9 6.7 %collective-permute-done.20.b1 = bf16[4,64,1024]{2,1,0:T(8,128)(2,1)S(1)} collective-permute-done((bf16[4,64,1024]{2,1,0:T(8,128)(2,1)S(1)}, bf16[4,64,1024]{2,1,0:T(8,128)(2,1)S(1)}, u32[]{:S(2)}, u32[]{:S(2)}) %collective-permute-start.20) | collective-permute-done | bytes 524320 | tf_op jit(solution)/shard_map/ppermute | solution.py:341
  161.5 6.4 %collective-permute-done.24 = bf16[704,512]{1,0:T(8,128)(2,1)S(1)} collective-permute-done((bf16[704,512]{1,0:T(8,128)(2,1)S(1)}, bf16[704,512]{1,0:T(8,128)(2,1)S(1)}, u32[]{:S(2)}, u32[]{:S(2)}) %collective-permute-start.24) | collective-permute-done | bytes 720928 | tf_op jit(solution)/shard_map/ppermute | solution.py:488
  167.9 2.3 collective-permute-done.23
  172.2 1.4 collective-permute-start.25
  173.9 5.1 %collective-permute-start.27 = (bf16[704,512]{1,0:T(8,128)(2,1)S(1)}, bf16[704,512]{1,0:T(8,128)(2,1)S(1)}, u32[]{:S(2)}, u32[]{:S(2)}) collective-permute-start(bf16[704,512]{1,0:T(8,128)(2,1)S(1)} %add_convert_fusion.6), channel_id=1, source_target_pairs={{0,4},{12,8},{1,5},{13,9},{2,6},{14,10},{3,7},{15,11},{16,20},{28,... | collective-permute-start | bytes 2162696 | tf_op jit(solution)/shard_map/ppermute | solution.py:488
  179.1 21.4 %attend_back.1 = (bf16[4,4,64,256]{3,2,1,0:T(8,128)(2,1)}, f32[4,64,1024]{2,1,0:T(8,128)}, f32[4,64,1024]{2,1,0:T(8,128)S(1)}, bf16[2,4,64,1024]{3,2,1,0:T(8,128...) custom-call(s32[4]{0:T(128)S(1)} %get-tuple-element.297.seg.where, ...), custom_call_target="tpu_custom_call" | custom-call | flops 30000001024 | bytes 102000000 | tf_op jit(solution)/shard_map/attend_back/pallas_call | solution.py:37
  203.3 2.7 collective-permute-done.29.got_core
  210.3 1.7 collective-permute-start.32
  213.0 1.4 collective-permute-start.31
  215.6 6.4 %collective-permute-start.33 = (bf16[704,512]{1,0:T(8,128)(2,1)}, bf16[704,512]{1,0:T(8,128)(2,1)}, u32[]{:S(2)}, u32[]{:S(2)}) collective-permute-start(bf16[704,512]{1,0:T(8,128)(2,1)} %add_convert_fusion.3), channel_id=1, source_target_pairs={{0,4},{12,8},{1,5},{13,9},{2,6},{14,10},{3,7},{15,11},{16,20},{28,... | collective-permute-start | bytes 2162696 | tf_op jit(solution)/shard_map/ppermute | solution.py:488
  222.9 2.1 norm_back_attn.1
  225.1 3.6 %all-to-all-start.4 = ((bf16[4,64,1024]{2,1,0:T(8,128)(2,1)}), bf16[4,64,1024]{2,1,0:T(8,128)(2,1)S(1)}, u32[]{:S(2)}, u32[]{:S(2)}) async-start(bf16[4,64,1024]{2,1,0:T(8,128)(2,1)} %get-tuple-element.245), calls=%async_computation.4 | async-start | bytes 1048576 | tf_op jit(solution)/shard_map/all_to_all | solution.py:605
  228.7 1.5 collective-permute-start.36
  231.4 2.6 add_convert_fusion.2
  233.9 3.9 %collective-permute-done.31 = bf16[704,512]{1,0:T(8,128)(2,1)} collective-permute-done((bf16[704,512]{1,0:T(8,128)(2,1)}, bf16[704,512]{1,0:T(8,128)(2,1)}, u32[]{:S(2)}, u32[]{:S(2)}) %collective-permute-start.31) | collective-permute-done | bytes 720928 | tf_op jit(solution)/shard_map/ppermute | solution.py:494
  237.9 2.3 convert_bitcast_fusion.1
  240.2 1.5 add_convert_fusion.1
  241.7 3.0 all-to-all-done.4.refs_0_
  246.7 8.0 %collective-permute-start.39 = (bf16[512,512]{1,0:T(8,128)(2,1)S(1)}, bf16[512,512]{1,0:T(8,128)(2,1)S(1)}, u32[]{:S(2)}, u32[]{:S(2)}) collective-permute-start(bf16[512,512]{1,0:T(8,128)(2,1)S(1)} %add_convert_fusion.14), channel_id=1, source_target_pairs={{0,4},{12,8},{1,5},{13,9},{2,6},{14,10},{3,7},{15,11},{16,20},{28,... | collective-permute-start | bytes 1572872 | tf_op jit(solution)/shard_map/ppermute | solution.py:488
  256.3 1.5 add_convert_fusion.11
  258.0 4.9 %collective-permute-done.39 = bf16[512,512]{1,0:T(8,128)(2,1)S(1)} collective-permute-done((bf16[512,512]{1,0:T(8,128)(2,1)S(1)}, bf16[512,512]{1,0:T(8,128)(2,1)S(1)}, u32[]{:S(2)}, u32[]{:S(2)}) %collective-permute-start.39) | collective-permute-done | bytes 524320 | tf_op jit(solution)/shard_map/ppermute | solution.py:488
  262.9 2.6 collective-permute-done.35.refs_1_
  267.4 3.5 all-to-all-start.5
  270.9 4.0 %collective-permute-start.44 = (bf16[528,512]{1,0:T(8,128)(2,1)S(1)}, bf16[528,512]{1,0:T(8,128)(2,1)S(1)}, u32[]{:S(2)}, u32[]{:S(2)}) collective-permute-start(bf16[528,512]{1,0:T(8,128)(2,1)S(1)} %add_convert_fusion.11), channel_id=1, source_target_pairs={{0,4},{12,8},{1,5},{13,9},{2,6},{14,10},{3,7},{15,11},{16,20},{28,... | collective-permute-start | bytes 1622024 | tf_op jit(solution)/shard_map/ppermute | solution.py:488
  279.5 3.0 place.2
  282.5 5.5 %collective-permute-done.44 = bf16[528,512]{1,0:T(8,128)(2,1)S(1)} collective-permute-done((bf16[528,512]{1,0:T(8,128)(2,1)S(1)}, bf16[528,512]{1,0:T(8,128)(2,1)S(1)}, u32[]{:S(2)}, u32[]{:S(2)}) %collective-permute-start.44) | collective-permute-done | bytes 540704 | tf_op jit(solution)/shard_map/ppermute | solution.py:488
  288.8 7.2 %collective-permute-done.42 = bf16[704,512]{1,0:T(8,128)(2,1)} collective-permute-done((bf16[704,512]{1,0:T(8,128)(2,1)}, bf16[704,512]{1,0:T(8,128)(2,1)}, u32[]{:S(2)}, u32[]{:S(2)}) %collective-permute-start.42) | collective-permute-done | bytes 720928 | tf_op jit(solution)/shard_map/ppermute | solution.py:494
  297.2 4.6 %all-to-all-start.6 = ((bf16[4,4,64,256]{3,2,1,0:T(8,128)(2,1)}), bf16[4,4,64,256]{3,2,1,0:T(8,128)(2,1)}, u32[]{:S(2)}, u32[]{:S(2)}) async-start(bf16[4,4,64,256]{3,2,1,0:T(8,128)(2,1)} %get-tuple-element.269), calls=%async_computation.6 | async-start | bytes 1048576 | tf_op jit(solution)/shard_map/all_to_all | solution.py:636
  301.8 1.5 collective-permute-start.47
  305.6 2.3 select_convert_fusion
  307.9 15.9 %collective-permute-done.46 = bf16[512,512]{1,0:T(8,128)(2,1)S(1)} collective-permute-done((bf16[512,512]{1,0:T(8,128)(2,1)S(1)}, bf16[512,512]{1,0:T(8,128)(2,1)S(1)}, u32[]{:S(2)}, u32[]{:S(2)}) %collective-permute-start.46) | collective-permute-done | bytes 524320 | tf_op jit(solution)/shard_map/ppermute | solution.py:494
  327.3 2.1 bitcast_convert_fusion
  329.5 2.4 place.3
  331.9 12.2 %collective-permute-done.50 = bf16[528,512]{1,0:T(8,128)(2,1)S(1)} collective-permute-done((bf16[528,512]{1,0:T(8,128)(2,1)S(1)}, bf16[528,512]{1,0:T(8,128)(2,1)S(1)}, u32[]{:S(2)}, u32[]{:S(2)}) %collective-permute-start.50) | collective-permute-done | bytes 540704 | tf_op jit(solution)/shard_map/ppermute | solution.py:494
  347.2 1.6 copy.28
  (247 shorter events, 63.0 us)
Async XLA Ops:
  3.7 20.8 %all-to-all-start = ((bf16[4,64,1024]{2,1,0:T(8,128)(2,1)}), bf16[4,64,1024]{2,1,0:T(8,128)(2,1)S(1)}, u32[]{:S(2)}, u32[]{:S(2)}) async-start(bf16[4,64,1024]{2,1,0:T(8,128)(2,1)} %own.2), calls=%async_computation | async-start | bytes 1048576 | tf_op jit(solution)/shard_map/all_to_all | solution.py:405
  10.1 19.3 %collective-permute-start = (bf16[3,512,256]{2,1,0:T(8,128)(2,1)}, bf16[3,512,256]{2,1,0:T(8,128)(2,1)}, u32[]{:S(2)}, u32[]{:S(2)}) collective-permute-start(bf16[3,512,256]{2,1,0:T(8,128)(2,1)} %bitcast.91), channel_id=1, source_target_pairs={{0,16},{16,0},{1,17},{17,1},{2,18},{18,2},{3,19},{19,3},{4,20},{20... | collective-permute-start | bytes 2359304 | tf_op jit(solution)/shard_map/ppermute | solution.py:345
  12.0 18.9 %copy-start.2 = (bf16[256,512]{1,0:T(8,128)(2,1)S(1)}, bf16[256,512]{1,0:T(8,128)(2,1)}, u32[]{:S(2)}) copy-start(bf16[256,512]{1,0:T(8,128)(2,1)} %woa.3) | copy-start | bytes 786436
  29.4 12.6 %collective-permute-start.1 = (bf16[4,64,1024]{2,1,0:T(8,128)(2,1)S(1)}, bf16[4,64,1024]{2,1,0:T(8,128)(2,1)}, u32[]{:S(2)}, u32[]{:S(2)}) collective-permute-start(bf16[4,64,1024]{2,1,0:T(8,128)(2,1)S(1)} %all-to-all-done.p0.x.values), channel_id=1, source_target_pairs={{0,2},{1,3},{2,0},{3,1},{4,6},{5,7},{6,4},{7,5},{8,10},{9,11},{10,... | collective-permute-start | bytes 1572872 | tf_op jit(solution)/shard_map/ppermute | solution.py:341
  31.7 23.7 %copy-start.6 = (bf16[512,3,256]{2,0,1:T(8,128)(2,1)S(1)}, bf16[512,3,256]{2,0,1:T(8,128)(2,1)}, u32[]{:S(2)}) copy-start(bf16[512,3,256]{2,0,1:T(8,128)(2,1)} %param.14) | copy-start | bytes 2359300
  31.7 7.1 %collective-permute-start.2 = (bf16[258,512]{1,0:T(8,128)(2,1)}, bf16[258,512]{1,0:T(8,128)(2,1)}, u32[]{:S(2)}, u32[]{:S(2)}) collective-permute-start(bf16[258,512]{1,0:T(8,128)(2,1)} %pad_maximum_fusion.1), channel_id=1, source_target_pairs={{0,16},{16,0},{1,17},{17,1},{2,18},{18,2},{3,19},{19,3},{4,20},{20... | collective-permute-start | bytes 792584 | tf_op jit(solution)/shard_map/ppermute | solution.py:345
  33.2 17.3 %all-to-all-start.1 = ((bf16[4,256,256]{2,1,0:T(8,128)(2,1)}), bf16[4,256,256]{2,1,0:T(8,128)(2,1)S(1)}, u32[]{:S(2)}, u32[]{:S(2)}) async-start(bf16[4,256,256]{2,1,0:T(8,128)(2,1)} %param.12), calls=%async_computation.1 | async-start | bytes 1048576 | tf_op jit(solution)/shard_map/all_to_all | solution.py:410
  40.5 10.0 %collective-permute-start.3 = (bf16[4,64,1024]{2,1,0:T(8,128)(2,1)S(1)}, bf16[4,64,1024]{2,1,0:T(8,128)(2,1)}, u32[]{:S(2)}, u32[]{:S(2)}) collective-permute-start(bf16[4,64,1024]{2,1,0:T(8,128)(2,1)S(1)} %all-to-all-done.p0.x.values), channel_id=1, source_target_pairs={{0,1},{1,0},{2,3},{3,2},{4,5},{5,4},{6,7},{7,6},{8,9},{9,8},{10,11... | collective-permute-start | bytes 1572872 | tf_op jit(solution)/shard_map/ppermute | solution.py:338
  42.0 8.5 %collective-permute-start.4 = (bf16[4,64,1024]{2,1,0:T(8,128)(2,1)}, bf16[4,64,1024]{2,1,0:T(8,128)(2,1)}, u32[]{:S(2)}, u32[]{:S(2)}) collective-permute-start(bf16[4,64,1024]{2,1,0:T(8,128)(2,1)} %collective-permute-done.1.p1), channel_id=1, source_target_pairs={{0,1},{1,0},{2,3},{3,2},{4,5},{5,4},{6,7},{7,6},{8,9},{9,8},{10,11... | collective-permute-start | bytes 1572872 | tf_op jit(solution)/shard_map/ppermute | solution.py:338
  50.5 22.3 %all-to-all-start.2 = ((bf16[4,64,1024]{2,1,0:T(8,128)(2,1)}), bf16[4,64,1024]{2,1,0:T(8,128)(2,1)}, u32[]{:S(2)}, u32[]{:S(2)}) async-start(bf16[4,64,1024]{2,1,0:T(8,128)(2,1)} %copy-done.9), calls=%async_computation.2 | async-start | bytes 1048576 | tf_op jit(solution)/shard_map/all_to_all | solution.py:419
  54.7 17.3 %collective-permute-start.5 = (bf16[704,512]{1,0:T(8,128)(2,1)}, bf16[704,512]{1,0:T(8,128)(2,1)S(1)}, u32[]{:S(2)}, u32[]{:S(2)}) collective-permute-start(bf16[704,512]{1,0:T(8,128)(2,1)} %bitcast.94), channel_id=1, source_target_pairs={{0,16},{16,0},{1,17},{17,1},{2,18},{18,2},{3,19},{19,3},{4,20},{20... | collective-permute-start | bytes 2162696 | tf_op jit(solution)/shard_map/ppermute | solution.py:345
  72.8 6.5 %collective-permute-start.6 = (bf16[2,4,64,1024]{3,2,1,0:T(8,128)(2,1)}, bf16[2,4,64,1024]{3,2,1,0:T(8,128)(2,1)}, u32[]{:S(2)}, u32[]{:S(2)}) collective-permute-start(bf16[2,4,64,1024]{3,2,1,0:T(8,128)(2,1)} %copy-done.13), channel_id=1, source_target_pairs={{0,1},{1,0},{2,3},{3,2},{4,5},{5,4},{6,7},{7,6},{8,9},{9,8},{10,11... | collective-permute-start | bytes 3145736 | tf_op jit(solution)/shard_map/ppermute | solution.py:338
  72.8 21.6 %collective-permute-start.8 = (bf16[704,512]{1,0:T(8,128)(2,1)}, bf16[704,512]{1,0:T(8,128)(2,1)}, u32[]{:S(2)}, u32[]{:S(2)}) collective-permute-start(bf16[704,512]{1,0:T(8,128)(2,1)} %bitcast.96), channel_id=1, source_target_pairs={{0,16},{16,0},{1,17},{17,1},{2,18},{18,2},{3,19},{19,3},{4,20},{20... | collective-permute-start | bytes 2162696 | tf_op jit(solution)/shard_map/ppermute | solution.py:345
  74.2 20.1 %all-to-all-start.3 = ((bf16[4,64,1024]{2,1,0:T(8,128)(2,1)}), bf16[4,64,1024]{2,1,0:T(8,128)(2,1)}, u32[]{:S(2)}, u32[]{:S(2)}) async-start(bf16[4,64,1024]{2,1,0:T(8,128)(2,1)} %copy-done.8), calls=%async_computation.3 | async-start | bytes 1048576 | tf_op jit(solution)/shard_map/all_to_all | solution.py:433
  81.2 13.9 %collective-permute-start.7 = (bf16[4,64,1024]{2,1,0:T(8,128)(2,1)}, bf16[4,64,1024]{2,1,0:T(8,128)(2,1)S(1)}, u32[]{:S(2)}, u32[]{:S(2)}) collective-permute-start(bf16[4,64,1024]{2,1,0:T(8,128)(2,1)} %fusion.7), channel_id=1, source_target_pairs={{0,2},{1,3},{2,0},{3,1},{4,6},{5,7},{6,4},{7,5},{8,10},{9,11},{10,... | collective-permute-start | bytes 1572872 | tf_op jit(solution)/shard_map/ppermute | solution.py:341
  82.7 11.7 %collective-permute-start.9 = (bf16[128,512]{1,0:T(8,128)(2,1)S(1)}, bf16[128,512]{1,0:T(8,128)(2,1)S(1)}, u32[]{:S(2)}, u32[]{:S(2)}) collective-permute-start(bf16[128,512]{1,0:T(8,128)(2,1)S(1)} %slice.63.da), channel_id=1, source_target_pairs={{0,16},{16,0},{1,17},{17,1},{2,18},{18,2},{3,19},{19,3},{4,20},{20... | collective-permute-start | bytes 393224 | tf_op jit(solution)/shard_map/ppermute | solution.py:345
  98.9 13.0 %collective-permute-start.10 = (bf16[4,64,1024]{2,1,0:T(8,128)(2,1)S(1)}, bf16[4,64,1024]{2,1,0:T(8,128)(2,1)S(1)}, u32[]{:S(2)}, u32[]{:S(2)}) collective-permute-start(bf16[4,64,1024]{2,1,0:T(8,128)(2,1)S(1)} %get-tuple-element.171.n0), channel_id=1, source_target_pairs={{0,2},{1,3},{2,0},{3,1},{4,6},{5,7},{6,4},{7,5},{8,10},{9,11},{10,... | collective-permute-start | bytes 1572872 | tf_op jit(solution)/shard_map/ppermute | solution.py:341
  99.5 14.1 %collective-permute-start.15 = (bf16[576,512]{1,0:T(8,128)(2,1)S(1)}, bf16[576,512]{1,0:T(8,128)(2,1)S(1)}, u32[]{:S(2)}, u32[]{:S(2)}) collective-permute-start(bf16[576,512]{1,0:T(8,128)(2,1)S(1)} %slice.65.la), channel_id=1, source_target_pairs={{0,16},{16,0},{1,17},{17,1},{2,18},{18,2},{3,19},{19,3},{4,20},{20... | collective-permute-start | bytes 1769480 | tf_op jit(solution)/shard_map/ppermute | solution.py:345
  100.2 13.4 %collective-permute-start.13 = (bf16[4,64,1024]{2,1,0:T(8,128)(2,1)}, bf16[4,64,1024]{2,1,0:T(8,128)(2,1)S(1)}, u32[]{:S(2)}, u32[]{:S(2)}) collective-permute-start(bf16[4,64,1024]{2,1,0:T(8,128)(2,1)} %all-to-all-done.2.g0.direct), channel_id=1, source_target_pairs={{0,1},{1,0},{2,3},{3,2},{4,5},{5,4},{6,7},{7,6},{8,9},{9,8},{10,11... | collective-permute-start | bytes 1572872 | tf_op jit(solution)/shard_map/ppermute | solution.py:338
  100.2 13.4 %collective-permute-start.11 = (bf16[4,64,1024]{2,1,0:T(8,128)(2,1)S(1)}, bf16[4,64,1024]{2,1,0:T(8,128)(2,1)S(1)}, u32[]{:S(2)}, u32[]{:S(2)}) collective-permute-start(bf16[4,64,1024]{2,1,0:T(8,128)(2,1)S(1)} %get-tuple-element.171.n0), channel_id=1, source_target_pairs={{0,1},{1,0},{2,3},{3,2},{4,5},{5,4},{6,7},{7,6},{8,9},{9,8},{10,11... | collective-permute-start | bytes 1572872 | tf_op jit(solution)/shard_map/ppermute | solution.py:338
  100.7 12.9 %collective-permute-start.14 = (bf16[4,64,1024]{2,1,0:T(8,128)(2,1)}, bf16[4,64,1024]{2,1,0:T(8,128)(2,1)S(1)}, u32[]{:S(2)}, u32[]{:S(2)}) collective-permute-start(bf16[4,64,1024]{2,1,0:T(8,128)(2,1)} %all-to-all-done.3.g1), channel_id=1, source_target_pairs={{0,1},{1,0},{2,3},{3,2},{4,5},{5,4},{6,7},{7,6},{8,9},{9,8},{10,11... | collective-permute-start | bytes 1572872 | tf_op jit(solution)/shard_map/ppermute | solution.py:338
  111.9 1.9 collective-permute-start.12
  124.6 2.7 collective-permute-start.16
  129.3 14.0 %collective-permute-start.17 = (bf16[4,64,1024]{2,1,0:T(8,128)(2,1)S(1)}, bf16[4,64,1024]{2,1,0:T(8,128)(2,1)S(1)}, u32[]{:S(2)}, u32[]{:S(2)}) collective-permute-start(bf16[4,64,1024]{2,1,0:T(8,128)(2,1)S(1)} %fusion.6), channel_id=1, source_target_pairs={{0,2},{1,3},{2,0},{3,1},{4,6},{5,7},{6,4},{7,5},{8,10},{9,11},{10,... | collective-permute-start | bytes 1572872 | tf_op jit(solution)/shard_map/ppermute | solution.py:341
  130.8 17.9 %collective-permute-start.18 = (bf16[704,512]{1,0:T(8,128)(2,1)S(1)}, bf16[704,512]{1,0:T(8,128)(2,1)S(1)}, u32[]{:S(2)}, u32[]{:S(2)}) collective-permute-start(bf16[704,512]{1,0:T(8,128)(2,1)S(1)} %fusion), channel_id=1, source_target_pairs={{0,16},{16,0},{1,17},{17,1},{2,18},{18,2},{3,19},{19,3},{4,20},{20... | collective-permute-start | bytes 2162696 | tf_op jit(solution)/shard_map/ppermute | solution.py:476
  134.2 12.6 %collective-permute-start.19 = (bf16[2,4,64,1024]{3,2,1,0:T(8,128)(2,1)S(1)}, bf16[2,4,64,1024]{3,2,1,0:T(8,128)(2,1)S(1)}, u32[]{:S(2)}, u32[]{:S(2)}) collective-permute-start(bf16[2,4,64,1024]{3,2,1,0:T(8,128)(2,1)S(1)} %get-tuple-element.195), channel_id=1, source_target_pairs={{0,1},{1,0},{2,3},{3,2},{4,5},{5,4},{6,7},{7,6},{8,9},{9,8},{10,11... | collective-permute-start | bytes 3145736 | tf_op jit(solution)/shard_map/ppermute | solution.py:338
  148.7 12.8 %collective-permute-start.20 = (bf16[4,64,1024]{2,1,0:T(8,128)(2,1)S(1)}, bf16[4,64,1024]{2,1,0:T(8,128)(2,1)S(1)}, u32[]{:S(2)}, u32[]{:S(2)}) collective-permute-start(bf16[4,64,1024]{2,1,0:T(8,128)(2,1)S(1)} %get-tuple-element.198.b0), channel_id=1, source_target_pairs={{0,2},{1,3},{2,0},{3,1},{4,6},{5,7},{6,4},{7,5},{8,10},{9,11},{10,... | collective-permute-start | bytes 1572872 | tf_op jit(solution)/shard_map/ppermute | solution.py:341
  149.9 18.0 %collective-permute-start.24 = (bf16[704,512]{1,0:T(8,128)(2,1)S(1)}, bf16[704,512]{1,0:T(8,128)(2,1)S(1)}, u32[]{:S(2)}, u32[]{:S(2)}) collective-permute-start(bf16[704,512]{1,0:T(8,128)(2,1)S(1)} %add_convert_fusion.8), channel_id=1, source_target_pairs={{0,4},{12,8},{1,5},{13,9},{2,6},{14,10},{3,7},{15,11},{16,20},{28,... | collective-permute-start | bytes 2162696 | tf_op jit(solution)/shard_map/ppermute | solution.py:488
  153.4 16.8 %collective-permute-start.23 = (bf16[704,512]{1,0:T(8,128)(2,1)S(1)}, bf16[704,512]{1,0:T(8,128)(2,1)S(1)}, u32[]{:S(2)}, u32[]{:S(2)}) collective-permute-start(bf16[704,512]{1,0:T(8,128)(2,1)S(1)} %fusion.1), channel_id=1, source_target_pairs={{0,16},{16,0},{1,17},{17,1},{2,18},{18,2},{3,19},{19,3},{4,20},{20... | collective-permute-start | bytes 2162696 | tf_op jit(solution)/shard_map/ppermute | solution.py:476
  154.9 6.7 %collective-permute-start.21 = (bf16[4,64,1024]{2,1,0:T(8,128)(2,1)S(1)}, bf16[4,64,1024]{2,1,0:T(8,128)(2,1)S(1)}, u32[]{:S(2)}, u32[]{:S(2)}) collective-permute-start(bf16[4,64,1024]{2,1,0:T(8,128)(2,1)S(1)} %get-tuple-element.198.b0), channel_id=1, source_target_pairs={{0,1},{1,0},{2,3},{3,2},{4,5},{5,4},{6,7},{7,6},{8,9},{9,8},{10,11... | collective-permute-start | bytes 1572872 | tf_op jit(solution)/shard_map/ppermute | solution.py:338
  161.5 8.7 %collective-permute-start.22 = (bf16[4,64,1024]{2,1,0:T(8,128)(2,1)S(1)}, bf16[4,64,1024]{2,1,0:T(8,128)(2,1)S(1)}, u32[]{:S(2)}, u32[]{:S(2)}) collective-permute-start(bf16[4,64,1024]{2,1,0:T(8,128)(2,1)S(1)} %collective-permute-done.20.b1), channel_id=1, source_target_pairs={{0,1},{1,0},{2,3},{3,2},{4,5},{5,4},{6,7},{7,6},{8,9},{9,8},{10,11... | collective-permute-start | bytes 1572872 | tf_op jit(solution)/shard_map/ppermute | solution.py:338
  170.2 31.3 %collective-permute-start.28 = (bf16[4,64,1024]{2,1,0:T(8,128)(2,1)S(1)}, bf16[4,64,1024]{2,1,0:T(8,128)(2,1)S(1)}, u32[]{:S(2)}, u32[]{:S(2)}) collective-permute-start(bf16[4,64,1024]{2,1,0:T(8,128)(2,1)S(1)} %get-tuple-element.224), channel_id=1, source_target_pairs={{0,2},{1,3},{2,0},{3,1},{4,6},{5,7},{6,4},{7,5},{8,10},{9,11},{10,... | collective-permute-start | bytes 1572872 | tf_op jit(solution)/shard_map/ppermute | solution.py:341
  171.3 30.2 %collective-permute-start.26 = (bf16[704,512]{1,0:T(8,128)(2,1)S(1)}, bf16[704,512]{1,0:T(8,128)(2,1)S(1)}, u32[]{:S(2)}, u32[]{:S(2)}) collective-permute-start(bf16[704,512]{1,0:T(8,128)(2,1)S(1)} %add_convert_fusion.7), channel_id=1, source_target_pairs={{4,8},{8,4},{5,9},{9,5},{6,10},{10,6},{7,11},{11,7},{20,24},{24,20... | collective-permute-start | bytes 2162696 | tf_op jit(solution)/shard_map/ppermute | solution.py:491
  172.2 29.4 %collective-permute-start.25 = (bf16[704,512]{1,0:T(8,128)(2,1)S(1)}, bf16[704,512]{1,0:T(8,128)(2,1)S(1)}, u32[]{:S(2)}, u32[]{:S(2)}) collective-permute-start(bf16[704,512]{1,0:T(8,128)(2,1)S(1)} %fusion.2), channel_id=1, source_target_pairs={{0,16},{16,0},{1,17},{17,1},{2,18},{18,2},{3,19},{19,3},{4,20},{20... | collective-permute-start | bytes 2162696 | tf_op jit(solution)/shard_map/ppermute | solution.py:476
  173.9 26.7 %copy-start.28 = (bf16[704,512]{1,0:T(8,128)(2,1)}, bf16[704,512]{1,0:T(8,128)(2,1)S(1)}, u32[]{:S(2)}) copy-start(bf16[704,512]{1,0:T(8,128)(2,1)S(1)} %add_convert_fusion.6) | copy-start | bytes 2162692
  173.9 27.7 %collective-permute-start.27 = (bf16[704,512]{1,0:T(8,128)(2,1)S(1)}, bf16[704,512]{1,0:T(8,128)(2,1)S(1)}, u32[]{:S(2)}, u32[]{:S(2)}) collective-permute-start(bf16[704,512]{1,0:T(8,128)(2,1)S(1)} %add_convert_fusion.6), channel_id=1, source_target_pairs={{0,4},{12,8},{1,5},{13,9},{2,6},{14,10},{3,7},{15,11},{16,20},{28,... | collective-permute-start | bytes 2162696 | tf_op jit(solution)/shard_map/ppermute | solution.py:488
  203.3 2.7 collective-permute-start.29
  207.4 15.6 %collective-permute-start.30 = (bf16[4,64,1024]{2,1,0:T(8,128)(2,1)S(1)}, bf16[4,64,1024]{2,1,0:T(8,128)(2,1)S(1)}, u32[]{:S(2)}, u32[]{:S(2)}) collective-permute-start(bf16[4,64,1024]{2,1,0:T(8,128)(2,1)S(1)} %fusion.3), channel_id=1, source_target_pairs={{0,2},{1,3},{2,0},{3,1},{4,6},{5,7},{6,4},{7,5},{8,10},{9,11},{10,... | collective-permute-start | bytes 1572872 | tf_op jit(solution)/shard_map/ppermute | solution.py:341
  208.6 21.5 %collective-permute-start.34 = (bf16[512,512]{1,0:T(8,128)(2,1)}, bf16[512,512]{1,0:T(8,128)(2,1)}, u32[]{:S(2)}, u32[]{:S(2)}) collective-permute-start(bf16[512,512]{1,0:T(8,128)(2,1)} %get-tuple-element.252), channel_id=1, source_target_pairs={{0,16},{16,0},{1,17},{17,1},{2,18},{18,2},{3,19},{19,3},{4,20},{20... | collective-permute-start | bytes 1572872 | tf_op jit(solution)/shard_map/ppermute | solution.py:476
  210.3 21.1 %collective-permute-start.32 = (bf16[704,512]{1,0:T(8,128)(2,1)}, bf16[704,512]{1,0:T(8,128)(2,1)}, u32[]{:S(2)}, u32[]{:S(2)}) collective-permute-start(bf16[704,512]{1,0:T(8,128)(2,1)} %add_convert_fusion.4), channel_id=1, source_target_pairs={{4,8},{8,4},{5,9},{9,5},{6,10},{10,6},{7,11},{11,7},{20,24},{24,20... | collective-permute-start | bytes 2162696 | tf_op jit(solution)/shard_map/ppermute | solution.py:491
  213.0 24.8 %collective-permute-start.31 = (bf16[704,512]{1,0:T(8,128)(2,1)}, bf16[704,512]{1,0:T(8,128)(2,1)}, u32[]{:S(2)}, u32[]{:S(2)}) collective-permute-start(bf16[704,512]{1,0:T(8,128)(2,1)} %add_convert_fusion.5), channel_id=1, source_target_pairs={{4,0},{8,12},{5,1},{9,13},{6,2},{10,14},{7,3},{11,15},{20,16},{24,... | collective-permute-start | bytes 2162696 | tf_op jit(solution)/shard_map/ppermute | solution.py:494
  215.6 24.6 %collective-permute-start.33 = (bf16[704,512]{1,0:T(8,128)(2,1)}, bf16[704,512]{1,0:T(8,128)(2,1)}, u32[]{:S(2)}, u32[]{:S(2)}) collective-permute-start(bf16[704,512]{1,0:T(8,128)(2,1)} %add_convert_fusion.3), channel_id=1, source_target_pairs={{0,4},{12,8},{1,5},{13,9},{2,6},{14,10},{3,7},{15,11},{16,20},{28,... | collective-permute-start | bytes 2162696 | tf_op jit(solution)/shard_map/ppermute | solution.py:488
  225.1 19.6 %all-to-all-start.4 = ((bf16[4,64,1024]{2,1,0:T(8,128)(2,1)}), bf16[4,64,1024]{2,1,0:T(8,128)(2,1)S(1)}, u32[]{:S(2)}, u32[]{:S(2)}) async-start(bf16[4,64,1024]{2,1,0:T(8,128)(2,1)} %get-tuple-element.245), calls=%async_computation.4 | async-start | bytes 1048576 | tf_op jit(solution)/shard_map/all_to_all | solution.py:605
  228.7 26.9 %collective-permute-start.36 = (bf16[528,512]{1,0:T(8,128)(2,1)}, bf16[528,512]{1,0:T(8,128)(2,1)S(1)}, u32[]{:S(2)}, u32[]{:S(2)}) collective-permute-start(bf16[528,512]{1,0:T(8,128)(2,1)} %get-tuple-element.255), channel_id=1, source_target_pairs={{0,16},{16,0},{1,17},{17,1},{2,18},{18,2},{3,19},{19,3},{4,20},{20... | collective-permute-start | bytes 1622024 | tf_op jit(solution)/shard_map/ppermute | solution.py:476
  244.7 20.8 %collective-permute-start.37 = (bf16[704,512]{1,0:T(8,128)(2,1)}, bf16[704,512]{1,0:T(8,128)(2,1)S(1)}, u32[]{:S(2)}, u32[]{:S(2)}) collective-permute-start(bf16[704,512]{1,0:T(8,128)(2,1)} %add_convert_fusion.2), channel_id=1, source_target_pairs={{4,0},{8,12},{5,1},{9,13},{6,2},{10,14},{7,3},{11,15},{20,16},{24,... | collective-permute-start | bytes 2162696 | tf_op jit(solution)/shard_map/ppermute | solution.py:494
  246.0 19.5 %collective-permute-start.38 = (bf16[704,512]{1,0:T(8,128)(2,1)S(1)}, bf16[704,512]{1,0:T(8,128)(2,1)S(1)}, u32[]{:S(2)}, u32[]{:S(2)}) collective-permute-start(bf16[704,512]{1,0:T(8,128)(2,1)S(1)} %add_convert_fusion.1), channel_id=1, source_target_pairs={{4,8},{8,4},{5,9},{9,5},{6,10},{10,6},{7,11},{11,7},{20,24},{24,20... | collective-permute-start | bytes 2162696 | tf_op jit(solution)/shard_map/ppermute | solution.py:491
  246.7 16.2 %collective-permute-start.39 = (bf16[512,512]{1,0:T(8,128)(2,1)S(1)}, bf16[512,512]{1,0:T(8,128)(2,1)S(1)}, u32[]{:S(2)}, u32[]{:S(2)}) collective-permute-start(bf16[512,512]{1,0:T(8,128)(2,1)S(1)} %add_convert_fusion.14), channel_id=1, source_target_pairs={{0,4},{12,8},{1,5},{13,9},{2,6},{14,10},{3,7},{15,11},{16,20},{28,... | collective-permute-start | bytes 1572872 | tf_op jit(solution)/shard_map/ppermute | solution.py:488
  254.7 10.8 %collective-permute-start.35 = (bf16[4,64,1024]{2,1,0:T(8,128)(2,1)S(1)}, bf16[4,64,1024]{2,1,0:T(8,128)(2,1)S(1)}, u32[]{:S(2)}, u32[]{:S(2)}) collective-permute-start(bf16[4,64,1024]{2,1,0:T(8,128)(2,1)S(1)} %all-to-all-done.4.refs_0_), channel_id=1, source_target_pairs={{0,2},{1,3},{2,0},{3,1},{4,6},{5,7},{6,4},{7,5},{8,10},{9,11},{10,... | collective-permute-start | bytes 1572872 | tf_op jit(solution)/shard_map/ppermute | solution.py:341
  257.9 21.6 %collective-permute-start.40 = (bf16[4,64,1024]{2,1,0:T(8,128)(2,1)S(1)}, bf16[4,64,1024]{2,1,0:T(8,128)(2,1)S(1)}, u32[]{:S(2)}, u32[]{:S(2)}) collective-permute-start(bf16[4,64,1024]{2,1,0:T(8,128)(2,1)S(1)} %all-to-all-done.4.refs_0_), channel_id=1, source_target_pairs={{0,1},{1,0},{2,3},{3,2},{4,5},{5,4},{6,7},{7,6},{8,9},{9,8},{10,11... | collective-permute-start | bytes 1572872 | tf_op jit(solution)/shard_map/ppermute | solution.py:338
  267.4 28.6 %all-to-all-start.5 = ((bf16[4,64,1024]{2,1,0:T(8,128)(2,1)}), bf16[4,64,1024]{2,1,0:T(8,128)(2,1)S(1)}, u32[]{:S(2)}, u32[]{:S(2)}) async-start(bf16[4,64,1024]{2,1,0:T(8,128)(2,1)} %add_convert_fusion.15), calls=%async_computation.5 | async-start | bytes 1048576 | tf_op jit(solution)/shard_map/all_to_all | solution.py:623
  270.9 8.6 %collective-permute-start.41 = (bf16[4,64,1024]{2,1,0:T(8,128)(2,1)S(1)}, bf16[4,64,1024]{2,1,0:T(8,128)(2,1)S(1)}, u32[]{:S(2)}, u32[]{:S(2)}) collective-permute-start(bf16[4,64,1024]{2,1,0:T(8,128)(2,1)S(1)} %collective-permute-done.35.refs_1_), channel_id=1, source_target_pairs={{0,1},{1,0},{2,3},{3,2},{4,5},{5,4},{6,7},{7,6},{8,9},{9,8},{10,11... | collective-permute-start | bytes 1572872 | tf_op jit(solution)/shard_map/ppermute | solution.py:338
  270.9 17.0 %collective-permute-start.44 = (bf16[528,512]{1,0:T(8,128)(2,1)S(1)}, bf16[528,512]{1,0:T(8,128)(2,1)S(1)}, u32[]{:S(2)}, u32[]{:S(2)}) collective-permute-start(bf16[528,512]{1,0:T(8,128)(2,1)S(1)} %add_convert_fusion.11), channel_id=1, source_target_pairs={{0,4},{12,8},{1,5},{13,9},{2,6},{14,10},{3,7},{15,11},{16,20},{28,... | collective-permute-start | bytes 1622024 | tf_op jit(solution)/shard_map/ppermute | solution.py:488
  274.9 21.0 %collective-permute-start.42 = (bf16[704,512]{1,0:T(8,128)(2,1)}, bf16[704,512]{1,0:T(8,128)(2,1)}, u32[]{:S(2)}, u32[]{:S(2)}) collective-permute-start(bf16[704,512]{1,0:T(8,128)(2,1)} %add_convert_fusion), channel_id=1, source_target_pairs={{4,0},{8,12},{5,1},{9,13},{6,2},{10,14},{7,3},{11,15},{20,16},{24,... | collective-permute-start | bytes 2162696 | tf_op jit(solution)/shard_map/ppermute | solution.py:494
  277.6 4.9 %collective-permute-start.43 = (bf16[512,512]{1,0:T(8,128)(2,1)S(1)}, bf16[512,512]{1,0:T(8,128)(2,1)S(1)}, u32[]{:S(2)}, u32[]{:S(2)}) collective-permute-start(bf16[512,512]{1,0:T(8,128)(2,1)S(1)} %add_convert_fusion.13), channel_id=1, source_target_pairs={{4,8},{8,4},{5,9},{9,5},{6,10},{10,6},{7,11},{11,7},{20,24},{24,20... | collective-permute-start | bytes 1572872 | tf_op jit(solution)/shard_map/ppermute | solution.py:491
  282.5 20.8 %copy-start.32 = (bf16[512,512]{1,0:T(8,128)(2,1)S(1)}, bf16[512,512]{1,0:T(8,128)(2,1)}, u32[]{:S(2)}) copy-start(bf16[512,512]{1,0:T(8,128)(2,1)} %copy-done.31) | copy-start | bytes 1572868
  297.2 27.4 %all-to-all-start.6 = ((bf16[4,4,64,256]{3,2,1,0:T(8,128)(2,1)}), bf16[4,4,64,256]{3,2,1,0:T(8,128)(2,1)}, u32[]{:S(2)}, u32[]{:S(2)}) async-start(bf16[4,4,64,256]{3,2,1,0:T(8,128)(2,1)} %get-tuple-element.269), calls=%async_computation.6 | async-start | bytes 1048576 | tf_op jit(solution)/shard_map/all_to_all | solution.py:636
  301.8 22.9 %collective-permute-start.47 = (bf16[528,512]{1,0:T(8,128)(2,1)S(1)}, bf16[528,512]{1,0:T(8,128)(2,1)}, u32[]{:S(2)}, u32[]{:S(2)}) collective-permute-start(bf16[528,512]{1,0:T(8,128)(2,1)S(1)} %add_convert_fusion.10), channel_id=1, source_target_pairs={{4,8},{8,4},{5,9},{9,5},{6,10},{10,6},{7,11},{11,7},{20,24},{24,20... | collective-permute-start | bytes 1622024 | tf_op jit(solution)/shard_map/ppermute | solution.py:491
  303.4 20.4 %collective-permute-start.46 = (bf16[512,512]{1,0:T(8,128)(2,1)S(1)}, bf16[512,512]{1,0:T(8,128)(2,1)S(1)}, u32[]{:S(2)}, u32[]{:S(2)}) collective-permute-start(bf16[512,512]{1,0:T(8,128)(2,1)S(1)} %add_convert_fusion.12), channel_id=1, source_target_pairs={{4,0},{8,12},{5,1},{9,13},{6,2},{10,14},{7,3},{11,15},{20,16},{24,... | collective-permute-start | bytes 1572872 | tf_op jit(solution)/shard_map/ppermute | solution.py:494
  304.7 19.2 %collective-permute-start.45 = (bf16[4,64,1024]{2,1,0:T(8,128)(2,1)S(1)}, bf16[4,64,1024]{2,1,0:T(8,128)(2,1)S(1)}, u32[]{:S(2)}, u32[]{:S(2)}) collective-permute-start(bf16[4,64,1024]{2,1,0:T(8,128)(2,1)S(1)} %all-to-all-done.5.refs_0_), channel_id=1, source_target_pairs={{0,2},{1,3},{2,0},{3,1},{4,6},{5,7},{6,4},{7,5},{8,10},{9,11},{10,... | collective-permute-start | bytes 1572872 | tf_op jit(solution)/shard_map/ppermute | solution.py:341
  305.6 23.9 %collective-permute-start.48 = (bf16[4,64,1024]{2,1,0:T(8,128)(2,1)S(1)}, bf16[4,64,1024]{2,1,0:T(8,128)(2,1)S(1)}, u32[]{:S(2)}, u32[]{:S(2)}) collective-permute-start(bf16[4,64,1024]{2,1,0:T(8,128)(2,1)S(1)} %all-to-all-done.5.refs_0_), channel_id=1, source_target_pairs={{0,1},{1,0},{2,3},{3,2},{4,5},{5,4},{6,7},{7,6},{8,9},{9,8},{10,11... | collective-permute-start | bytes 1572872 | tf_op jit(solution)/shard_map/ppermute | solution.py:338
  325.9 3.6 %collective-permute-start.49 = (bf16[4,64,1024]{2,1,0:T(8,128)(2,1)S(1)}, bf16[4,64,1024]{2,1,0:T(8,128)(2,1)S(1)}, u32[]{:S(2)}, u32[]{:S(2)}) collective-permute-start(bf16[4,64,1024]{2,1,0:T(8,128)(2,1)S(1)} %collective-permute-done.45.refs_1_), channel_id=1, source_target_pairs={{0,1},{1,0},{2,3},{3,2},{4,5},{5,4},{6,7},{7,6},{8,9},{9,8},{10,11... | collective-permute-start | bytes 1572872 | tf_op jit(solution)/shard_map/ppermute | solution.py:338
  326.0 18.1 %collective-permute-start.50 = (bf16[528,512]{1,0:T(8,128)(2,1)S(1)}, bf16[528,512]{1,0:T(8,128)(2,1)S(1)}, u32[]{:S(2)}, u32[]{:S(2)}) collective-permute-start(bf16[528,512]{1,0:T(8,128)(2,1)S(1)} %add_convert_fusion.9), channel_id=1, source_target_pairs={{4,0},{8,12},{5,1},{9,13},{6,2},{10,14},{7,3},{11,15},{20,16},{24,... | collective-permute-start | bytes 1622024 | tf_op jit(solution)/shard_map/ppermute | solution.py:494
  345.1 1.2 collective-permute-start.51
  346.2 3.6 %collective-permute-start.52 = (f32[2,512]{1,0:T(2,128)S(1)}, f32[2,512]{1,0:T(2,128)S(1)}, u32[]{:S(2)}, u32[]{:S(2)}) collective-permute-start(f32[2,512]{1,0:T(2,128)S(1)} %slice_add_fusion), channel_id=1, source_target_pairs={{0,2},{1,3},{2,0},{3,1},{4,6},{5,7},{6,4},{7,5},{8,10},{9,11},{10,... | collective-permute-start | bytes 12296 | tf_op jit(solution)/shard_map/ppermute | solution.py:341
  (55 other events, 329.0 us)

commit v4 on v3

--- a/solution.py
+++ b/solution.py
@@ -403,10 +403,10 @@
     late_a, late_b = other_half(w_down[early:], 1)
 
     x_own = lax.all_to_all(x_part, "ctx", 0, 0)
+    x_second = across(x_own)
     x_own, qkv_b, cosine, sine, mix_row, g_part, g_late = tie(
         x_own, qkv_b, cosine, sine, mix_row, *own_rows(out_grad, 2)
     )
-    x_second = across(x_own)
     fv = lax.all_to_all(first_values, "ctx", 0, 0).reshape(ctx, tp, quarter, local)
     gains = jnp.concatenate([out_a[local:], out_b[local:]], axis=1).astype(F32)
     x_core = core(x_own)
@@ -519,7 +519,6 @@
     )
     down_core = core(down_send)
     down_onward = added(down_onward, down_core[1]).astype(BF)
-    output_own = residual + added(down_keep, down_core[0])
     grad_residual, branch_own, gain_sum_second = call(
         norm_back_kernel,
         [own_f32, own_low, gain_row],
@@ -531,10 +530,10 @@
     )
     (
         branch_own, grad_residual, gate_got, gate_first, up_first, up_second, down_first, down_second,
-        down_onward, output_own,
+        down_onward,
     ) = tie(
         branch_own, grad_residual, gate_got, gate_first, up_first, up_second, down_first, down_second,
-        down_onward, output_own,
+        down_onward,
     )
 
     b_second = across(branch_own)
@@ -544,8 +543,8 @@
     gate_shard = joined(gate_first, gate_got)
     gate_more = toward(gate_shard)
     (
-        b_second, b_core, b_both, up_got, gate_shard, gate_more, down_onward, output_own, down_second,
-    ) = tie(b_second, b_core, b_both, up_got, gate_shard, gate_more, down_onward, output_own, down_second)
+        b_second, b_core, b_both, up_got, gate_shard, gate_more, down_onward, down_second,
+    ) = tie(b_second, b_core, b_both, up_got, gate_shard, gate_more, down_onward, down_second)
 
     down_x = across(down_onward)
     down_got = exchange(down_first, down_second)
@@ -588,7 +587,7 @@
     down_shard = joined(down_first, down_got)
     down_more = toward(down_shard)
     qk_got = exchange(qk_first, qk_second)
-    output_own = (output_own + down_x.astype(F32)).astype(BF)
+    output_own = (residual + added(down_keep, down_core[0]) + down_x.astype(F32)).astype(BF)
     _, tokens_own, _ = call(
         norm_back_kernel,
         [own_f32, own_low, gain_row],
@@ -628,9 +627,7 @@
     out_more = toward(out_shard)
     grad_tokens = placed(tokens_home, tokens_second, tokens_core, core(tokens_second), F32)
     grad_w_up = settled(up_shard, up_more).T
-    output_home, gf, grad_tokens, grad_w_up, down_more, qk_more, out_more = tie(
-        output_home, gf, grad_tokens, grad_w_up, down_more, qk_more, out_more
-    )
+    output_home, gf, grad_tokens, grad_w_up = tie(output_home, gf, grad_tokens, grad_w_up)
     output_second = across(output_home)
     output_core = core(output_home)
     first_home = lax.all_to_all(gf, "ctx", 0, 0)
@@ -639,15 +636,12 @@
     out_shard = plus(out_shard, out_more)
     out_more = meet(out_shard)
     grad_w_down = settled(down_shard, down_more)
-    output_second, first_home, grad_w_down, qk_more, out_more = tie(
-        output_second, first_home, grad_w_down, qk_more, out_more
-    )
     out_shard = plus(out_shard, out_more)
     out_more = back(out_shard)
     output = placed(output_home, output_second, output_core, core(output_second), BF)
     grad_first = first_home.reshape(seqs, block, local).astype(F32)
     qk_full = settled(qk_shard, qk_more).T
-    output, grad_first, qk_full, out_more = tie(output, grad_first, qk_full, out_more)
+    output, grad_first, grad_w_down, qk_full, out_more = tie(output, grad_first, grad_w_down, qk_full, out_more)
     out_full = settled(out_shard, out_more)
     v_full = out_full[local:2 * local].T
     grad_w_qkv = jnp.stack([qk_full[:, :local], qk_full[:, local:], v_full], axis=1)

time: 352 us -> 340 us (0.966)
  waiting for transfers between devices: 131 us -> 109 us
  starting transfers between devices: 94.3 us -> 98.8 us
    ppermute x5, waiting for transfers between devices: 39.2 us -> 7.41 us  [back(): return lax.ppermute(shard, 'ctx', [(1, 0), (2, 3)])]
    ppermute x10, waiting for transfers between devices: 29.2 us -> 37.4 us  [across(): return lax.ppermute(value, 'tp', by_x)]
    all_to_all x1, waiting for transfers between devices: 8.46 us -> 0.9 us  [on_device(): lax.all_to_all(first_values, 'ctx', 0, 0).reshape(ctx, tp, quarter, local)]
    ppermute x6, waiting for transfers between devices: 18.4 us -> 12.9 us  [other_half(): return (value, lax.ppermute(value, 'fsdp', swap_y))]
    all_to_all x1, waiting for transfers between devices: 0.01 us -> 4.17 us  [on_device(): first_home = lax.all_to_all(gf, 'ctx', 0, 0)]
    unnamed x119 -> x121, local copies, waits for them, and re-layouts: 15.9 us -> 17.9 us
  transfers between devices with their start and end apart: 60 -> 60, of which waited for: 27 -> 27; matrix products, arithmetic and copies ran while one was open for 11% -> 12% of each run, Pallas kernels for 14% -> 15%
where the time goes in v4:
time: 340 us; the launch traced here: 338 us
  waiting for transfers between devices  109 us (32%)
  starting transfers between devices  98.8 us (29%)
  Pallas kernels  64.2 us (19%)
  other arithmetic  35.1 us (10%)
  local copies, waits for them, and re-layouts  22.4 us (7%)
  matrix products  6.75 us (2%)
    pallas_call x11, Pallas kernels, call(): pl.pallas_call(kernel, out_shape=out_shapes, scratch_shapes=list(scratch)...  64.2 us
    ppermute x10, waiting for transfers between devices, across(): return lax.ppermute(value, 'tp', by_x)  37.4 us
    ppermute x5, starting transfers between devices, toward(): return lax.ppermute(shard, 'ctx', [(0, 1), (3, 2)])  29.1 us
    ppermute x5, waiting for transfers between devices, toward(): return lax.ppermute(shard, 'ctx', [(0, 1), (3, 2)])  19.6 us
    unnamed x121, local copies, waits for them, and re-layouts  17.9 us
    ppermute x6, waiting for transfers between devices, other_half(): return (value, lax.ppermute(value, 'fsdp', swap_y))  12.9 us
    convert_element_type x10, other arithmetic, plus(): return (shard.astype(F32) + received.astype(F32)).astype(BF)  11.6 us
    all_to_all x1, waiting for transfers between devices, on_device(): x_own = lax.all_to_all(x_part, 'ctx', 0, 0)  11.5 us
  transfers between devices with their start and end apart: 60, of which 27 were waited for; matrix products, arithmetic and copies ran while one was open for 12% of the time, Pallas kernels for 15%

profile of v4, /device:TPU:0, one launch (start us, length us, event | category | flops | bytes accessed | tf_op | source)
XLA Modules:
  0.0 338.1 jit_solution(5091120331763410552)
XLA Ops:
  0.7 1.6 copy-done.1
  2.3 1.4 own.2
  3.8 6.5 %all-to-all-start = ((bf16[4,64,1024]{2,1,0:T(8,128)(2,1)}), bf16[4,64,1024]{2,1,0:T(8,128)(2,1)S(1)}, u32[]{:S(2)}, u32[]{:S(2)}) async-start(bf16[4,64,1024]{2,1,0:T(8,128)(2,1)} %own.2), calls=%async_computation | async-start | bytes 1048576 | tf_op jit(solution)/shard_map/all_to_all | solution.py:405
  11.0 1.5 collective-permute-start.2
  13.3 11.5 %all-to-all-done.p0.x.values = bf16[4,64,1024]{2,1,0:T(8,128)(2,1)S(1)} async-done(((bf16[4,64,1024]{2,1,0:T(8,128)(2,1)}), bf16[4,64,1024]{2,1,0:T(8,128)(2,1)S(1)}, u32[]{:S(2)}, u32[]{:S(2)}) %all-to-all-start) | async-done | bytes 524320 | tf_op jit(solution)/shard_map/all_to_all | solution.py:405
  24.7 3.5 %all-to-all-start.1 = ((bf16[4,256,256]{2,1,0:T(8,128)(2,1)}), bf16[4,256,256]{2,1,0:T(8,128)(2,1)S(1)}, u32[]{:S(2)}, u32[]{:S(2)}) async-start(bf16[4,256,256]{2,1,0:T(8,128)(2,1)} %param.12), calls=%async_computation.1 | async-start | bytes 1048576 | tf_op jit(solution)/shard_map/all_to_all | solution.py:410
  28.2 1.6 collective-permute-start.1
  32.3 1.9 multiply_sine_fusion
  36.1 5.2 %collective-permute-done.1.p1 = bf16[4,64,1024]{2,1,0:T(8,128)(2,1)} collective-permute-done((bf16[4,64,1024]{2,1,0:T(8,128)(2,1)S(1)}, bf16[4,64,1024]{2,1,0:T(8,128)(2,1)}, u32[]{:S(2)}, u32[]{:S(2)}) %collective-permute-start.1) | collective-permute-done | bytes 524320 | tf_op jit(solution)/shard_map/ppermute | solution.py:341
  43.6 4.7 %all-to-all-start.2 = ((bf16[4,64,1024]{2,1,0:T(8,128)(2,1)}), bf16[4,64,1024]{2,1,0:T(8,128)(2,1)}, u32[]{:S(2)}, u32[]{:S(2)}) async-start(bf16[4,64,1024]{2,1,0:T(8,128)(2,1)} %copy-done.13), calls=%async_computation.2 | async-start | bytes 1048576 | tf_op jit(solution)/shard_map/all_to_all | solution.py:419
  48.3 1.5 collective-permute-start.5
  49.8 14.6 %attend.1 = (bf16[4,256,512]{2,1,0:T(8,128)(2,1)}, bf16[4,256,512]{2,1,0:T(8,128)(2,1)}, bf16[4,256,256]{2,1,0:T(8,128)(2,1)}, bf16[4,256,256]{2,1,0:T(8,128)(2,...) custom-call(s32[4]{0:T(128)S(1)} %get-tuple-element.279.seg.where, ...), custom_call_target="tpu_custom_call" | custom-call | tf_op jit(solution)/shard_map/attend/pallas_call | solution.py:37
  67.3 1.6 collective-permute-start.8
  68.9 4.8 %all-to-all-start.3 = ((bf16[4,64,1024]{2,1,0:T(8,128)(2,1)}), bf16[4,64,1024]{2,1,0:T(8,128)(2,1)}, u32[]{:S(2)}, u32[]{:S(2)}) async-start(bf16[4,64,1024]{2,1,0:T(8,128)(2,1)} %copy-done.12), calls=%async_computation.3 | async-start | bytes 1048576 | tf_op jit(solution)/shard_map/all_to_all | solution.py:433
  73.7 2.0 fusion.9
  75.7 1.5 collective-permute-start.7
  78.9 9.9 %collective-permute-done.9.db = bf16[128,512]{1,0:T(8,128)(2,1)S(1)} collective-permute-done((bf16[128,512]{1,0:T(8,128)(2,1)S(1)}, bf16[128,512]{1,0:T(8,128)(2,1)S(1)}, u32[]{:S(2)}, u32[]{:S(2)}) %collective-permute-start.9) | collective-permute-done | bytes 131104 | tf_op jit(solution)/shard_map/ppermute | solution.py:345
  92.7 2.5 residual_norm.1
  95.2 1.6 collective-permute-start.10
  98.1 10.0 %collective-permute-done.10.n1 = bf16[4,64,1024]{2,1,0:T(8,128)(2,1)S(1)} collective-permute-done((bf16[4,64,1024]{2,1,0:T(8,128)(2,1)S(1)}, bf16[4,64,1024]{2,1,0:T(8,128)(2,1)S(1)}, u32[]{:S(2)}, u32[]{:S(2)}) %collective-permute-start.10) | collective-permute-done | bytes 524320 | tf_op jit(solution)/shard_map/ppermute | solution.py:341
  108.2 2.7 collective-permute-done.15.lb
  111.0 10.7 %mlp.1 = (bf16[4,256,512]{2,1,0:T(8,128)(2,1)S(1)}, bf16[4,256,512]{2,1,0:T(8,128)(2,1)S(1)}, bf16[4,256,512]{2,1,0:T(8,128)(2,1)S(1)}, bf16[4,256,512]{2,1,0:T(...) custom-call(bf16[4,64,1024]{2,1,0:T(8,128)(2,1)S(1)} %get-tuple-elem, ...), custom_call_target="tpu_custom_call" | custom-call | flops 10000000000 | bytes 34000000 | tf_op jit(solution)/shard_map/mlp/pallas_call | solution.py:37
  128.4 2.3 down.1
  131.7 2.0 convolution_bitcast_fusion.1
  134.7 5.8 %collective-permute-done.17.got_x = bf16[4,64,1024]{2,1,0:T(8,128)(2,1)S(1)} collective-permute-done((bf16[4,64,1024]{2,1,0:T(8,128)(2,1)S(1)}, bf16[4,64,1024]{2,1,0:T(8,128)(2,1)S(1)}, u32[]{:S(2)}, u32[]{:S(2)}) %collective-permute-start.17) | collective-permute-done | bytes 524320 | tf_op jit(solution)/shard_map/ppermute | solution.py:341
  140.5 2.4 norm_back_mlp.1
  143.1 1.9 collective-permute-done.18
  146.8 3.7 %collective-permute-start.24 = (bf16[704,512]{1,0:T(8,128)(2,1)S(1)}, bf16[704,512]{1,0:T(8,128)(2,1)S(1)}, u32[]{:S(2)}, u32[]{:S(2)}) collective-permute-start(bf16[704,512]{1,0:T(8,128)(2,1)S(1)} %add_convert_fusion.8), channel_id=1, source_target_pairs={{0,4},{12,8},{1,5},{13,9},{2,6},{14,10},{3,7},{15,11},{16,20},{28,... | collective-permute-start | bytes 2162696 | tf_op jit(solution)/shard_map/ppermute | solution.py:488
  151.8 6.1 %collective-permute-done.20.b1 = bf16[4,64,1024]{2,1,0:T(8,128)(2,1)S(1)} collective-permute-done((bf16[4,64,1024]{2,1,0:T(8,128)(2,1)S(1)}, bf16[4,64,1024]{2,1,0:T(8,128)(2,1)S(1)}, u32[]{:S(2)}, u32[]{:S(2)}) %collective-permute-start.20) | collective-permute-done | bytes 524320 | tf_op jit(solution)/shard_map/ppermute | solution.py:341
  157.9 6.8 %collective-permute-done.24 = bf16[704,512]{1,0:T(8,128)(2,1)S(1)} collective-permute-done((bf16[704,512]{1,0:T(8,128)(2,1)S(1)}, bf16[704,512]{1,0:T(8,128)(2,1)S(1)}, u32[]{:S(2)}, u32[]{:S(2)}) %collective-permute-start.24) | collective-permute-done | bytes 720928 | tf_op jit(solution)/shard_map/ppermute | solution.py:488
  164.7 2.3 collective-permute-done.23
  170.4 5.1 %collective-permute-start.27 = (bf16[704,512]{1,0:T(8,128)(2,1)S(1)}, bf16[704,512]{1,0:T(8,128)(2,1)S(1)}, u32[]{:S(2)}, u32[]{:S(2)}) collective-permute-start(bf16[704,512]{1,0:T(8,128)(2,1)S(1)} %add_convert_fusion.6), channel_id=1, source_target_pairs={{0,4},{12,8},{1,5},{13,9},{2,6},{14,10},{3,7},{15,11},{16,20},{28,... | collective-permute-start | bytes 2162696 | tf_op jit(solution)/shard_map/ppermute | solution.py:488
  175.6 22.0 %attend_back.1 = (bf16[4,4,64,256]{3,2,1,0:T(8,128)(2,1)}, f32[4,64,1024]{2,1,0:T(8,128)}, f32[4,64,1024]{2,1,0:T(8,128)S(1)}, bf16[2,4,64,1024]{3,2,1,0:T(8,128...) custom-call(s32[4]{0:T(128)S(1)} %get-tuple-element.279.seg.where, ...), custom_call_target="tpu_custom_call" | custom-call | flops 30000001024 | bytes 102000000 | tf_op jit(solution)/shard_map/attend_back/pallas_call | solution.py:37
  200.4 2.9 collective-permute-done.29.got_core
  203.3 1.7 fusion.6
  205.0 1.4 collective-permute-start.30
  208.3 1.6 collective-permute-start.32
  211.0 1.5 collective-permute-start.31
  213.7 6.3 %collective-permute-start.33 = (bf16[704,512]{1,0:T(8,128)(2,1)}, bf16[704,512]{1,0:T(8,128)(2,1)}, u32[]{:S(2)}, u32[]{:S(2)}) collective-permute-start(bf16[704,512]{1,0:T(8,128)(2,1)} %add_convert_fusion.3), channel_id=1, source_target_pairs={{0,4},{12,8},{1,5},{13,9},{2,6},{14,10},{3,7},{15,11},{16,20},{28,... | collective-permute-start | bytes 2162696 | tf_op jit(solution)/shard_map/ppermute | solution.py:488
  222.0 2.1 norm_back_attn.1
  224.2 3.6 %all-to-all-start.4 = ((bf16[4,64,1024]{2,1,0:T(8,128)(2,1)}), bf16[4,64,1024]{2,1,0:T(8,128)(2,1)S(1)}, u32[]{:S(2)}, u32[]{:S(2)}) async-start(bf16[4,64,1024]{2,1,0:T(8,128)(2,1)} %get-tuple-element.234), calls=%async_computation.4 | async-start | bytes 1048576 | tf_op jit(solution)/shard_map/all_to_all | solution.py:604
  230.3 2.4 add_convert_fusion.2
  233.6 2.3 convert_bitcast_fusion.1
  235.9 1.5 add_convert_fusion.1
  237.5 5.2 %all-to-all-done.4.refs_0_ = bf16[4,64,1024]{2,1,0:T(8,128)(2,1)S(1)} async-done(((bf16[4,64,1024]{2,1,0:T(8,128)(2,1)}), bf16[4,64,1024]{2,1,0:T(8,128)(2,1)S(1)}, u32[]{:S(2)}, u32[]{:S(2)}) %all-to-all-start.4) | async-done | bytes 524320 | tf_op jit(solution)/shard_map/all_to_all | solution.py:604
  245.0 7.4 %collective-permute-start.39 = (bf16[512,512]{1,0:T(8,128)(2,1)S(1)}, bf16[512,512]{1,0:T(8,128)(2,1)S(1)}, u32[]{:S(2)}, u32[]{:S(2)}) collective-permute-start(bf16[512,512]{1,0:T(8,128)(2,1)S(1)} %add_convert_fusion.14), channel_id=1, source_target_pairs={{0,4},{12,8},{1,5},{13,9},{2,6},{14,10},{3,7},{15,11},{16,20},{28,... | collective-permute-start | bytes 1572872 | tf_op jit(solution)/shard_map/ppermute | solution.py:488
  253.9 1.5 add_convert_fusion.11
  255.5 5.3 %collective-permute-done.39 = bf16[512,512]{1,0:T(8,128)(2,1)S(1)} collective-permute-done((bf16[512,512]{1,0:T(8,128)(2,1)S(1)}, bf16[512,512]{1,0:T(8,128)(2,1)S(1)}, u32[]{:S(2)}, u32[]{:S(2)}) %collective-permute-start.39) | collective-permute-done | bytes 524320 | tf_op jit(solution)/shard_map/ppermute | solution.py:488
  260.9 2.3 collective-permute-done.35.refs_1_
  265.9 3.5 %all-to-all-start.5 = ((bf16[4,64,1024]{2,1,0:T(8,128)(2,1)}), bf16[4,64,1024]{2,1,0:T(8,128)(2,1)S(1)}, u32[]{:S(2)}, u32[]{:S(2)}) async-start(bf16[4,64,1024]{2,1,0:T(8,128)(2,1)} %fusion.5), calls=%async_computation.5 | async-start | bytes 1048576 | tf_op jit(solution)/shard_map/all_to_all | solution.py:622
  270.3 6.6 %collective-permute-start.48 = (bf16[528,512]{1,0:T(8,128)(2,1)S(1)}, bf16[528,512]{1,0:T(8,128)(2,1)S(1)}, u32[]{:S(2)}, u32[]{:S(2)}) collective-permute-start(bf16[528,512]{1,0:T(8,128)(2,1)S(1)} %add_convert_fusion.11), channel_id=1, source_target_pairs={{0,4},{12,8},{1,5},{13,9},{2,6},{14,10},{3,7},{15,11},{16,20},{28,... | collective-permute-start | bytes 1622024 | tf_op jit(solution)/shard_map/ppermute | solution.py:488
  276.8 2.2 add_convert_fusion
  281.5 7.5 %collective-permute-done.48 = bf16[528,512]{1,0:T(8,128)(2,1)S(1)} collective-permute-done((bf16[528,512]{1,0:T(8,128)(2,1)S(1)}, bf16[528,512]{1,0:T(8,128)(2,1)S(1)}, u32[]{:S(2)}, u32[]{:S(2)}) %collective-permute-start.48) | collective-permute-done | bytes 540704 | tf_op jit(solution)/shard_map/ppermute | solution.py:488
  289.1 1.5 collective-permute-start.49
  292.1 3.0 place.2
  295.1 6.4 %all-to-all-start.6 = ((bf16[4,4,64,256]{3,2,1,0:T(8,128)(2,1)}), bf16[4,4,64,256]{3,2,1,0:T(8,128)(2,1)}, u32[]{:S(2)}, u32[]{:S(2)}) async-start(bf16[4,4,64,256]{3,2,1,0:T(8,128)(2,1)} %get-tuple-element.255), calls=%async_computation.6 | async-start | bytes 1048576 | tf_op jit(solution)/shard_map/all_to_all | solution.py:633
  302.2 2.3 select_convert_fusion
  304.5 2.0 add_convert_fusion.9
  307.8 6.6 %collective-permute-done.42.refs_1_ = bf16[4,64,1024]{2,1,0:T(8,128)(2,1)S(1)} collective-permute-done((bf16[4,64,1024]{2,1,0:T(8,128)(2,1)S(1)}, bf16[4,64,1024]{2,1,0:T(8,128)(2,1)S(1)}, u32[]{:S(2)}, u32[]{:S(2)}) %collective-permute-start.42) | collective-permute-done | bytes 524320 | tf_op jit(solution)/shard_map/ppermute | solution.py:341
  315.7 4.2 %all-to-all-done.6 = bf16[4,4,64,256]{3,2,1,0:T(8,128)(2,1)} async-done(((bf16[4,4,64,256]{3,2,1,0:T(8,128)(2,1)}), bf16[4,4,64,256]{3,2,1,0:T(8,128)(2,1)}, u32[]{:S(2)}, u32[]{:S(2)}) %all-to-all-start.6) | async-done | bytes 524320 | tf_op jit(solution)/shard_map/all_to_all | solution.py:633
  319.9 2.1 bitcast_convert_fusion
  322.0 2.4 place.3
  324.4 6.3 %collective-permute-done.50 = bf16[528,512]{1,0:T(8,128)(2,1)} collective-permute-done((bf16[528,512]{1,0:T(8,128)(2,1)}, bf16[528,512]{1,0:T(8,128)(2,1)}, u32[]{:S(2)}, u32[]{:S(2)}) %collective-permute-start.50) | collective-permute-done | bytes 540704 | tf_op jit(solution)/shard_map/ppermute | solution.py:494
  334.6 1.6 copy.28
  (249 shorter events, 65.9 us)
Async XLA Ops:
  3.7 26.3 %copy-start = (bf16[4,256,1024]{2,1,0:T(8,128)(2,1)S(1)}, bf16[4,256,1024]{2,1,0:T(8,128)(2,1)}, u32[]{:S(2)}) copy-start(bf16[4,256,1024]{2,1,0:T(8,128)(2,1)} %param.13) | copy-start | bytes 6291460
  3.8 21.0 %all-to-all-start = ((bf16[4,64,1024]{2,1,0:T(8,128)(2,1)}), bf16[4,64,1024]{2,1,0:T(8,128)(2,1)S(1)}, u32[]{:S(2)}, u32[]{:S(2)}) async-start(bf16[4,64,1024]{2,1,0:T(8,128)(2,1)} %own.2), calls=%async_computation | async-start | bytes 1048576 | tf_op jit(solution)/shard_map/all_to_all | solution.py:405
  11.0 23.2 %collective-permute-start.2 = (bf16[258,512]{1,0:T(8,128)(2,1)}, bf16[258,512]{1,0:T(8,128)(2,1)}, u32[]{:S(2)}, u32[]{:S(2)}) collective-permute-start(bf16[258,512]{1,0:T(8,128)(2,1)} %pad_maximum_fusion.1), channel_id=1, source_target_pairs={{0,16},{16,0},{1,17},{17,1},{2,18},{18,2},{3,19},{19,3},{4,20},{20... | collective-permute-start | bytes 792584 | tf_op jit(solution)/shard_map/ppermute | solution.py:345
  12.5 23.6 %collective-permute-start = (bf16[3,512,256]{2,1,0:T(8,128)(2,1)}, bf16[3,512,256]{2,1,0:T(8,128)(2,1)}, u32[]{:S(2)}, u32[]{:S(2)}) collective-permute-start(bf16[3,512,256]{2,1,0:T(8,128)(2,1)} %bitcast.91), channel_id=1, source_target_pairs={{0,16},{16,0},{1,17},{17,1},{2,18},{18,2},{3,19},{19,3},{4,20},{20... | collective-permute-start | bytes 2359304 | tf_op jit(solution)/shard_map/ppermute | solution.py:345
  24.7 17.5 %all-to-all-start.1 = ((bf16[4,256,256]{2,1,0:T(8,128)(2,1)}), bf16[4,256,256]{2,1,0:T(8,128)(2,1)S(1)}, u32[]{:S(2)}, u32[]{:S(2)}) async-start(bf16[4,256,256]{2,1,0:T(8,128)(2,1)} %param.12), calls=%async_computation.1 | async-start | bytes 1048576 | tf_op jit(solution)/shard_map/all_to_all | solution.py:410
  28.2 13.1 %collective-permute-start.1 = (bf16[4,64,1024]{2,1,0:T(8,128)(2,1)S(1)}, bf16[4,64,1024]{2,1,0:T(8,128)(2,1)}, u32[]{:S(2)}, u32[]{:S(2)}) collective-permute-start(bf16[4,64,1024]{2,1,0:T(8,128)(2,1)S(1)} %all-to-all-done.p0.x.values), channel_id=1, source_target_pairs={{0,2},{1,3},{2,0},{3,1},{4,6},{5,7},{6,4},{7,5},{8,10},{9,11},{10,... | collective-permute-start | bytes 1572872 | tf_op jit(solution)/shard_map/ppermute | solution.py:341
  35.9 28.6 %copy-start.5 = (bf16[256,512]{1,0:T(8,128)(2,1)}, bf16[256,512]{1,0:T(8,128)(2,1)S(1)}, u32[]{:S(2)}) copy-start(bf16[256,512]{1,0:T(8,128)(2,1)S(1)} %slice.78.wob) | copy-start | bytes 786436
  36.1 6.1 %collective-permute-start.3 = (bf16[4,64,1024]{2,1,0:T(8,128)(2,1)S(1)}, bf16[4,64,1024]{2,1,0:T(8,128)(2,1)}, u32[]{:S(2)}, u32[]{:S(2)}) collective-permute-start(bf16[4,64,1024]{2,1,0:T(8,128)(2,1)S(1)} %all-to-all-done.p0.x.values), channel_id=1, source_target_pairs={{0,1},{1,0},{2,3},{3,2},{4,5},{5,4},{6,7},{7,6},{8,9},{9,8},{10,11... | collective-permute-start | bytes 1572872 | tf_op jit(solution)/shard_map/ppermute | solution.py:338
  41.3 2.3 collective-permute-start.4
  43.6 23.7 %all-to-all-start.2 = ((bf16[4,64,1024]{2,1,0:T(8,128)(2,1)}), bf16[4,64,1024]{2,1,0:T(8,128)(2,1)}, u32[]{:S(2)}, u32[]{:S(2)}) async-start(bf16[4,64,1024]{2,1,0:T(8,128)(2,1)} %copy-done.13), calls=%async_computation.2 | async-start | bytes 1048576 | tf_op jit(solution)/shard_map/all_to_all | solution.py:419
  48.3 18.1 %collective-permute-start.5 = (bf16[704,512]{1,0:T(8,128)(2,1)}, bf16[704,512]{1,0:T(8,128)(2,1)S(1)}, u32[]{:S(2)}, u32[]{:S(2)}) collective-permute-start(bf16[704,512]{1,0:T(8,128)(2,1)} %bitcast.94), channel_id=1, source_target_pairs={{0,16},{16,0},{1,17},{17,1},{2,18},{18,2},{3,19},{19,3},{4,20},{20... | collective-permute-start | bytes 2162696 | tf_op jit(solution)/shard_map/ppermute | solution.py:345
  67.3 6.4 %collective-permute-start.6 = (bf16[2,4,64,1024]{3,2,1,0:T(8,128)(2,1)}, bf16[2,4,64,1024]{3,2,1,0:T(8,128)(2,1)}, u32[]{:S(2)}, u32[]{:S(2)}) collective-permute-start(bf16[2,4,64,1024]{3,2,1,0:T(8,128)(2,1)} %copy-done.19), channel_id=1, source_target_pairs={{0,1},{1,0},{2,3},{3,2},{4,5},{5,4},{6,7},{7,6},{8,9},{9,8},{10,11... | collective-permute-start | bytes 3145736 | tf_op jit(solution)/shard_map/ppermute | solution.py:338
  67.3 21.6 %collective-permute-start.8 = (bf16[704,512]{1,0:T(8,128)(2,1)}, bf16[704,512]{1,0:T(8,128)(2,1)}, u32[]{:S(2)}, u32[]{:S(2)}) collective-permute-start(bf16[704,512]{1,0:T(8,128)(2,1)} %bitcast.96), channel_id=1, source_target_pairs={{0,16},{16,0},{1,17},{17,1},{2,18},{18,2},{3,19},{19,3},{4,20},{20... | collective-permute-start | bytes 2162696 | tf_op jit(solution)/shard_map/ppermute | solution.py:345
  68.9 20.0 %all-to-all-start.3 = ((bf16[4,64,1024]{2,1,0:T(8,128)(2,1)}), bf16[4,64,1024]{2,1,0:T(8,128)(2,1)}, u32[]{:S(2)}, u32[]{:S(2)}) async-start(bf16[4,64,1024]{2,1,0:T(8,128)(2,1)} %copy-done.12), calls=%async_computation.3 | async-start | bytes 1048576 | tf_op jit(solution)/shard_map/all_to_all | solution.py:433
  75.7 13.9 %collective-permute-start.7 = (bf16[4,64,1024]{2,1,0:T(8,128)(2,1)}, bf16[4,64,1024]{2,1,0:T(8,128)(2,1)S(1)}, u32[]{:S(2)}, u32[]{:S(2)}) collective-permute-start(bf16[4,64,1024]{2,1,0:T(8,128)(2,1)} %fusion.9), channel_id=1, source_target_pairs={{0,2},{1,3},{2,0},{3,1},{4,6},{5,7},{6,4},{7,5},{8,10},{9,11},{10,... | collective-permute-start | bytes 1572872 | tf_op jit(solution)/shard_map/ppermute | solution.py:341
  78.1 10.8 %collective-permute-start.9 = (bf16[128,512]{1,0:T(8,128)(2,1)S(1)}, bf16[128,512]{1,0:T(8,128)(2,1)S(1)}, u32[]{:S(2)}, u32[]{:S(2)}) collective-permute-start(bf16[128,512]{1,0:T(8,128)(2,1)S(1)} %slice.63.da), channel_id=1, source_target_pairs={{0,16},{16,0},{1,17},{17,1},{2,18},{18,2},{3,19},{19,3},{4,20},{20... | collective-permute-start | bytes 393224 | tf_op jit(solution)/shard_map/ppermute | solution.py:345
  95.2 13.0 %collective-permute-start.10 = (bf16[4,64,1024]{2,1,0:T(8,128)(2,1)S(1)}, bf16[4,64,1024]{2,1,0:T(8,128)(2,1)S(1)}, u32[]{:S(2)}, u32[]{:S(2)}) collective-permute-start(bf16[4,64,1024]{2,1,0:T(8,128)(2,1)S(1)} %get-tuple-element.162.n0), channel_id=1, source_target_pairs={{0,2},{1,3},{2,0},{3,1},{4,6},{5,7},{6,4},{7,5},{8,10},{9,11},{10,... | collective-permute-start | bytes 1572872 | tf_op jit(solution)/shard_map/ppermute | solution.py:341
  96.8 14.1 %collective-permute-start.15 = (bf16[576,512]{1,0:T(8,128)(2,1)S(1)}, bf16[576,512]{1,0:T(8,128)(2,1)S(1)}, u32[]{:S(2)}, u32[]{:S(2)}) collective-permute-start(bf16[576,512]{1,0:T(8,128)(2,1)S(1)} %slice.65.la), channel_id=1, source_target_pairs={{0,16},{16,0},{1,17},{17,1},{2,18},{18,2},{3,19},{19,3},{4,20},{20... | collective-permute-start | bytes 1769480 | tf_op jit(solution)/shard_map/ppermute | solution.py:345
  97.6 13.3 %collective-permute-start.13 = (bf16[4,64,1024]{2,1,0:T(8,128)(2,1)}, bf16[4,64,1024]{2,1,0:T(8,128)(2,1)S(1)}, u32[]{:S(2)}, u32[]{:S(2)}) collective-permute-start(bf16[4,64,1024]{2,1,0:T(8,128)(2,1)} %all-to-all-done.2.g0.direct), channel_id=1, source_target_pairs={{0,1},{1,0},{2,3},{3,2},{4,5},{5,4},{6,7},{7,6},{8,9},{9,8},{10,11... | collective-permute-start | bytes 1572872 | tf_op jit(solution)/shard_map/ppermute | solution.py:338
  97.6 13.3 %collective-permute-start.11 = (bf16[4,64,1024]{2,1,0:T(8,128)(2,1)S(1)}, bf16[4,64,1024]{2,1,0:T(8,128)(2,1)S(1)}, u32[]{:S(2)}, u32[]{:S(2)}) collective-permute-start(bf16[4,64,1024]{2,1,0:T(8,128)(2,1)S(1)} %get-tuple-element.162.n0), channel_id=1, source_target_pairs={{0,1},{1,0},{2,3},{3,2},{4,5},{5,4},{6,7},{7,6},{8,9},{9,8},{10,11... | collective-permute-start | bytes 1572872 | tf_op jit(solution)/shard_map/ppermute | solution.py:338
  98.1 12.8 %collective-permute-start.14 = (bf16[4,64,1024]{2,1,0:T(8,128)(2,1)}, bf16[4,64,1024]{2,1,0:T(8,128)(2,1)S(1)}, u32[]{:S(2)}, u32[]{:S(2)}) collective-permute-start(bf16[4,64,1024]{2,1,0:T(8,128)(2,1)} %all-to-all-done.3.g1), channel_id=1, source_target_pairs={{0,1},{1,0},{2,3},{3,2},{4,5},{5,4},{6,7},{7,6},{8,9},{9,8},{10,11... | collective-permute-start | bytes 1572872 | tf_op jit(solution)/shard_map/ppermute | solution.py:338
  108.2 2.7 collective-permute-start.12
  121.7 2.7 collective-permute-start.16
  126.5 14.0 %collective-permute-start.17 = (bf16[4,64,1024]{2,1,0:T(8,128)(2,1)S(1)}, bf16[4,64,1024]{2,1,0:T(8,128)(2,1)S(1)}, u32[]{:S(2)}, u32[]{:S(2)}) collective-permute-start(bf16[4,64,1024]{2,1,0:T(8,128)(2,1)S(1)} %fusion.8), channel_id=1, source_target_pairs={{0,2},{1,3},{2,0},{3,1},{4,6},{5,7},{6,4},{7,5},{8,10},{9,11},{10,... | collective-permute-start | bytes 1572872 | tf_op jit(solution)/shard_map/ppermute | solution.py:341
  127.2 17.9 %collective-permute-start.18 = (bf16[704,512]{1,0:T(8,128)(2,1)S(1)}, bf16[704,512]{1,0:T(8,128)(2,1)S(1)}, u32[]{:S(2)}, u32[]{:S(2)}) collective-permute-start(bf16[704,512]{1,0:T(8,128)(2,1)S(1)} %fusion), channel_id=1, source_target_pairs={{0,16},{16,0},{1,17},{17,1},{2,18},{18,2},{3,19},{19,3},{4,20},{20... | collective-permute-start | bytes 2162696 | tf_op jit(solution)/shard_map/ppermute | solution.py:476
  131.7 11.2 %collective-permute-start.19 = (bf16[2,4,64,1024]{3,2,1,0:T(8,128)(2,1)S(1)}, bf16[2,4,64,1024]{3,2,1,0:T(8,128)(2,1)S(1)}, u32[]{:S(2)}, u32[]{:S(2)}) collective-permute-start(bf16[2,4,64,1024]{3,2,1,0:T(8,128)(2,1)S(1)} %get-tuple-element.186), channel_id=1, source_target_pairs={{0,1},{1,0},{2,3},{3,2},{4,5},{5,4},{6,7},{7,6},{8,9},{9,8},{10,11... | collective-permute-start | bytes 3145736 | tf_op jit(solution)/shard_map/ppermute | solution.py:338
  145.1 12.8 %collective-permute-start.20 = (bf16[4,64,1024]{2,1,0:T(8,128)(2,1)S(1)}, bf16[4,64,1024]{2,1,0:T(8,128)(2,1)S(1)}, u32[]{:S(2)}, u32[]{:S(2)}) collective-permute-start(bf16[4,64,1024]{2,1,0:T(8,128)(2,1)S(1)} %get-tuple-element.188.b0), channel_id=1, source_target_pairs={{0,2},{1,3},{2,0},{3,1},{4,6},{5,7},{6,4},{7,5},{8,10},{9,11},{10,... | collective-permute-start | bytes 1572872 | tf_op jit(solution)/shard_map/ppermute | solution.py:341
  146.5 29.1 %copy-start.27 = (bf16[4,256,256]{2,1,0:T(8,128)(2,1)S(1)}, bf16[4,256,256]{2,1,0:T(8,128)(2,1)}, u32[]{:S(2)}) copy-start(bf16[4,256,256]{2,1,0:T(8,128)(2,1)} %get-tuple-element.200.att) | copy-start | bytes 1572868
  146.8 17.9 %collective-permute-start.24 = (bf16[704,512]{1,0:T(8,128)(2,1)S(1)}, bf16[704,512]{1,0:T(8,128)(2,1)S(1)}, u32[]{:S(2)}, u32[]{:S(2)}) collective-permute-start(bf16[704,512]{1,0:T(8,128)(2,1)S(1)} %add_convert_fusion.8), channel_id=1, source_target_pairs={{0,4},{12,8},{1,5},{13,9},{2,6},{14,10},{3,7},{15,11},{16,20},{28,... | collective-permute-start | bytes 2162696 | tf_op jit(solution)/shard_map/ppermute | solution.py:488
  150.5 16.5 %collective-permute-start.23 = (bf16[704,512]{1,0:T(8,128)(2,1)S(1)}, bf16[704,512]{1,0:T(8,128)(2,1)S(1)}, u32[]{:S(2)}, u32[]{:S(2)}) collective-permute-start(bf16[704,512]{1,0:T(8,128)(2,1)S(1)} %fusion.1), channel_id=1, source_target_pairs={{0,16},{16,0},{1,17},{17,1},{2,18},{18,2},{3,19},{19,3},{4,20},{20... | collective-permute-start | bytes 2162696 | tf_op jit(solution)/shard_map/ppermute | solution.py:476
  151.8 6.1 %collective-permute-start.21 = (bf16[4,64,1024]{2,1,0:T(8,128)(2,1)S(1)}, bf16[4,64,1024]{2,1,0:T(8,128)(2,1)S(1)}, u32[]{:S(2)}, u32[]{:S(2)}) collective-permute-start(bf16[4,64,1024]{2,1,0:T(8,128)(2,1)S(1)} %get-tuple-element.188.b0), channel_id=1, source_target_pairs={{0,1},{1,0},{2,3},{3,2},{4,5},{5,4},{6,7},{7,6},{8,9},{9,8},{10,11... | collective-permute-start | bytes 1572872 | tf_op jit(solution)/shard_map/ppermute | solution.py:338
  157.9 9.1 %collective-permute-start.22 = (bf16[4,64,1024]{2,1,0:T(8,128)(2,1)S(1)}, bf16[4,64,1024]{2,1,0:T(8,128)(2,1)S(1)}, u32[]{:S(2)}, u32[]{:S(2)}) collective-permute-start(bf16[4,64,1024]{2,1,0:T(8,128)(2,1)S(1)} %collective-permute-done.20.b1), channel_id=1, source_target_pairs={{0,1},{1,0},{2,3},{3,2},{4,5},{5,4},{6,7},{7,6},{8,9},{9,8},{10,11... | collective-permute-start | bytes 1572872 | tf_op jit(solution)/shard_map/ppermute | solution.py:338
  167.0 31.6 %collective-permute-start.28 = (bf16[4,64,1024]{2,1,0:T(8,128)(2,1)S(1)}, bf16[4,64,1024]{2,1,0:T(8,128)(2,1)S(1)}, u32[]{:S(2)}, u32[]{:S(2)}) collective-permute-start(bf16[4,64,1024]{2,1,0:T(8,128)(2,1)S(1)} %fusion.7), channel_id=1, source_target_pairs={{0,2},{1,3},{2,0},{3,1},{4,6},{5,7},{6,4},{7,5},{8,10},{9,11},{10,... | collective-permute-start | bytes 1572872 | tf_op jit(solution)/shard_map/ppermute | solution.py:341
  167.9 30.7 %collective-permute-start.26 = (bf16[704,512]{1,0:T(8,128)(2,1)S(1)}, bf16[704,512]{1,0:T(8,128)(2,1)S(1)}, u32[]{:S(2)}, u32[]{:S(2)}) collective-permute-start(bf16[704,512]{1,0:T(8,128)(2,1)S(1)} %add_convert_fusion.7), channel_id=1, source_target_pairs={{4,8},{8,4},{5,9},{9,5},{6,10},{10,6},{7,11},{11,7},{20,24},{24,20... | collective-permute-start | bytes 2162696 | tf_op jit(solution)/shard_map/ppermute | solution.py:491
  168.8 29.8 %collective-permute-start.25 = (bf16[704,512]{1,0:T(8,128)(2,1)S(1)}, bf16[704,512]{1,0:T(8,128)(2,1)S(1)}, u32[]{:S(2)}, u32[]{:S(2)}) collective-permute-start(bf16[704,512]{1,0:T(8,128)(2,1)S(1)} %fusion.2), channel_id=1, source_target_pairs={{0,16},{16,0},{1,17},{17,1},{2,18},{18,2},{3,19},{19,3},{4,20},{20... | collective-permute-start | bytes 2162696 | tf_op jit(solution)/shard_map/ppermute | solution.py:476
  170.4 27.2 %copy-start.35 = (bf16[704,512]{1,0:T(8,128)(2,1)}, bf16[704,512]{1,0:T(8,128)(2,1)S(1)}, u32[]{:S(2)}) copy-start(bf16[704,512]{1,0:T(8,128)(2,1)S(1)} %add_convert_fusion.6) | copy-start | bytes 2162692
  170.4 28.2 %collective-permute-start.27 = (bf16[704,512]{1,0:T(8,128)(2,1)S(1)}, bf16[704,512]{1,0:T(8,128)(2,1)S(1)}, u32[]{:S(2)}, u32[]{:S(2)}) collective-permute-start(bf16[704,512]{1,0:T(8,128)(2,1)S(1)} %add_convert_fusion.6), channel_id=1, source_target_pairs={{0,4},{12,8},{1,5},{13,9},{2,6},{14,10},{3,7},{15,11},{16,20},{28,... | collective-permute-start | bytes 2162696 | tf_op jit(solution)/shard_map/ppermute | solution.py:488
  200.4 2.9 collective-permute-start.29
  205.0 16.1 %collective-permute-start.30 = (bf16[4,64,1024]{2,1,0:T(8,128)(2,1)S(1)}, bf16[4,64,1024]{2,1,0:T(8,128)(2,1)S(1)}, u32[]{:S(2)}, u32[]{:S(2)}) collective-permute-start(bf16[4,64,1024]{2,1,0:T(8,128)(2,1)S(1)} %fusion.6), channel_id=1, source_target_pairs={{0,2},{1,3},{2,0},{3,1},{4,6},{5,7},{6,4},{7,5},{8,10},{9,11},{10,... | collective-permute-start | bytes 1572872 | tf_op jit(solution)/shard_map/ppermute | solution.py:341
  206.5 22.6 %collective-permute-start.34 = (bf16[512,512]{1,0:T(8,128)(2,1)}, bf16[512,512]{1,0:T(8,128)(2,1)}, u32[]{:S(2)}, u32[]{:S(2)}) collective-permute-start(bf16[512,512]{1,0:T(8,128)(2,1)} %get-tuple-element.241), channel_id=1, source_target_pairs={{0,16},{16,0},{1,17},{17,1},{2,18},{18,2},{3,19},{19,3},{4,20},{20... | collective-permute-start | bytes 1572872 | tf_op jit(solution)/shard_map/ppermute | solution.py:476
  208.3 22.0 %collective-permute-start.32 = (bf16[704,512]{1,0:T(8,128)(2,1)}, bf16[704,512]{1,0:T(8,128)(2,1)}, u32[]{:S(2)}, u32[]{:S(2)}) collective-permute-start(bf16[704,512]{1,0:T(8,128)(2,1)} %add_convert_fusion.4), channel_id=1, source_target_pairs={{4,8},{8,4},{5,9},{9,5},{6,10},{10,6},{7,11},{11,7},{20,24},{24,20... | collective-permute-start | bytes 2162696 | tf_op jit(solution)/shard_map/ppermute | solution.py:491
  211.0 22.6 %collective-permute-start.31 = (bf16[704,512]{1,0:T(8,128)(2,1)}, bf16[704,512]{1,0:T(8,128)(2,1)}, u32[]{:S(2)}, u32[]{:S(2)}) collective-permute-start(bf16[704,512]{1,0:T(8,128)(2,1)} %add_convert_fusion.5), channel_id=1, source_target_pairs={{4,0},{8,12},{5,1},{9,13},{6,2},{10,14},{7,3},{11,15},{20,16},{24,... | collective-permute-start | bytes 2162696 | tf_op jit(solution)/shard_map/ppermute | solution.py:494
  213.7 22.2 %collective-permute-start.33 = (bf16[704,512]{1,0:T(8,128)(2,1)}, bf16[704,512]{1,0:T(8,128)(2,1)}, u32[]{:S(2)}, u32[]{:S(2)}) collective-permute-start(bf16[704,512]{1,0:T(8,128)(2,1)} %add_convert_fusion.3), channel_id=1, source_target_pairs={{0,4},{12,8},{1,5},{13,9},{2,6},{14,10},{3,7},{15,11},{16,20},{28,... | collective-permute-start | bytes 2162696 | tf_op jit(solution)/shard_map/ppermute | solution.py:488
  224.2 18.5 %all-to-all-start.4 = ((bf16[4,64,1024]{2,1,0:T(8,128)(2,1)}), bf16[4,64,1024]{2,1,0:T(8,128)(2,1)S(1)}, u32[]{:S(2)}, u32[]{:S(2)}) async-start(bf16[4,64,1024]{2,1,0:T(8,128)(2,1)} %get-tuple-element.234), calls=%async_computation.4 | async-start | bytes 1048576 | tf_op jit(solution)/shard_map/all_to_all | solution.py:604
  227.8 25.3 %collective-permute-start.36 = (bf16[528,512]{1,0:T(8,128)(2,1)}, bf16[528,512]{1,0:T(8,128)(2,1)S(1)}, u32[]{:S(2)}, u32[]{:S(2)}) collective-permute-start(bf16[528,512]{1,0:T(8,128)(2,1)} %get-tuple-element.244), channel_id=1, source_target_pairs={{0,16},{16,0},{1,17},{17,1},{2,18},{18,2},{3,19},{19,3},{4,20},{20... | collective-permute-start | bytes 1622024 | tf_op jit(solution)/shard_map/ppermute | solution.py:476
  242.7 20.5 %collective-permute-start.37 = (bf16[704,512]{1,0:T(8,128)(2,1)}, bf16[704,512]{1,0:T(8,128)(2,1)S(1)}, u32[]{:S(2)}, u32[]{:S(2)}) collective-permute-start(bf16[704,512]{1,0:T(8,128)(2,1)} %add_convert_fusion.2), channel_id=1, source_target_pairs={{4,0},{8,12},{5,1},{9,13},{6,2},{10,14},{7,3},{11,15},{20,16},{24,... | collective-permute-start | bytes 2162696 | tf_op jit(solution)/shard_map/ppermute | solution.py:494
  244.0 19.2 %collective-permute-start.38 = (bf16[704,512]{1,0:T(8,128)(2,1)S(1)}, bf16[704,512]{1,0:T(8,128)(2,1)S(1)}, u32[]{:S(2)}, u32[]{:S(2)}) collective-permute-start(bf16[704,512]{1,0:T(8,128)(2,1)S(1)} %add_convert_fusion.1), channel_id=1, source_target_pairs={{4,8},{8,4},{5,9},{9,5},{6,10},{10,6},{7,11},{11,7},{20,24},{24,20... | collective-permute-start | bytes 2162696 | tf_op jit(solution)/shard_map/ppermute | solution.py:491
  245.0 15.9 %collective-permute-start.39 = (bf16[512,512]{1,0:T(8,128)(2,1)S(1)}, bf16[512,512]{1,0:T(8,128)(2,1)S(1)}, u32[]{:S(2)}, u32[]{:S(2)}) collective-permute-start(bf16[512,512]{1,0:T(8,128)(2,1)S(1)} %add_convert_fusion.14), channel_id=1, source_target_pairs={{0,4},{12,8},{1,5},{13,9},{2,6},{14,10},{3,7},{15,11},{16,20},{28,... | collective-permute-start | bytes 1572872 | tf_op jit(solution)/shard_map/ppermute | solution.py:488
  252.4 10.8 %collective-permute-start.35 = (bf16[4,64,1024]{2,1,0:T(8,128)(2,1)S(1)}, bf16[4,64,1024]{2,1,0:T(8,128)(2,1)S(1)}, u32[]{:S(2)}, u32[]{:S(2)}) collective-permute-start(bf16[4,64,1024]{2,1,0:T(8,128)(2,1)S(1)} %all-to-all-done.4.refs_0_), channel_id=1, source_target_pairs={{0,2},{1,3},{2,0},{3,1},{4,6},{5,7},{6,4},{7,5},{8,10},{9,11},{10,... | collective-permute-start | bytes 1572872 | tf_op jit(solution)/shard_map/ppermute | solution.py:341
  255.5 36.6 %collective-permute-start.40 = (bf16[4,64,1024]{2,1,0:T(8,128)(2,1)S(1)}, bf16[4,64,1024]{2,1,0:T(8,128)(2,1)S(1)}, u32[]{:S(2)}, u32[]{:S(2)}) collective-permute-start(bf16[4,64,1024]{2,1,0:T(8,128)(2,1)S(1)} %all-to-all-done.4.refs_0_), channel_id=1, source_target_pairs={{0,1},{1,0},{2,3},{3,2},{4,5},{5,4},{6,7},{7,6},{8,9},{9,8},{10,11... | collective-permute-start | bytes 1572872 | tf_op jit(solution)/shard_map/ppermute | solution.py:338
  265.9 29.2 %all-to-all-start.5 = ((bf16[4,64,1024]{2,1,0:T(8,128)(2,1)}), bf16[4,64,1024]{2,1,0:T(8,128)(2,1)S(1)}, u32[]{:S(2)}, u32[]{:S(2)}) async-start(bf16[4,64,1024]{2,1,0:T(8,128)(2,1)} %fusion.5), calls=%async_computation.5 | async-start | bytes 1048576 | tf_op jit(solution)/shard_map/all_to_all | solution.py:622
  269.3 21.2 %collective-permute-start.46 = (bf16[512,512]{1,0:T(8,128)(2,1)}, bf16[512,512]{1,0:T(8,128)(2,1)S(1)}, u32[]{:S(2)}, u32[]{:S(2)}) collective-permute-start(bf16[512,512]{1,0:T(8,128)(2,1)} %add_convert_fusion.13), channel_id=1, source_target_pairs={{4,8},{8,4},{5,9},{9,5},{6,10},{10,6},{7,11},{11,7},{20,24},{24,20... | collective-permute-start | bytes 1572872 | tf_op jit(solution)/shard_map/ppermute | solution.py:491
  270.2 21.9 %collective-permute-start.41 = (bf16[4,64,1024]{2,1,0:T(8,128)(2,1)S(1)}, bf16[4,64,1024]{2,1,0:T(8,128)(2,1)S(1)}, u32[]{:S(2)}, u32[]{:S(2)}) collective-permute-start(bf16[4,64,1024]{2,1,0:T(8,128)(2,1)S(1)} %collective-permute-done.35.refs_1_), channel_id=1, source_target_pairs={{0,1},{1,0},{2,3},{3,2},{4,5},{5,4},{6,7},{7,6},{8,9},{9,8},{10,11... | collective-permute-start | bytes 1572872 | tf_op jit(solution)/shard_map/ppermute | solution.py:338
  270.3 18.7 %collective-permute-start.48 = (bf16[528,512]{1,0:T(8,128)(2,1)S(1)}, bf16[528,512]{1,0:T(8,128)(2,1)S(1)}, u32[]{:S(2)}, u32[]{:S(2)}) collective-permute-start(bf16[528,512]{1,0:T(8,128)(2,1)S(1)} %add_convert_fusion.11), channel_id=1, source_target_pairs={{0,4},{12,8},{1,5},{13,9},{2,6},{14,10},{3,7},{15,11},{16,20},{28,... | collective-permute-start | bytes 1622024 | tf_op jit(solution)/shard_map/ppermute | solution.py:488
  279.0 23.2 %collective-permute-start.45 = (bf16[704,512]{1,0:T(8,128)(2,1)}, bf16[704,512]{1,0:T(8,128)(2,1)}, u32[]{:S(2)}, u32[]{:S(2)}) collective-permute-start(bf16[704,512]{1,0:T(8,128)(2,1)} %add_convert_fusion), channel_id=1, source_target_pairs={{4,0},{8,12},{5,1},{9,13},{6,2},{10,14},{7,3},{11,15},{20,16},{24,... | collective-permute-start | bytes 2162696 | tf_op jit(solution)/shard_map/ppermute | solution.py:494
  289.1 15.4 %collective-permute-start.49 = (bf16[528,512]{1,0:T(8,128)(2,1)S(1)}, bf16[528,512]{1,0:T(8,128)(2,1)}, u32[]{:S(2)}, u32[]{:S(2)}) collective-permute-start(bf16[528,512]{1,0:T(8,128)(2,1)S(1)} %add_convert_fusion.10), channel_id=1, source_target_pairs={{4,8},{8,4},{5,9},{9,5},{6,10},{10,6},{7,11},{11,7},{20,24},{24,20... | collective-permute-start | bytes 1622024 | tf_op jit(solution)/shard_map/ppermute | solution.py:491
  290.7 23.8 %collective-permute-start.47 = (bf16[512,512]{1,0:T(8,128)(2,1)S(1)}, bf16[512,512]{1,0:T(8,128)(2,1)}, u32[]{:S(2)}, u32[]{:S(2)}) collective-permute-start(bf16[512,512]{1,0:T(8,128)(2,1)S(1)} %add_convert_fusion.12), channel_id=1, source_target_pairs={{4,0},{8,12},{5,1},{9,13},{6,2},{10,14},{7,3},{11,15},{20,16},{24,... | collective-permute-start | bytes 1572872 | tf_op jit(solution)/shard_map/ppermute | solution.py:494
  295.1 24.8 %all-to-all-start.6 = ((bf16[4,4,64,256]{3,2,1,0:T(8,128)(2,1)}), bf16[4,4,64,256]{3,2,1,0:T(8,128)(2,1)}, u32[]{:S(2)}, u32[]{:S(2)}) async-start(bf16[4,4,64,256]{3,2,1,0:T(8,128)(2,1)} %get-tuple-element.255), calls=%async_computation.6 | async-start | bytes 1048576 | tf_op jit(solution)/shard_map/all_to_all | solution.py:633
  301.5 12.9 %collective-permute-start.42 = (bf16[4,64,1024]{2,1,0:T(8,128)(2,1)S(1)}, bf16[4,64,1024]{2,1,0:T(8,128)(2,1)S(1)}, u32[]{:S(2)}, u32[]{:S(2)}) collective-permute-start(bf16[4,64,1024]{2,1,0:T(8,128)(2,1)S(1)} %all-to-all-done.5.refs_0_), channel_id=1, source_target_pairs={{0,2},{1,3},{2,0},{3,1},{4,6},{5,7},{6,4},{7,5},{8,10},{9,11},{10,... | collective-permute-start | bytes 1572872 | tf_op jit(solution)/shard_map/ppermute | solution.py:341
  304.5 17.5 %collective-permute-start.43 = (bf16[4,64,1024]{2,1,0:T(8,128)(2,1)S(1)}, bf16[4,64,1024]{2,1,0:T(8,128)(2,1)S(1)}, u32[]{:S(2)}, u32[]{:S(2)}) collective-permute-start(bf16[4,64,1024]{2,1,0:T(8,128)(2,1)S(1)} %all-to-all-done.5.refs_0_), channel_id=1, source_target_pairs={{0,1},{1,0},{2,3},{3,2},{4,5},{5,4},{6,7},{7,6},{8,9},{9,8},{10,11... | collective-permute-start | bytes 1572872 | tf_op jit(solution)/shard_map/ppermute | solution.py:338
  306.5 24.2 %collective-permute-start.50 = (bf16[528,512]{1,0:T(8,128)(2,1)}, bf16[528,512]{1,0:T(8,128)(2,1)}, u32[]{:S(2)}, u32[]{:S(2)}) collective-permute-start(bf16[528,512]{1,0:T(8,128)(2,1)} %add_convert_fusion.9), channel_id=1, source_target_pairs={{4,0},{8,12},{5,1},{9,13},{6,2},{10,14},{7,3},{11,15},{20,16},{24,... | collective-permute-start | bytes 1622024 | tf_op jit(solution)/shard_map/ppermute | solution.py:494
  314.4 7.6 %collective-permute-start.44 = (bf16[4,64,1024]{2,1,0:T(8,128)(2,1)S(1)}, bf16[4,64,1024]{2,1,0:T(8,128)(2,1)S(1)}, u32[]{:S(2)}, u32[]{:S(2)}) collective-permute-start(bf16[4,64,1024]{2,1,0:T(8,128)(2,1)S(1)} %collective-permute-done.42.refs_1_), channel_id=1, source_target_pairs={{0,1},{1,0},{2,3},{3,2},{4,5},{5,4},{6,7},{7,6},{8,9},{9,8},{10,11... | collective-permute-start | bytes 1572872 | tf_op jit(solution)/shard_map/ppermute | solution.py:338
  332.7 1.2 collective-permute-start.51
  333.9 3.6 %collective-permute-start.52 = (f32[2,512]{1,0:T(2,128)S(1)}, f32[2,512]{1,0:T(2,128)S(1)}, u32[]{:S(2)}, u32[]{:S(2)}) collective-permute-start(f32[2,512]{1,0:T(2,128)S(1)} %slice_add_fusion), channel_id=1, source_target_pairs={{0,2},{1,3},{2,0},{3,1},{4,6},{5,7},{6,4},{7,5},{8,10},{9,11},{10,... | collective-permute-start | bytes 12296 | tf_op jit(solution)/shard_map/ppermute | solution.py:341
  (56 other events, 328.8 us)

commit v5 on v4

--- a/solution.py
+++ b/solution.py
@@ -575,16 +575,16 @@
     send, down_got, gate_more, up_more, down_x = tie(send, down_got, gate_more, up_more, down_x)
     got_core = core(send)
     onward = added(onward, got_core[1]).astype(BF)
-    (
-        onward, qk_second, out_second, down_got, gate_shard, gate_more, up_shard, up_more, down_x,
-    ) = tie(onward, qk_second, out_second, down_got, gate_shard, gate_more, up_shard, up_more, down_x)
+    gate_shard = plus(gate_shard, gate_more)
+    up_shard = plus(up_shard, up_more)
+    down_shard = joined(down_first, down_got)
+    onward, qk_second, out_second, gate_shard, up_shard, down_shard, down_x = tie(
+        onward, qk_second, out_second, gate_shard, up_shard, down_shard, down_x
+    )
 
     got_x = across(onward)
-    gate_shard = plus(gate_shard, gate_more)
     gate_more = back(gate_shard)
-    up_shard = plus(up_shard, up_more)
     up_more = meet(up_shard)
-    down_shard = joined(down_first, down_got)
     down_more = toward(down_shard)
     qk_got = exchange(qk_first, qk_second)
     output_own = (residual + added(down_keep, down_core[0]) + down_x.astype(F32)).astype(BF)
@@ -616,18 +616,18 @@
     down_more = meet(down_shard)
     qk_more = toward(qk_shard)
     out_shard = joined(out_first, out_got)
-    tokens_second, out_shard, output_own, gf, up_more, down_more, qk_more = tie(
-        tokens_second, out_shard, output_own, gf, up_more, down_more, qk_more
+    out_more = toward(out_shard)
+    tokens_second, output_own, gf, up_more, down_more, qk_more = tie(
+        tokens_second, output_own, gf, up_more, down_more, qk_more
     )
     output_home = lax.all_to_all(output_own, "ctx", 0, 0)
     down_shard = plus(down_shard, down_more)
     down_more = back(down_shard)
     qk_shard = plus(qk_shard, qk_more)
     qk_more = meet(qk_shard)
-    out_more = toward(out_shard)
     grad_tokens = placed(tokens_home, tokens_second, tokens_core, core(tokens_second), F32)
     grad_w_up = settled(up_shard, up_more).T
-    output_home, gf, grad_tokens, grad_w_up = tie(output_home, gf, grad_tokens, grad_w_up)
+    output_home, gf, grad_tokens, grad_w_up, out_more = tie(output_home, gf, grad_tokens, grad_w_up, out_more)
     output_second = across(output_home)
     output_core = core(output_home)
     first_home = lax.all_to_all(gf, "ctx", 0, 0)

time: 340 us -> 334 us (0.982)
  waiting for transfers between devices: 109 us -> 102 us
  local copies, waits for them, and re-layouts: 22.4 us -> 17.2 us
  other arithmetic: 35.1 us -> 39.4 us
    ppermute x10, waiting for transfers between devices: 37.4 us -> 29.6 us  [across(): return lax.ppermute(value, 'tp', by_x)]
    ppermute x5, waiting for transfers between devices: 19.6 us -> 13.4 us  [toward(): return lax.ppermute(shard, 'ctx', [(0, 1), (3, 2)])]
    ppermute x5, waiting for transfers between devices: 7.41 us -> 12.9 us  [back(): return lax.ppermute(shard, 'ctx', [(1, 0), (2, 3)])]
    unnamed x121 -> x95, local copies, waits for them, and re-layouts: 17.9 us -> 12.7 us
    all_to_all x1, starting transfers between devices: 6.43 us -> 10.7 us  [on_device(): first_home = lax.all_to_all(gf, 'ctx', 0, 0)]
    ppermute x5, starting transfers between devices: 29.1 us -> 25.7 us  [toward(): return lax.ppermute(shard, 'ctx', [(0, 1), (3, 2)])]
    convert_element_type x10 -> x9, other arithmetic: 11.6 us -> 13.7 us  [plus(): return (shard.astype(F32) + received.astype(F32)).astype(BF)]
  transfers between devices with their start and end apart: 60 -> 60, of which waited for: 27 -> 24; matrix products, arithmetic and copies ran while one was open for 12% -> 14% of each run, Pallas kernels for 15% -> 15%
where the time goes in v5:
time: 334 us; the launch traced here: 332 us
  starting transfers between devices  102 us (31%)
  waiting for transfers between devices  102 us (31%)
  Pallas kernels  64.1 us (19%)
  other arithmetic  39.4 us (12%)
  local copies, waits for them, and re-layouts  17.2 us (5%)
  matrix products  5.65 us (2%)
    pallas_call x11, Pallas kernels, call(): pl.pallas_call(kernel, out_shape=out_shapes, scratch_shapes=list(scratch)...  64.1 us
    ppermute x10, waiting for transfers between devices, across(): return lax.ppermute(value, 'tp', by_x)  29.6 us
    ppermute x5, starting transfers between devices, toward(): return lax.ppermute(shard, 'ctx', [(0, 1), (3, 2)])  25.7 us
    convert_element_type x9, other arithmetic, plus(): return (shard.astype(F32) + received.astype(F32)).astype(BF)  13.7 us
    ppermute x5, waiting for transfers between devices, toward(): return lax.ppermute(shard, 'ctx', [(0, 1), (3, 2)])  13.4 us
    ppermute x6, waiting for transfers between devices, other_half(): return (value, lax.ppermute(value, 'fsdp', swap_y))  12.9 us
    ppermute x5, waiting for transfers between devices, back(): return lax.ppermute(shard, 'ctx', [(1, 0), (2, 3)])  12.9 us
    unnamed x95, local copies, waits for them, and re-layouts  12.7 us
  transfers between devices with their start and end apart: 60, of which 24 were waited for; matrix products, arithmetic and copies ran while one was open for 14% of the time, Pallas kernels for 15%

profile of v5, /device:TPU:0, one launch (start us, length us, event | category | flops | bytes accessed | tf_op | source)
XLA Modules:
  0.0 332.2 jit_solution(17470735894367860994)
XLA Ops:
  0.7 1.6 copy-done.1
  2.3 1.4 own.2
  3.8 6.5 %all-to-all-start = ((bf16[4,64,1024]{2,1,0:T(8,128)(2,1)}), bf16[4,64,1024]{2,1,0:T(8,128)(2,1)S(1)}, u32[]{:S(2)}, u32[]{:S(2)}) async-start(bf16[4,64,1024]{2,1,0:T(8,128)(2,1)} %own.2), calls=%async_computation | async-start | bytes 1048576 | tf_op jit(solution)/shard_map/all_to_all | solution.py:405
  11.0 1.5 collective-permute-start.2
  13.3 11.5 %all-to-all-done.p0.x.values = bf16[4,64,1024]{2,1,0:T(8,128)(2,1)S(1)} async-done(((bf16[4,64,1024]{2,1,0:T(8,128)(2,1)}), bf16[4,64,1024]{2,1,0:T(8,128)(2,1)S(1)}, u32[]{:S(2)}, u32[]{:S(2)}) %all-to-all-start) | async-done | bytes 524320 | tf_op jit(solution)/shard_map/all_to_all | solution.py:405
  24.7 3.5 %all-to-all-start.1 = ((bf16[4,256,256]{2,1,0:T(8,128)(2,1)}), bf16[4,256,256]{2,1,0:T(8,128)(2,1)S(1)}, u32[]{:S(2)}, u32[]{:S(2)}) async-start(bf16[4,256,256]{2,1,0:T(8,128)(2,1)} %param.12), calls=%async_computation.1 | async-start | bytes 1048576 | tf_op jit(solution)/shard_map/all_to_all | solution.py:410
  28.2 1.6 collective-permute-start.1
  32.3 1.9 multiply_sine_fusion
  36.1 5.2 %collective-permute-done.1.p1 = bf16[4,64,1024]{2,1,0:T(8,128)(2,1)} collective-permute-done((bf16[4,64,1024]{2,1,0:T(8,128)(2,1)S(1)}, bf16[4,64,1024]{2,1,0:T(8,128)(2,1)}, u32[]{:S(2)}, u32[]{:S(2)}) %collective-permute-start.1) | collective-permute-done | bytes 524320 | tf_op jit(solution)/shard_map/ppermute | solution.py:341
  43.6 4.7 %all-to-all-start.2 = ((bf16[4,64,1024]{2,1,0:T(8,128)(2,1)}), bf16[4,64,1024]{2,1,0:T(8,128)(2,1)}, u32[]{:S(2)}, u32[]{:S(2)}) async-start(bf16[4,64,1024]{2,1,0:T(8,128)(2,1)} %copy-done.12), calls=%async_computation.2 | async-start | bytes 1048576 | tf_op jit(solution)/shard_map/all_to_all | solution.py:419
  48.3 1.5 collective-permute-start.5
  49.8 14.6 %attend.1 = (bf16[4,256,512]{2,1,0:T(8,128)(2,1)}, bf16[4,256,512]{2,1,0:T(8,128)(2,1)}, bf16[4,256,256]{2,1,0:T(8,128)(2,1)}, bf16[4,256,256]{2,1,0:T(8,128)(2,...) custom-call(s32[4]{0:T(128)S(1)} %get-tuple-element.275.seg.where, ...), custom_call_target="tpu_custom_call" | custom-call | tf_op jit(solution)/shard_map/attend/pallas_call | solution.py:37
  67.3 1.6 collective-permute-start.8
  68.9 4.8 %all-to-all-start.3 = ((bf16[4,64,1024]{2,1,0:T(8,128)(2,1)}), bf16[4,64,1024]{2,1,0:T(8,128)(2,1)}, u32[]{:S(2)}, u32[]{:S(2)}) async-start(bf16[4,64,1024]{2,1,0:T(8,128)(2,1)} %copy-done.11), calls=%async_computation.3 | async-start | bytes 1048576 | tf_op jit(solution)/shard_map/all_to_all | solution.py:433
  73.7 2.0 fusion.9
  75.7 1.5 collective-permute-start.7
  78.9 9.9 %collective-permute-done.9.db = bf16[128,512]{1,0:T(8,128)(2,1)S(1)} collective-permute-done((bf16[128,512]{1,0:T(8,128)(2,1)S(1)}, bf16[128,512]{1,0:T(8,128)(2,1)S(1)}, u32[]{:S(2)}, u32[]{:S(2)}) %collective-permute-start.9) | collective-permute-done | bytes 131104 | tf_op jit(solution)/shard_map/ppermute | solution.py:345
  92.7 2.5 residual_norm.1
  95.2 1.6 collective-permute-start.10
  98.1 10.0 %collective-permute-done.10.n1 = bf16[4,64,1024]{2,1,0:T(8,128)(2,1)S(1)} collective-permute-done((bf16[4,64,1024]{2,1,0:T(8,128)(2,1)S(1)}, bf16[4,64,1024]{2,1,0:T(8,128)(2,1)S(1)}, u32[]{:S(2)}, u32[]{:S(2)}) %collective-permute-start.10) | collective-permute-done | bytes 524320 | tf_op jit(solution)/shard_map/ppermute | solution.py:341
  108.2 2.7 collective-permute-done.15.lb
  111.0 10.7 %mlp.1 = (bf16[4,256,512]{2,1,0:T(8,128)(2,1)S(1)}, bf16[4,256,512]{2,1,0:T(8,128)(2,1)S(1)}, bf16[4,256,512]{2,1,0:T(8,128)(2,1)S(1)}, bf16[4,256,512]{2,1,0:T(...) custom-call(bf16[4,64,1024]{2,1,0:T(8,128)(2,1)S(1)} %get-tuple-elem, ...), custom_call_target="tpu_custom_call" | custom-call | flops 10000000000 | bytes 34000000 | tf_op jit(solution)/shard_map/mlp/pallas_call | solution.py:37
  128.4 2.3 down.1
  133.6 6.9 %collective-permute-done.17.got_x = bf16[4,64,1024]{2,1,0:T(8,128)(2,1)S(1)} collective-permute-done((bf16[4,64,1024]{2,1,0:T(8,128)(2,1)S(1)}, bf16[4,64,1024]{2,1,0:T(8,128)(2,1)S(1)}, u32[]{:S(2)}, u32[]{:S(2)}) %collective-permute-start.17) | collective-permute-done | bytes 524320 | tf_op jit(solution)/shard_map/ppermute | solution.py:341
  140.5 2.4 norm_back_mlp.1
  143.1 1.9 collective-permute-done.18
  146.8 3.7 %collective-permute-start.24 = (bf16[704,512]{1,0:T(8,128)(2,1)S(1)}, bf16[704,512]{1,0:T(8,128)(2,1)S(1)}, u32[]{:S(2)}, u32[]{:S(2)}) collective-permute-start(bf16[704,512]{1,0:T(8,128)(2,1)S(1)} %add_convert_fusion.8), channel_id=1, source_target_pairs={{0,4},{12,8},{1,5},{13,9},{2,6},{14,10},{3,7},{15,11},{16,20},{28,... | collective-permute-start | bytes 2162696 | tf_op jit(solution)/shard_map/ppermute | solution.py:488
  151.8 6.1 %collective-permute-done.20.b1 = bf16[4,64,1024]{2,1,0:T(8,128)(2,1)S(1)} collective-permute-done((bf16[4,64,1024]{2,1,0:T(8,128)(2,1)S(1)}, bf16[4,64,1024]{2,1,0:T(8,128)(2,1)S(1)}, u32[]{:S(2)}, u32[]{:S(2)}) %collective-permute-start.20) | collective-permute-done | bytes 524320 | tf_op jit(solution)/shard_map/ppermute | solution.py:341
  157.9 6.8 %collective-permute-done.24 = bf16[704,512]{1,0:T(8,128)(2,1)S(1)} collective-permute-done((bf16[704,512]{1,0:T(8,128)(2,1)S(1)}, bf16[704,512]{1,0:T(8,128)(2,1)S(1)}, u32[]{:S(2)}, u32[]{:S(2)}) %collective-permute-start.24) | collective-permute-done | bytes 720928 | tf_op jit(solution)/shard_map/ppermute | solution.py:488
  164.7 2.3 collective-permute-done.23
  170.4 5.1 %collective-permute-start.27 = (bf16[704,512]{1,0:T(8,128)(2,1)S(1)}, bf16[704,512]{1,0:T(8,128)(2,1)S(1)}, u32[]{:S(2)}, u32[]{:S(2)}) collective-permute-start(bf16[704,512]{1,0:T(8,128)(2,1)S(1)} %add_convert_fusion.6), channel_id=1, source_target_pairs={{0,4},{12,8},{1,5},{13,9},{2,6},{14,10},{3,7},{15,11},{16,20},{28,... | collective-permute-start | bytes 2162696 | tf_op jit(solution)/shard_map/ppermute | solution.py:488
  175.6 21.9 %attend_back.1 = (bf16[4,4,64,256]{3,2,1,0:T(8,128)(2,1)}, f32[4,64,1024]{2,1,0:T(8,128)}, f32[4,64,1024]{2,1,0:T(8,128)S(1)}, bf16[2,4,64,1024]{3,2,1,0:T(8,128...) custom-call(s32[4]{0:T(128)S(1)} %get-tuple-element.275.seg.where, ...), custom_call_target="tpu_custom_call" | custom-call | flops 30000001024 | bytes 102000000 | tf_op jit(solution)/shard_map/attend_back/pallas_call | solution.py:37
  198.7 1.6 add_convert_fusion.3
  201.4 1.4 collective-permute-start.30
  204.8 1.5 collective-permute-start.32
  206.3 7.2 %collective-permute-start.33 = (bf16[704,512]{1,0:T(8,128)(2,1)}, bf16[704,512]{1,0:T(8,128)(2,1)}, u32[]{:S(2)}, u32[]{:S(2)}) collective-permute-start(bf16[704,512]{1,0:T(8,128)(2,1)} %get-tuple-element.235), channel_id=1, source_target_pairs={{0,4},{12,8},{1,5},{13,9},{2,6},{14,10},{3,7},{15,11},{16,20},{28,... | collective-permute-start | bytes 2162696 | tf_op jit(solution)/shard_map/ppermute | solution.py:488
  213.6 2.5 fusion.5
  216.1 2.2 norm_back_attn.1
  218.2 3.8 %all-to-all-start.4 = ((bf16[4,64,1024]{2,1,0:T(8,128)(2,1)}), bf16[4,64,1024]{2,1,0:T(8,128)(2,1)S(1)}, u32[]{:S(2)}, u32[]{:S(2)}) async-start(bf16[4,64,1024]{2,1,0:T(8,128)(2,1)} %get-tuple-element.230), calls=%async_computation.4 | async-start | bytes 1048576 | tf_op jit(solution)/shard_map/all_to_all | solution.py:604
  224.5 2.4 add_convert_fusion.2
  226.9 2.4 convert_bitcast_fusion.1
  230.8 6.4 %all-to-all-done.4.refs_0_ = bf16[4,64,1024]{2,1,0:T(8,128)(2,1)S(1)} async-done(((bf16[4,64,1024]{2,1,0:T(8,128)(2,1)}), bf16[4,64,1024]{2,1,0:T(8,128)(2,1)S(1)}, u32[]{:S(2)}, u32[]{:S(2)}) %all-to-all-start.4) | async-done | bytes 524320 | tf_op jit(solution)/shard_map/all_to_all | solution.py:604
  238.6 1.5 collective-permute-start.37
  240.1 7.5 %collective-permute-start.38 = (bf16[512,512]{1,0:T(8,128)(2,1)S(1)}, bf16[512,512]{1,0:T(8,128)(2,1)}, u32[]{:S(2)}, u32[]{:S(2)}) collective-permute-start(bf16[512,512]{1,0:T(8,128)(2,1)S(1)} %add_convert_fusion.14), channel_id=1, source_target_pairs={{0,4},{12,8},{1,5},{13,9},{2,6},{14,10},{3,7},{15,11},{16,20},{28,... | collective-permute-start | bytes 1572872 | tf_op jit(solution)/shard_map/ppermute | solution.py:488
  249.1 1.5 add_convert_fusion.11
  250.6 2.1 collective-permute-start.42
  252.7 6.4 %collective-permute-done.38 = bf16[512,512]{1,0:T(8,128)(2,1)} collective-permute-done((bf16[512,512]{1,0:T(8,128)(2,1)S(1)}, bf16[512,512]{1,0:T(8,128)(2,1)}, u32[]{:S(2)}, u32[]{:S(2)}) %collective-permute-start.38) | collective-permute-done | bytes 524320 | tf_op jit(solution)/shard_map/ppermute | solution.py:488
  259.2 4.4 %all-to-all-start.5 = ((bf16[4,64,1024]{2,1,0:T(8,128)(2,1)}), bf16[4,64,1024]{2,1,0:T(8,128)(2,1)S(1)}, u32[]{:S(2)}, u32[]{:S(2)}) async-start(bf16[4,64,1024]{2,1,0:T(8,128)(2,1)} %fusion.5), calls=%async_computation.5 | async-start | bytes 1048576 | tf_op jit(solution)/shard_map/all_to_all | solution.py:623
  263.5 2.1 add_convert_fusion.13
  265.7 1.6 collective-permute-start.47
  267.5 2.2 add_convert_fusion
  270.9 2.3 convert_bitcast_fusion
  273.2 3.0 place.2
  276.2 3.2 all-to-all-done.5.refs_0_
  281.3 1.5 collective-permute-start.49
  285.4 10.7 %all-to-all-start.6 = ((bf16[4,4,64,256]{3,2,1,0:T(8,128)(2,1)}), bf16[4,4,64,256]{3,2,1,0:T(8,128)(2,1)}, u32[]{:S(2)}, u32[]{:S(2)}) async-start(bf16[4,4,64,256]{3,2,1,0:T(8,128)(2,1)} %get-tuple-element.251), calls=%async_computation.6 | async-start | bytes 1048576 | tf_op jit(solution)/shard_map/all_to_all | solution.py:633
  296.1 2.3 select_convert_fusion
  298.9 2.0 add_convert_fusion.9
  302.2 7.8 %collective-permute-done.48 = bf16[512,512]{1,0:T(8,128)(2,1)} collective-permute-done((bf16[512,512]{1,0:T(8,128)(2,1)S(1)}, bf16[512,512]{1,0:T(8,128)(2,1)}, u32[]{:S(2)}, u32[]{:S(2)}) %collective-permute-start.48) | collective-permute-done | bytes 524320 | tf_op jit(solution)/shard_map/ppermute | solution.py:494
  311.1 4.1 %all-to-all-done.6 = bf16[4,4,64,256]{3,2,1,0:T(8,128)(2,1)} async-done(((bf16[4,4,64,256]{3,2,1,0:T(8,128)(2,1)}), bf16[4,4,64,256]{3,2,1,0:T(8,128)(2,1)}, u32[]{:S(2)}, u32[]{:S(2)}) %all-to-all-start.6) | async-done | bytes 524320 | tf_op jit(solution)/shard_map/all_to_all | solution.py:633
  315.3 2.1 bitcast_convert_fusion
  317.4 2.4 place.3
  319.8 5.0 %collective-permute-done.50 = bf16[528,512]{1,0:T(8,128)(2,1)} collective-permute-done((bf16[528,512]{1,0:T(8,128)(2,1)}, bf16[528,512]{1,0:T(8,128)(2,1)}, u32[]{:S(2)}, u32[]{:S(2)}) %collective-permute-start.50) | collective-permute-done | bytes 540704 | tf_op jit(solution)/shard_map/ppermute | solution.py:494
  328.7 1.6 copy.28
  (222 shorter events, 59.8 us)
Async XLA Ops:
  3.7 26.1 %copy-start.46 = (f32[4]{0:T(128)S(1)}, f32[4]{0:T(128)}, u32[]{:S(2)}) copy-start(f32[4]{0:T(128)} %param.21) | copy-start | bytes 52
  3.7 26.3 %copy-start = (bf16[4,256,1024]{2,1,0:T(8,128)(2,1)S(1)}, bf16[4,256,1024]{2,1,0:T(8,128)(2,1)}, u32[]{:S(2)}) copy-start(bf16[4,256,1024]{2,1,0:T(8,128)(2,1)} %param.13) | copy-start | bytes 6291460
  3.8 21.0 %all-to-all-start = ((bf16[4,64,1024]{2,1,0:T(8,128)(2,1)}), bf16[4,64,1024]{2,1,0:T(8,128)(2,1)S(1)}, u32[]{:S(2)}, u32[]{:S(2)}) async-start(bf16[4,64,1024]{2,1,0:T(8,128)(2,1)} %own.2), calls=%async_computation | async-start | bytes 1048576 | tf_op jit(solution)/shard_map/all_to_all | solution.py:405
  11.0 23.2 %collective-permute-start.2 = (bf16[258,512]{1,0:T(8,128)(2,1)}, bf16[258,512]{1,0:T(8,128)(2,1)}, u32[]{:S(2)}, u32[]{:S(2)}) collective-permute-start(bf16[258,512]{1,0:T(8,128)(2,1)} %pad_maximum_fusion.1), channel_id=1, source_target_pairs={{0,16},{16,0},{1,17},{17,1},{2,18},{18,2},{3,19},{19,3},{4,20},{20... | collective-permute-start | bytes 792584 | tf_op jit(solution)/shard_map/ppermute | solution.py:345
  12.5 23.6 %collective-permute-start = (bf16[3,512,256]{2,1,0:T(8,128)(2,1)}, bf16[3,512,256]{2,1,0:T(8,128)(2,1)}, u32[]{:S(2)}, u32[]{:S(2)}) collective-permute-start(bf16[3,512,256]{2,1,0:T(8,128)(2,1)} %bitcast.91), channel_id=1, source_target_pairs={{0,16},{16,0},{1,17},{17,1},{2,18},{18,2},{3,19},{19,3},{4,20},{20... | collective-permute-start | bytes 2359304 | tf_op jit(solution)/shard_map/ppermute | solution.py:345
  24.7 17.5 %all-to-all-start.1 = ((bf16[4,256,256]{2,1,0:T(8,128)(2,1)}), bf16[4,256,256]{2,1,0:T(8,128)(2,1)S(1)}, u32[]{:S(2)}, u32[]{:S(2)}) async-start(bf16[4,256,256]{2,1,0:T(8,128)(2,1)} %param.12), calls=%async_computation.1 | async-start | bytes 1048576 | tf_op jit(solution)/shard_map/all_to_all | solution.py:410
  28.2 13.1 %collective-permute-start.1 = (bf16[4,64,1024]{2,1,0:T(8,128)(2,1)S(1)}, bf16[4,64,1024]{2,1,0:T(8,128)(2,1)}, u32[]{:S(2)}, u32[]{:S(2)}) collective-permute-start(bf16[4,64,1024]{2,1,0:T(8,128)(2,1)S(1)} %all-to-all-done.p0.x.values), channel_id=1, source_target_pairs={{0,2},{1,3},{2,0},{3,1},{4,6},{5,7},{6,4},{7,5},{8,10},{9,11},{10,... | collective-permute-start | bytes 1572872 | tf_op jit(solution)/shard_map/ppermute | solution.py:341
  35.9 28.6 %copy-start.5 = (bf16[256,512]{1,0:T(8,128)(2,1)}, bf16[256,512]{1,0:T(8,128)(2,1)S(1)}, u32[]{:S(2)}) copy-start(bf16[256,512]{1,0:T(8,128)(2,1)S(1)} %slice.78.wob) | copy-start | bytes 786436
  36.1 6.1 %collective-permute-start.3 = (bf16[4,64,1024]{2,1,0:T(8,128)(2,1)S(1)}, bf16[4,64,1024]{2,1,0:T(8,128)(2,1)}, u32[]{:S(2)}, u32[]{:S(2)}) collective-permute-start(bf16[4,64,1024]{2,1,0:T(8,128)(2,1)S(1)} %all-to-all-done.p0.x.values), channel_id=1, source_target_pairs={{0,1},{1,0},{2,3},{3,2},{4,5},{5,4},{6,7},{7,6},{8,9},{9,8},{10,11... | collective-permute-start | bytes 1572872 | tf_op jit(solution)/shard_map/ppermute | solution.py:338
  41.3 2.3 collective-permute-start.4
  43.6 23.7 %all-to-all-start.2 = ((bf16[4,64,1024]{2,1,0:T(8,128)(2,1)}), bf16[4,64,1024]{2,1,0:T(8,128)(2,1)}, u32[]{:S(2)}, u32[]{:S(2)}) async-start(bf16[4,64,1024]{2,1,0:T(8,128)(2,1)} %copy-done.12), calls=%async_computation.2 | async-start | bytes 1048576 | tf_op jit(solution)/shard_map/all_to_all | solution.py:419
  48.3 18.1 %collective-permute-start.5 = (bf16[704,512]{1,0:T(8,128)(2,1)}, bf16[704,512]{1,0:T(8,128)(2,1)S(1)}, u32[]{:S(2)}, u32[]{:S(2)}) collective-permute-start(bf16[704,512]{1,0:T(8,128)(2,1)} %bitcast.94), channel_id=1, source_target_pairs={{0,16},{16,0},{1,17},{17,1},{2,18},{18,2},{3,19},{19,3},{4,20},{20... | collective-permute-start | bytes 2162696 | tf_op jit(solution)/shard_map/ppermute | solution.py:345
  67.3 6.4 %collective-permute-start.6 = (bf16[2,4,64,1024]{3,2,1,0:T(8,128)(2,1)}, bf16[2,4,64,1024]{3,2,1,0:T(8,128)(2,1)}, u32[]{:S(2)}, u32[]{:S(2)}) collective-permute-start(bf16[2,4,64,1024]{3,2,1,0:T(8,128)(2,1)} %copy-done.18), channel_id=1, source_target_pairs={{0,1},{1,0},{2,3},{3,2},{4,5},{5,4},{6,7},{7,6},{8,9},{9,8},{10,11... | collective-permute-start | bytes 3145736 | tf_op jit(solution)/shard_map/ppermute | solution.py:338
  67.3 21.6 %collective-permute-start.8 = (bf16[704,512]{1,0:T(8,128)(2,1)}, bf16[704,512]{1,0:T(8,128)(2,1)}, u32[]{:S(2)}, u32[]{:S(2)}) collective-permute-start(bf16[704,512]{1,0:T(8,128)(2,1)} %bitcast.96), channel_id=1, source_target_pairs={{0,16},{16,0},{1,17},{17,1},{2,18},{18,2},{3,19},{19,3},{4,20},{20... | collective-permute-start | bytes 2162696 | tf_op jit(solution)/shard_map/ppermute | solution.py:345
  68.9 20.0 %all-to-all-start.3 = ((bf16[4,64,1024]{2,1,0:T(8,128)(2,1)}), bf16[4,64,1024]{2,1,0:T(8,128)(2,1)}, u32[]{:S(2)}, u32[]{:S(2)}) async-start(bf16[4,64,1024]{2,1,0:T(8,128)(2,1)} %copy-done.11), calls=%async_computation.3 | async-start | bytes 1048576 | tf_op jit(solution)/shard_map/all_to_all | solution.py:433
  75.7 13.9 %collective-permute-start.7 = (bf16[4,64,1024]{2,1,0:T(8,128)(2,1)}, bf16[4,64,1024]{2,1,0:T(8,128)(2,1)S(1)}, u32[]{:S(2)}, u32[]{:S(2)}) collective-permute-start(bf16[4,64,1024]{2,1,0:T(8,128)(2,1)} %fusion.9), channel_id=1, source_target_pairs={{0,2},{1,3},{2,0},{3,1},{4,6},{5,7},{6,4},{7,5},{8,10},{9,11},{10,... | collective-permute-start | bytes 1572872 | tf_op jit(solution)/shard_map/ppermute | solution.py:341
  78.1 10.8 %collective-permute-start.9 = (bf16[128,512]{1,0:T(8,128)(2,1)S(1)}, bf16[128,512]{1,0:T(8,128)(2,1)S(1)}, u32[]{:S(2)}, u32[]{:S(2)}) collective-permute-start(bf16[128,512]{1,0:T(8,128)(2,1)S(1)} %slice.63.da), channel_id=1, source_target_pairs={{0,16},{16,0},{1,17},{17,1},{2,18},{18,2},{3,19},{19,3},{4,20},{20... | collective-permute-start | bytes 393224 | tf_op jit(solution)/shard_map/ppermute | solution.py:345
  95.2 13.0 %collective-permute-start.10 = (bf16[4,64,1024]{2,1,0:T(8,128)(2,1)S(1)}, bf16[4,64,1024]{2,1,0:T(8,128)(2,1)S(1)}, u32[]{:S(2)}, u32[]{:S(2)}) collective-permute-start(bf16[4,64,1024]{2,1,0:T(8,128)(2,1)S(1)} %get-tuple-element.160.n0), channel_id=1, source_target_pairs={{0,2},{1,3},{2,0},{3,1},{4,6},{5,7},{6,4},{7,5},{8,10},{9,11},{10,... | collective-permute-start | bytes 1572872 | tf_op jit(solution)/shard_map/ppermute | solution.py:341
  96.8 14.1 %collective-permute-start.15 = (bf16[576,512]{1,0:T(8,128)(2,1)S(1)}, bf16[576,512]{1,0:T(8,128)(2,1)S(1)}, u32[]{:S(2)}, u32[]{:S(2)}) collective-permute-start(bf16[576,512]{1,0:T(8,128)(2,1)S(1)} %slice.65.la), channel_id=1, source_target_pairs={{0,16},{16,0},{1,17},{17,1},{2,18},{18,2},{3,19},{19,3},{4,20},{20... | collective-permute-start | bytes 1769480 | tf_op jit(solution)/shard_map/ppermute | solution.py:345
  97.6 13.3 %collective-permute-start.13 = (bf16[4,64,1024]{2,1,0:T(8,128)(2,1)}, bf16[4,64,1024]{2,1,0:T(8,128)(2,1)S(1)}, u32[]{:S(2)}, u32[]{:S(2)}) collective-permute-start(bf16[4,64,1024]{2,1,0:T(8,128)(2,1)} %all-to-all-done.2.g0.direct), channel_id=1, source_target_pairs={{0,1},{1,0},{2,3},{3,2},{4,5},{5,4},{6,7},{7,6},{8,9},{9,8},{10,11... | collective-permute-start | bytes 1572872 | tf_op jit(solution)/shard_map/ppermute | solution.py:338
  97.6 13.3 %collective-permute-start.11 = (bf16[4,64,1024]{2,1,0:T(8,128)(2,1)S(1)}, bf16[4,64,1024]{2,1,0:T(8,128)(2,1)S(1)}, u32[]{:S(2)}, u32[]{:S(2)}) collective-permute-start(bf16[4,64,1024]{2,1,0:T(8,128)(2,1)S(1)} %get-tuple-element.160.n0), channel_id=1, source_target_pairs={{0,1},{1,0},{2,3},{3,2},{4,5},{5,4},{6,7},{7,6},{8,9},{9,8},{10,11... | collective-permute-start | bytes 1572872 | tf_op jit(solution)/shard_map/ppermute | solution.py:338
  98.1 12.8 %collective-permute-start.14 = (bf16[4,64,1024]{2,1,0:T(8,128)(2,1)}, bf16[4,64,1024]{2,1,0:T(8,128)(2,1)S(1)}, u32[]{:S(2)}, u32[]{:S(2)}) collective-permute-start(bf16[4,64,1024]{2,1,0:T(8,128)(2,1)} %all-to-all-done.3.g1), channel_id=1, source_target_pairs={{0,1},{1,0},{2,3},{3,2},{4,5},{5,4},{6,7},{7,6},{8,9},{9,8},{10,11... | collective-permute-start | bytes 1572872 | tf_op jit(solution)/shard_map/ppermute | solution.py:338
  108.2 2.7 collective-permute-start.12
  121.7 2.7 collective-permute-start.16
  126.5 14.0 %collective-permute-start.17 = (bf16[4,64,1024]{2,1,0:T(8,128)(2,1)S(1)}, bf16[4,64,1024]{2,1,0:T(8,128)(2,1)S(1)}, u32[]{:S(2)}, u32[]{:S(2)}) collective-permute-start(bf16[4,64,1024]{2,1,0:T(8,128)(2,1)S(1)} %fusion.8), channel_id=1, source_target_pairs={{0,2},{1,3},{2,0},{3,1},{4,6},{5,7},{6,4},{7,5},{8,10},{9,11},{10,... | collective-permute-start | bytes 1572872 | tf_op jit(solution)/shard_map/ppermute | solution.py:341
  127.2 17.9 %collective-permute-start.18 = (bf16[704,512]{1,0:T(8,128)(2,1)S(1)}, bf16[704,512]{1,0:T(8,128)(2,1)S(1)}, u32[]{:S(2)}, u32[]{:S(2)}) collective-permute-start(bf16[704,512]{1,0:T(8,128)(2,1)S(1)} %fusion), channel_id=1, source_target_pairs={{0,16},{16,0},{1,17},{17,1},{2,18},{18,2},{3,19},{19,3},{4,20},{20... | collective-permute-start | bytes 2162696 | tf_op jit(solution)/shard_map/ppermute | solution.py:476
  131.7 11.2 %collective-permute-start.19 = (bf16[2,4,64,1024]{3,2,1,0:T(8,128)(2,1)S(1)}, bf16[2,4,64,1024]{3,2,1,0:T(8,128)(2,1)S(1)}, u32[]{:S(2)}, u32[]{:S(2)}) collective-permute-start(bf16[2,4,64,1024]{3,2,1,0:T(8,128)(2,1)S(1)} %get-tuple-element.184), channel_id=1, source_target_pairs={{0,1},{1,0},{2,3},{3,2},{4,5},{5,4},{6,7},{7,6},{8,9},{9,8},{10,11... | collective-permute-start | bytes 3145736 | tf_op jit(solution)/shard_map/ppermute | solution.py:338
  145.1 12.8 %collective-permute-start.20 = (bf16[4,64,1024]{2,1,0:T(8,128)(2,1)S(1)}, bf16[4,64,1024]{2,1,0:T(8,128)(2,1)S(1)}, u32[]{:S(2)}, u32[]{:S(2)}) collective-permute-start(bf16[4,64,1024]{2,1,0:T(8,128)(2,1)S(1)} %get-tuple-element.186.b0), channel_id=1, source_target_pairs={{0,2},{1,3},{2,0},{3,1},{4,6},{5,7},{6,4},{7,5},{8,10},{9,11},{10,... | collective-permute-start | bytes 1572872 | tf_op jit(solution)/shard_map/ppermute | solution.py:341
  146.5 29.1 %copy-start.26 = (bf16[4,256,256]{2,1,0:T(8,128)(2,1)S(1)}, bf16[4,256,256]{2,1,0:T(8,128)(2,1)}, u32[]{:S(2)}) copy-start(bf16[4,256,256]{2,1,0:T(8,128)(2,1)} %get-tuple-element.198.att) | copy-start | bytes 1572868
  146.8 17.9 %collective-permute-start.24 = (bf16[704,512]{1,0:T(8,128)(2,1)S(1)}, bf16[704,512]{1,0:T(8,128)(2,1)S(1)}, u32[]{:S(2)}, u32[]{:S(2)}) collective-permute-start(bf16[704,512]{1,0:T(8,128)(2,1)S(1)} %add_convert_fusion.8), channel_id=1, source_target_pairs={{0,4},{12,8},{1,5},{13,9},{2,6},{14,10},{3,7},{15,11},{16,20},{28,... | collective-permute-start | bytes 2162696 | tf_op jit(solution)/shard_map/ppermute | solution.py:488
  150.5 16.5 %collective-permute-start.23 = (bf16[704,512]{1,0:T(8,128)(2,1)S(1)}, bf16[704,512]{1,0:T(8,128)(2,1)S(1)}, u32[]{:S(2)}, u32[]{:S(2)}) collective-permute-start(bf16[704,512]{1,0:T(8,128)(2,1)S(1)} %fusion.1), channel_id=1, source_target_pairs={{0,16},{16,0},{1,17},{17,1},{2,18},{18,2},{3,19},{19,3},{4,20},{20... | collective-permute-start | bytes 2162696 | tf_op jit(solution)/shard_map/ppermute | solution.py:476
  151.8 6.1 %collective-permute-start.21 = (bf16[4,64,1024]{2,1,0:T(8,128)(2,1)S(1)}, bf16[4,64,1024]{2,1,0:T(8,128)(2,1)S(1)}, u32[]{:S(2)}, u32[]{:S(2)}) collective-permute-start(bf16[4,64,1024]{2,1,0:T(8,128)(2,1)S(1)} %get-tuple-element.186.b0), channel_id=1, source_target_pairs={{0,1},{1,0},{2,3},{3,2},{4,5},{5,4},{6,7},{7,6},{8,9},{9,8},{10,11... | collective-permute-start | bytes 1572872 | tf_op jit(solution)/shard_map/ppermute | solution.py:338
  157.9 9.1 %collective-permute-start.22 = (bf16[4,64,1024]{2,1,0:T(8,128)(2,1)S(1)}, bf16[4,64,1024]{2,1,0:T(8,128)(2,1)S(1)}, u32[]{:S(2)}, u32[]{:S(2)}) collective-permute-start(bf16[4,64,1024]{2,1,0:T(8,128)(2,1)S(1)} %collective-permute-done.20.b1), channel_id=1, source_target_pairs={{0,1},{1,0},{2,3},{3,2},{4,5},{5,4},{6,7},{7,6},{8,9},{9,8},{10,11... | collective-permute-start | bytes 1572872 | tf_op jit(solution)/shard_map/ppermute | solution.py:338
  167.0 30.5 %collective-permute-start.28 = (bf16[4,64,1024]{2,1,0:T(8,128)(2,1)S(1)}, bf16[4,64,1024]{2,1,0:T(8,128)(2,1)S(1)}, u32[]{:S(2)}, u32[]{:S(2)}) collective-permute-start(bf16[4,64,1024]{2,1,0:T(8,128)(2,1)S(1)} %fusion.7), channel_id=1, source_target_pairs={{0,2},{1,3},{2,0},{3,1},{4,6},{5,7},{6,4},{7,5},{8,10},{9,11},{10,... | collective-permute-start | bytes 1572872 | tf_op jit(solution)/shard_map/ppermute | solution.py:341
  167.9 29.6 %collective-permute-start.26 = (bf16[704,512]{1,0:T(8,128)(2,1)S(1)}, bf16[704,512]{1,0:T(8,128)(2,1)S(1)}, u32[]{:S(2)}, u32[]{:S(2)}) collective-permute-start(bf16[704,512]{1,0:T(8,128)(2,1)S(1)} %add_convert_fusion.7), channel_id=1, source_target_pairs={{4,8},{8,4},{5,9},{9,5},{6,10},{10,6},{7,11},{11,7},{20,24},{24,20... | collective-permute-start | bytes 2162696 | tf_op jit(solution)/shard_map/ppermute | solution.py:491
  168.8 28.7 %collective-permute-start.25 = (bf16[704,512]{1,0:T(8,128)(2,1)S(1)}, bf16[704,512]{1,0:T(8,128)(2,1)S(1)}, u32[]{:S(2)}, u32[]{:S(2)}) collective-permute-start(bf16[704,512]{1,0:T(8,128)(2,1)S(1)} %fusion.2), channel_id=1, source_target_pairs={{0,16},{16,0},{1,17},{17,1},{2,18},{18,2},{3,19},{19,3},{4,20},{20... | collective-permute-start | bytes 2162696 | tf_op jit(solution)/shard_map/ppermute | solution.py:476
  170.4 27.1 %collective-permute-start.27 = (bf16[704,512]{1,0:T(8,128)(2,1)S(1)}, bf16[704,512]{1,0:T(8,128)(2,1)S(1)}, u32[]{:S(2)}, u32[]{:S(2)}) collective-permute-start(bf16[704,512]{1,0:T(8,128)(2,1)S(1)} %add_convert_fusion.6), channel_id=1, source_target_pairs={{0,4},{12,8},{1,5},{13,9},{2,6},{14,10},{3,7},{15,11},{16,20},{28,... | collective-permute-start | bytes 2162696 | tf_op jit(solution)/shard_map/ppermute | solution.py:488
  197.5 2.7 collective-permute-start.29
  201.4 14.7 %collective-permute-start.30 = (bf16[4,64,1024]{2,1,0:T(8,128)(2,1)}, bf16[4,64,1024]{2,1,0:T(8,128)(2,1)S(1)}, u32[]{:S(2)}, u32[]{:S(2)}) collective-permute-start(bf16[4,64,1024]{2,1,0:T(8,128)(2,1)} %fusion.6), channel_id=1, source_target_pairs={{0,2},{1,3},{2,0},{3,1},{4,6},{5,7},{6,4},{7,5},{8,10},{9,11},{10,... | collective-permute-start | bytes 1572872 | tf_op jit(solution)/shard_map/ppermute | solution.py:341
  202.8 20.5 %collective-permute-start.34 = (bf16[512,512]{1,0:T(8,128)(2,1)}, bf16[512,512]{1,0:T(8,128)(2,1)}, u32[]{:S(2)}, u32[]{:S(2)}) collective-permute-start(bf16[512,512]{1,0:T(8,128)(2,1)} %get-tuple-element.237), channel_id=1, source_target_pairs={{0,16},{16,0},{1,17},{17,1},{2,18},{18,2},{3,19},{19,3},{4,20},{20... | collective-permute-start | bytes 1572872 | tf_op jit(solution)/shard_map/ppermute | solution.py:476
  203.5 23.4 %collective-permute-start.31 = (bf16[704,512]{1,0:T(8,128)(2,1)}, bf16[704,512]{1,0:T(8,128)(2,1)}, u32[]{:S(2)}, u32[]{:S(2)}) collective-permute-start(bf16[704,512]{1,0:T(8,128)(2,1)} %add_convert_fusion.5), channel_id=1, source_target_pairs={{4,0},{8,12},{5,1},{9,13},{6,2},{10,14},{7,3},{11,15},{20,16},{24,... | collective-permute-start | bytes 2162696 | tf_op jit(solution)/shard_map/ppermute | solution.py:494
  204.8 19.7 %collective-permute-start.32 = (bf16[704,512]{1,0:T(8,128)(2,1)}, bf16[704,512]{1,0:T(8,128)(2,1)}, u32[]{:S(2)}, u32[]{:S(2)}) collective-permute-start(bf16[704,512]{1,0:T(8,128)(2,1)} %get-tuple-element.234), channel_id=1, source_target_pairs={{4,8},{8,4},{5,9},{9,5},{6,10},{10,6},{7,11},{11,7},{20,24},{24,20... | collective-permute-start | bytes 2162696 | tf_op jit(solution)/shard_map/ppermute | solution.py:491
  206.3 23.2 %collective-permute-start.33 = (bf16[704,512]{1,0:T(8,128)(2,1)}, bf16[704,512]{1,0:T(8,128)(2,1)}, u32[]{:S(2)}, u32[]{:S(2)}) collective-permute-start(bf16[704,512]{1,0:T(8,128)(2,1)} %get-tuple-element.235), channel_id=1, source_target_pairs={{0,4},{12,8},{1,5},{13,9},{2,6},{14,10},{3,7},{15,11},{16,20},{28,... | collective-permute-start | bytes 2162696 | tf_op jit(solution)/shard_map/ppermute | solution.py:488
  218.2 19.0 %all-to-all-start.4 = ((bf16[4,64,1024]{2,1,0:T(8,128)(2,1)}), bf16[4,64,1024]{2,1,0:T(8,128)(2,1)S(1)}, u32[]{:S(2)}, u32[]{:S(2)}) async-start(bf16[4,64,1024]{2,1,0:T(8,128)(2,1)} %get-tuple-element.230), calls=%async_computation.4 | async-start | bytes 1048576 | tf_op jit(solution)/shard_map/all_to_all | solution.py:604
  222.0 26.3 %collective-permute-start.41 = (bf16[528,512]{1,0:T(8,128)(2,1)}, bf16[528,512]{1,0:T(8,128)(2,1)S(1)}, u32[]{:S(2)}, u32[]{:S(2)}) collective-permute-start(bf16[528,512]{1,0:T(8,128)(2,1)} %get-tuple-element.249), channel_id=1, source_target_pairs={{0,16},{16,0},{1,17},{17,1},{2,18},{18,2},{3,19},{19,3},{4,20},{20... | collective-permute-start | bytes 1622024 | tf_op jit(solution)/shard_map/ppermute | solution.py:476
  237.3 21.9 %collective-permute-start.36 = (bf16[704,512]{1,0:T(8,128)(2,1)}, bf16[704,512]{1,0:T(8,128)(2,1)}, u32[]{:S(2)}, u32[]{:S(2)}) collective-permute-start(bf16[704,512]{1,0:T(8,128)(2,1)} %add_convert_fusion.2), channel_id=1, source_target_pairs={{4,0},{8,12},{5,1},{9,13},{6,2},{10,14},{7,3},{11,15},{20,16},{24,... | collective-permute-start | bytes 2162696 | tf_op jit(solution)/shard_map/ppermute | solution.py:494
  238.6 20.6 %collective-permute-start.37 = (bf16[704,512]{1,0:T(8,128)(2,1)S(1)}, bf16[704,512]{1,0:T(8,128)(2,1)}, u32[]{:S(2)}, u32[]{:S(2)}) collective-permute-start(bf16[704,512]{1,0:T(8,128)(2,1)S(1)} %add_convert_fusion.1), channel_id=1, source_target_pairs={{4,8},{8,4},{5,9},{9,5},{6,10},{10,6},{7,11},{11,7},{20,24},{24,20... | collective-permute-start | bytes 2162696 | tf_op jit(solution)/shard_map/ppermute | solution.py:491
  240.1 19.0 %collective-permute-start.38 = (bf16[512,512]{1,0:T(8,128)(2,1)S(1)}, bf16[512,512]{1,0:T(8,128)(2,1)}, u32[]{:S(2)}, u32[]{:S(2)}) collective-permute-start(bf16[512,512]{1,0:T(8,128)(2,1)S(1)} %add_convert_fusion.14), channel_id=1, source_target_pairs={{0,4},{12,8},{1,5},{13,9},{2,6},{14,10},{3,7},{15,11},{16,20},{28,... | collective-permute-start | bytes 1572872 | tf_op jit(solution)/shard_map/ppermute | solution.py:488
  247.6 11.5 %collective-permute-start.35 = (bf16[4,64,1024]{2,1,0:T(8,128)(2,1)S(1)}, bf16[4,64,1024]{2,1,0:T(8,128)(2,1)S(1)}, u32[]{:S(2)}, u32[]{:S(2)}) collective-permute-start(bf16[4,64,1024]{2,1,0:T(8,128)(2,1)S(1)} %all-to-all-done.4.refs_0_), channel_id=1, source_target_pairs={{0,2},{1,3},{2,0},{3,1},{4,6},{5,7},{6,4},{7,5},{8,10},{9,11},{10,... | collective-permute-start | bytes 1572872 | tf_op jit(solution)/shard_map/ppermute | solution.py:341
  250.6 25.6 %collective-permute-start.42 = (bf16[528,512]{1,0:T(8,128)(2,1)S(1)}, bf16[528,512]{1,0:T(8,128)(2,1)}, u32[]{:S(2)}, u32[]{:S(2)}) collective-permute-start(bf16[528,512]{1,0:T(8,128)(2,1)S(1)} %add_convert_fusion.11), channel_id=1, source_target_pairs={{0,4},{12,8},{1,5},{13,9},{2,6},{14,10},{3,7},{15,11},{16,20},{28,... | collective-permute-start | bytes 1622024 | tf_op jit(solution)/shard_map/ppermute | solution.py:488
  259.1 14.1 %collective-permute-start.39 = (bf16[4,64,1024]{2,1,0:T(8,128)(2,1)S(1)}, bf16[4,64,1024]{2,1,0:T(8,128)(2,1)S(1)}, u32[]{:S(2)}, u32[]{:S(2)}) collective-permute-start(bf16[4,64,1024]{2,1,0:T(8,128)(2,1)S(1)} %all-to-all-done.4.refs_0_), channel_id=1, source_target_pairs={{0,1},{1,0},{2,3},{3,2},{4,5},{5,4},{6,7},{7,6},{8,9},{9,8},{10,11... | collective-permute-start | bytes 1572872 | tf_op jit(solution)/shard_map/ppermute | solution.py:338
  259.2 20.3 %all-to-all-start.5 = ((bf16[4,64,1024]{2,1,0:T(8,128)(2,1)}), bf16[4,64,1024]{2,1,0:T(8,128)(2,1)S(1)}, u32[]{:S(2)}, u32[]{:S(2)}) async-start(bf16[4,64,1024]{2,1,0:T(8,128)(2,1)} %fusion.5), calls=%async_computation.5 | async-start | bytes 1048576 | tf_op jit(solution)/shard_map/all_to_all | solution.py:623
  265.7 17.1 %collective-permute-start.47 = (bf16[512,512]{1,0:T(8,128)(2,1)}, bf16[512,512]{1,0:T(8,128)(2,1)}, u32[]{:S(2)}, u32[]{:S(2)}) collective-permute-start(bf16[512,512]{1,0:T(8,128)(2,1)} %add_convert_fusion.13), channel_id=1, source_target_pairs={{4,8},{8,4},{5,9},{9,5},{6,10},{10,6},{7,11},{11,7},{20,24},{24,20... | collective-permute-start | bytes 1572872 | tf_op jit(solution)/shard_map/ppermute | solution.py:491
  267.2 6.0 %collective-permute-start.40 = (bf16[4,64,1024]{2,1,0:T(8,128)(2,1)S(1)}, bf16[4,64,1024]{2,1,0:T(8,128)(2,1)S(1)}, u32[]{:S(2)}, u32[]{:S(2)}) collective-permute-start(bf16[4,64,1024]{2,1,0:T(8,128)(2,1)S(1)} %collective-permute-done.35.refs_1_), channel_id=1, source_target_pairs={{0,1},{1,0},{2,3},{3,2},{4,5},{5,4},{6,7},{7,6},{8,9},{9,8},{10,11... | collective-permute-start | bytes 1572872 | tf_op jit(solution)/shard_map/ppermute | solution.py:338
  269.6 26.4 %collective-permute-start.46 = (bf16[704,512]{1,0:T(8,128)(2,1)}, bf16[704,512]{1,0:T(8,128)(2,1)}, u32[]{:S(2)}, u32[]{:S(2)}) collective-permute-start(bf16[704,512]{1,0:T(8,128)(2,1)} %add_convert_fusion), channel_id=1, source_target_pairs={{4,0},{8,12},{5,1},{9,13},{6,2},{10,14},{7,3},{11,15},{20,16},{24,... | collective-permute-start | bytes 2162696 | tf_op jit(solution)/shard_map/ppermute | solution.py:494
  279.4 18.9 %collective-permute-start.43 = (bf16[4,64,1024]{2,1,0:T(8,128)(2,1)S(1)}, bf16[4,64,1024]{2,1,0:T(8,128)(2,1)S(1)}, u32[]{:S(2)}, u32[]{:S(2)}) collective-permute-start(bf16[4,64,1024]{2,1,0:T(8,128)(2,1)S(1)} %all-to-all-done.5.refs_0_), channel_id=1, source_target_pairs={{0,2},{1,3},{2,0},{3,1},{4,6},{5,7},{6,4},{7,5},{8,10},{9,11},{10,... | collective-permute-start | bytes 1572872 | tf_op jit(solution)/shard_map/ppermute | solution.py:341
  281.3 17.6 %collective-permute-start.49 = (bf16[528,512]{1,0:T(8,128)(2,1)S(1)}, bf16[528,512]{1,0:T(8,128)(2,1)}, u32[]{:S(2)}, u32[]{:S(2)}) collective-permute-start(bf16[528,512]{1,0:T(8,128)(2,1)S(1)} %add_convert_fusion.10), channel_id=1, source_target_pairs={{4,8},{8,4},{5,9},{9,5},{6,10},{10,6},{7,11},{11,7},{20,24},{24,20... | collective-permute-start | bytes 1622024 | tf_op jit(solution)/shard_map/ppermute | solution.py:491
  284.1 25.9 %collective-permute-start.48 = (bf16[512,512]{1,0:T(8,128)(2,1)S(1)}, bf16[512,512]{1,0:T(8,128)(2,1)}, u32[]{:S(2)}, u32[]{:S(2)}) collective-permute-start(bf16[512,512]{1,0:T(8,128)(2,1)S(1)} %add_convert_fusion.12), channel_id=1, source_target_pairs={{4,0},{8,12},{5,1},{9,13},{6,2},{10,14},{7,3},{11,15},{20,16},{24,... | collective-permute-start | bytes 1572872 | tf_op jit(solution)/shard_map/ppermute | solution.py:494
  285.4 29.9 %all-to-all-start.6 = ((bf16[4,4,64,256]{3,2,1,0:T(8,128)(2,1)}), bf16[4,4,64,256]{3,2,1,0:T(8,128)(2,1)}, u32[]{:S(2)}, u32[]{:S(2)}) async-start(bf16[4,4,64,256]{3,2,1,0:T(8,128)(2,1)} %get-tuple-element.251), calls=%async_computation.6 | async-start | bytes 1048576 | tf_op jit(solution)/shard_map/all_to_all | solution.py:633
  298.4 19.0 %collective-permute-start.44 = (bf16[4,64,1024]{2,1,0:T(8,128)(2,1)S(1)}, bf16[4,64,1024]{2,1,0:T(8,128)(2,1)S(1)}, u32[]{:S(2)}, u32[]{:S(2)}) collective-permute-start(bf16[4,64,1024]{2,1,0:T(8,128)(2,1)S(1)} %all-to-all-done.5.refs_0_), channel_id=1, source_target_pairs={{0,1},{1,0},{2,3},{3,2},{4,5},{5,4},{6,7},{7,6},{8,9},{9,8},{10,11... | collective-permute-start | bytes 1572872 | tf_op jit(solution)/shard_map/ppermute | solution.py:338
  298.4 19.0 %collective-permute-start.45 = (bf16[4,64,1024]{2,1,0:T(8,128)(2,1)S(1)}, bf16[4,64,1024]{2,1,0:T(8,128)(2,1)S(1)}, u32[]{:S(2)}, u32[]{:S(2)}) collective-permute-start(bf16[4,64,1024]{2,1,0:T(8,128)(2,1)S(1)} %collective-permute-done.43.refs_1_), channel_id=1, source_target_pairs={{0,1},{1,0},{2,3},{3,2},{4,5},{5,4},{6,7},{7,6},{8,9},{9,8},{10,11... | collective-permute-start | bytes 1572872 | tf_op jit(solution)/shard_map/ppermute | solution.py:338
  300.9 23.9 %collective-permute-start.50 = (bf16[528,512]{1,0:T(8,128)(2,1)}, bf16[528,512]{1,0:T(8,128)(2,1)}, u32[]{:S(2)}, u32[]{:S(2)}) collective-permute-start(bf16[528,512]{1,0:T(8,128)(2,1)} %add_convert_fusion.9), channel_id=1, source_target_pairs={{4,0},{8,12},{5,1},{9,13},{6,2},{10,14},{7,3},{11,15},{20,16},{24,... | collective-permute-start | bytes 1622024 | tf_op jit(solution)/shard_map/ppermute | solution.py:494
  326.8 1.2 collective-permute-start.51
  328.0 3.6 %collective-permute-start.52 = (f32[2,512]{1,0:T(2,128)S(1)}, f32[2,512]{1,0:T(2,128)S(1)}, u32[]{:S(2)}, u32[]{:S(2)}) collective-permute-start(f32[2,512]{1,0:T(2,128)S(1)} %slice_add_fusion), channel_id=1, source_target_pairs={{0,2},{1,3},{2,0},{3,1},{4,6},{5,7},{6,4},{7,5},{8,10},{9,11},{10,... | collective-permute-start | bytes 12296 | tf_op jit(solution)/shard_map/ppermute | solution.py:341
  (43 other events, 267.4 us)

commit v6 on v5

--- a/solution.py
+++ b/solution.py
@@ -425,7 +425,7 @@
         seg, *x_pieces, gain_first, qkv_a, qkv_b, fv, cosine, sine, mix_row, out_a, out_b,
         in_specs=[smem] + [pl.BlockSpec(memory_space=pltpu.VMEM)] * 13,
         scratch=[pltpu.VMEM((local, rows), BF), pltpu.VMEM((ctx, local, block), F32)],
-        name="attend", vmem=20,
+        name="attend", vmem=16,
     )
     send, gate_b, g_first, g_late = tie(send, gate_b, g_first, g_late)
     got_core = core(send)
@@ -529,12 +529,11 @@
         name="norm_back_mlp", vmem=6, us=20,
     )
     (
-        branch_own, grad_residual, gate_got, gate_first, up_first, up_second, down_first, down_second,
-        down_onward,
+        branch_own, grad_residual, gate_first, up_first, up_second, down_first, down_second, down_onward,
     ) = tie(
-        branch_own, grad_residual, gate_got, gate_first, up_first, up_second, down_first, down_second,
-        down_onward,
-    )
+        branch_own, grad_residual, gate_first, up_first, up_second, down_first, down_second, down_onward,
+    )
+    grad_residual, gate_got = tie(grad_residual, gate_got)
 
     b_second = across(branch_own)
     b_core = core(branch_own)
@@ -570,7 +569,7 @@
             pltpu.VMEM((2 * local, width), F32),
             pltpu.VMEM((2 * local, width), F32),
         ],
-        name="attend_back", vmem=40, us=30,
+        name="attend_back", vmem=30, us=30,
     )
     send, down_got, gate_more, up_more, down_x = tie(send, down_got, gate_more, up_more, down_x)
     got_core = core(send)

time: 334 us -> 333 us (level)
    unnamed x95 -> x97, local copies, waits for them, and re-layouts: 12.7 us -> 12.7 us
where the time goes in v6:
time: 333 us; the launch traced here: 331 us
  starting transfers between devices  103 us (31%)
  waiting for transfers between devices  101 us (30%)
  Pallas kernels  64 us (19%)
  other arithmetic  39.3 us (12%)
  local copies, waits for them, and re-layouts  17.2 us (5%)
  matrix products  5.64 us (2%)
    pallas_call x11, Pallas kernels, call(): pl.pallas_call(kernel, out_shape=out_shapes, scratch_shapes=list(scratch)...  64 us
    ppermute x10, waiting for transfers between devices, across(): return lax.ppermute(value, 'tp', by_x)  29.3 us
    ppermute x5, starting transfers between devices, toward(): return lax.ppermute(shard, 'ctx', [(0, 1), (3, 2)])  25.8 us
    convert_element_type x9, other arithmetic, plus(): return (shard.astype(F32) + received.astype(F32)).astype(BF)  13.7 us
    ppermute x5, waiting for transfers between devices, toward(): return lax.ppermute(shard, 'ctx', [(0, 1), (3, 2)])  13.2 us
    ppermute x6, waiting for transfers between devices, other_half(): return (value, lax.ppermute(value, 'fsdp', swap_y))  12.9 us
    ppermute x5, waiting for transfers between devices, back(): return lax.ppermute(shard, 'ctx', [(1, 0), (2, 3)])  12.9 us
    unnamed x97, local copies, waits for them, and re-layouts  12.7 us
  transfers between devices with their start and end apart: 60, of which 24 were waited for; matrix products, arithmetic and copies ran while one was open for 14% of the time, Pallas kernels for 15%

profile of v6, /device:TPU:0, one launch (start us, length us, event | category | flops | bytes accessed | tf_op | source)
XLA Modules:
  0.0 331.1 jit_solution(16564217331299236349)
XLA Ops:
  0.7 1.6 copy-done.1
  2.3 1.4 own.2
  3.8 6.5 %all-to-all-start = ((bf16[4,64,1024]{2,1,0:T(8,128)(2,1)}), bf16[4,64,1024]{2,1,0:T(8,128)(2,1)S(1)}, u32[]{:S(2)}, u32[]{:S(2)}) async-start(bf16[4,64,1024]{2,1,0:T(8,128)(2,1)} %own.2), calls=%async_computation | async-start | bytes 1048576 | tf_op jit(solution)/shard_map/all_to_all | solution.py:405
  11.0 1.5 collective-permute-start.2
  13.3 11.5 %all-to-all-done.p0.x.values = bf16[4,64,1024]{2,1,0:T(8,128)(2,1)S(1)} async-done(((bf16[4,64,1024]{2,1,0:T(8,128)(2,1)}), bf16[4,64,1024]{2,1,0:T(8,128)(2,1)S(1)}, u32[]{:S(2)}, u32[]{:S(2)}) %all-to-all-start) | async-done | bytes 524320 | tf_op jit(solution)/shard_map/all_to_all | solution.py:405
  24.7 3.5 %all-to-all-start.1 = ((bf16[4,256,256]{2,1,0:T(8,128)(2,1)}), bf16[4,256,256]{2,1,0:T(8,128)(2,1)S(1)}, u32[]{:S(2)}, u32[]{:S(2)}) async-start(bf16[4,256,256]{2,1,0:T(8,128)(2,1)} %param.12), calls=%async_computation.1 | async-start | bytes 1048576 | tf_op jit(solution)/shard_map/all_to_all | solution.py:410
  28.2 1.6 collective-permute-start.1
  32.3 1.9 multiply_sine_fusion
  36.1 5.2 %collective-permute-done.1.p1 = bf16[4,64,1024]{2,1,0:T(8,128)(2,1)} collective-permute-done((bf16[4,64,1024]{2,1,0:T(8,128)(2,1)S(1)}, bf16[4,64,1024]{2,1,0:T(8,128)(2,1)}, u32[]{:S(2)}, u32[]{:S(2)}) %collective-permute-start.1) | collective-permute-done | bytes 524320 | tf_op jit(solution)/shard_map/ppermute | solution.py:341
  43.6 4.7 %all-to-all-start.2 = ((bf16[4,64,1024]{2,1,0:T(8,128)(2,1)}), bf16[4,64,1024]{2,1,0:T(8,128)(2,1)}, u32[]{:S(2)}, u32[]{:S(2)}) async-start(bf16[4,64,1024]{2,1,0:T(8,128)(2,1)} %copy-done.12), calls=%async_computation.2 | async-start | bytes 1048576 | tf_op jit(solution)/shard_map/all_to_all | solution.py:419
  48.3 1.5 collective-permute-start.5
  49.8 14.6 %attend.1 = (bf16[4,256,512]{2,1,0:T(8,128)(2,1)}, bf16[4,256,512]{2,1,0:T(8,128)(2,1)}, bf16[4,256,256]{2,1,0:T(8,128)(2,1)}, bf16[4,256,256]{2,1,0:T(8,128)(2,...) custom-call(s32[4]{0:T(128)S(1)} %get-tuple-element.277.seg.where, ...), custom_call_target="tpu_custom_call" | custom-call | tf_op jit(solution)/shard_map/attend/pallas_call | solution.py:37
  67.3 1.6 collective-permute-start.8
  68.9 4.8 %all-to-all-start.3 = ((bf16[4,64,1024]{2,1,0:T(8,128)(2,1)}), bf16[4,64,1024]{2,1,0:T(8,128)(2,1)}, u32[]{:S(2)}, u32[]{:S(2)}) async-start(bf16[4,64,1024]{2,1,0:T(8,128)(2,1)} %copy-done.11), calls=%async_computation.3 | async-start | bytes 1048576 | tf_op jit(solution)/shard_map/all_to_all | solution.py:433
  73.7 2.0 fusion.9
  75.7 1.5 collective-permute-start.7
  78.9 9.9 %collective-permute-done.9.db = bf16[128,512]{1,0:T(8,128)(2,1)S(1)} collective-permute-done((bf16[128,512]{1,0:T(8,128)(2,1)S(1)}, bf16[128,512]{1,0:T(8,128)(2,1)S(1)}, u32[]{:S(2)}, u32[]{:S(2)}) %collective-permute-start.9) | collective-permute-done | bytes 131104 | tf_op jit(solution)/shard_map/ppermute | solution.py:345
  92.7 2.5 residual_norm.1
  95.2 1.6 collective-permute-start.10
  98.1 10.0 %collective-permute-done.10.n1 = bf16[4,64,1024]{2,1,0:T(8,128)(2,1)S(1)} collective-permute-done((bf16[4,64,1024]{2,1,0:T(8,128)(2,1)S(1)}, bf16[4,64,1024]{2,1,0:T(8,128)(2,1)S(1)}, u32[]{:S(2)}, u32[]{:S(2)}) %collective-permute-start.10) | collective-permute-done | bytes 524320 | tf_op jit(solution)/shard_map/ppermute | solution.py:341
  108.2 2.7 collective-permute-done.15.lb
  111.0 10.7 %mlp.1 = (bf16[4,256,512]{2,1,0:T(8,128)(2,1)S(1)}, bf16[4,256,512]{2,1,0:T(8,128)(2,1)S(1)}, bf16[4,256,512]{2,1,0:T(8,128)(2,1)S(1)}, bf16[4,256,512]{2,1,0:T(...) custom-call(bf16[4,64,1024]{2,1,0:T(8,128)(2,1)S(1)} %get-tuple-elem, ...), custom_call_target="tpu_custom_call" | custom-call | flops 10000000000 | bytes 34000000 | tf_op jit(solution)/shard_map/mlp/pallas_call | solution.py:37
  128.4 2.3 down.1
  133.6 6.9 %collective-permute-done.17.got_x = bf16[4,64,1024]{2,1,0:T(8,128)(2,1)S(1)} collective-permute-done((bf16[4,64,1024]{2,1,0:T(8,128)(2,1)S(1)}, bf16[4,64,1024]{2,1,0:T(8,128)(2,1)S(1)}, u32[]{:S(2)}, u32[]{:S(2)}) %collective-permute-start.17) | collective-permute-done | bytes 524320 | tf_op jit(solution)/shard_map/ppermute | solution.py:341
  140.5 2.4 norm_back_mlp.1
  145.4 3.8 %collective-permute-start.24 = (bf16[704,512]{1,0:T(8,128)(2,1)S(1)}, bf16[704,512]{1,0:T(8,128)(2,1)S(1)}, u32[]{:S(2)}, u32[]{:S(2)}) collective-permute-start(bf16[704,512]{1,0:T(8,128)(2,1)S(1)} %add_convert_fusion.8), channel_id=1, source_target_pairs={{0,4},{12,8},{1,5},{13,9},{2,6},{14,10},{3,7},{15,11},{16,20},{28,... | collective-permute-start | bytes 2162696 | tf_op jit(solution)/shard_map/ppermute | solution.py:488
  150.5 5.8 %collective-permute-done.20.b1 = bf16[4,64,1024]{2,1,0:T(8,128)(2,1)S(1)} collective-permute-done((bf16[4,64,1024]{2,1,0:T(8,128)(2,1)S(1)}, bf16[4,64,1024]{2,1,0:T(8,128)(2,1)S(1)}, u32[]{:S(2)}, u32[]{:S(2)}) %collective-permute-start.20) | collective-permute-done | bytes 524320 | tf_op jit(solution)/shard_map/ppermute | solution.py:341
  156.3 7.3 %collective-permute-done.24 = bf16[704,512]{1,0:T(8,128)(2,1)S(1)} collective-permute-done((bf16[704,512]{1,0:T(8,128)(2,1)S(1)}, bf16[704,512]{1,0:T(8,128)(2,1)S(1)}, u32[]{:S(2)}, u32[]{:S(2)}) %collective-permute-start.24) | collective-permute-done | bytes 720928 | tf_op jit(solution)/shard_map/ppermute | solution.py:488
  163.7 2.3 collective-permute-done.23
  166.0 1.4 collective-permute-start.28
  170.1 5.1 %collective-permute-start.27 = (bf16[704,512]{1,0:T(8,128)(2,1)S(1)}, bf16[704,512]{1,0:T(8,128)(2,1)S(1)}, u32[]{:S(2)}, u32[]{:S(2)}) collective-permute-start(bf16[704,512]{1,0:T(8,128)(2,1)S(1)} %add_convert_fusion.6), channel_id=1, source_target_pairs={{0,4},{12,8},{1,5},{13,9},{2,6},{14,10},{3,7},{15,11},{16,20},{28,... | collective-permute-start | bytes 2162696 | tf_op jit(solution)/shard_map/ppermute | solution.py:488
  175.3 21.7 %attend_back.1 = (bf16[4,4,64,256]{3,2,1,0:T(8,128)(2,1)}, f32[4,64,1024]{2,1,0:T(8,128)}, f32[4,64,1024]{2,1,0:T(8,128)S(1)}, bf16[2,4,64,1024]{3,2,1,0:T(8,128...) custom-call(s32[4]{0:T(128)S(1)} %get-tuple-element.277.seg.where, ...), custom_call_target="tpu_custom_call" | custom-call | flops 30000001024 | bytes 102000000 | tf_op jit(solution)/shard_map/attend_back/pallas_call | solution.py:37
  198.2 1.6 add_convert_fusion.3
  203.6 1.5 collective-permute-start.32
  205.1 7.2 %collective-permute-start.33 = (bf16[704,512]{1,0:T(8,128)(2,1)}, bf16[704,512]{1,0:T(8,128)(2,1)}, u32[]{:S(2)}, u32[]{:S(2)}) collective-permute-start(bf16[704,512]{1,0:T(8,128)(2,1)} %get-tuple-element.237), channel_id=1, source_target_pairs={{0,4},{12,8},{1,5},{13,9},{2,6},{14,10},{3,7},{15,11},{16,20},{28,... | collective-permute-start | bytes 2162696 | tf_op jit(solution)/shard_map/ppermute | solution.py:488
  212.4 2.5 fusion.5
  215.5 2.2 norm_back_attn.1
  217.6 3.6 %all-to-all-start.4 = ((bf16[4,64,1024]{2,1,0:T(8,128)(2,1)}), bf16[4,64,1024]{2,1,0:T(8,128)(2,1)S(1)}, u32[]{:S(2)}, u32[]{:S(2)}) async-start(bf16[4,64,1024]{2,1,0:T(8,128)(2,1)} %get-tuple-element.232), calls=%async_computation.4 | async-start | bytes 1048576 | tf_op jit(solution)/shard_map/all_to_all | solution.py:603
  223.3 2.4 add_convert_fusion.2
  225.7 2.4 convert_bitcast_fusion.1
  229.6 6.5 %all-to-all-done.4.refs_0_ = bf16[4,64,1024]{2,1,0:T(8,128)(2,1)S(1)} async-done(((bf16[4,64,1024]{2,1,0:T(8,128)(2,1)}), bf16[4,64,1024]{2,1,0:T(8,128)(2,1)S(1)}, u32[]{:S(2)}, u32[]{:S(2)}) %all-to-all-start.4) | async-done | bytes 524320 | tf_op jit(solution)/shard_map/all_to_all | solution.py:603
  237.3 1.5 collective-permute-start.37
  238.9 7.5 %collective-permute-start.38 = (bf16[512,512]{1,0:T(8,128)(2,1)S(1)}, bf16[512,512]{1,0:T(8,128)(2,1)}, u32[]{:S(2)}, u32[]{:S(2)}) collective-permute-start(bf16[512,512]{1,0:T(8,128)(2,1)S(1)} %add_convert_fusion.14), channel_id=1, source_target_pairs={{0,4},{12,8},{1,5},{13,9},{2,6},{14,10},{3,7},{15,11},{16,20},{28,... | collective-permute-start | bytes 1572872 | tf_op jit(solution)/shard_map/ppermute | solution.py:488
  246.4 1.4 collective-permute-start.35
  248.6 1.5 add_convert_fusion.11
  250.2 2.1 collective-permute-start.42
  252.3 5.7 %collective-permute-done.38 = bf16[512,512]{1,0:T(8,128)(2,1)} collective-permute-done((bf16[512,512]{1,0:T(8,128)(2,1)S(1)}, bf16[512,512]{1,0:T(8,128)(2,1)}, u32[]{:S(2)}, u32[]{:S(2)}) %collective-permute-start.38) | collective-permute-done | bytes 524320 | tf_op jit(solution)/shard_map/ppermute | solution.py:488
  257.9 4.4 %all-to-all-start.5 = ((bf16[4,64,1024]{2,1,0:T(8,128)(2,1)}), bf16[4,64,1024]{2,1,0:T(8,128)(2,1)S(1)}, u32[]{:S(2)}, u32[]{:S(2)}) async-start(bf16[4,64,1024]{2,1,0:T(8,128)(2,1)} %fusion.5), calls=%async_computation.5 | async-start | bytes 1048576 | tf_op jit(solution)/shard_map/all_to_all | solution.py:622
  262.3 2.1 add_convert_fusion.13
  264.5 1.6 collective-permute-start.47
  266.3 2.2 add_convert_fusion
  269.7 2.3 convert_bitcast_fusion
  272.0 3.0 place.2
  275.0 3.2 all-to-all-done.5.refs_0_
  280.8 1.5 collective-permute-start.49
  285.0 9.9 %all-to-all-start.6 = ((bf16[4,4,64,256]{3,2,1,0:T(8,128)(2,1)}), bf16[4,4,64,256]{3,2,1,0:T(8,128)(2,1)}, u32[]{:S(2)}, u32[]{:S(2)}) async-start(bf16[4,4,64,256]{3,2,1,0:T(8,128)(2,1)} %get-tuple-element.253), calls=%async_computation.6 | async-start | bytes 1048576 | tf_op jit(solution)/shard_map/all_to_all | solution.py:632
  294.9 2.3 select_convert_fusion
  297.7 2.0 add_convert_fusion.9
  301.0 7.8 %collective-permute-done.48 = bf16[512,512]{1,0:T(8,128)(2,1)} collective-permute-done((bf16[512,512]{1,0:T(8,128)(2,1)S(1)}, bf16[512,512]{1,0:T(8,128)(2,1)}, u32[]{:S(2)}, u32[]{:S(2)}) %collective-permute-start.48) | collective-permute-done | bytes 524320 | tf_op jit(solution)/shard_map/ppermute | solution.py:494
  309.9 4.1 %all-to-all-done.6 = bf16[4,4,64,256]{3,2,1,0:T(8,128)(2,1)} async-done(((bf16[4,4,64,256]{3,2,1,0:T(8,128)(2,1)}), bf16[4,4,64,256]{3,2,1,0:T(8,128)(2,1)}, u32[]{:S(2)}, u32[]{:S(2)}) %all-to-all-start.6) | async-done | bytes 524320 | tf_op jit(solution)/shard_map/all_to_all | solution.py:632
  314.1 2.1 bitcast_convert_fusion
  316.2 2.4 place.3
  318.6 5.0 %collective-permute-done.50 = bf16[528,512]{1,0:T(8,128)(2,1)} collective-permute-done((bf16[528,512]{1,0:T(8,128)(2,1)}, bf16[528,512]{1,0:T(8,128)(2,1)}, u32[]{:S(2)}, u32[]{:S(2)}) %collective-permute-start.50) | collective-permute-done | bytes 540704 | tf_op jit(solution)/shard_map/ppermute | solution.py:494
  328.3 1.6 copy.28
  (224 shorter events, 60.7 us)
Async XLA Ops:
  3.8 21.0 %all-to-all-start = ((bf16[4,64,1024]{2,1,0:T(8,128)(2,1)}), bf16[4,64,1024]{2,1,0:T(8,128)(2,1)S(1)}, u32[]{:S(2)}, u32[]{:S(2)}) async-start(bf16[4,64,1024]{2,1,0:T(8,128)(2,1)} %own.2), calls=%async_computation | async-start | bytes 1048576 | tf_op jit(solution)/shard_map/all_to_all | solution.py:405
  11.0 23.2 %collective-permute-start.2 = (bf16[258,512]{1,0:T(8,128)(2,1)}, bf16[258,512]{1,0:T(8,128)(2,1)}, u32[]{:S(2)}, u32[]{:S(2)}) collective-permute-start(bf16[258,512]{1,0:T(8,128)(2,1)} %pad_maximum_fusion.1), channel_id=1, source_target_pairs={{0,16},{16,0},{1,17},{17,1},{2,18},{18,2},{3,19},{19,3},{4,20},{20... | collective-permute-start | bytes 792584 | tf_op jit(solution)/shard_map/ppermute | solution.py:345
  12.5 23.6 %collective-permute-start = (bf16[3,512,256]{2,1,0:T(8,128)(2,1)}, bf16[3,512,256]{2,1,0:T(8,128)(2,1)}, u32[]{:S(2)}, u32[]{:S(2)}) collective-permute-start(bf16[3,512,256]{2,1,0:T(8,128)(2,1)} %bitcast.91), channel_id=1, source_target_pairs={{0,16},{16,0},{1,17},{17,1},{2,18},{18,2},{3,19},{19,3},{4,20},{20... | collective-permute-start | bytes 2359304 | tf_op jit(solution)/shard_map/ppermute | solution.py:345
  24.7 17.5 %all-to-all-start.1 = ((bf16[4,256,256]{2,1,0:T(8,128)(2,1)}), bf16[4,256,256]{2,1,0:T(8,128)(2,1)S(1)}, u32[]{:S(2)}, u32[]{:S(2)}) async-start(bf16[4,256,256]{2,1,0:T(8,128)(2,1)} %param.12), calls=%async_computation.1 | async-start | bytes 1048576 | tf_op jit(solution)/shard_map/all_to_all | solution.py:410
  28.2 13.1 %collective-permute-start.1 = (bf16[4,64,1024]{2,1,0:T(8,128)(2,1)S(1)}, bf16[4,64,1024]{2,1,0:T(8,128)(2,1)}, u32[]{:S(2)}, u32[]{:S(2)}) collective-permute-start(bf16[4,64,1024]{2,1,0:T(8,128)(2,1)S(1)} %all-to-all-done.p0.x.values), channel_id=1, source_target_pairs={{0,2},{1,3},{2,0},{3,1},{4,6},{5,7},{6,4},{7,5},{8,10},{9,11},{10,... | collective-permute-start | bytes 1572872 | tf_op jit(solution)/shard_map/ppermute | solution.py:341
  35.9 28.6 %copy-start.5 = (bf16[256,512]{1,0:T(8,128)(2,1)}, bf16[256,512]{1,0:T(8,128)(2,1)S(1)}, u32[]{:S(2)}) copy-start(bf16[256,512]{1,0:T(8,128)(2,1)S(1)} %slice.78.wob) | copy-start | bytes 786436
  36.1 6.1 %collective-permute-start.3 = (bf16[4,64,1024]{2,1,0:T(8,128)(2,1)S(1)}, bf16[4,64,1024]{2,1,0:T(8,128)(2,1)}, u32[]{:S(2)}, u32[]{:S(2)}) collective-permute-start(bf16[4,64,1024]{2,1,0:T(8,128)(2,1)S(1)} %all-to-all-done.p0.x.values), channel_id=1, source_target_pairs={{0,1},{1,0},{2,3},{3,2},{4,5},{5,4},{6,7},{7,6},{8,9},{9,8},{10,11... | collective-permute-start | bytes 1572872 | tf_op jit(solution)/shard_map/ppermute | solution.py:338
  41.3 2.3 collective-permute-start.4
  43.6 23.7 %all-to-all-start.2 = ((bf16[4,64,1024]{2,1,0:T(8,128)(2,1)}), bf16[4,64,1024]{2,1,0:T(8,128)(2,1)}, u32[]{:S(2)}, u32[]{:S(2)}) async-start(bf16[4,64,1024]{2,1,0:T(8,128)(2,1)} %copy-done.12), calls=%async_computation.2 | async-start | bytes 1048576 | tf_op jit(solution)/shard_map/all_to_all | solution.py:419
  48.3 18.1 %collective-permute-start.5 = (bf16[704,512]{1,0:T(8,128)(2,1)}, bf16[704,512]{1,0:T(8,128)(2,1)S(1)}, u32[]{:S(2)}, u32[]{:S(2)}) collective-permute-start(bf16[704,512]{1,0:T(8,128)(2,1)} %bitcast.94), channel_id=1, source_target_pairs={{0,16},{16,0},{1,17},{17,1},{2,18},{18,2},{3,19},{19,3},{4,20},{20... | collective-permute-start | bytes 2162696 | tf_op jit(solution)/shard_map/ppermute | solution.py:345
  67.3 6.4 %collective-permute-start.6 = (bf16[2,4,64,1024]{3,2,1,0:T(8,128)(2,1)}, bf16[2,4,64,1024]{3,2,1,0:T(8,128)(2,1)}, u32[]{:S(2)}, u32[]{:S(2)}) collective-permute-start(bf16[2,4,64,1024]{3,2,1,0:T(8,128)(2,1)} %copy-done.19), channel_id=1, source_target_pairs={{0,1},{1,0},{2,3},{3,2},{4,5},{5,4},{6,7},{7,6},{8,9},{9,8},{10,11... | collective-permute-start | bytes 3145736 | tf_op jit(solution)/shard_map/ppermute | solution.py:338
  67.3 21.6 %collective-permute-start.8 = (bf16[704,512]{1,0:T(8,128)(2,1)}, bf16[704,512]{1,0:T(8,128)(2,1)}, u32[]{:S(2)}, u32[]{:S(2)}) collective-permute-start(bf16[704,512]{1,0:T(8,128)(2,1)} %bitcast.96), channel_id=1, source_target_pairs={{0,16},{16,0},{1,17},{17,1},{2,18},{18,2},{3,19},{19,3},{4,20},{20... | collective-permute-start | bytes 2162696 | tf_op jit(solution)/shard_map/ppermute | solution.py:345
  68.9 20.0 %all-to-all-start.3 = ((bf16[4,64,1024]{2,1,0:T(8,128)(2,1)}), bf16[4,64,1024]{2,1,0:T(8,128)(2,1)}, u32[]{:S(2)}, u32[]{:S(2)}) async-start(bf16[4,64,1024]{2,1,0:T(8,128)(2,1)} %copy-done.11), calls=%async_computation.3 | async-start | bytes 1048576 | tf_op jit(solution)/shard_map/all_to_all | solution.py:433
  75.7 13.9 %collective-permute-start.7 = (bf16[4,64,1024]{2,1,0:T(8,128)(2,1)}, bf16[4,64,1024]{2,1,0:T(8,128)(2,1)S(1)}, u32[]{:S(2)}, u32[]{:S(2)}) collective-permute-start(bf16[4,64,1024]{2,1,0:T(8,128)(2,1)} %fusion.9), channel_id=1, source_target_pairs={{0,2},{1,3},{2,0},{3,1},{4,6},{5,7},{6,4},{7,5},{8,10},{9,11},{10,... | collective-permute-start | bytes 1572872 | tf_op jit(solution)/shard_map/ppermute | solution.py:341
  78.1 10.8 %collective-permute-start.9 = (bf16[128,512]{1,0:T(8,128)(2,1)S(1)}, bf16[128,512]{1,0:T(8,128)(2,1)S(1)}, u32[]{:S(2)}, u32[]{:S(2)}) collective-permute-start(bf16[128,512]{1,0:T(8,128)(2,1)S(1)} %slice.63.da), channel_id=1, source_target_pairs={{0,16},{16,0},{1,17},{17,1},{2,18},{18,2},{3,19},{19,3},{4,20},{20... | collective-permute-start | bytes 393224 | tf_op jit(solution)/shard_map/ppermute | solution.py:345
  95.2 13.0 %collective-permute-start.10 = (bf16[4,64,1024]{2,1,0:T(8,128)(2,1)S(1)}, bf16[4,64,1024]{2,1,0:T(8,128)(2,1)S(1)}, u32[]{:S(2)}, u32[]{:S(2)}) collective-permute-start(bf16[4,64,1024]{2,1,0:T(8,128)(2,1)S(1)} %get-tuple-element.161.n0), channel_id=1, source_target_pairs={{0,2},{1,3},{2,0},{3,1},{4,6},{5,7},{6,4},{7,5},{8,10},{9,11},{10,... | collective-permute-start | bytes 1572872 | tf_op jit(solution)/shard_map/ppermute | solution.py:341
  96.8 14.1 %collective-permute-start.15 = (bf16[576,512]{1,0:T(8,128)(2,1)S(1)}, bf16[576,512]{1,0:T(8,128)(2,1)S(1)}, u32[]{:S(2)}, u32[]{:S(2)}) collective-permute-start(bf16[576,512]{1,0:T(8,128)(2,1)S(1)} %slice.65.la), channel_id=1, source_target_pairs={{0,16},{16,0},{1,17},{17,1},{2,18},{18,2},{3,19},{19,3},{4,20},{20... | collective-permute-start | bytes 1769480 | tf_op jit(solution)/shard_map/ppermute | solution.py:345
  97.6 13.3 %collective-permute-start.13 = (bf16[4,64,1024]{2,1,0:T(8,128)(2,1)}, bf16[4,64,1024]{2,1,0:T(8,128)(2,1)S(1)}, u32[]{:S(2)}, u32[]{:S(2)}) collective-permute-start(bf16[4,64,1024]{2,1,0:T(8,128)(2,1)} %all-to-all-done.2.g0.direct), channel_id=1, source_target_pairs={{0,1},{1,0},{2,3},{3,2},{4,5},{5,4},{6,7},{7,6},{8,9},{9,8},{10,11... | collective-permute-start | bytes 1572872 | tf_op jit(solution)/shard_map/ppermute | solution.py:338
  97.6 13.3 %collective-permute-start.11 = (bf16[4,64,1024]{2,1,0:T(8,128)(2,1)S(1)}, bf16[4,64,1024]{2,1,0:T(8,128)(2,1)S(1)}, u32[]{:S(2)}, u32[]{:S(2)}) collective-permute-start(bf16[4,64,1024]{2,1,0:T(8,128)(2,1)S(1)} %get-tuple-element.161.n0), channel_id=1, source_target_pairs={{0,1},{1,0},{2,3},{3,2},{4,5},{5,4},{6,7},{7,6},{8,9},{9,8},{10,11... | collective-permute-start | bytes 1572872 | tf_op jit(solution)/shard_map/ppermute | solution.py:338
  98.1 12.8 %collective-permute-start.14 = (bf16[4,64,1024]{2,1,0:T(8,128)(2,1)}, bf16[4,64,1024]{2,1,0:T(8,128)(2,1)S(1)}, u32[]{:S(2)}, u32[]{:S(2)}) collective-permute-start(bf16[4,64,1024]{2,1,0:T(8,128)(2,1)} %all-to-all-done.3.g1), channel_id=1, source_target_pairs={{0,1},{1,0},{2,3},{3,2},{4,5},{5,4},{6,7},{7,6},{8,9},{9,8},{10,11... | collective-permute-start | bytes 1572872 | tf_op jit(solution)/shard_map/ppermute | solution.py:338
  108.2 2.7 collective-permute-start.12
  121.7 2.7 collective-permute-start.16
  126.5 14.0 %collective-permute-start.17 = (bf16[4,64,1024]{2,1,0:T(8,128)(2,1)S(1)}, bf16[4,64,1024]{2,1,0:T(8,128)(2,1)S(1)}, u32[]{:S(2)}, u32[]{:S(2)}) collective-permute-start(bf16[4,64,1024]{2,1,0:T(8,128)(2,1)S(1)} %fusion.8), channel_id=1, source_target_pairs={{0,2},{1,3},{2,0},{3,1},{4,6},{5,7},{6,4},{7,5},{8,10},{9,11},{10,... | collective-permute-start | bytes 1572872 | tf_op jit(solution)/shard_map/ppermute | solution.py:341
  127.2 17.9 %collective-permute-start.19 = (bf16[704,512]{1,0:T(8,128)(2,1)S(1)}, bf16[704,512]{1,0:T(8,128)(2,1)S(1)}, u32[]{:S(2)}, u32[]{:S(2)}) collective-permute-start(bf16[704,512]{1,0:T(8,128)(2,1)S(1)} %fusion), channel_id=1, source_target_pairs={{0,16},{16,0},{1,17},{17,1},{2,18},{18,2},{3,19},{19,3},{4,20},{20... | collective-permute-start | bytes 2162696 | tf_op jit(solution)/shard_map/ppermute | solution.py:476
  131.7 11.2 %collective-permute-start.18 = (bf16[2,4,64,1024]{3,2,1,0:T(8,128)(2,1)S(1)}, bf16[2,4,64,1024]{3,2,1,0:T(8,128)(2,1)S(1)}, u32[]{:S(2)}, u32[]{:S(2)}) collective-permute-start(bf16[2,4,64,1024]{3,2,1,0:T(8,128)(2,1)S(1)} %get-tuple-element.184), channel_id=1, source_target_pairs={{0,1},{1,0},{2,3},{3,2},{4,5},{5,4},{6,7},{7,6},{8,9},{9,8},{10,11... | collective-permute-start | bytes 3145736 | tf_op jit(solution)/shard_map/ppermute | solution.py:338
  143.1 13.2 %collective-permute-start.20 = (bf16[4,64,1024]{2,1,0:T(8,128)(2,1)S(1)}, bf16[4,64,1024]{2,1,0:T(8,128)(2,1)S(1)}, u32[]{:S(2)}, u32[]{:S(2)}) collective-permute-start(bf16[4,64,1024]{2,1,0:T(8,128)(2,1)S(1)} %get-tuple-element.188.b0), channel_id=1, source_target_pairs={{0,2},{1,3},{2,0},{3,1},{4,6},{5,7},{6,4},{7,5},{8,10},{9,11},{10,... | collective-permute-start | bytes 1572872 | tf_op jit(solution)/shard_map/ppermute | solution.py:341
  145.1 30.1 %copy-start.25 = (bf16[4,256,256]{2,1,0:T(8,128)(2,1)S(1)}, bf16[4,256,256]{2,1,0:T(8,128)(2,1)}, u32[]{:S(2)}) copy-start(bf16[4,256,256]{2,1,0:T(8,128)(2,1)} %get-tuple-element.198.k) | copy-start | bytes 1572868
  145.1 30.1 %copy-start.26 = (bf16[4,256,256]{2,1,0:T(8,128)(2,1)S(1)}, bf16[4,256,256]{2,1,0:T(8,128)(2,1)}, u32[]{:S(2)}) copy-start(bf16[4,256,256]{2,1,0:T(8,128)(2,1)} %get-tuple-element.199.v) | copy-start | bytes 1572868
  145.1 30.1 %copy-start.27 = (bf16[4,256,256]{2,1,0:T(8,128)(2,1)S(1)}, bf16[4,256,256]{2,1,0:T(8,128)(2,1)}, u32[]{:S(2)}) copy-start(bf16[4,256,256]{2,1,0:T(8,128)(2,1)} %get-tuple-element.200.att) | copy-start | bytes 1572868
  145.4 18.3 %collective-permute-start.24 = (bf16[704,512]{1,0:T(8,128)(2,1)S(1)}, bf16[704,512]{1,0:T(8,128)(2,1)S(1)}, u32[]{:S(2)}, u32[]{:S(2)}) collective-permute-start(bf16[704,512]{1,0:T(8,128)(2,1)S(1)} %add_convert_fusion.8), channel_id=1, source_target_pairs={{0,4},{12,8},{1,5},{13,9},{2,6},{14,10},{3,7},{15,11},{16,20},{28,... | collective-permute-start | bytes 2162696 | tf_op jit(solution)/shard_map/ppermute | solution.py:488
  149.2 16.8 %collective-permute-start.23 = (bf16[704,512]{1,0:T(8,128)(2,1)S(1)}, bf16[704,512]{1,0:T(8,128)(2,1)S(1)}, u32[]{:S(2)}, u32[]{:S(2)}) collective-permute-start(bf16[704,512]{1,0:T(8,128)(2,1)S(1)} %fusion.1), channel_id=1, source_target_pairs={{0,16},{16,0},{1,17},{17,1},{2,18},{18,2},{3,19},{19,3},{4,20},{20... | collective-permute-start | bytes 2162696 | tf_op jit(solution)/shard_map/ppermute | solution.py:476
  150.5 5.8 %collective-permute-start.21 = (bf16[4,64,1024]{2,1,0:T(8,128)(2,1)S(1)}, bf16[4,64,1024]{2,1,0:T(8,128)(2,1)S(1)}, u32[]{:S(2)}, u32[]{:S(2)}) collective-permute-start(bf16[4,64,1024]{2,1,0:T(8,128)(2,1)S(1)} %get-tuple-element.188.b0), channel_id=1, source_target_pairs={{0,1},{1,0},{2,3},{3,2},{4,5},{5,4},{6,7},{7,6},{8,9},{9,8},{10,11... | collective-permute-start | bytes 1572872 | tf_op jit(solution)/shard_map/ppermute | solution.py:338
  156.3 9.7 %collective-permute-start.22 = (bf16[4,64,1024]{2,1,0:T(8,128)(2,1)S(1)}, bf16[4,64,1024]{2,1,0:T(8,128)(2,1)S(1)}, u32[]{:S(2)}, u32[]{:S(2)}) collective-permute-start(bf16[4,64,1024]{2,1,0:T(8,128)(2,1)S(1)} %collective-permute-done.20.b1), channel_id=1, source_target_pairs={{0,1},{1,0},{2,3},{3,2},{4,5},{5,4},{6,7},{7,6},{8,9},{9,8},{10,11... | collective-permute-start | bytes 1572872 | tf_op jit(solution)/shard_map/ppermute | solution.py:338
  166.0 31.0 %collective-permute-start.28 = (bf16[4,64,1024]{2,1,0:T(8,128)(2,1)S(1)}, bf16[4,64,1024]{2,1,0:T(8,128)(2,1)S(1)}, u32[]{:S(2)}, u32[]{:S(2)}) collective-permute-start(bf16[4,64,1024]{2,1,0:T(8,128)(2,1)S(1)} %fusion.7), channel_id=1, source_target_pairs={{0,2},{1,3},{2,0},{3,1},{4,6},{5,7},{6,4},{7,5},{8,10},{9,11},{10,... | collective-permute-start | bytes 1572872 | tf_op jit(solution)/shard_map/ppermute | solution.py:341
  167.6 29.4 %collective-permute-start.26 = (bf16[704,512]{1,0:T(8,128)(2,1)S(1)}, bf16[704,512]{1,0:T(8,128)(2,1)S(1)}, u32[]{:S(2)}, u32[]{:S(2)}) collective-permute-start(bf16[704,512]{1,0:T(8,128)(2,1)S(1)} %add_convert_fusion.7), channel_id=1, source_target_pairs={{4,8},{8,4},{5,9},{9,5},{6,10},{10,6},{7,11},{11,7},{20,24},{24,20... | collective-permute-start | bytes 2162696 | tf_op jit(solution)/shard_map/ppermute | solution.py:491
  168.5 28.5 %collective-permute-start.25 = (bf16[704,512]{1,0:T(8,128)(2,1)S(1)}, bf16[704,512]{1,0:T(8,128)(2,1)S(1)}, u32[]{:S(2)}, u32[]{:S(2)}) collective-permute-start(bf16[704,512]{1,0:T(8,128)(2,1)S(1)} %fusion.2), channel_id=1, source_target_pairs={{0,16},{16,0},{1,17},{17,1},{2,18},{18,2},{3,19},{19,3},{4,20},{20... | collective-permute-start | bytes 2162696 | tf_op jit(solution)/shard_map/ppermute | solution.py:476
  170.1 27.0 %collective-permute-start.27 = (bf16[704,512]{1,0:T(8,128)(2,1)S(1)}, bf16[704,512]{1,0:T(8,128)(2,1)S(1)}, u32[]{:S(2)}, u32[]{:S(2)}) collective-permute-start(bf16[704,512]{1,0:T(8,128)(2,1)S(1)} %add_convert_fusion.6), channel_id=1, source_target_pairs={{0,4},{12,8},{1,5},{13,9},{2,6},{14,10},{3,7},{15,11},{16,20},{28,... | collective-permute-start | bytes 2162696 | tf_op jit(solution)/shard_map/ppermute | solution.py:488
  197.0 2.7 collective-permute-start.29
  200.9 14.5 %collective-permute-start.30 = (bf16[4,64,1024]{2,1,0:T(8,128)(2,1)}, bf16[4,64,1024]{2,1,0:T(8,128)(2,1)S(1)}, u32[]{:S(2)}, u32[]{:S(2)}) collective-permute-start(bf16[4,64,1024]{2,1,0:T(8,128)(2,1)} %fusion.6), channel_id=1, source_target_pairs={{0,2},{1,3},{2,0},{3,1},{4,6},{5,7},{6,4},{7,5},{8,10},{9,11},{10,... | collective-permute-start | bytes 1572872 | tf_op jit(solution)/shard_map/ppermute | solution.py:341
  201.6 20.5 %collective-permute-start.34 = (bf16[512,512]{1,0:T(8,128)(2,1)}, bf16[512,512]{1,0:T(8,128)(2,1)}, u32[]{:S(2)}, u32[]{:S(2)}) collective-permute-start(bf16[512,512]{1,0:T(8,128)(2,1)} %get-tuple-element.239), channel_id=1, source_target_pairs={{0,16},{16,0},{1,17},{17,1},{2,18},{18,2},{3,19},{19,3},{4,20},{20... | collective-permute-start | bytes 1572872 | tf_op jit(solution)/shard_map/ppermute | solution.py:476
  202.3 23.4 %collective-permute-start.31 = (bf16[704,512]{1,0:T(8,128)(2,1)}, bf16[704,512]{1,0:T(8,128)(2,1)}, u32[]{:S(2)}, u32[]{:S(2)}) collective-permute-start(bf16[704,512]{1,0:T(8,128)(2,1)} %add_convert_fusion.5), channel_id=1, source_target_pairs={{4,0},{8,12},{5,1},{9,13},{6,2},{10,14},{7,3},{11,15},{20,16},{24,... | collective-permute-start | bytes 2162696 | tf_op jit(solution)/shard_map/ppermute | solution.py:494
  203.6 19.7 %collective-permute-start.32 = (bf16[704,512]{1,0:T(8,128)(2,1)}, bf16[704,512]{1,0:T(8,128)(2,1)}, u32[]{:S(2)}, u32[]{:S(2)}) collective-permute-start(bf16[704,512]{1,0:T(8,128)(2,1)} %get-tuple-element.236), channel_id=1, source_target_pairs={{4,8},{8,4},{5,9},{9,5},{6,10},{10,6},{7,11},{11,7},{20,24},{24,20... | collective-permute-start | bytes 2162696 | tf_op jit(solution)/shard_map/ppermute | solution.py:491
  205.1 23.1 %collective-permute-start.33 = (bf16[704,512]{1,0:T(8,128)(2,1)}, bf16[704,512]{1,0:T(8,128)(2,1)}, u32[]{:S(2)}, u32[]{:S(2)}) collective-permute-start(bf16[704,512]{1,0:T(8,128)(2,1)} %get-tuple-element.237), channel_id=1, source_target_pairs={{0,4},{12,8},{1,5},{13,9},{2,6},{14,10},{3,7},{15,11},{16,20},{28,... | collective-permute-start | bytes 2162696 | tf_op jit(solution)/shard_map/ppermute | solution.py:488
  217.6 18.4 %all-to-all-start.4 = ((bf16[4,64,1024]{2,1,0:T(8,128)(2,1)}), bf16[4,64,1024]{2,1,0:T(8,128)(2,1)S(1)}, u32[]{:S(2)}, u32[]{:S(2)}) async-start(bf16[4,64,1024]{2,1,0:T(8,128)(2,1)} %get-tuple-element.232), calls=%async_computation.4 | async-start | bytes 1048576 | tf_op jit(solution)/shard_map/all_to_all | solution.py:603
  221.3 26.6 %collective-permute-start.41 = (bf16[528,512]{1,0:T(8,128)(2,1)}, bf16[528,512]{1,0:T(8,128)(2,1)S(1)}, u32[]{:S(2)}, u32[]{:S(2)}) collective-permute-start(bf16[528,512]{1,0:T(8,128)(2,1)} %get-tuple-element.251), channel_id=1, source_target_pairs={{0,16},{16,0},{1,17},{17,1},{2,18},{18,2},{3,19},{19,3},{4,20},{20... | collective-permute-start | bytes 1622024 | tf_op jit(solution)/shard_map/ppermute | solution.py:476
  236.1 21.9 %collective-permute-start.36 = (bf16[704,512]{1,0:T(8,128)(2,1)}, bf16[704,512]{1,0:T(8,128)(2,1)}, u32[]{:S(2)}, u32[]{:S(2)}) collective-permute-start(bf16[704,512]{1,0:T(8,128)(2,1)} %add_convert_fusion.2), channel_id=1, source_target_pairs={{4,0},{8,12},{5,1},{9,13},{6,2},{10,14},{7,3},{11,15},{20,16},{24,... | collective-permute-start | bytes 2162696 | tf_op jit(solution)/shard_map/ppermute | solution.py:494
  237.3 20.6 %collective-permute-start.37 = (bf16[704,512]{1,0:T(8,128)(2,1)S(1)}, bf16[704,512]{1,0:T(8,128)(2,1)}, u32[]{:S(2)}, u32[]{:S(2)}) collective-permute-start(bf16[704,512]{1,0:T(8,128)(2,1)S(1)} %add_convert_fusion.1), channel_id=1, source_target_pairs={{4,8},{8,4},{5,9},{9,5},{6,10},{10,6},{7,11},{11,7},{20,24},{24,20... | collective-permute-start | bytes 2162696 | tf_op jit(solution)/shard_map/ppermute | solution.py:491
  238.9 19.0 %collective-permute-start.38 = (bf16[512,512]{1,0:T(8,128)(2,1)S(1)}, bf16[512,512]{1,0:T(8,128)(2,1)}, u32[]{:S(2)}, u32[]{:S(2)}) collective-permute-start(bf16[512,512]{1,0:T(8,128)(2,1)S(1)} %add_convert_fusion.14), channel_id=1, source_target_pairs={{0,4},{12,8},{1,5},{13,9},{2,6},{14,10},{3,7},{15,11},{16,20},{28,... | collective-permute-start | bytes 1572872 | tf_op jit(solution)/shard_map/ppermute | solution.py:488
  246.4 11.5 %collective-permute-start.35 = (bf16[4,64,1024]{2,1,0:T(8,128)(2,1)S(1)}, bf16[4,64,1024]{2,1,0:T(8,128)(2,1)S(1)}, u32[]{:S(2)}, u32[]{:S(2)}) collective-permute-start(bf16[4,64,1024]{2,1,0:T(8,128)(2,1)S(1)} %all-to-all-done.4.refs_0_), channel_id=1, source_target_pairs={{0,2},{1,3},{2,0},{3,1},{4,6},{5,7},{6,4},{7,5},{8,10},{9,11},{10,... | collective-permute-start | bytes 1572872 | tf_op jit(solution)/shard_map/ppermute | solution.py:341
  250.2 24.9 %collective-permute-start.42 = (bf16[528,512]{1,0:T(8,128)(2,1)S(1)}, bf16[528,512]{1,0:T(8,128)(2,1)}, u32[]{:S(2)}, u32[]{:S(2)}) collective-permute-start(bf16[528,512]{1,0:T(8,128)(2,1)S(1)} %add_convert_fusion.11), channel_id=1, source_target_pairs={{0,4},{12,8},{1,5},{13,9},{2,6},{14,10},{3,7},{15,11},{16,20},{28,... | collective-permute-start | bytes 1622024 | tf_op jit(solution)/shard_map/ppermute | solution.py:488
  257.9 14.1 %collective-permute-start.39 = (bf16[4,64,1024]{2,1,0:T(8,128)(2,1)S(1)}, bf16[4,64,1024]{2,1,0:T(8,128)(2,1)S(1)}, u32[]{:S(2)}, u32[]{:S(2)}) collective-permute-start(bf16[4,64,1024]{2,1,0:T(8,128)(2,1)S(1)} %all-to-all-done.4.refs_0_), channel_id=1, source_target_pairs={{0,1},{1,0},{2,3},{3,2},{4,5},{5,4},{6,7},{7,6},{8,9},{9,8},{10,11... | collective-permute-start | bytes 1572872 | tf_op jit(solution)/shard_map/ppermute | solution.py:338
  257.9 20.3 %all-to-all-start.5 = ((bf16[4,64,1024]{2,1,0:T(8,128)(2,1)}), bf16[4,64,1024]{2,1,0:T(8,128)(2,1)S(1)}, u32[]{:S(2)}, u32[]{:S(2)}) async-start(bf16[4,64,1024]{2,1,0:T(8,128)(2,1)} %fusion.5), calls=%async_computation.5 | async-start | bytes 1048576 | tf_op jit(solution)/shard_map/all_to_all | solution.py:622
  264.5 17.8 %collective-permute-start.47 = (bf16[512,512]{1,0:T(8,128)(2,1)}, bf16[512,512]{1,0:T(8,128)(2,1)}, u32[]{:S(2)}, u32[]{:S(2)}) collective-permute-start(bf16[512,512]{1,0:T(8,128)(2,1)} %add_convert_fusion.13), channel_id=1, source_target_pairs={{4,8},{8,4},{5,9},{9,5},{6,10},{10,6},{7,11},{11,7},{20,24},{24,20... | collective-permute-start | bytes 1572872 | tf_op jit(solution)/shard_map/ppermute | solution.py:491
  266.0 6.0 %collective-permute-start.40 = (bf16[4,64,1024]{2,1,0:T(8,128)(2,1)S(1)}, bf16[4,64,1024]{2,1,0:T(8,128)(2,1)S(1)}, u32[]{:S(2)}, u32[]{:S(2)}) collective-permute-start(bf16[4,64,1024]{2,1,0:T(8,128)(2,1)S(1)} %collective-permute-done.35.refs_1_), channel_id=1, source_target_pairs={{0,1},{1,0},{2,3},{3,2},{4,5},{5,4},{6,7},{7,6},{8,9},{9,8},{10,11... | collective-permute-start | bytes 1572872 | tf_op jit(solution)/shard_map/ppermute | solution.py:338
  268.4 26.4 %collective-permute-start.46 = (bf16[704,512]{1,0:T(8,128)(2,1)}, bf16[704,512]{1,0:T(8,128)(2,1)}, u32[]{:S(2)}, u32[]{:S(2)}) collective-permute-start(bf16[704,512]{1,0:T(8,128)(2,1)} %add_convert_fusion), channel_id=1, source_target_pairs={{4,0},{8,12},{5,1},{9,13},{6,2},{10,14},{7,3},{11,15},{20,16},{24,... | collective-permute-start | bytes 2162696 | tf_op jit(solution)/shard_map/ppermute | solution.py:494
  278.2 18.9 %collective-permute-start.43 = (bf16[4,64,1024]{2,1,0:T(8,128)(2,1)S(1)}, bf16[4,64,1024]{2,1,0:T(8,128)(2,1)S(1)}, u32[]{:S(2)}, u32[]{:S(2)}) collective-permute-start(bf16[4,64,1024]{2,1,0:T(8,128)(2,1)S(1)} %all-to-all-done.5.refs_0_), channel_id=1, source_target_pairs={{0,2},{1,3},{2,0},{3,1},{4,6},{5,7},{6,4},{7,5},{8,10},{9,11},{10,... | collective-permute-start | bytes 1572872 | tf_op jit(solution)/shard_map/ppermute | solution.py:341
  280.8 16.9 %collective-permute-start.49 = (bf16[528,512]{1,0:T(8,128)(2,1)S(1)}, bf16[528,512]{1,0:T(8,128)(2,1)}, u32[]{:S(2)}, u32[]{:S(2)}) collective-permute-start(bf16[528,512]{1,0:T(8,128)(2,1)S(1)} %add_convert_fusion.10), channel_id=1, source_target_pairs={{4,8},{8,4},{5,9},{9,5},{6,10},{10,6},{7,11},{11,7},{20,24},{24,20... | collective-permute-start | bytes 1622024 | tf_op jit(solution)/shard_map/ppermute | solution.py:491
  283.7 25.2 %collective-permute-start.48 = (bf16[512,512]{1,0:T(8,128)(2,1)S(1)}, bf16[512,512]{1,0:T(8,128)(2,1)}, u32[]{:S(2)}, u32[]{:S(2)}) collective-permute-start(bf16[512,512]{1,0:T(8,128)(2,1)S(1)} %add_convert_fusion.12), channel_id=1, source_target_pairs={{4,0},{8,12},{5,1},{9,13},{6,2},{10,14},{7,3},{11,15},{20,16},{24,... | collective-permute-start | bytes 1572872 | tf_op jit(solution)/shard_map/ppermute | solution.py:494
  285.0 29.1 %all-to-all-start.6 = ((bf16[4,4,64,256]{3,2,1,0:T(8,128)(2,1)}), bf16[4,4,64,256]{3,2,1,0:T(8,128)(2,1)}, u32[]{:S(2)}, u32[]{:S(2)}) async-start(bf16[4,4,64,256]{3,2,1,0:T(8,128)(2,1)} %get-tuple-element.253), calls=%async_computation.6 | async-start | bytes 1048576 | tf_op jit(solution)/shard_map/all_to_all | solution.py:632
  297.2 19.0 %collective-permute-start.44 = (bf16[4,64,1024]{2,1,0:T(8,128)(2,1)S(1)}, bf16[4,64,1024]{2,1,0:T(8,128)(2,1)S(1)}, u32[]{:S(2)}, u32[]{:S(2)}) collective-permute-start(bf16[4,64,1024]{2,1,0:T(8,128)(2,1)S(1)} %all-to-all-done.5.refs_0_), channel_id=1, source_target_pairs={{0,1},{1,0},{2,3},{3,2},{4,5},{5,4},{6,7},{7,6},{8,9},{9,8},{10,11... | collective-permute-start | bytes 1572872 | tf_op jit(solution)/shard_map/ppermute | solution.py:338
  297.2 19.0 %collective-permute-start.45 = (bf16[4,64,1024]{2,1,0:T(8,128)(2,1)S(1)}, bf16[4,64,1024]{2,1,0:T(8,128)(2,1)S(1)}, u32[]{:S(2)}, u32[]{:S(2)}) collective-permute-start(bf16[4,64,1024]{2,1,0:T(8,128)(2,1)S(1)} %collective-permute-done.43.refs_1_), channel_id=1, source_target_pairs={{0,1},{1,0},{2,3},{3,2},{4,5},{5,4},{6,7},{7,6},{8,9},{9,8},{10,11... | collective-permute-start | bytes 1572872 | tf_op jit(solution)/shard_map/ppermute | solution.py:338
  299.7 23.9 %collective-permute-start.50 = (bf16[528,512]{1,0:T(8,128)(2,1)}, bf16[528,512]{1,0:T(8,128)(2,1)}, u32[]{:S(2)}, u32[]{:S(2)}) collective-permute-start(bf16[528,512]{1,0:T(8,128)(2,1)} %add_convert_fusion.9), channel_id=1, source_target_pairs={{4,0},{8,12},{5,1},{9,13},{6,2},{10,14},{7,3},{11,15},{20,16},{24,... | collective-permute-start | bytes 1622024 | tf_op jit(solution)/shard_map/ppermute | solution.py:494
  325.6 1.2 collective-permute-start.51
  326.8 3.7 %collective-permute-start.52 = (f32[2,512]{1,0:T(2,128)S(1)}, f32[2,512]{1,0:T(2,128)S(1)}, u32[]{:S(2)}, u32[]{:S(2)}) collective-permute-start(f32[2,512]{1,0:T(2,128)S(1)} %slice_add_fusion), channel_id=1, source_target_pairs={{0,2},{1,3},{2,0},{3,1},{4,6},{5,7},{6,4},{7,5},{8,10},{9,11},{10,... | collective-permute-start | bytes 12296 | tf_op jit(solution)/shard_map/ppermute | solution.py:341
  (44 other events, 307.9 us)
